TPU v7x, 32 devices: a whole 2x2x4 slice. The times are simulated.
32 devices in a mesh: dp: 8 (over z, y), fsdp: 4 (over x, core).
Axes of the slice: x: 2, y: 2, z: 4, core: 2. Of those that a mesh axis runs over, the one named last changes fastest.
Arguments:
- doc_hidden: bfloat16 [32, 1024, 1024], P(('dp', 'fsdp')), may hold values from -6 to 6
- query_hidden: bfloat16 [32, 32, 1024], P(('dp', 'fsdp')), may hold values from -6 to 6
- w_query: bfloat16 [1024, 1024], P(('dp', 'fsdp')), may hold values from -0.25 to 0.25
- w_key: bfloat16 [1024, 1024], P(('dp', 'fsdp')), may hold values from -0.25 to 0.25
- w_value: bfloat16 [1024, 1024], P(('dp', 'fsdp')), may hold values from -0.1875 to 0.1875
- w_out: bfloat16 [1024, 1024], P(('dp', 'fsdp')), may hold values from -0.75 to 0.75
- w_up: bfloat16 [1024, 4096], P(('dp', 'fsdp')), may hold values from -0.1875 to 0.1875
- w_down: bfloat16 [4096, 1024], P(('dp', 'fsdp')), may hold values from -0.125 to 0.125
- w_proj: bfloat16 [1024, 128], P(('dp', 'fsdp')), may hold values from -0.1875 to 0.1875
- biases: bfloat16 [6, 1024], P(None, ('dp', 'fsdp')), may hold values from -2 to 2
- gains: bfloat16 [2, 1024], P(None, ('dp', 'fsdp')), may hold values from 0.5 to 1.5
- up_bias: bfloat16 [4096], P(('dp', 'fsdp')), may hold values from -2 to 2
- seg_lengths: int32 [32, 9], P(('dp', 'fsdp')), may hold values from 1 to 512, 1024 in all within a row
- positives: int32 [32], replicated, may hold values from 0 to 255
Outputs:
- loss: float32 [], replicated
- doc_grad: float32 [32, 1024, 1024], P(('dp', 'fsdp'))
- query_grad: float32 [32, 32, 1024], P(('dp', 'fsdp'))
- w_query_grad: float32 [1024, 1024], P(('dp', 'fsdp'))
- w_key_grad: float32 [1024, 1024], P(('dp', 'fsdp'))
- w_value_grad: float32 [1024, 1024], P(('dp', 'fsdp'))
- w_out_grad: float32 [1024, 1024], P(('dp', 'fsdp'))
- w_up_grad: float32 [1024, 4096], P(('dp', 'fsdp'))
- w_down_grad: float32 [4096, 1024], P(('dp', 'fsdp'))
- w_proj_grad: float32 [1024, 128], P(('dp', 'fsdp'))
- biases_grad: float32 [6, 1024], P(None, ('dp', 'fsdp'))
- gains_grad: float32 [2, 1024], P(None, ('dp', 'fsdp'))
- up_bias_grad: float32 [4096], P(('dp', 'fsdp'))
Inputs may be any that keep to these rules, and one draw needn't show every extreme that they name: `seg_lengths`: in each row the first 8 entries are the lengths of the row's documents in order and the last is the padding at the row's end; a row's entries sum to 1024. positives[q] = r * 8 + c names document slot c of packed row r.
All inputs are finite; a program needn't handle non-finite values.
Results may differ from a plain program's by a relative error of at most 0.019.
The roundings to bfloat16 on the way count: a program that leaves them out, or rounds other values in their place, can miss the bound.
Values may be sent and summed in bfloat16 or wider, within the bound.
A program may use at most 256 MiB of HBM per device.

v0:
```python
from functools import partial

import jax
import jax.numpy as jnp
from jax import lax
from jax.sharding import PartitionSpec as P

softness = 0.1
sharpness_divisor = 0.2
norm_eps = 1e-05
unit_eps = 1e-06
head_width = 64
block_queries = 16
masked_score = -1e30


def matmul_plain(left, right):
    return jnp.dot(left, right, preferred_element_type=jnp.float32)


def matmul_right_t(left, right):
    return lax.dot_general(
        left, right, (((1,), (1,)), ((), ())), preferred_element_type=jnp.float32
    )


def matmul_left_t(left, right):
    return lax.dot_general(
        left, right, (((0,), (0,)), ((), ())), preferred_element_type=jnp.float32
    )


def layer_norm_parts(values, gain_row, bias_row):
    center = values - jnp.mean(values, axis=-1, keepdims=True)
    spread = jnp.mean(center * center, axis=-1, keepdims=True)
    inv_scale = lax.rsqrt(spread + norm_eps)
    normed = center * inv_scale
    return (normed * gain_row + bias_row, normed, inv_scale)


def layer_norm_back(grad_out, normed, inv_scale, gain_row):
    grad_norm = grad_out * gain_row
    mean_grad = jnp.mean(grad_norm, axis=-1, keepdims=True)
    mean_proj = jnp.mean(grad_norm * normed, axis=-1, keepdims=True)
    grad_in = inv_scale * (grad_norm - mean_grad - normed * mean_proj)
    return (grad_in, jnp.sum(grad_out * normed, axis=0), jnp.sum(grad_out, axis=0))


def heads_first(matrix, head_count):
    return matrix.reshape(matrix.shape[0], head_count, head_width).transpose(1, 0, 2)


def heads_last(piled_entries):
    return piled_entries.transpose(1, 0, 2).reshape(
        piled_entries.shape[1], piled_entries.shape[0] * piled_entries.shape[2]
    )


def doc_head_forward(operands, allowed):
    query_one, key_one, value_one = operands
    scores = jnp.where(allowed, matmul_right_t(query_one, key_one) * 0.125, masked_score)
    row_top = jnp.max(scores, axis=-1, keepdims=True)
    powers = jnp.exp(scores - row_top)
    denominator = jnp.sum(powers, axis=-1, keepdims=True)
    attn_probs = (powers / denominator).astype(jnp.bfloat16)
    context = matmul_plain(attn_probs, value_one).astype(jnp.bfloat16)
    return (context, (row_top + jnp.log(denominator))[:, 0])


def doc_head_backward(operands, allowed):
    query_one, key_one, value_one, grad_one, logsum_one = operands
    scores = jnp.where(allowed, matmul_right_t(query_one, key_one) * 0.125, masked_score)
    attn_probs = jnp.exp(scores - logsum_one[:, None])
    grad_probs = matmul_right_t(grad_one, value_one)
    inner_sum = jnp.sum(attn_probs * grad_probs, axis=-1, keepdims=True)
    grad_scores = (attn_probs * (grad_probs - inner_sum)).astype(jnp.bfloat16)
    grad_query = matmul_plain(grad_scores, key_one) * 0.125
    grad_key = matmul_left_t(grad_scores, query_one) * 0.125
    grad_value = matmul_left_t(attn_probs.astype(jnp.bfloat16), grad_one)
    return (grad_query, grad_key, grad_value)


def query_attention_forward(query_t, key_t, value_t):
    scores = (
        jnp.einsum("aihw,ajhw->ahij", query_t, key_t, preferred_element_type=jnp.float32) * 0.125
    )
    row_top = jnp.max(scores, axis=-1, keepdims=True)
    powers = jnp.exp(scores - row_top)
    denominator = jnp.sum(powers, axis=-1, keepdims=True)
    attn_probs = (powers / denominator).astype(jnp.bfloat16)
    context = jnp.einsum("ahij,ajhw->aihw", attn_probs, value_t, preferred_element_type=jnp.float32)
    return (context.astype(jnp.bfloat16), row_top + jnp.log(denominator))


def query_attention_backward(query_t, key_t, value_t, grad_t, logsum):
    scores = (
        jnp.einsum("aihw,ajhw->ahij", query_t, key_t, preferred_element_type=jnp.float32) * 0.125
    )
    attn_probs = jnp.exp(scores - logsum)
    grad_probs = jnp.einsum("aihw,ajhw->ahij", grad_t, value_t, preferred_element_type=jnp.float32)
    inner_sum = jnp.sum(attn_probs * grad_probs, axis=-1, keepdims=True)
    grad_scores = (attn_probs * (grad_probs - inner_sum)).astype(jnp.bfloat16)
    grad_query = (
        jnp.einsum("ahij,ajhw->aihw", grad_scores, key_t, preferred_element_type=jnp.float32)
        * 0.125
    )
    grad_key = (
        jnp.einsum("ahij,aihw->ajhw", grad_scores, query_t, preferred_element_type=jnp.float32)
        * 0.125
    )
    grad_value = jnp.einsum(
        "ahij,aihw->ajhw",
        attn_probs.astype(jnp.bfloat16),
        grad_t,
        preferred_element_type=jnp.float32,
    )
    return (grad_query, grad_key, grad_value)


def unit_prefix(vectors, level_width):
    part_cols = vectors[..., :level_width].astype(jnp.float32)
    inv_scale = lax.rsqrt(jnp.sum(part_cols * part_cols, axis=-1, keepdims=True) + unit_eps)
    return (part_cols * inv_scale, inv_scale)


def body(
    doc_hidden,
    query_hidden,
    w_query,
    w_key,
    w_value,
    w_out,
    w_up,
    w_down,
    w_proj,
    biases,
    gains,
    up_bias,
    seg_lengths,
    positives,
):
    params = (
        lax.all_gather(w_query, ("dp", "fsdp"), axis=0, tiled=True),
        lax.all_gather(w_key, ("dp", "fsdp"), axis=0, tiled=True),
        lax.all_gather(w_value, ("dp", "fsdp"), axis=0, tiled=True),
        lax.all_gather(w_out, ("dp", "fsdp"), axis=0, tiled=True),
        lax.all_gather(w_up, ("dp", "fsdp"), axis=0, tiled=True),
        lax.all_gather(w_down, ("dp", "fsdp"), axis=0, tiled=True),
        lax.all_gather(w_proj, ("dp", "fsdp"), axis=0, tiled=True),
        lax.all_gather(biases, ("dp", "fsdp"), axis=1, tiled=True),
        lax.all_gather(gains, ("dp", "fsdp"), axis=1, tiled=True),
        lax.all_gather(up_bias, ("dp", "fsdp"), axis=0, tiled=True),
    )
    (
        full_query,
        full_key,
        full_value,
        full_out,
        full_up,
        full_down,
        full_proj,
        full_biases,
        full_gains,
        full_upbias,
    ) = params
    row_len = doc_hidden.shape[1]
    model_width = doc_hidden.shape[2]
    query_count = query_hidden.shape[0]
    search_span_count = query_hidden.shape[1]
    head_count = model_width // head_width
    doc_slots = seg_lengths.shape[1] - 1
    proj_width = full_proj.shape[1]
    tokens = jnp.concatenate(
        [doc_hidden[0], query_hidden.reshape(query_count * search_span_count, model_width)], axis=0
    )
    doc_ends = jnp.cumsum(seg_lengths[0])
    places = jnp.arange(row_len, dtype=jnp.int32)
    segment = jnp.sum((places[:, None] >= doc_ends[None, :]).astype(jnp.int32), axis=1)
    allowed = segment[:, None] == segment[None, :]
    slot_ids = jnp.arange(doc_slots, dtype=jnp.int32)
    member = (segment[:, None] == slot_ids[None, :]).astype(jnp.float32)
    member_t = (slot_ids[:, None] == segment[None, :]).astype(jnp.float32)
    query_all = (matmul_plain(tokens, full_query) + full_biases[0]).astype(jnp.bfloat16)
    key_all = matmul_plain(tokens, full_key).astype(jnp.bfloat16)
    value_all = (matmul_plain(tokens, full_value) + full_biases[1]).astype(jnp.bfloat16)
    doc_parts = tuple(
        (heads_first(matrix[:row_len], head_count) for matrix in (query_all, key_all, value_all))
    )
    query_parts = tuple(
        (
            matrix[row_len:].reshape(query_count, search_span_count, head_count, head_width)
            for matrix in (query_all, key_all, value_all)
        )
    )
    doc_context, doc_logsum = lax.map(partial(doc_head_forward, allowed=allowed), doc_parts)
    query_context, query_logsum = query_attention_forward(
        query_parts[0], query_parts[1], query_parts[2]
    )
    context = jnp.concatenate(
        [
            heads_last(doc_context),
            query_context.reshape(query_count * search_span_count, model_width),
        ],
        axis=0,
    )
    attn_out = matmul_plain(context, full_out) + full_biases[2]
    first_out, first_normed, first_scale = layer_norm_parts(
        tokens.astype(jnp.float32) + attn_out, full_gains[0], full_biases[3]
    )
    first_low = first_out.astype(jnp.bfloat16)
    up_pre = matmul_plain(first_low, full_up) + full_upbias
    gelu_out = jax.nn.gelu(up_pre, approximate=False).astype(jnp.bfloat16)
    ffn_out = matmul_plain(gelu_out, full_down) + full_biases[4]
    second_out, second_normed, second_scale = layer_norm_parts(
        first_out + ffn_out, full_gains[1], full_biases[5]
    )
    second_low = second_out.astype(jnp.bfloat16)
    vectors = matmul_plain(second_low, full_proj).astype(jnp.bfloat16)
    doc_vectors = vectors[:row_len]
    query_vectors = vectors[row_len:].reshape(query_count, search_span_count, proj_width)
    every_query = lax.all_gather(query_vectors, ("dp", "fsdp"), axis=0, tiled=True)
    query_total = every_query.shape[0]
    block_count = query_total // block_queries
    levels = (proj_width, proj_width * 3 // 4, proj_width // 2)
    doc_prefix = tuple((unit_prefix(doc_vectors, level_width) for level_width in levels))
    doc_lows = tuple((prefix_pair[0].astype(jnp.bfloat16) for prefix_pair in doc_prefix))

    def block_logits(one_block):
        row_total = one_block.shape[0] * search_span_count
        piled_entries = []
        for position in range(3):
            level_width = levels[position]
            unit_rows = (
                unit_prefix(one_block, level_width)[0]
                .astype(jnp.bfloat16)
                .reshape(row_total, level_width)
            )
            scores = matmul_right_t(unit_rows, doc_lows[position])
            doc_sums = jnp.dot(jnp.exp(scores / softness), member, precision=lax.Precision.HIGHEST)
            peak_match_score = jnp.sum(
                (softness * jnp.log(doc_sums)).reshape(
                    one_block.shape[0], search_span_count, doc_slots
                ),
                axis=1,
            )
            piled_entries.append(peak_match_score / (search_span_count * sharpness_divisor))
        return jnp.stack(piled_entries, axis=1)

    blocks = every_query.reshape(block_count, block_queries, search_span_count, proj_width)
    logits = lax.map(block_logits, blocks).reshape(query_total, 3, doc_slots)
    powers = jnp.exp(logits)
    local_sum = jnp.sum(powers, axis=-1)
    my_row = lax.axis_index(("dp", "fsdp"))
    chosen = ((positives - my_row * doc_slots)[:, None] == slot_ids[None, :]).astype(jnp.float32)
    local_pick = jnp.sum(logits * chosen[:, None, :], axis=-1)
    all_sums, picked = lax.psum((local_sum, local_pick), ("dp", "fsdp"))
    loss = jnp.sum(jnp.log(all_sums) - picked) / query_total
    score_derivative = (powers / all_sums[:, :, None] - chosen[:, None, :]) / query_total
    peak_match_derivative = score_derivative / (search_span_count * sharpness_divisor)

    def block_back(carry, inputs):
        one_block, grad_block = inputs
        block_size = one_block.shape[0]
        row_total = block_size * search_span_count
        grad_vectors = jnp.zeros((block_size, search_span_count, proj_width), jnp.float32)
        new_carry = []
        for position in range(3):
            level_width = levels[position]
            unit_full, inv_scale = unit_prefix(one_block, level_width)
            unit_rows = unit_full.astype(jnp.bfloat16).reshape(row_total, level_width)
            scores = matmul_right_t(unit_rows, doc_lows[position])
            score_powers = jnp.exp(scores / softness)
            doc_sums = jnp.dot(score_powers, member, precision=lax.Precision.HIGHEST)
            grad_rows = jnp.broadcast_to(
                grad_block[:, None, position, :], (block_size, search_span_count, doc_slots)
            ).reshape(row_total, doc_slots)
            spread_rows = jnp.dot(grad_rows / doc_sums, member_t, precision=lax.Precision.HIGHEST)
            grad_scores = (score_powers * spread_rows).astype(jnp.bfloat16)
            grad_unit = matmul_plain(grad_scores, doc_lows[position]).reshape(
                block_size, search_span_count, level_width
            )
            new_carry.append(carry[position] + matmul_left_t(grad_scores, unit_rows))
            grad_part = inv_scale * (
                grad_unit - unit_full * jnp.sum(grad_unit * unit_full, axis=-1, keepdims=True)
            )
            grad_vectors = grad_vectors + jnp.pad(
                grad_part, ((0, 0), (0, 0), (0, proj_width - level_width))
            )
        return (tuple(new_carry), grad_vectors)

    start_carry = tuple((jnp.zeros((row_len, level_width), jnp.float32) for level_width in levels))
    grad_blocks = peak_match_derivative.reshape(block_count, block_queries, 3, doc_slots)
    doc_unit_grads, query_terms = lax.scan(block_back, start_carry, (blocks, grad_blocks))
    query_terms = query_terms.reshape(query_total, search_span_count, proj_width)
    query_vec_grad = lax.psum_scatter(query_terms, ("dp", "fsdp"), scatter_dimension=0, tiled=True)
    doc_vec_grad = jnp.zeros((row_len, proj_width), jnp.float32)
    for position in range(3):
        unit_full, inv_scale = doc_prefix[position]
        grad_unit = doc_unit_grads[position]
        grad_part = inv_scale * (
            grad_unit - unit_full * jnp.sum(grad_unit * unit_full, axis=-1, keepdims=True)
        )
        doc_vec_grad = doc_vec_grad + jnp.pad(
            grad_part, ((0, 0), (0, proj_width - levels[position]))
        )
    grad_vectors = jnp.concatenate(
        [doc_vec_grad, query_vec_grad.reshape(query_count * search_span_count, proj_width)], axis=0
    ).astype(jnp.bfloat16)
    params = (
        lax.all_gather(w_query, ("dp", "fsdp"), axis=0, tiled=True),
        lax.all_gather(w_key, ("dp", "fsdp"), axis=0, tiled=True),
        lax.all_gather(w_value, ("dp", "fsdp"), axis=0, tiled=True),
        lax.all_gather(w_out, ("dp", "fsdp"), axis=0, tiled=True),
        lax.all_gather(w_up, ("dp", "fsdp"), axis=0, tiled=True),
        lax.all_gather(w_down, ("dp", "fsdp"), axis=0, tiled=True),
        lax.all_gather(w_proj, ("dp", "fsdp"), axis=0, tiled=True),
        lax.all_gather(biases, ("dp", "fsdp"), axis=1, tiled=True),
        lax.all_gather(gains, ("dp", "fsdp"), axis=1, tiled=True),
        lax.all_gather(up_bias, ("dp", "fsdp"), axis=0, tiled=True),
    )
    (
        full_query,
        full_key,
        full_value,
        full_out,
        full_up,
        full_down,
        full_proj,
        full_biases,
        full_gains,
        full_upbias,
    ) = params
    proj_grad = matmul_left_t(second_low, grad_vectors)
    grad_second = matmul_right_t(grad_vectors, full_proj)
    grad_mid, gain_two, bias_two = layer_norm_back(
        grad_second, second_normed, second_scale, full_gains[1]
    )
    grad_ffn = grad_mid.astype(jnp.bfloat16)
    down_grad = matmul_left_t(gelu_out, grad_ffn)
    down_bias = jnp.sum(grad_ffn, axis=0, dtype=jnp.float32)
    grad_gelu = matmul_right_t(grad_ffn, full_down)
    gelu_back = jax.vjp(lambda pre_act: jax.nn.gelu(pre_act, approximate=False), up_pre)[1]
    grad_up = gelu_back(grad_gelu)[0].astype(jnp.bfloat16)
    upbias_grad = jnp.sum(grad_up, axis=0, dtype=jnp.float32)
    up_grad = matmul_left_t(first_low, grad_up)
    grad_first = grad_mid + matmul_right_t(grad_up, full_up)
    grad_res, gain_one, bias_one = layer_norm_back(
        grad_first, first_normed, first_scale, full_gains[0]
    )
    grad_attn = grad_res.astype(jnp.bfloat16)
    out_bias = jnp.sum(grad_attn, axis=0, dtype=jnp.float32)
    out_grad = matmul_left_t(context, grad_attn)
    grad_context = matmul_right_t(grad_attn, full_out).astype(jnp.bfloat16)
    doc_grad_ctx = heads_first(grad_context[:row_len], head_count)
    doc_back = lax.map(
        partial(doc_head_backward, allowed=allowed), doc_parts + (doc_grad_ctx, doc_logsum)
    )
    query_grad_ctx = grad_context[row_len:].reshape(
        query_count, search_span_count, head_count, head_width
    )
    query_back = query_attention_backward(
        query_parts[0], query_parts[1], query_parts[2], query_grad_ctx, query_logsum
    )
    grad_lows = tuple(
        (
            jnp.concatenate(
                [
                    heads_last(doc_back[number]),
                    query_back[number].reshape(query_count * search_span_count, model_width),
                ],
                axis=0,
            ).astype(jnp.bfloat16)
            for number in range(3)
        )
    )
    grad_q, grad_k, grad_v = grad_lows
    query_bias = jnp.sum(grad_q, axis=0, dtype=jnp.float32)
    value_bias = jnp.sum(grad_v, axis=0, dtype=jnp.float32)
    query_w_grad = matmul_left_t(tokens, grad_q)
    key_w_grad = matmul_left_t(tokens, grad_k)
    value_w_grad = matmul_left_t(tokens, grad_v)
    input_grad = (
        grad_res
        + matmul_right_t(grad_q, full_query)
        + matmul_right_t(grad_k, full_key)
        + matmul_right_t(grad_v, full_value)
    )
    bias_grads = jnp.stack(
        [query_bias, value_bias, out_bias, bias_one, down_bias, bias_two], axis=0
    )
    gain_grads = jnp.stack([gain_one, gain_two], axis=0)
    shards = (
        lax.psum_scatter(query_w_grad, ("dp", "fsdp"), scatter_dimension=0, tiled=True),
        lax.psum_scatter(key_w_grad, ("dp", "fsdp"), scatter_dimension=0, tiled=True),
        lax.psum_scatter(value_w_grad, ("dp", "fsdp"), scatter_dimension=0, tiled=True),
        lax.psum_scatter(out_grad, ("dp", "fsdp"), scatter_dimension=0, tiled=True),
        lax.psum_scatter(up_grad, ("dp", "fsdp"), scatter_dimension=0, tiled=True),
        lax.psum_scatter(down_grad, ("dp", "fsdp"), scatter_dimension=0, tiled=True),
        lax.psum_scatter(proj_grad, ("dp", "fsdp"), scatter_dimension=0, tiled=True),
        lax.psum_scatter(bias_grads, ("dp", "fsdp"), scatter_dimension=1, tiled=True),
        lax.psum_scatter(gain_grads, ("dp", "fsdp"), scatter_dimension=1, tiled=True),
        lax.psum_scatter(upbias_grad, ("dp", "fsdp"), scatter_dimension=0, tiled=True),
    )
    doc_out = input_grad[:row_len].reshape(1, row_len, model_width)
    query_out = input_grad[row_len:].reshape(query_count, search_span_count, model_width)
    return (
        loss,
        doc_out,
        query_out,
        shards[0],
        shards[1],
        shards[2],
        shards[3],
        shards[4],
        shards[5],
        shards[6],
        shards[7],
        shards[8],
        shards[9],
    )


def solution(mesh):
    return jax.shard_map(
        body,
        mesh=mesh,
        in_specs=(
            P(("dp", "fsdp"), None, None),
            P(("dp", "fsdp"), None, None),
            P(("dp", "fsdp"), None),
            P(("dp", "fsdp"), None),
            P(("dp", "fsdp"), None),
            P(("dp", "fsdp"), None),
            P(("dp", "fsdp"), None),
            P(("dp", "fsdp"), None),
            P(("dp", "fsdp"), None),
            P(None, ("dp", "fsdp")),
            P(None, ("dp", "fsdp")),
            P(("dp", "fsdp")),
            P(("dp", "fsdp"), None),
            P(),
        ),
        out_specs=(
            P(),
            P(("dp", "fsdp"), None, None),
            P(("dp", "fsdp"), None, None),
            P(("dp", "fsdp"), None),
            P(("dp", "fsdp"), None),
            P(("dp", "fsdp"), None),
            P(("dp", "fsdp"), None),
            P(("dp", "fsdp"), None),
            P(("dp", "fsdp"), None),
            P(("dp", "fsdp"), None),
            P(None, ("dp", "fsdp")),
            P(None, ("dp", "fsdp")),
            P(("dp", "fsdp")),
        ),
        check_vma=False,
    )
```

profile of v0, /device:TPU:0, one launch (start us, length us, event | category | flops | bytes accessed | tf_op | source)
XLA Modules:
  0.0 2358.2 jit_solution(4018637614217438848)
XLA Ops:
  11.3 43.7 %all-gather.1 = bf16[32,32,6]{1,2,0:T(8,128)(2,1)S(1)} all-gather(bf16[1,32,6]{1,2,0:T(8,128)(2,1)} %bitcast.459), channel_id=1, replica_groups=mesh['dp'=8,'fsdp'=4] {'dp','fsdp'}, dimensions={0}, use_global_device_ids=true | all-gather | bytes 12672 | tf_op jit(solution)/shard_map/all_gather | solution.py:150
  55.7 36.8 %all-gather.3 = bf16[32,1,128]{2,1,0:T(2,128)(2,1)S(1)} all-gather(bf16[1,1,128]{2,1,0:T(2,128)(2,1)} %bitcast.460), channel_id=1, replica_groups=mesh['dp'=8,'fsdp'=4] {'dp','fsdp'}, dimensions={0}, use_global_device_ids=true | all-gather | bytes 8448 | tf_op jit(solution)/shard_map/all_gather | solution.py:152
  93.5 38.3 %all-gather.2 = bf16[32,32,2]{1,2,0:T(2,128)(2,1)S(1)} all-gather(bf16[1,32,2]{1,2,0:T(2,128)(2,1)} %bitcast.461), channel_id=1, replica_groups=mesh['dp'=8,'fsdp'=4] {'dp','fsdp'}, dimensions={0}, use_global_device_ids=true | all-gather | bytes 4224 | tf_op jit(solution)/shard_map/all_gather | solution.py:151
  132.4 40.2 %all_gather.50 = bf16[1024,128]{1,0:T(8,128)(2,1)} all-gather(bf16[32,128]{1,0:T(8,128)(2,1)} %param.30), channel_id=1, replica_groups=mesh['dp'=8,'fsdp'=4] {'dp','fsdp'}, dimensions={0}, use_global_device_ids=true | all-gather | bytes 270336 | tf_op jit(solution)/shard_map/all_gather | solution.py:149
  174.0 4.7 fusion.173
  184.5 3.1 copy.140
  187.6 4.6 convolution_convert_fusion.1
  197.9 3.2 copy.141
  201.1 4.6 fusion.174
  211.5 3.1 copy.142
  214.6 114.9 %while.60 = (s32[]{:T(128)}, bf16[16,1024,64]{1,2,0:T(8,128)(2,1)}, f32[16,1024]{1,0:T(8,128)}, bf16[16,1024,64]{2,1,0:T(8,128)(2,1)}, bf16[16,1024,64]{2,1,0:T(...) while((s32[]{:T(128)}, bf16[16,1024,64]{1,2,0:T(8,128)(2,1)}, ...), condition=%wide.region_5.6_spmd.clone, body=%wide.region_2.5_spmd.clone.sunk | while | flops 284228608 | bytes 13564009 | solution.py:195
  238.9 3.0 fusion.398
  253.2 3.0 fusion.398
  281.9 3.0 fusion.398
  303.3 3.0 fusion.398
  310.5 3.0 fusion.398
  331.5 5.8 fusion.250
  340.7 52.0 %multiply_convert_fusion.4 = (bf16[1056,4096]{1,0:T(8,128)(2,1)}, f32[1056,4096]{1,0:T(8,128)}, f32[1056,4096]{1,0:T(8,128)}) fusion(f32[4096]{0:T(1024)S(1)} %bitcast.447, bf16[1024,4096]{1,0:T(8,128)(2,1)} %all-gather.19.cloned.1.call-done, f32[1056,1024]{1,0:T(8,128)} %copy-done.15, f32[1024]{0:T(1024)S(1)} %bitcast.450, f32[1024]{0:T(1024)S(1)} %bitcast.440, ...), kind=kOutput, calls=%fused_computation.196 | convolution fusion | flops 9149251584 | bytes 56000768 | tf_op jit(solution)/shard_map/dot_general | solution.py:18
  392.7 8.0 all-gather.21.cloned.1.call-done
  400.8 16.3 fusion.251
  420.6 42.5 %all-gather = bf16[1024,128]{1,0:T(8,128)(2,1)} all-gather(bf16[32,128]{1,0:T(8,128)(2,1)S(1)} %slice.166), channel_id=2, replica_groups=mesh['dp'=8,'fsdp'=4] {'dp','fsdp'}, dimensions={0}, use_global_device_ids=true | all-gather | bytes 270336 | tf_op jit(solution)/shard_map/all_gather | solution.py:221
  465.2 24.2 %while.61 = (s32[]{:T(128)}, f32[2,16,3,8]{1,3,2,0:T(8,128)S(1)}, bf16[2,16,32,128]{3,2,1,0:T(8,128)(2,1)}, bf16[1024,128]{1,0:T(8,128)(2,1)}, bf16[1024,96]{1,0...) while((s32[]{:T(128)}, f32[2,16,3,8]{1,3,2,0:T(8,128)S(1)}, ...), condition=%wide.region_22.23_spmd.clone, body=%wide.region_15.22_spmd.clone.sunk | while | flops 455516928 | bytes 14488185 | solution.py:250
  490.2 36.8 %psum.14 = f32[32,3]{0,1:T(4,128)S(1)} all-reduce(f32[32,3]{0,1:T(4,128)S(1)} %reduce_sum.416), channel_id=1, replica_groups=mesh['dp'=8,'fsdp'=4] {'dp','fsdp'}, use_global_device_ids=true, to_apply=%region_24.25 | all-reduce | flops 96 | bytes 768 | tf_op jit(solution)/shard_map/psum | solution.py:256
  527.7 81.5 %while.63 = (s32[]{:T(128)}, f32[1024,128]{1,0:T(8,128)}, f32[1024,96]{0,1:T(8,128)}, f32[1024,64]{0,1:T(8,128)}, f32[2,16,32,128]{3,2,1,0:T(8,128)}, /*index=5*...) while((s32[]{:T(128)}, f32[1024,128]{1,0:T(8,128)}, ...), condition=%wide.region_35.36_spmd.clone.clone.clone, body=%wide.region_28.35_spmd.clone.clone.clone.sunk | while | flops 1217213056 | bytes 57366676 | solution.py:293
  553.1 3.0 fusion.474
  593.7 3.0 fusion.474
  617.1 128.5 %reduce-scatter.15.cloned.1.call-done = f32[1,32,128]{2,1,0:T(8,128)} async-done(((f32[32,32,128]{2,1,0:T(8,128)}), f32[1,32,128]{2,1,0:T(8,128)}) %reduce-scatter.15.cloned.1.call-update) | async-done | bytes 16400 | tf_op jit(solution)/shard_map/reduce_scatter | solution.py:295
  746.3 4.2 multiply_reduce_fusion.2
  753.4 25.0 %convert_reduce_fusion = (f32[4096]{0:T(1024)}, bf16[1056,4096]{1,0:T(8,128)(2,1)}) fusion(f32[1056,4096]{1,0:T(8,128)} %get-tuple-element.603, f32[1056,4096]{1,0:T(8,128)} %get-tuple-element.627, bf16[4096,1024]{1,0:T(8,128)(2,1)} %all-gather.21.cloned.1.call-done, f32[1056,1024]{1,0:T(8,128)} %get-tuple-element.599), kind=kOutput, calls=%fused_computation.194 | convolution fusion | flops 8928653312 | bytes 55984128 | tf_op jit(solution)/shard_map/dot_general | solution.py:22
  778.4 17.7 multiply_reduce_fusion.3
  796.2 3.4 convert_reduce_fusion.4
  806.5 208.3 %while.62 = (s32[]{:T(128)}, bf16[16,1024,64]{1,2,0:T(8,128)(2,1)}, bf16[16,1024,64]{1,2,0:T(8,128)(2,1)}, bf16[16,1024,64]{1,2,0:T(8,128)(2,1)}, bf16[16,1024,6...) while((s32[]{:T(128)}, bf16[16,1024,64]{1,2,0:T(8,128)(2,1)}, ...), condition=%wide.region_46.47_spmd.clone, body=%wide.region_44.46_spmd.clone.sunk | while | flops 681704448 | bytes 33850488 | solution.py:355
  1023.5 7.1 fusion.184
  1031.9 7.2 fusion.175
  1040.7 6.2 fusion.183
  1047.8 7.8 fusion.176
  1056.3 18.6 fusion.245
  1075.0 18.1 fusion.239
  1093.9 37.2 %all-reduce.5 = (f32[32,3]{0,1:T(4,128)S(1)}, f32[4096]{0:T(1024)S(1)}) all-reduce(f32[32,3]{0,1:T(4,128)S(1)} %reduce_sum.418, f32[4096]{0:T(1024)S(1)} %copy-done.71), channel_id=1, replica_groups=mesh['dp'=8,'fsdp'=4] {'dp','fsdp'}, use_global_device_ids=true, to_apply=%region_26.27 | all-reduce | flops 4192 | bytes 33536 | tf_op jit(solution)/shard_map/psum | solution.py:256
  1133.0 5.8 convolution_add_fusion.8
  1149.3 132.4 %reduce-scatter.31.cloned.1.call-done = f32[32,6]{1,0:T(8,128)} async-done(((f32[1024,6]{1,0:T(8,128)}), f32[32,6]{1,0:T(8,128)}) %reduce-scatter.31.cloned.1.call-update) | async-done | bytes 784
  1283.1 132.6 %reduce-scatter.29.cloned.1.call-done = f32[32,128]{1,0:T(8,128)} async-done(((f32[1024,128]{1,0:T(8,128)}), f32[32,128]{1,0:T(8,128)}) %reduce-scatter.29.cloned.1.call-update) | async-done | bytes 16400 | tf_op jit(solution)/shard_map/reduce_scatter | solution.py:399
  1415.7 141.7 %reduce-scatter.17.cloned.1.call-done = f32[32,1024]{1,0:T(8,128)} async-done(((f32[1024,1024]{1,0:T(8,128)}), f32[32,1024]{1,0:T(8,128)}) %reduce-scatter.17.cloned.1.call-update) | async-done | bytes 131088 | tf_op jit(solution)/shard_map/reduce_scatter | solution.py:393
  1557.4 141.3 %reduce-scatter.19.cloned.1.call-done = f32[32,1024]{1,0:T(8,128)} async-done(((f32[1024,1024]{1,0:T(8,128)}), f32[32,1024]{1,0:T(8,128)}) %reduce-scatter.19.cloned.1.call-update) | async-done | bytes 131088 | tf_op jit(solution)/shard_map/reduce_scatter | solution.py:394
  1698.7 141.4 %reduce-scatter.21.cloned.1.call-done = f32[32,1024]{1,0:T(8,128)} async-done(((f32[1024,1024]{1,0:T(8,128)}), f32[32,1024]{1,0:T(8,128)}) %reduce-scatter.21.cloned.1.call-update) | async-done | bytes 131088 | tf_op jit(solution)/shard_map/reduce_scatter | solution.py:395
  1840.2 141.3 %reduce-scatter.23.cloned.1.call-done = f32[32,1024]{1,0:T(8,128)} async-done(((f32[1024,1024]{1,0:T(8,128)}), f32[32,1024]{1,0:T(8,128)}) %reduce-scatter.23.cloned.1.call-update) | async-done | bytes 131088 | tf_op jit(solution)/shard_map/reduce_scatter | solution.py:396
  1981.4 181.5 %reduce-scatter.25.cloned.1.call-done = f32[32,4096]{1,0:T(8,128)} async-done(((f32[1024,4096]{1,0:T(8,128)}), f32[32,4096]{1,0:T(8,128)}) %reduce-scatter.25.cloned.1.call-update) | async-done | bytes 524304 | tf_op jit(solution)/shard_map/reduce_scatter | solution.py:397
  2162.9 187.4 %reduce-scatter.27.cloned.1.call-done = f32[128,1024]{1,0:T(8,128)} async-done(((f32[4096,1024]{1,0:T(8,128)}), f32[128,1024]{1,0:T(8,128)}) %reduce-scatter.27.cloned.1.call-update) | async-done | bytes 524304 | tf_op jit(solution)/shard_map/reduce_scatter | solution.py:398
  (657 shorter events, 487.4 us)
Async XLA Ops:
  7.2 166.8 %all-gather.11.cloned.1.call-start = ((), (), s32[]{:S(2)}) async-start(), calls=%async_computation.10 | async-start | bytes 2162688 | tf_op jit(solution)/shard_map/all_gather | solution.py:143
  7.9 179.7 %all-gather.13.cloned.1.call-start = ((), (), s32[]{:S(2)}) async-start(), calls=%async_computation.11 | async-start | bytes 2162688 | tf_op jit(solution)/shard_map/all_gather | solution.py:144
  8.7 192.5 %all-gather.15.cloned.1.call-start = ((), (), s32[]{:S(2)}) async-start(), calls=%async_computation.12 | async-start | bytes 2162688 | tf_op jit(solution)/shard_map/all_gather | solution.py:145
  9.4 322.1 %all-gather.17.cloned.1.call-start = ((), (), s32[]{:S(2)}) async-start(), calls=%async_computation.13 | async-start | bytes 2162688 | tf_op jit(solution)/shard_map/all_gather | solution.py:146
  10.0 330.7 %all-gather.19.cloned.1.call-start = ((), (), s32[]{:S(2)}) async-start(), calls=%async_computation.14 | async-start | bytes 8650752 | tf_op jit(solution)/shard_map/all_gather | solution.py:147
  10.6 390.2 %all-gather.21.cloned.1.call-start = ((), (), s32[]{:S(2)}) async-start(), calls=%async_computation.15 | async-start | bytes 8650752 | tf_op jit(solution)/shard_map/all_gather | solution.py:148
  11.1 734.5 %reduce-scatter.15.cloned.1.call-start = ((), (), s32[]{:S(2)}) async-start(), calls=%async_computation.16 | async-start | bytes 540672 | tf_op jit(solution)/shard_map/reduce_scatter | solution.py:295
  55.7 345.0 %copy-start.72 = (f32[1,1024]{1,0:T(1,128)}, f32[1,1024]{1,0:T(1,128)S(1)}, u32[]{:S(2)}) copy-start(f32[1,1024]{1,0:T(1,128)S(1)} %get-tuple-element.617) | copy-start | bytes 12292
  132.4 268.3 %copy-start.68 = (f32[1,1024]{1,0:T(1,128)}, f32[1,1024]{1,0:T(1,128)S(1)}, u32[]{:S(2)}) copy-start(f32[1,1024]{1,0:T(1,128)S(1)} %get-tuple-element.622) | copy-start | bytes 12292
  214.6 115.0 %slice-start.3 = ((bf16[1056,1024]{1,0:T(8,128)(2,1)}), bf16[32,1024]{1,0:T(8,128)(2,1)S(1)}, s32[]{:S(2)}) async-start(bf16[1056,1024]{1,0:T(8,128)(2,1)} %copy-done.24), calls=%async_computation.29 | async-start | bytes 131072 | tf_op jit(solution)/shard_map/slice | solution.py:191
  214.6 115.1 %slice-start.2 = ((bf16[1056,1024]{1,0:T(8,128)(2,1)}), bf16[32,1024]{1,0:T(8,128)(2,1)S(1)}, s32[]{:S(2)}) async-start(bf16[1056,1024]{1,0:T(8,128)(2,1)} %copy-done.23), calls=%async_computation.28 | async-start | bytes 131072 | tf_op jit(solution)/shard_map/slice | solution.py:191
  214.6 115.3 %slice-start.4 = ((bf16[1056,1024]{1,0:T(8,128)(2,1)}), bf16[32,1024]{1,0:T(8,128)(2,1)S(1)}, s32[]{:S(2)}) async-start(bf16[1056,1024]{1,0:T(8,128)(2,1)} %copy-done.25), calls=%async_computation.30 | async-start | bytes 131072 | tf_op jit(solution)/shard_map/slice | solution.py:191
  329.6 7.8 copy-start.13
  329.8 7.6 copy-start.35
  329.9 7.4 copy-start.33
  337.4 63.3 %copy-start.51 = (f32[1056]{0:T(1024)}, f32[1056]{0:T(1024)S(1)}, u32[]{:S(2)}) copy-start(f32[1056]{0:T(1024)S(1)} %broadcast_multiply_fusion.5) | copy-start | bytes 12676
  340.1 60.7 %copy-start.63 = (f32[1056]{0:T(1024)}, f32[1056]{0:T(1024)S(1)}, u32[]{:S(2)}) copy-start(f32[1056]{0:T(1024)S(1)} %add_rsqrt_fusion.7) | copy-start | bytes 12676
  340.7 60.1 %copy-start.74 = (f32[1,1024]{1,0:T(1,128)S(1)}, f32[1,1024]{1,0:T(1,128)}, u32[]{:S(2)}) copy-start(f32[1,1024]{1,0:T(1,128)} %get-tuple-element.616) | copy-start | bytes 12292
  419.2 46.0 %copy-start.4 = (bf16[1056,1024]{1,0:T(8,128)(2,1)}, bf16[1056,1024]{1,0:T(8,128)(2,1)S(1)}, u32[]{:S(2)}) copy-start(bf16[1056,1024]{1,0:T(8,128)(2,1)S(1)} %add_convert_fusion.1) | copy-start | bytes 6488068
  419.2 46.0 %copy-start.14 = (s32[1024]{0:T(1024)S(1)}, s32[1024]{0:T(1024)}, u32[]{:S(2)}) copy-start(s32[1024]{0:T(1024)} %copy-done.13) | copy-start | bytes 12292
  419.2 46.0 %copy-start.49 = (f32[2,16,3,8]{1,3,2,0:T(8,128)S(1)}, f32[2,16,3,8]{1,3,2,0:T(8,128)}, u32[]{:S(2)}) copy-start(f32[2,16,3,8]{1,3,2,0:T(8,128)} %custom-call.5) | copy-start | bytes 9220
  419.9 44.3 %copy-start.2 = (bf16[1056,128]{1,0:T(8,128)(2,1)}, bf16[1056,128]{1,0:T(8,128)(2,1)S(1)}, u32[]{:S(2)}) copy-start(bf16[1056,128]{1,0:T(8,128)(2,1)S(1)} %convolution_convert_fusion.2) | copy-start | bytes 811012
  465.2 24.3 %copy-start.50 = (f32[2,16,8]{1,2,0:T(8,128)S(1)}, f32[2,16,8]{1,2,0:T(8,128)}, u32[]{:S(2)}) copy-start(f32[2,16,8]{1,2,0:T(8,128)} %fusion.226) | copy-start | bytes 3076
  558.0 9.3 copy-start.41
  558.4 8.8 copy-start.19
  598.7 9.3 copy-start.41
  599.1 8.8 copy-start.19
  609.2 7.5 copy-start.12
  609.2 7.5 copy-start.56
  609.3 538.7 %reduce-scatter.33.cloned.1.call-start = ((), (), s32[]{:S(2)}) async-start(), calls=%async_computation.25 | async-start | bytes 540672
  610.5 135.8 %copy-start.38 = (bf16[1024,128]{1,0:T(8,128)(2,1)S(1)}, bf16[1024,128]{1,0:T(8,128)(2,1)}, u32[]{:S(2)}) copy-start(bf16[1024,128]{1,0:T(8,128)(2,1)} %all_gather.50) | copy-start | bytes 786436
  610.5 135.8 %copy-start.48 = (f32[1056]{0:T(1024)S(1)}, f32[1056]{0:T(1024)}, u32[]{:S(2)}) copy-start(f32[1056]{0:T(1024)} %copy-done.47) | copy-start | bytes 12676
  610.5 135.8 %copy-start.54 = (f32[1056]{0:T(1024)S(1)}, f32[1056]{0:T(1024)}, u32[]{:S(2)}) copy-start(f32[1056]{0:T(1024)} %copy-done.53) | copy-start | bytes 12676
  610.6 135.8 %copy-start.62 = (f32[1,1024]{1,0:T(1,128)S(1)}, f32[1,1024]{1,0:T(1,128)}, u32[]{:S(2)}) copy-start(f32[1,1024]{1,0:T(1,128)} %get-tuple-element.621) | copy-start | bytes 12292
  616.3 134.2 %slice-start = ((s8[4325376]{0:T(1024)(128)(4,1)}), s8[131072]{0:T(1024)(128)(4,1)S(1)}, s32[]{:S(2)}) async-start(s8[4325376]{0:T(1024)(128)(4,1)} %bitcast.394), calls=%async_computation.26 | async-start | bytes 262144
  753.4 25.0 %copy-start.52 = (f32[1056]{0:T(1024)S(1)}, f32[1056]{0:T(1024)}, u32[]{:S(2)}) copy-start(f32[1056]{0:T(1024)} %copy-done.51) | copy-start | bytes 12676
  753.4 25.0 %copy-start.64 = (f32[1056]{0:T(1024)S(1)}, f32[1056]{0:T(1024)}, u32[]{:S(2)}) copy-start(f32[1056]{0:T(1024)} %copy-done.63) | copy-start | bytes 12676
  753.4 25.0 %copy-start.69 = (f32[1,1024]{1,0:T(1,128)S(1)}, f32[1,1024]{1,0:T(1,128)}, u32[]{:S(2)}) copy-start(f32[1,1024]{1,0:T(1,128)} %copy-done.68) | copy-start | bytes 12292
  1016.1 265.6 %reduce-scatter.31.cloned.1.call-start = ((), (), s32[]{:S(2)}) async-start(), calls=%async_computation.24 | async-start | bytes 540672
  1021.3 394.4 %reduce-scatter.29.cloned.1.call-start = ((), (), s32[]{:S(2)}) async-start(), calls=%async_computation.23 | async-start | bytes 540672 | tf_op jit(solution)/shard_map/reduce_scatter | solution.py:399
  1023.0 534.4 %reduce-scatter.17.cloned.1.call-start = ((), (), s32[]{:S(2)}) async-start(), calls=%async_computation.17 | async-start | bytes 4325376 | tf_op jit(solution)/shard_map/reduce_scatter | solution.py:393
  1030.6 668.1 %reduce-scatter.19.cloned.1.call-start = ((), (), s32[]{:S(2)}) async-start(), calls=%async_computation.18 | async-start | bytes 4325376 | tf_op jit(solution)/shard_map/reduce_scatter | solution.py:394
  1039.1 801.0 %reduce-scatter.21.cloned.1.call-start = ((), (), s32[]{:S(2)}) async-start(), calls=%async_computation.19 | async-start | bytes 4325376 | tf_op jit(solution)/shard_map/reduce_scatter | solution.py:395
  1046.9 934.5 %reduce-scatter.23.cloned.1.call-start = ((), (), s32[]{:S(2)}) async-start(), calls=%async_computation.20 | async-start | bytes 4325376 | tf_op jit(solution)/shard_map/reduce_scatter | solution.py:396
  1055.6 1107.3 %reduce-scatter.25.cloned.1.call-start = ((), (), s32[]{:S(2)}) async-start(), calls=%async_computation.21 | async-start | bytes 17301504 | tf_op jit(solution)/shard_map/reduce_scatter | solution.py:397
  1074.9 1275.4 %reduce-scatter.27.cloned.1.call-start = ((), (), s32[]{:S(2)}) async-start(), calls=%async_computation.22 | async-start | bytes 17301504 | tf_op jit(solution)/shard_map/reduce_scatter | solution.py:398
  1093.1 38.0 %copy-start.66 = (f32[32,3]{0,1:T(4,128)S(1)}, f32[32,3]{0,1:T(4,128)}, u32[]{:S(2)}) copy-start(f32[32,3]{0,1:T(4,128)} %copy-done.65) | copy-start | bytes 1156
  1093.1 39.9 %copy-start.26 = (bf16[16,1024,64]{1,2,0:T(8,128)(2,1)S(1)}, bf16[16,1024,64]{1,2,0:T(8,128)(2,1)}, u32[]{:S(2)}) copy-start(bf16[16,1024,64]{1,2,0:T(8,128)(2,1)} %get-tuple-element.301) | copy-start | bytes 6291460
  (72 other events, 223.4 us)
Sparse Core Ops, SparseCore 0:
  10.8 58.9 all-gather.10
  72.7 55.0 all-gather.12
  130.6 55.1 all-gather.14
  188.6 55.0 all-gather.16
  246.4 75.9 all-gather.18
  325.1 75.6 all-gather.20
  609.4 136.1 reduce-scatter.14
  1016.2 131.7 reduce-scatter.32
  1150.2 131.4 reduce-scatter.30
  1284.4 131.2 reduce-scatter.28
  1418.5 138.8 reduce-scatter.16
  1560.1 138.5 reduce-scatter.18
  1701.6 138.5 reduce-scatter.20
  1842.9 138.5 reduce-scatter.22
  1984.1 178.7 reduce-scatter.24
  2165.7 184.5 reduce-scatter.26
where the time goes:
time: 2370 us; the launch traced here: 2360 us
  waiting for transfers between devices  1340 us (57%)
  matrix products  537 us (23%)
  blocking collectives  276 us (12%)
  local copies, waits for them, and re-layouts  104 us (4%)
  other arithmetic  80 us (3%)
    reduce_scatter x1, waiting for transfers between devices, body(): lax.psum_scatter(down_grad, ('dp', 'fsdp'), scatter_dimension=0, tiled=True)  187 us
    reduce_scatter x1, waiting for transfers between devices, body(): lax.psum_scatter(up_grad, ('dp', 'fsdp'), scatter_dimension=0, tiled=True)  182 us
    dot_general x45, matrix products, matmul_plain(): return jnp.dot(left, right, preferred_element_type=jnp.float32)  177 us
    dot_general x67, matrix products, matmul_right_t(): lax.dot_general(left, right, (((1,), (1,)), ((), ())), preferred_element_...  170 us
    dot_general x45, matrix products, matmul_left_t(): lax.dot_general(left, right, (((0,), (0,)), ((), ())), preferred_element_...  148 us
    reduce_scatter x1, waiting for transfers between devices, body(): lax.psum_scatter(query_w_grad, ('dp', 'fsdp'), scatter_dimension=0, tiled...  142 us
    reduce_scatter x1, waiting for transfers between devices, body(): lax.psum_scatter(value_w_grad, ('dp', 'fsdp'), scatter_dimension=0, tiled...  141 us
    reduce_scatter x1, waiting for transfers between devices, body(): lax.psum_scatter(key_w_grad, ('dp', 'fsdp'), scatter_dimension=0, tiled=T...  141 us
  transfers between devices with their start and end apart: 16, of which 11 were waited for; matrix products, arithmetic and copies ran while one was open for 13% of the time, Pallas kernels for 0%

commit v1 on v0

v1 whole, which is shorter than its diff:
```python
from functools import partial

import jax
import jax.numpy as jnp
from jax import lax
from jax.experimental import pallas as pl
from jax.experimental.pallas import tpu as pltpu
from jax.sharding import PartitionSpec as P

softness = 0.1
sharpness_divisor = 0.2
norm_eps = 1e-05
unit_eps = 1e-06
head_width = 64
block_queries = 16
masked_score = -1e30
rate = 0.125 * 1.4426950408889634
q_rows = 256
k_rows = 256
f32 = jnp.float32
bf16 = jnp.bfloat16
AXES = ("dp", "fsdp")

def matmul_plain(left, right):
    return jnp.dot(left, right, preferred_element_type=jnp.float32)


def matmul_right_t(left, right):
    return lax.dot_general(
        left, right, (((1,), (1,)), ((), ())), preferred_element_type=jnp.float32
    )


def matmul_left_t(left, right):
    return lax.dot_general(
        left, right, (((0,), (0,)), ((), ())), preferred_element_type=jnp.float32
    )


def layer_norm_parts(values, gain_row, bias_row):
    center = values - jnp.mean(values, axis=-1, keepdims=True)
    spread = jnp.mean(center * center, axis=-1, keepdims=True)
    inv_scale = lax.rsqrt(spread + norm_eps)
    normed = center * inv_scale
    return (normed * gain_row + bias_row, normed, inv_scale)


def layer_norm_back(grad_out, normed, inv_scale, gain_row):
    grad_norm = grad_out * gain_row
    mean_grad = jnp.mean(grad_norm, axis=-1, keepdims=True)
    mean_proj = jnp.mean(grad_norm * normed, axis=-1, keepdims=True)
    grad_in = inv_scale * (grad_norm - mean_grad - normed * mean_proj)
    return (grad_in, jnp.sum(grad_out * normed, axis=0), jnp.sum(grad_out, axis=0))


def unit_prefix(vectors, level_width):
    part_cols = vectors[..., :level_width].astype(jnp.float32)
    inv_scale = lax.rsqrt(jnp.sum(part_cols * part_cols, axis=-1, keepdims=True) + unit_eps)
    return (part_cols * inv_scale, inv_scale)


def dot_nt(a,b): return lax.dot_general(a,b,(((1,),(1,)),((),())),preferred_element_type=f32)
def dot_nn(a,b): return jnp.dot(a,b,preferred_element_type=f32)

def stack_heads(block, first):
    zero=jnp.zeros_like(block)
    return jnp.concatenate([jnp.where(first,block,zero),jnp.where(first,zero,block)],axis=0)

def attend_forward(row_len, qb, kb, lanes, span, bounds, segrow, segcol, q_ref,k_ref,v_ref,ctx_ref,lse_ref,qlse_ref,vt_ref):
    units=lanes//128
    tokens=q_ref.shape[0]
    first_q=lax.broadcasted_iota(jnp.int32,(qb,128),1)<64
    top=lax.broadcasted_iota(jnp.int32,(128,qb),0)<64
    vt_ref[...]=v_ref[...].T
    def q_step(i,_):
        rows=pl.ds(pl.multiple_of(i*qb,qb),qb)
        own=segrow[pl.ds(i,1),:]
        stacked=[stack_heads(q_ref[rows,pl.ds(u*128,128)],first_q) for u in range(units)]
        def k_step(j,carry):
            keys=pl.ds(pl.multiple_of(j*kb,kb),kb)
            allowed=segcol[keys,:]==own
            out=[]
            for u in range(units):
                peak,total,acc=carry[u]
                s=jnp.where(allowed,dot_nt(k_ref[keys,pl.ds(u*128,128)],stacked[u]),masked_score)
                new=jnp.maximum(peak,jnp.max(s,axis=0,keepdims=True))
                p=jnp.exp2((s-new)*rate)
                fade=jnp.exp2((peak-new)*rate)
                total=total*fade+jnp.sum(p,axis=0,keepdims=True)
                acc=acc*fade+dot_nn(vt_ref[pl.ds(u*128,128),keys],p.astype(bf16))
                out.append((new,total,acc))
            return tuple(out)
        start=tuple((jnp.full((1,2*qb),masked_score,f32),jnp.zeros((1,2*qb),f32),jnp.zeros((128,2*qb),f32)) for u in range(units))
        res=lax.fori_loop(bounds[0,i],bounds[1,i],k_step,start)
        for u in range(units):
            peak,total,acc=res[u]
            acc=acc/total
            o=jnp.where(top,acc[:,:qb],acc[:,qb:])
            ctx_ref[rows,pl.ds(u*128,128)]=o.T.astype(bf16)
            lse_ref[u,pl.ds(i,1),:]=peak*rate+jnp.log2(total)
        return 0
    lax.fori_loop(0,row_len//qb,q_step,0)
    nq=tokens-row_len
    firstn=lax.broadcasted_iota(jnp.int32,(nq,128),1)<64
    own=lax.broadcasted_iota(jnp.int32,(nq,2*nq),0)//span
    other=(lax.broadcasted_iota(jnp.int32,(nq,2*nq),1)%nq)//span
    keep=own==other
    for u in range(units):
        cols=pl.ds(u*128,128)
        st=stack_heads(q_ref[row_len:,cols],firstn)
        s=jnp.where(keep,dot_nt(k_ref[row_len:,cols],st),masked_score)
        peak=jnp.max(s,axis=0,keepdims=True)
        p=jnp.exp2((s-peak)*rate)
        total=jnp.sum(p,axis=0,keepdims=True)
        p=(p/total).astype(bf16)
        acc=lax.dot_general(p,v_ref[row_len:,cols],(((0,),(0,)),((),())),preferred_element_type=f32)
        ctx_ref[row_len:,cols]=jnp.where(firstn,acc[:nq],acc[nq:]).astype(bf16)
        qlse_ref[u,:,:]=peak*rate+jnp.log2(total)

def attention_forward(qkv,segrow,segcol,bounds,row_len,span):
    tokens=qkv.shape[0]
    width=qkv.shape[1]//3
    qb,kb,lanes=q_rows,k_rows,width
    nq=tokens-row_len
    steps=width//lanes
    def spec(off): return pl.BlockSpec((tokens,lanes),lambda p,*_:(0,p+off))
    full=lambda a: pl.BlockSpec(a.shape,lambda p,*_:(0,)*a.ndim)
    return pl.pallas_call(
        partial(attend_forward,row_len,qb,kb,lanes,span),
        out_shape=(jax.ShapeDtypeStruct((tokens,width),bf16),jax.ShapeDtypeStruct((width//128,row_len//qb,2*qb),f32),jax.ShapeDtypeStruct((width//128,1,2*nq),f32)),
        grid_spec=pltpu.PrefetchScalarGridSpec(num_scalar_prefetch=1,grid=(steps,),
            in_specs=[full(segrow),full(segcol),spec(0),spec(steps),spec(2*steps)],
            out_specs=[pl.BlockSpec((tokens,lanes),lambda p,*_:(0,p)),pl.BlockSpec((lanes//128,row_len//qb,2*qb),lambda p,*_:(p,0,0)),pl.BlockSpec((lanes//128,1,2*nq),lambda p,*_:(p,0,0))],
            scratch_shapes=[pltpu.VMEM((lanes,tokens),bf16)]),
        compiler_params=pltpu.CompilerParams(vmem_limit_bytes=48<<20),
    )(bounds,segrow,segcol,qkv,qkv,qkv)

def attend_backward(row_len, qb, kb, lanes, span, bounds, segrow, segcol, q_ref,k_ref,v_ref,g_ref,o_ref,lse_ref,qlse_ref,out_ref,kt_ref,dka,dva):
    dq_ref=out_ref.at[:,:lanes]; dk_ref=out_ref.at[:,lanes:2*lanes]; dv_ref=out_ref.at[:,2*lanes:]
    units=lanes//128
    tokens=q_ref.shape[0]
    first_q=lax.broadcasted_iota(jnp.int32,(qb,128),1)<64
    top=lax.broadcasted_iota(jnp.int32,(128,qb),0)<64
    kt_ref[...]=k_ref[...].T
    dka[...]=jnp.zeros_like(dka); dva[...]=jnp.zeros_like(dva)
    def q_step(i,_):
        rows=pl.ds(pl.multiple_of(i*qb,qb),qb)
        own=segrow[pl.ds(i,1),:]
        sq=[];sg=[];dr=[];ls=[]
        for u in range(units):
            cols=pl.ds(u*128,128)
            g=g_ref[rows,cols]
            sq.append(stack_heads(q_ref[rows,cols],first_q)); sg.append(stack_heads(g,first_q))
            t=(g.astype(f32)*o_ref[rows,cols].astype(f32)).T
            dr.append(jnp.concatenate([jnp.sum(t[:64],axis=0,keepdims=True),jnp.sum(t[64:],axis=0,keepdims=True)],axis=1))
            ls.append(lse_ref[u,pl.ds(i,1),:])
        def k_step(j,carry):
            keys=pl.ds(pl.multiple_of(j*kb,kb),kb)
            allowed=segcol[keys,:]==own
            out=[]
            for u in range(units):
                cols=pl.ds(u*128,128)
                s=jnp.where(allowed,dot_nt(k_ref[keys,cols],sq[u]),masked_score)
                p=jnp.exp2(s*rate-ls[u])
                dp=dot_nt(v_ref[keys,cols],sg[u])
                ds=(p*(dp-dr[u])).astype(bf16)
                dva[keys,cols]+=dot_nn(p.astype(bf16),sg[u])
                dka[keys,cols]+=dot_nn(ds,sq[u])
                out.append(carry[u]+dot_nn(kt_ref[cols,keys],ds))
            return tuple(out)
        res=lax.fori_loop(bounds[0,i],bounds[1,i],k_step,tuple(jnp.zeros((128,2*qb),f32) for u in range(units)))
        for u in range(units):
            d=jnp.where(top,res[u][:,:qb],res[u][:,qb:])*0.125
            dq_ref[rows,pl.ds(u*128,128)]=d.T.astype(bf16)
        return 0
    lax.fori_loop(0,row_len//qb,q_step,0)
    dk_ref[:row_len,:]=(dka[...]*0.125).astype(bf16)
    dv_ref[:row_len,:]=dva[...].astype(bf16)
    nq=tokens-row_len
    firstn=lax.broadcasted_iota(jnp.int32,(nq,128),1)<64
    own=lax.broadcasted_iota(jnp.int32,(nq,2*nq),0)//span
    other=(lax.broadcasted_iota(jnp.int32,(nq,2*nq),1)%nq)//span
    keep=own==other
    for u in range(units):
        cols=pl.ds(u*128,128)
        q=q_ref[row_len:,cols]; k=k_ref[row_len:,cols]; v=v_ref[row_len:,cols]; g=g_ref[row_len:,cols]
        st=stack_heads(q,firstn); sg=stack_heads(g,firstn)
        s=jnp.where(keep,dot_nt(k,st),masked_score)
        p=jnp.exp2(s*rate-qlse_ref[u])
        dp=dot_nt(v,sg)
        ds=(p*(dp-jnp.sum(p*dp,axis=0,keepdims=True))).astype(bf16)
        dv_ref[row_len:,cols]=dot_nn(p.astype(bf16),sg).astype(bf16)
        dk_ref[row_len:,cols]=(dot_nn(ds,st)*0.125).astype(bf16)
        d=lax.dot_general(ds,k,(((0,),(0,)),((),())),preferred_element_type=f32)
        dq_ref[row_len:,cols]=(jnp.where(firstn,d[:nq],d[nq:])*0.125).astype(bf16)

def attention_backward(qkv,g,o,lse,qlse,segrow,segcol,bounds,row_len,span):
    tokens,width=g.shape
    qb,kb,lanes=q_rows,k_rows,width
    nq=tokens-row_len
    steps=width//lanes
    def spec(off): return pl.BlockSpec((tokens,lanes),lambda p,*_:(0,p+off))
    full=lambda a: pl.BlockSpec(a.shape,lambda p,*_:(0,)*a.ndim)
    sd=jax.ShapeDtypeStruct((tokens,3*width),bf16)
    return pl.pallas_call(
        partial(attend_backward,row_len,qb,kb,lanes,span),
        out_shape=sd,
        grid_spec=pltpu.PrefetchScalarGridSpec(num_scalar_prefetch=1,grid=(steps,),
            in_specs=[full(segrow),full(segcol)]+[spec(0),spec(1),spec(2),spec(0),spec(0)]+[pl.BlockSpec((lanes//128,row_len//qb,2*qb),lambda p,*_:(p,0,0)),pl.BlockSpec((lanes//128,1,2*nq),lambda p,*_:(p,0,0))],
            out_specs=pl.BlockSpec((tokens,3*lanes),lambda p,*_:(0,0)),
            scratch_shapes=[pltpu.VMEM((lanes,tokens),bf16),pltpu.VMEM((row_len,lanes),f32),pltpu.VMEM((row_len,lanes),f32)]),
        compiler_params=pltpu.CompilerParams(vmem_limit_bytes=56<<20),
    )(bounds,segrow,segcol,qkv,qkv,qkv,g,o,lse,qlse)


class Links:
    def __init__(self, dp, fsdp):
        self.dp, self.fsdp, self.count = dp, fsdp, dp * fsdp
        low = [1 << b for b in range(fsdp.bit_length() - 1)]
        high = [fsdp << b for b in range(dp.bit_length() - 1)]
        inner, rest = low[:1], low[1:]
        near, far = high[:1], high[1:][::-1]
        self.orders = (far + rest[::-1] + near + inner, far + near + rest[::-1] + inner)

    def swap(self, value, bit):
        return lax.ppermute(value, AXES, [(d, d ^ bit) for d in range(self.count)])

    def owners(self, order):
        slots = jnp.arange(self.count, dtype=jnp.int32)
        mixed = jnp.zeros_like(slots)
        for place, bit in enumerate(order):
            mixed = mixed + ((slots >> place) & 1) * bit
        return mixed ^ lax.axis_index(AXES)

    def places(self, order):
        other = jnp.arange(self.count, dtype=jnp.int32) ^ lax.axis_index(AXES)
        slots = jnp.zeros_like(other)
        for place, bit in enumerate(order):
            slots = slots + jnp.where((other & bit) != 0, 1 << place, 0)
        return slots

    def gather_slots(self, shard, order):
        held = shard[None]
        for bit in order:
            held = jnp.concatenate([held, self.swap(held, bit)], axis=0)
        return held

    def gather(self, shard, lane=0):
        order = self.orders[lane]
        return jnp.take(self.gather_slots(shard, order), self.places(order), axis=0)

    def scatter_sum(self, blocks, lane=0, wire=bf16):
        order = self.orders[lane]
        held = jnp.take(blocks.astype(wire), self.owners(order), axis=0)
        for bit in order[::-1]:
            half = held.shape[0] // 2
            arrived = self.swap(held[half:], bit)
            held = held[:half].astype(f32) + arrived.astype(f32)
            if half > 1:
                held = held.astype(wire)
        return held[0]

    def total(self, value):
        for bit in self.orders[0]:
            value = value + self.swap(value, bit)
        return value


class PlainLinks(Links):
    def gather(self, shard, lane=0):
        return lax.all_gather(shard, AXES, axis=0)

    def scatter_sum(self, blocks, lane=0, wire=bf16):
        return lax.psum_scatter(blocks, AXES, scatter_dimension=0, tiled=False)

    def total(self, value):
        return lax.psum(value, AXES)


def make_links(mesh):
    dp, fsdp = mesh.shape["dp"], mesh.shape["fsdp"]
    paired = (dp & (dp - 1)) == 0 and (fsdp & (fsdp - 1)) == 0 and dp * fsdp <= 64
    return (Links if paired else PlainLinks)(dp, fsdp)


def tables(lengths, row_len):
    ends = jnp.cumsum(lengths)
    starts = ends - lengths
    places = jnp.arange(row_len, dtype=jnp.int32)
    segment = jnp.sum((places[:, None] >= ends[None, :]).astype(jnp.int32), axis=1)
    rows = segment.reshape(row_len // q_rows, q_rows)
    ids = jnp.arange(lengths.shape[0])
    low = jnp.sum(jnp.where(rows[:, :1] == ids[None, :], starts[None, :], 0), axis=1)
    high = jnp.sum(jnp.where(rows[:, -1:] == ids[None, :], ends[None, :], 0), axis=1)
    bounds = jnp.stack([low // k_rows, (high + k_rows - 1) // k_rows]).astype(jnp.int32)
    return segment, jnp.concatenate([rows, rows], axis=1), segment[:, None], bounds


def body(
    links,
    doc_hidden,
    query_hidden,
    w_query,
    w_key,
    w_value,
    w_out,
    w_up,
    w_down,
    w_proj,
    biases,
    gains,
    up_bias,
    seg_lengths,
    positives,
):
    count = links.count
    row_len = doc_hidden.shape[1]
    model_width = doc_hidden.shape[2]
    query_count = query_hidden.shape[0]
    span = query_hidden.shape[1]
    doc_slots = seg_lengths.shape[1] - 1
    proj_width = w_proj.shape[1]
    ff = up_bias.shape[0] * count
    shard_cols = biases.shape[1]
    shard_rows = w_query.shape[0]
    part = model_width // 2
    small = jnp.concatenate(
        [biases.reshape(-1), gains.reshape(-1), up_bias.reshape(-1)], axis=0
    )[None]

    def rows_of(full):
        return full.reshape(full.shape[0] * full.shape[1], full.shape[2])

    small_full = links.gather(small, 0).reshape(count, -1)
    full_biases = (
        small_full[:, : 6 * shard_cols]
        .reshape(count, 6, shard_cols)
        .transpose(1, 0, 2)
        .reshape(6, model_width)
        .astype(f32)
    )
    full_gains = (
        small_full[:, 6 * shard_cols : 8 * shard_cols]
        .reshape(count, 2, shard_cols)
        .transpose(1, 0, 2)
        .reshape(2, model_width)
        .astype(f32)
    )
    full_upbias = small_full[:, 8 * shard_cols :].reshape(ff).astype(f32)

    full_qkv = []
    for side in range(2):
        cut = slice(side * part, (side + 1) * part)
        shard = jnp.concatenate([w_query[:, cut], w_key[:, cut], w_value[:, cut]], axis=1)
        full_qkv.append(rows_of(links.gather(shard, side)))
    out_proj = rows_of(links.gather(jnp.concatenate([w_out, w_proj], axis=1), 0))
    full_out, full_proj = out_proj[:, :model_width], out_proj[:, model_width:]
    full_up = rows_of(links.gather(w_up, 0))
    full_down = rows_of(links.gather(w_down, 1))

    tokens = jnp.concatenate(
        [doc_hidden[0], query_hidden.reshape(query_count * span, model_width)], axis=0
    )
    segment, segrow, segcol, bounds = tables(seg_lengths[0], row_len)
    slot_ids = jnp.arange(doc_slots, dtype=jnp.int32)
    member = (segment[:, None] == slot_ids[None, :]).astype(f32)
    member_t = (slot_ids[:, None] == segment[None, :]).astype(f32)
    zero_row = jnp.zeros((part,), f32)
    qkv, contexts, saved = [], [], []
    for side in range(2):
        cut = slice(side * part, (side + 1) * part)
        bias = jnp.concatenate([full_biases[0, cut], zero_row, full_biases[1, cut]])
        qkv.append((matmul_plain(tokens, full_qkv[side]) + bias).astype(bf16))
        context, lse, query_lse = attention_forward(
            qkv[side], segrow, segcol, bounds, row_len, span
        )
        contexts.append(context)
        saved.append((lse, query_lse))
    attn_out = (
        matmul_plain(contexts[0], full_out[:part])
        + matmul_plain(contexts[1], full_out[part:])
        + full_biases[2]
    )
    first_out, first_normed, first_scale = layer_norm_parts(
        tokens.astype(f32) + attn_out, full_gains[0], full_biases[3]
    )
    first_low = first_out.astype(bf16)
    up_pre = matmul_plain(first_low, full_up) + full_upbias
    gelu_out = jax.nn.gelu(up_pre, approximate=False).astype(bf16)
    ffn_out = matmul_plain(gelu_out, full_down) + full_biases[4]
    second_out, second_normed, second_scale = layer_norm_parts(
        first_out + ffn_out, full_gains[1], full_biases[5]
    )
    second_low = second_out.astype(bf16)
    vectors = matmul_plain(second_low, full_proj).astype(bf16)
    doc_vectors = vectors[:row_len]
    query_vectors = vectors[row_len:].reshape(query_count * span, proj_width)
    every_query = links.gather(query_vectors).reshape(count * query_count, span, proj_width)
    query_total = every_query.shape[0]
    block_count = query_total // block_queries
    levels = (proj_width, proj_width * 3 // 4, proj_width // 2)
    doc_prefix = tuple((unit_prefix(doc_vectors, level_width) for level_width in levels))
    doc_lows = tuple((prefix_pair[0].astype(bf16) for prefix_pair in doc_prefix))

    def block_logits(one_block):
        row_total = one_block.shape[0] * span
        piled_entries = []
        for position in range(3):
            level_width = levels[position]
            unit_rows = (
                unit_prefix(one_block, level_width)[0].astype(bf16).reshape(row_total, level_width)
            )
            scores = matmul_right_t(unit_rows, doc_lows[position])
            doc_sums = jnp.dot(jnp.exp(scores / softness), member, precision=lax.Precision.HIGHEST)
            peak_match_score = jnp.sum(
                (softness * jnp.log(doc_sums)).reshape(one_block.shape[0], span, doc_slots),
                axis=1,
            )
            piled_entries.append(peak_match_score / (span * sharpness_divisor))
        return jnp.stack(piled_entries, axis=1)

    blocks = every_query.reshape(block_count, block_queries, span, proj_width)
    logits = lax.map(block_logits, blocks).reshape(query_total, 3, doc_slots)
    powers = jnp.exp(logits)
    local_sum = jnp.sum(powers, axis=-1)
    my_row = lax.axis_index(AXES)
    chosen = ((positives - my_row * doc_slots)[:, None] == slot_ids[None, :]).astype(f32)
    local_pick = jnp.sum(logits * chosen[:, None, :], axis=-1)
    both = links.total(jnp.concatenate([local_sum, local_pick], axis=1))
    all_sums, picked = both[:, :3], both[:, 3:]
    loss = jnp.sum(jnp.log(all_sums) - picked) / query_total
    score_derivative = (powers / all_sums[:, :, None] - chosen[:, None, :]) / query_total
    peak_match_derivative = score_derivative / (span * sharpness_divisor)

    def block_back(carry, inputs):
        one_block, grad_block = inputs
        block_size = one_block.shape[0]
        row_total = block_size * span
        grad_vectors = jnp.zeros((block_size, span, proj_width), f32)
        new_carry = []
        for position in range(3):
            level_width = levels[position]
            unit_full, inv_scale = unit_prefix(one_block, level_width)
            unit_rows = unit_full.astype(bf16).reshape(row_total, level_width)
            scores = matmul_right_t(unit_rows, doc_lows[position])
            score_powers = jnp.exp(scores / softness)
            doc_sums = jnp.dot(score_powers, member, precision=lax.Precision.HIGHEST)
            grad_rows = jnp.broadcast_to(
                grad_block[:, None, position, :], (block_size, span, doc_slots)
            ).reshape(row_total, doc_slots)
            spread_rows = jnp.dot(grad_rows / doc_sums, member_t, precision=lax.Precision.HIGHEST)
            grad_scores = (score_powers * spread_rows).astype(bf16)
            grad_unit = matmul_plain(grad_scores, doc_lows[position]).reshape(
                block_size, span, level_width
            )
            new_carry.append(carry[position] + matmul_left_t(grad_scores, unit_rows))
            grad_part = inv_scale * (
                grad_unit - unit_full * jnp.sum(grad_unit * unit_full, axis=-1, keepdims=True)
            )
            grad_vectors = grad_vectors + jnp.pad(
                grad_part, ((0, 0), (0, 0), (0, proj_width - level_width))
            )
        return (tuple(new_carry), grad_vectors)

    start_carry = tuple((jnp.zeros((row_len, level_width), f32) for level_width in levels))
    grad_blocks = peak_match_derivative.reshape(block_count, block_queries, 3, doc_slots)
    doc_unit_grads, query_terms = lax.scan(block_back, start_carry, (blocks, grad_blocks))
    query_terms = query_terms.reshape(count, query_count * span, proj_width)
    query_vec_grad = links.scatter_sum(query_terms, wire=f32)
    doc_vec_grad = jnp.zeros((row_len, proj_width), f32)
    for position in range(3):
        unit_full, inv_scale = doc_prefix[position]
        grad_unit = doc_unit_grads[position]
        grad_part = inv_scale * (
            grad_unit - unit_full * jnp.sum(grad_unit * unit_full, axis=-1, keepdims=True)
        )
        doc_vec_grad = doc_vec_grad + jnp.pad(
            grad_part, ((0, 0), (0, proj_width - levels[position]))
        )
    grad_vectors = jnp.concatenate([doc_vec_grad, query_vec_grad], axis=0).astype(bf16)

    def spread_rows_of(full):
        return full.reshape(count, full.shape[0] // count, full.shape[1])

    proj_grad = matmul_left_t(second_low, grad_vectors)
    grad_second = matmul_right_t(grad_vectors, full_proj)
    grad_mid, gain_two, bias_two = layer_norm_back(
        grad_second, second_normed, second_scale, full_gains[1]
    )
    grad_ffn = grad_mid.astype(bf16)
    down_grad = matmul_left_t(gelu_out, grad_ffn)
    down_shard = links.scatter_sum(spread_rows_of(down_grad), 1)
    down_bias = jnp.sum(grad_ffn, axis=0, dtype=f32)
    grad_gelu = matmul_right_t(grad_ffn, full_down)
    gelu_back = jax.vjp(lambda pre_act: jax.nn.gelu(pre_act, approximate=False), up_pre)[1]
    grad_up = gelu_back(grad_gelu)[0].astype(bf16)
    upbias_grad = jnp.sum(grad_up, axis=0, dtype=f32)
    up_grad = matmul_left_t(first_low, grad_up)
    up_shard = links.scatter_sum(spread_rows_of(up_grad), 0)
    grad_first = grad_mid + matmul_right_t(grad_up, full_up)
    grad_res, gain_one, bias_one = layer_norm_back(
        grad_first, first_normed, first_scale, full_gains[0]
    )
    grad_attn = grad_res.astype(bf16)
    out_bias = jnp.sum(grad_attn, axis=0, dtype=f32)
    out_grad = jnp.concatenate([matmul_left_t(c, grad_attn) for c in contexts], axis=0)
    out_proj_shard = links.scatter_sum(
        spread_rows_of(jnp.concatenate([out_grad, proj_grad], axis=1)), 0
    )
    input_grad = grad_res
    query_bias, value_bias, qkv_shards = [], [], []
    for side in range(2):
        grad_context = matmul_right_t(
            grad_attn, full_out[side * part : (side + 1) * part]
        ).astype(bf16)
        grad_qkv = attention_backward(
            qkv[side], grad_context, contexts[side], *saved[side], segrow, segcol, bounds,
            row_len, span,
        )
        query_bias.append(jnp.sum(grad_qkv[:, :part], axis=0, dtype=f32))
        value_bias.append(jnp.sum(grad_qkv[:, 2 * part :], axis=0, dtype=f32))
        qkv_grad = matmul_left_t(tokens, grad_qkv)
        qkv_shards.append(links.scatter_sum(spread_rows_of(qkv_grad), side))
        input_grad = input_grad + matmul_right_t(grad_qkv, full_qkv[side])
    bias_grads = jnp.stack(
        [
            jnp.concatenate(query_bias),
            jnp.concatenate(value_bias),
            out_bias,
            bias_one,
            down_bias,
            bias_two,
            gain_one,
            gain_two,
        ],
        axis=0,
    )
    small_grads = jnp.concatenate(
        [
            bias_grads.reshape(8, count, shard_cols).transpose(1, 0, 2).reshape(count, -1),
            upbias_grad.reshape(count, -1),
        ],
        axis=1,
    )
    small_shard = links.scatter_sum(small_grads[:, None, :], 0, wire=f32)[0]
    shards = [
        jnp.concatenate([s[:, i * part : (i + 1) * part] for s in qkv_shards], axis=1)
        for i in range(3)
    ]
    return (
        loss,
        input_grad[:row_len].reshape(1, row_len, model_width),
        input_grad[row_len:].reshape(query_count, span, model_width),
        shards[0],
        shards[1],
        shards[2],
        out_proj_shard[:, :model_width],
        up_shard,
        down_shard,
        out_proj_shard[:, model_width:],
        small_shard[: 6 * shard_cols].reshape(6, shard_cols),
        small_shard[6 * shard_cols : 8 * shard_cols].reshape(2, shard_cols),
        small_shard[8 * shard_cols :],
    )


def solution(mesh):
    return jax.shard_map(
        partial(body, make_links(mesh)),
        mesh=mesh,
        in_specs=(
            P(("dp", "fsdp"), None, None),
            P(("dp", "fsdp"), None, None),
            P(("dp", "fsdp"), None),
            P(("dp", "fsdp"), None),
            P(("dp", "fsdp"), None),
            P(("dp", "fsdp"), None),
            P(("dp", "fsdp"), None),
            P(("dp", "fsdp"), None),
            P(("dp", "fsdp"), None),
            P(None, ("dp", "fsdp")),
            P(None, ("dp", "fsdp")),
            P(("dp", "fsdp")),
            P(("dp", "fsdp"), None),
            P(),
        ),
        out_specs=(
            P(),
            P(("dp", "fsdp"), None, None),
            P(("dp", "fsdp"), None, None),
            P(("dp", "fsdp"), None),
            P(("dp", "fsdp"), None),
            P(("dp", "fsdp"), None),
            P(("dp", "fsdp"), None),
            P(("dp", "fsdp"), None),
            P(("dp", "fsdp"), None),
            P(("dp", "fsdp"), None),
            P(None, ("dp", "fsdp")),
            P(None, ("dp", "fsdp")),
            P(("dp", "fsdp")),
        ),
        check_vma=False,
    )
```

time: 2370 us -> 903 us (0.38)
  waiting for transfers between devices: 1340 us -> 205 us
  matrix products: 537 us -> 245 us
  blocking collectives: 276 us -> 0 us
  Pallas kernels: 0 us -> 98.3 us
  starting transfers between devices: 1.22 us -> 85.8 us
  local copies, waits for them, and re-layouts: 104 us -> 140 us
  other arithmetic: 80 us -> 115 us
    reduce_scatter x8 -> x0, waiting for transfers between devices: 1200 us -> none  [the longest x1 187 us: body(): lax.psum_scatter(down_grad, ('dp', 'fsdp'), scatter_dimension=0, tiled=True)]
    ppermute x0 -> x75, waiting for transfers between devices: none -> 205 us  [swap(): return lax.ppermute(value, AXES, [(d, d ^ bit) for d in range(self.count)])]
    all_gather x5 -> x0, blocking collectives: 201 us -> none  [the longest x1 43.7 us: body(): lax.all_gather(biases, ('dp', 'fsdp'), axis=1, tiled=True)]
    unnamed x18 -> x0, waiting for transfers between devices: 137 us -> none
    dot_general x67 -> x19, matrix products: 170 us -> 68.7 us  [matmul_right_t(): lax.dot_general(left, right, (((1,), (1,)), ((), ())), preferred_element_...]
    pallas_call x0 -> x4, Pallas kernels: none -> 98.3 us  [the longest x2 54.7 us: attention_backward(): pl.pallas_call(partial(attend_backward, row_len, qb, kb, lanes, span), ou...]
    dot_general x45 -> x13, matrix products: 177 us -> 81.4 us  [matmul_plain(): return jnp.dot(left, right, preferred_element_type=jnp.float32)]
    dot_general x45 -> x13, matrix products: 148 us -> 56.8 us  [matmul_left_t(): lax.dot_general(left, right, (((0,), (0,)), ((), ())), preferred_element_...]
  transfers between devices with their start and end apart: 16 -> 75, of which waited for: 11 -> 42; matrix products, arithmetic and copies ran while one was open for 13% -> 19% of each run, Pallas kernels for 0% -> 5%
where the time goes in v1:
time: 903 us; the launch traced here: 895 us
  matrix products  245 us (27%)
  waiting for transfers between devices  205 us (23%)
  local copies, waits for them, and re-layouts  140 us (16%)
  other arithmetic  115 us (13%)
  Pallas kernels  98.3 us (11%)
  starting transfers between devices  85.8 us (10%)
    ppermute x75, waiting for transfers between devices, swap(): return lax.ppermute(value, AXES, [(d, d ^ bit) for d in range(self.count)])  205 us
    ppermute x75, starting transfers between devices, swap(): return lax.ppermute(value, AXES, [(d, d ^ bit) for d in range(self.count)])  85.8 us
    dot_general x13, matrix products, matmul_plain(): return jnp.dot(left, right, preferred_element_type=jnp.float32)  81.4 us
    dot_general x19, matrix products, matmul_right_t(): lax.dot_general(left, right, (((1,), (1,)), ((), ())), preferred_element_...  68.7 us
    dot_general x13, matrix products, matmul_left_t(): lax.dot_general(left, right, (((0,), (0,)), ((), ())), preferred_element_...  56.8 us
    pallas_call x2, Pallas kernels, attention_backward(): pl.pallas_call(partial(attend_backward, row_len, qb, kb, lanes, span), ou...  54.7 us
    pallas_call x2, Pallas kernels, attention_forward(): pl.pallas_call(partial(attend_forward, row_len, qb, kb, lanes, span), out...  43.6 us
    gather x7, local copies, waits for them, and re-layouts, gather(): return jnp.take(self.gather_slots(shard, order), self.places(order), axis=0)  29.8 us
  transfers between devices with their start and end apart: 75, of which 42 were waited for; matrix products, arithmetic and copies ran while one was open for 19% of the time, Pallas kernels for 5%

profile of v1, /device:TPU:0, one launch (start us, length us, event | category | flops | bytes accessed | tf_op | source)
XLA Modules:
  0.0 894.6 jit_solution(6659855949272273412)
XLA Ops:
  48.7 5.1 collective-permute-done.11
  78.6 5.3 collective-permute-done.26
  88.8 15.1 %collective-permute-done.3 = bf16[8,32,1536]{2,1,0:T(8,128)(2,1)S(1)} collective-permute-done((bf16[8,32,1536]{2,1,0:T(8,128)(2,1)S(1)}, bf16[8,32,1536]{2,1,0:T(8,128)(2,1)S(1)}, u32[]{:S(2)}, u32[]{:S(2)}) %collective-permute-start.3) | collective-permute-done | bytes 786464 | tf_op jit(solution)/shard_map/ppermute | solution.py:226
  107.0 4.8 collective-permute-done.22
  114.1 12.3 %collective-permute-done.27 = bf16[4,128,1024]{2,1,0:T(8,128)(2,1)S(1)} collective-permute-done((bf16[4,128,1024]{2,1,0:T(8,128)(2,1)S(1)}, bf16[4,128,1024]{2,1,0:T(8,128)(2,1)S(1)}, u32[]{:S(2)}, u32[]{:S(2)}) %collective-permute-start.27) | collective-permute-done | bytes 1048608 | tf_op jit(solution)/shard_map/ppermute | solution.py:226
  141.0 4.3 gather_fusion.4
  151.9 4.3 gather_fusion.6
  156.2 12.7 %collective-permute-done.23 = bf16[8,32,4096]{2,1,0:T(8,128)(2,1)} collective-permute-done((bf16[8,32,4096]{2,1,0:T(8,128)(2,1)}, bf16[8,32,4096]{2,1,0:T(8,128)(2,1)}, u32[]{:S(2)}, u32[]{:S(2)}) %collective-permute-start.23) | collective-permute-done | bytes 2097184 | tf_op jit(solution)/shard_map/ppermute | solution.py:226
  169.0 4.2 constant_dynamic-update-slice_fusion.35
  173.2 4.3 fusion.117.q_ref.k_ref.v_ref
  177.5 21.8 %shard_map.237 = (bf16[1056,512]{1,0:T(8,128)(2,1)S(1)}, f32[4,4,512]{2,1,0:T(4,128)S(1)}, f32[4,1,64]{2,1,0:T(1,128)S(1)}) custom-call(s32[2,4]{1,0:T(2,128)S(1)} %pad_add_fusion.bounds, s32[4,512]{1,0:T(4,128)S(1)} %constant_dynamic-update-slice_fusion.segrow, s32[1024,1]{1,0:T(8,128)S(1)} %copy.74.segcol, ...), custom_call_target="tpu_custom_call" | custom-call | tf_op jit(solution)/shard_map/pallas_call | solution.py:128
  199.7 5.4 constant_dynamic-update-slice_fusion.46
  209.7 21.8 %shard_map.238 = (bf16[1056,512]{1,0:T(8,128)(2,1)S(1)}, f32[4,4,512]{2,1,0:T(4,128)S(1)}, f32[4,1,64]{2,1,0:T(1,128)S(1)}) custom-call(s32[2,4]{1,0:T(2,128)S(1)} %pad_add_fusion.bounds, s32[4,512]{1,0:T(4,128)S(1)} %constant_dynamic-update-slice_fusion.segrow, s32[1024,1]{1,0:T(8,128)S(1)} %copy.74.segcol, ...), custom_call_target="tpu_custom_call" | custom-call | tf_op jit(solution)/shard_map/pallas_call | solution.py:128
  240.0 8.9 gather_fusion.7
  248.9 7.6 broadcast_select_fusion.3
  256.5 4.8 constant_dynamic-update-slice_fusion.51
  261.3 8.4 gather_fusion.8
  269.7 7.6 broadcast_select_fusion.2
  277.4 51.9 %multiply_convert_fusion.3 = (bf16[1056,4096]{1,0:T(8,128)(2,1)}, f32[1056,4096]{1,0:T(8,128)}, f32[1056,4096]{1,0:T(8,128)}) fusion(f32[4096]{0:T(1024)S(1)} %fusion.159, bf16[1024,4096]{1,0:T(8,128)(2,1)} %bitcast.347, f32[1056,1024]{1,0:T(8,128)S(1)} %bitcast.323, f32[1024]{0:T(1024)S(1)} %add.697, f32[1024]{0:T(1024)S(1)} %mul.558, ...), kind=kOutput, calls=%fused_computation.153 | convolution fusion | flops 9149251584 | bytes 56000768 | tf_op jit(solution)/shard_map/dot_general | solution.py:25
  329.3 13.2 %fusion.221 = (f32[1056]{0:T(1024)S(1)}, f32[1056,1024]{1,0:T(8,128)S(1)}) fusion(f32[1024]{0:T(1024)S(1)} %copy-done.47, bf16[1056,4096]{1,0:T(8,128)(2,1)} %get-tuple-element.407, bf16[4096,1024]{1,0:T(8,128)(2,1)S(1)} %bitcast.350, f32[1024]{0:T(1024)S(1)} %add.697, f32[1024]{0:T(1024)S(1)} %mul.558, f32[1056]{0:T(1024)S(1)} %add_rsqrt_fusion.7, ...), kind=kOutput, calls=%fused_computation.561 | convolution fusion | flops 8865938432 | bytes 25715072 | tf_op jit(solution)/shard_map/dot_general | solution.py:25
  366.6 18.8 %while.32 = (s32[]{:T(128)}, f32[2,16,3,8]{1,3,2,0:T(8,128)S(1)}, bf16[2,16,32,128]{3,2,1,0:T(8,128)(2,1)S(1)}, bf16[1024,128]{1,0:T(8,128)(2,1)S(1)}, bf16[1024...) while((s32[]{:T(128)}, f32[2,16,3,8]{1,3,2,0:T(8,128)S(1)}, ...), condition=%wide.region_18.23_spmd.clone, body=%wide.region_11.22_spmd.clone.sunk | while | flops 455516928 | bytes 14488185 | solution.py:423
  403.1 49.4 %while.33 = (s32[]{:T(128)}, f32[1024,128]{1,0:T(8,128)S(1)}, f32[1024,96]{0,1:T(8,128)S(1)}, f32[1024,64]{0,1:T(8,128)S(1)}, f32[2,16,32,128]{3,2,1,0:T(8,128)}...) while((s32[]{:T(128)}, f32[1024,128]{1,0:T(8,128)S(1)}, ...), condition=%wide.region_29.34_spmd.clone.clone.clone, body=%wide.region_22.33_spmd.clone.clone.clone.sunk | while | flops 1217213056 | bytes 37461660 | solution.py:467
  458.2 4.2 collective-permute-done.41
  478.9 4.3 multiply_reduce_fusion.1
  484.7 13.5 %convolution_convert_fusion = bf16[4096,1024]{1,0:T(8,128)(2,1)} fusion(bf16[1056,4096]{1,0:T(8,128)(2,1)S(1)} %bitcast.399, f32[1056,1024]{1,0:T(8,128)S(1)} %get-tuple-element.403), kind=kOutput, calls=%fused_computation.175 | convolution fusion | flops 8863645696 | bytes 21364736 | tf_op jit(solution)/shard_map/dot_general | solution.py:35
  498.2 24.8 %convert_reduce_fusion = (f32[4096]{0:T(1024)S(1)}, bf16[1056,4096]{1,0:T(8,128)(2,1)}) fusion(f32[1056,4096]{1,0:T(8,128)} %get-tuple-element.408, f32[1056,4096]{1,0:T(8,128)} %get-tuple-element.498, bf16[4096,1024]{1,0:T(8,128)(2,1)} %bitcast.349, f32[1056,1024]{1,0:T(8,128)} %copy-done.26), kind=kOutput, calls=%fused_computation.151 | convolution fusion | flops 8928653312 | bytes 55984128 | tf_op jit(solution)/shard_map/dot_general | solution.py:29
  523.0 17.8 %multiply_reduce_fusion.2 = (f32[1024]{0:T(1024)S(1)}, f32[1056]{0:T(1024)S(1)}, f32[1056]{0:T(1024)S(1)}, f32[1024]{0:T(1024)S(1)}, f32[1056,1024]{1,0:T(8,128)S(1)}) fusion(f32[1056,1024]{1,0:T(8,128)} %copy-done.13, f32[1056]{0:T(1024)S(1)} %add_rsqrt_fusion.7, f32[1056]{0:T(1024)S(1)} %broadcast_multiply_fusion.5, f32[1024]{0:T(1024)S(1)} %mul.558, ...), kind=kOutput, calls=%fused_computation.188 | convolution fusion | flops 8869179392 | bytes 30044672 | tf_op jit(solution)/shard_map/dot_general | solution.py:29
  540.9 18.0 %convolution_convert_fusion.1 = bf16[1024,4096]{1,0:T(8,128)(2,1)} fusion(bf16[1056,4096]{1,0:T(8,128)(2,1)} %get-tuple-element.504, f32[1056,1024]{1,0:T(8,128)} %copy-done.13, f32[1024]{0:T(1024)S(1)} %copy-done.46, f32[1024]{0:T(1024)S(1)} %mul.558, f32[1056]{0:T(1024)S(1)} %add_rsqrt_fusion.7, f32[1056]{0:T(1024)S(1)} %broadcast_multiply_fusion.5), kind=kOutput, calls=%fused_computation.178 | convolution fusion | flops 8867971072 | bytes 21381376 | tf_op jit(solution)/shard_map/dot_general | solution.py:35
  570.6 27.5 %shard_map.240 = bf16[1056,1536]{1,0:T(8,128)(2,1)} custom-call(s32[2,4]{1,0:T(2,128)} %copy-done.10, s32[4,512]{1,0:T(4,128)} %copy-done.7, s32[1024,1]{1,0:T(8,128)} %copy-done.2, bf16[1056,1536]{1,0:T(8,128)(2,1)} %copy-done.1, bf16[1056,1536]{1,0:T(8,128)(2,1)} %copy-done.1, bf16[1056,1536]{1,0:T(8,128)(2,1)} %copy-done.1, ...), custom_call_target="tpu_custom_call" | custom-call | tf_op jit(solution)/shard_map/pallas_call | solution.py:205
  600.0 7.6 convolution_convert_fusion.2
  607.6 27.2 %shard_map.239 = bf16[1056,1536]{1,0:T(8,128)(2,1)} custom-call(s32[2,4]{1,0:T(2,128)} %copy-done.10, s32[4,512]{1,0:T(4,128)} %copy-done.7, s32[1024,1]{1,0:T(8,128)} %copy-done.2, bf16[1056,1536]{1,0:T(8,128)(2,1)} %copy-done, bf16[1056,1536]{1,0:T(8,128)(2,1)} %copy-done, bf16[1056,1536]{1,0:T(8,128)(2,1)} %copy-done, ...), custom_call_target="tpu_custom_call" | custom-call | tf_op jit(solution)/shard_map/pallas_call | solution.py:205
  636.7 7.6 convolution_convert_fusion.3
  644.8 8.6 gather_fusion.12
  653.4 7.5 broadcast_select_fusion.1
  668.6 6.6 convolution_add_fusion.10
  675.2 5.2 convolution_add_fusion.9
  680.5 8.8 gather_fusion.13
  693.4 7.6 broadcast_select_fusion
  703.1 4.6 gather_fusion.9
  712.2 4.9 slice_bitcast_fusion.3
  739.8 6.6 collective-permute-done.57
  759.3 10.7 %collective-permute-done.51 = bf16[8,32,1536]{2,1,0:T(8,128)(2,1)S(1)} collective-permute-done((bf16[8,32,1536]{2,1,0:T(8,128)(2,1)S(1)}, bf16[8,32,1536]{2,1,0:T(8,128)(2,1)S(1)}, u32[]{:S(2)}, u32[]{:S(2)}) %collective-permute-start.51) | collective-permute-done | bytes 786464 | tf_op jit(solution)/shard_map/ppermute | solution.py:226
  776.4 5.0 add_convert_fusion.1
  801.8 26.6 %collective-permute-done.66 = bf16[8,128,1024]{2,1,0:T(8,128)(2,1)S(1)} collective-permute-done((bf16[8,128,1024]{2,1,0:T(8,128)(2,1)S(1)}, bf16[8,128,1024]{2,1,0:T(8,128)(2,1)S(1)}, u32[]{:S(2)}, u32[]{:S(2)}) %collective-permute-start.66) | collective-permute-done | bytes 2097184 | tf_op jit(solution)/shard_map/ppermute | solution.py:226
  833.1 19.1 %collective-permute-done.67 = bf16[4,128,1024]{2,1,0:T(8,128)(2,1)S(1)} collective-permute-done((bf16[4,128,1024]{2,1,0:T(8,128)(2,1)S(1)}, bf16[4,128,1024]{2,1,0:T(8,128)(2,1)S(1)}, u32[]{:S(2)}, u32[]{:S(2)}) %collective-permute-start.67) | collective-permute-done | bytes 1048608 | tf_op jit(solution)/shard_map/ppermute | solution.py:226
  856.5 13.9 %collective-permute-done.68 = bf16[2,128,1024]{2,1,0:T(8,128)(2,1)S(1)} collective-permute-done((bf16[2,128,1024]{2,1,0:T(8,128)(2,1)S(1)}, bf16[2,128,1024]{2,1,0:T(8,128)(2,1)S(1)}, u32[]{:S(2)}, u32[]{:S(2)}) %collective-permute-start.68) | collective-permute-done | bytes 524320 | tf_op jit(solution)/shard_map/ppermute | solution.py:226
  871.0 8.8 collective-permute-done.63
  881.7 6.6 collective-permute-done.69
  (691 shorter events, 361.1 us)
Async XLA Ops:
  2.9 23.4 %collective-permute-start.5 = (bf16[1,1,384]{2,0,1:T(2,128)(2,1)S(1)}, bf16[1,1,384]{2,0,1:T(2,128)(2,1)S(1)}, u32[]{:S(2)}, u32[]{:S(2)}) collective-permute-start(bf16[1,1,384]{2,0,1:T(2,128)(2,1)S(1)} %broadcast_in_dim_broadcast_in_dim.3), channel_id=1, source_target_pairs={{0,16},{1,17},{2,18},{3,19},{4,20},{5,21},{6,22},{7,23},{8,24},{9,... | collective-permute-start | bytes 2312 | tf_op jit(solution)/shard_map/ppermute | solution.py:226
  7.9 34.5 %collective-permute-start.10 = (bf16[1,32,1152]{2,1,0:T(8,128)(2,1)S(1)}, bf16[1,32,1152]{2,1,0:T(8,128)(2,1)S(1)}, u32[]{:S(2)}, u32[]{:S(2)}) collective-permute-start(bf16[1,32,1152]{2,1,0:T(8,128)(2,1)S(1)} %maximum_bitcast_fusion.3), channel_id=1, source_target_pairs={{0,16},{1,17},{2,18},{3,19},{4,20},{5,21},{6,22},{7,23},{8,24},{9,... | collective-permute-start | bytes 221192 | tf_op jit(solution)/shard_map/ppermute | solution.py:226
  10.2 34.9 %collective-permute-start = (bf16[1,32,1536]{2,1,0:T(8,128)(2,1)S(1)}, bf16[1,32,1536]{2,1,0:T(8,128)(2,1)S(1)}, u32[]{:S(2)}, u32[]{:S(2)}) collective-permute-start(bf16[1,32,1536]{2,1,0:T(8,128)(2,1)S(1)} %maximum_bitcast_fusion.1), channel_id=1, source_target_pairs={{0,16},{1,17},{2,18},{3,19},{4,20},{5,21},{6,22},{7,23},{8,24},{9,... | collective-permute-start | bytes 294920 | tf_op jit(solution)/shard_map/ppermute | solution.py:226
  13.2 32.1 %collective-permute-start.15 = (bf16[1,32,1536]{2,1,0:T(8,128)(2,1)S(1)}, bf16[1,32,1536]{2,1,0:T(8,128)(2,1)S(1)}, u32[]{:S(2)}, u32[]{:S(2)}) collective-permute-start(bf16[1,32,1536]{2,1,0:T(8,128)(2,1)S(1)} %maximum_bitcast_fusion.2), channel_id=1, source_target_pairs={{0,16},{1,17},{2,18},{3,19},{4,20},{5,21},{6,22},{7,23},{8,24},{9,... | collective-permute-start | bytes 294920 | tf_op jit(solution)/shard_map/ppermute | solution.py:226
  13.3 43.1 %collective-permute-start.20 = (bf16[1,32,4096]{2,1,0:T(8,128)(2,1)}, bf16[1,32,4096]{2,1,0:T(8,128)(2,1)S(1)}, u32[]{:S(2)}, u32[]{:S(2)}) collective-permute-start(bf16[1,32,4096]{2,1,0:T(8,128)(2,1)} %bitcast.359), channel_id=1, source_target_pairs={{0,16},{1,17},{2,18},{3,19},{4,20},{5,21},{6,22},{7,23},{8,24},{9,... | collective-permute-start | bytes 786440 | tf_op jit(solution)/shard_map/ppermute | solution.py:226
  38.7 17.9 %collective-permute-start.25 = (bf16[1,128,1024]{2,1,0:T(8,128)(2,1)S(1)}, bf16[1,128,1024]{2,1,0:T(8,128)(2,1)S(1)}, u32[]{:S(2)}, u32[]{:S(2)}) collective-permute-start(bf16[1,128,1024]{2,1,0:T(8,128)(2,1)S(1)} %bitcast.363), channel_id=1, source_target_pairs={{0,16},{1,17},{2,18},{3,19},{4,20},{5,21},{6,22},{7,23},{8,24},{9,... | collective-permute-start | bytes 786440 | tf_op jit(solution)/shard_map/ppermute | solution.py:226
  42.4 11.4 %collective-permute-start.11 = (bf16[2,32,1152]{2,1,0:T(8,128)(2,1)S(1)}, bf16[2,32,1152]{2,1,0:T(8,128)(2,1)S(1)}, u32[]{:S(2)}, u32[]{:S(2)}) collective-permute-start(bf16[2,32,1152]{2,1,0:T(8,128)(2,1)S(1)} %pad_maximum_fusion.19), channel_id=1, source_target_pairs={{0,8},{1,9},{2,10},{3,11},{4,12},{5,13},{6,14},{7,15},{8,0},{9,1},... | collective-permute-start | bytes 442376 | tf_op jit(solution)/shard_map/ppermute | solution.py:226
  45.1 15.3 %collective-permute-start.1 = (bf16[2,32,1536]{2,1,0:T(8,128)(2,1)S(1)}, bf16[2,32,1536]{2,1,0:T(8,128)(2,1)S(1)}, u32[]{:S(2)}, u32[]{:S(2)}) collective-permute-start(bf16[2,32,1536]{2,1,0:T(8,128)(2,1)S(1)} %pad_maximum_fusion.15), channel_id=1, source_target_pairs={{0,8},{1,9},{2,10},{3,11},{4,12},{5,13},{6,14},{7,15},{8,0},{9,1},... | collective-permute-start | bytes 589832 | tf_op jit(solution)/shard_map/ppermute | solution.py:226
  45.3 16.9 %collective-permute-start.16 = (bf16[2,32,1536]{2,1,0:T(8,128)(2,1)S(1)}, bf16[2,32,1536]{2,1,0:T(8,128)(2,1)S(1)}, u32[]{:S(2)}, u32[]{:S(2)}) collective-permute-start(bf16[2,32,1536]{2,1,0:T(8,128)(2,1)S(1)} %pad_maximum_fusion.16), channel_id=1, source_target_pairs={{0,8},{1,9},{2,10},{3,11},{4,12},{5,13},{6,14},{7,15},{8,0},{9,1},... | collective-permute-start | bytes 589832 | tf_op jit(solution)/shard_map/ppermute | solution.py:226
  53.9 11.8 %collective-permute-start.12 = (bf16[4,32,1152]{2,1,0:T(8,128)(2,1)S(1)}, bf16[4,32,1152]{2,1,0:T(8,128)(2,1)S(1)}, u32[]{:S(2)}, u32[]{:S(2)}) collective-permute-start(bf16[4,32,1152]{2,1,0:T(8,128)(2,1)S(1)} %pad_maximum_fusion.13), channel_id=1, source_target_pairs={{0,2},{1,3},{2,0},{3,1},{4,6},{5,7},{6,4},{7,5},{8,10},{9,11},{10,... | collective-permute-start | bytes 884744 | tf_op jit(solution)/shard_map/ppermute | solution.py:226
  56.5 21.7 %collective-permute-start.21 = (bf16[2,32,4096]{2,1,0:T(8,128)(2,1)S(1)}, bf16[2,32,4096]{2,1,0:T(8,128)(2,1)S(1)}, u32[]{:S(2)}, u32[]{:S(2)}) collective-permute-start(bf16[2,32,4096]{2,1,0:T(8,128)(2,1)S(1)} %pad_maximum_fusion.9), channel_id=1, source_target_pairs={{0,8},{1,9},{2,10},{3,11},{4,12},{5,13},{6,14},{7,15},{8,0},{9,1},... | collective-permute-start | bytes 1572872 | tf_op jit(solution)/shard_map/ppermute | solution.py:226
  56.6 27.3 %collective-permute-start.26 = (bf16[2,128,1024]{2,1,0:T(8,128)(2,1)S(1)}, bf16[2,128,1024]{2,1,0:T(8,128)(2,1)S(1)}, u32[]{:S(2)}, u32[]{:S(2)}) collective-permute-start(bf16[2,128,1024]{2,1,0:T(8,128)(2,1)S(1)} %pad_maximum_fusion.10), channel_id=1, source_target_pairs={{0,8},{1,9},{2,10},{3,11},{4,12},{5,13},{6,14},{7,15},{8,0},{9,1},... | collective-permute-start | bytes 1572872 | tf_op jit(solution)/shard_map/ppermute | solution.py:226
  62.3 12.1 %collective-permute-start.17 = (bf16[4,32,1536]{2,1,0:T(8,128)(2,1)S(1)}, bf16[4,32,1536]{2,1,0:T(8,128)(2,1)S(1)}, u32[]{:S(2)}, u32[]{:S(2)}) collective-permute-start(bf16[4,32,1536]{2,1,0:T(8,128)(2,1)S(1)} %pad_maximum_fusion.12), channel_id=1, source_target_pairs={{0,4},{1,5},{2,6},{3,7},{4,0},{5,1},{6,2},{7,3},{8,12},{9,13},{10,... | collective-permute-start | bytes 1179656 | tf_op jit(solution)/shard_map/ppermute | solution.py:226
  65.8 22.1 %collective-permute-start.13 = (bf16[8,32,1152]{2,1,0:T(8,128)(2,1)S(1)}, bf16[8,32,1152]{2,1,0:T(8,128)(2,1)S(1)}, u32[]{:S(2)}, u32[]{:S(2)}) collective-permute-start(bf16[8,32,1152]{2,1,0:T(8,128)(2,1)S(1)} %pad_maximum_fusion.8), channel_id=1, source_target_pairs={{0,4},{1,5},{2,6},{3,7},{4,0},{5,1},{6,2},{7,3},{8,12},{9,13},{10,... | collective-permute-start | bytes 1769480 | tf_op jit(solution)/shard_map/ppermute | solution.py:226
  69.2 34.7 %collective-permute-start.3 = (bf16[8,32,1536]{2,1,0:T(8,128)(2,1)S(1)}, bf16[8,32,1536]{2,1,0:T(8,128)(2,1)S(1)}, u32[]{:S(2)}, u32[]{:S(2)}) collective-permute-start(bf16[8,32,1536]{2,1,0:T(8,128)(2,1)S(1)} %pad_maximum_fusion.6), channel_id=1, source_target_pairs={{0,4},{1,5},{2,6},{3,7},{4,0},{5,1},{6,2},{7,3},{8,12},{9,13},{10,... | collective-permute-start | bytes 2359304 | tf_op jit(solution)/shard_map/ppermute | solution.py:226
  74.4 30.7 %collective-permute-start.18 = (bf16[8,32,1536]{2,1,0:T(8,128)(2,1)S(1)}, bf16[8,32,1536]{2,1,0:T(8,128)(2,1)S(1)}, u32[]{:S(2)}, u32[]{:S(2)}) collective-permute-start(bf16[8,32,1536]{2,1,0:T(8,128)(2,1)S(1)} %pad_maximum_fusion.7), channel_id=1, source_target_pairs={{0,2},{1,3},{2,0},{3,1},{4,6},{5,7},{6,4},{7,5},{8,10},{9,11},{10,... | collective-permute-start | bytes 2359304 | tf_op jit(solution)/shard_map/ppermute | solution.py:226
  78.3 33.5 %collective-permute-start.22 = (bf16[4,32,4096]{2,1,0:T(8,128)(2,1)S(1)}, bf16[4,32,4096]{2,1,0:T(8,128)(2,1)S(1)}, u32[]{:S(2)}, u32[]{:S(2)}) collective-permute-start(bf16[4,32,4096]{2,1,0:T(8,128)(2,1)S(1)} %pad_maximum_fusion.4), channel_id=1, source_target_pairs={{0,2},{1,3},{2,0},{3,1},{4,6},{5,7},{6,4},{7,5},{8,10},{9,11},{10,... | collective-permute-start | bytes 3145736 | tf_op jit(solution)/shard_map/ppermute | solution.py:226
  84.1 42.3 %collective-permute-start.27 = (bf16[4,128,1024]{2,1,0:T(8,128)(2,1)S(1)}, bf16[4,128,1024]{2,1,0:T(8,128)(2,1)S(1)}, u32[]{:S(2)}, u32[]{:S(2)}) collective-permute-start(bf16[4,128,1024]{2,1,0:T(8,128)(2,1)S(1)} %pad_maximum_fusion.5), channel_id=1, source_target_pairs={{0,4},{1,5},{2,6},{3,7},{4,0},{5,1},{6,2},{7,3},{8,12},{9,13},{10,... | collective-permute-start | bytes 3145736 | tf_op jit(solution)/shard_map/ppermute | solution.py:226
  88.8 44.0 %collective-permute-start.14 = (bf16[16,32,1152]{2,1,0:T(8,128)(2,1)S(1)}, bf16[16,32,1152]{2,1,0:T(8,128)(2,1)S(1)}, u32[]{:S(2)}, u32[]{:S(2)}) collective-permute-start(bf16[16,32,1152]{2,1,0:T(8,128)(2,1)S(1)} %get-tuple-element.428), channel_id=1, source_target_pairs={{0,1},{1,0},{2,3},{3,2},{4,5},{5,4},{6,7},{7,6},{8,9},{9,8},{10,11... | collective-permute-start | bytes 3538952 | tf_op jit(solution)/shard_map/ppermute | solution.py:226
  105.2 33.1 %collective-permute-start.4 = (bf16[16,32,1536]{2,1,0:T(8,128)(2,1)}, bf16[16,32,1536]{2,1,0:T(8,128)(2,1)}, u32[]{:S(2)}, u32[]{:S(2)}) collective-permute-start(bf16[16,32,1536]{2,1,0:T(8,128)(2,1)} %get-tuple-element.426), channel_id=1, source_target_pairs={{0,1},{1,0},{2,3},{3,2},{4,5},{5,4},{6,7},{7,6},{8,9},{9,8},{10,11... | collective-permute-start | bytes 4718600 | tf_op jit(solution)/shard_map/ppermute | solution.py:226
  106.4 42.8 %collective-permute-start.19 = (bf16[16,32,1536]{2,1,0:T(8,128)(2,1)}, bf16[16,32,1536]{2,1,0:T(8,128)(2,1)}, u32[]{:S(2)}, u32[]{:S(2)}) collective-permute-start(bf16[16,32,1536]{2,1,0:T(8,128)(2,1)} %get-tuple-element.424), channel_id=1, source_target_pairs={{0,1},{1,0},{2,3},{3,2},{4,5},{5,4},{6,7},{7,6},{8,9},{9,8},{10,11... | collective-permute-start | bytes 4718600 | tf_op jit(solution)/shard_map/ppermute | solution.py:226
  113.2 55.7 %collective-permute-start.23 = (bf16[8,32,4096]{2,1,0:T(8,128)(2,1)}, bf16[8,32,4096]{2,1,0:T(8,128)(2,1)}, u32[]{:S(2)}, u32[]{:S(2)}) collective-permute-start(bf16[8,32,4096]{2,1,0:T(8,128)(2,1)} %pad_maximum_fusion.2), channel_id=1, source_target_pairs={{0,4},{1,5},{2,6},{3,7},{4,0},{5,1},{6,2},{7,3},{8,12},{9,13},{10,... | collective-permute-start | bytes 6291464 | tf_op jit(solution)/shard_map/ppermute | solution.py:226
  127.9 71.9 %collective-permute-start.28 = (bf16[8,128,1024]{2,1,0:T(8,128)(2,1)}, bf16[8,128,1024]{2,1,0:T(8,128)(2,1)}, u32[]{:S(2)}, u32[]{:S(2)}) collective-permute-start(bf16[8,128,1024]{2,1,0:T(8,128)(2,1)} %pad_maximum_fusion.3), channel_id=1, source_target_pairs={{0,2},{1,3},{2,0},{3,1},{4,6},{5,7},{6,4},{7,5},{8,10},{9,11},{10,... | collective-permute-start | bytes 6291464 | tf_op jit(solution)/shard_map/ppermute | solution.py:226
  173.2 64.4 %collective-permute-start.24 = (bf16[16,32,4096]{2,1,0:T(8,128)(2,1)}, bf16[16,32,4096]{2,1,0:T(8,128)(2,1)S(1)}, u32[]{:S(2)}, u32[]{:S(2)}) collective-permute-start(bf16[16,32,4096]{2,1,0:T(8,128)(2,1)} %get-tuple-element.418), channel_id=1, source_target_pairs={{0,1},{1,0},{2,3},{3,2},{4,5},{5,4},{6,7},{7,6},{8,9},{9,8},{10,11... | collective-permute-start | bytes 12582920 | tf_op jit(solution)/shard_map/ppermute | solution.py:226
  205.1 51.4 %collective-permute-start.29 = (bf16[16,128,1024]{2,1,0:T(8,128)(2,1)}, bf16[16,128,1024]{2,1,0:T(8,128)(2,1)}, u32[]{:S(2)}, u32[]{:S(2)}) collective-permute-start(bf16[16,128,1024]{2,1,0:T(8,128)(2,1)} %get-tuple-element.416), channel_id=1, source_target_pairs={{0,1},{1,0},{2,3},{3,2},{4,5},{5,4},{6,7},{7,6},{8,9},{9,8},{10,11... | collective-permute-start | bytes 12582920 | tf_op jit(solution)/shard_map/ppermute | solution.py:226
  693.4 14.9 %collective-permute-start.70 = (f32[16,1,384]{2,0,1:T(8,128)S(1)}, f32[16,1,384]{2,0,1:T(8,128)S(1)}, u32[]{:S(2)}, u32[]{:S(2)}) collective-permute-start(f32[16,1,384]{2,0,1:T(8,128)S(1)} %slice.674), channel_id=1, source_target_pairs={{0,1},{1,0},{2,3},{3,2},{4,5},{5,4},{6,7},{7,6},{8,9},{9,8},{10,11... | collective-permute-start | bytes 73736 | tf_op jit(solution)/shard_map/ppermute | solution.py:226
  707.7 12.6 %collective-permute-start.55 = (bf16[16,32,1152]{2,1,0:T(8,128)(2,1)S(1)}, bf16[16,32,1152]{2,1,0:T(8,128)(2,1)S(1)}, u32[]{:S(2)}, u32[]{:S(2)}) collective-permute-start(bf16[16,32,1152]{2,1,0:T(8,128)(2,1)S(1)} %slice.638), channel_id=1, source_target_pairs={{0,1},{1,0},{2,3},{3,2},{4,5},{5,4},{6,7},{7,6},{8,9},{9,8},{10,11... | collective-permute-start | bytes 3538952 | tf_op jit(solution)/shard_map/ppermute | solution.py:226
  720.7 14.9 %collective-permute-start.56 = (bf16[8,32,1152]{2,1,0:T(8,128)(2,1)S(1)}, bf16[8,32,1152]{2,1,0:T(8,128)(2,1)S(1)}, u32[]{:S(2)}, u32[]{:S(2)}) collective-permute-start(bf16[8,32,1152]{2,1,0:T(8,128)(2,1)S(1)} %slice.640), channel_id=1, source_target_pairs={{0,4},{1,5},{2,6},{3,7},{4,0},{5,1},{6,2},{7,3},{8,12},{9,13},{10,... | collective-permute-start | bytes 1769480 | tf_op jit(solution)/shard_map/ppermute | solution.py:226
  722.2 12.8 %collective-permute-start.74 = (f32[1,1,384]{2,0,1:T(1,128)S(1)}, f32[1,1,384]{2,0,1:T(1,128)S(1)}, u32[]{:S(2)}, u32[]{:S(2)}) collective-permute-start(f32[1,1,384]{2,0,1:T(1,128)S(1)} %slice.682), channel_id=1, source_target_pairs={{0,16},{1,17},{2,18},{3,19},{4,20},{5,21},{6,22},{7,23},{8,24},{9,... | collective-permute-start | bytes 4616 | tf_op jit(solution)/shard_map/ppermute | solution.py:226
  729.3 19.9 %collective-permute-start.50 = (bf16[16,32,1536]{2,1,0:T(8,128)(2,1)}, bf16[16,32,1536]{2,1,0:T(8,128)(2,1)}, u32[]{:S(2)}, u32[]{:S(2)}) collective-permute-start(bf16[16,32,1536]{2,1,0:T(8,128)(2,1)} %slice.623), channel_id=1, source_target_pairs={{0,1},{1,0},{2,3},{3,2},{4,5},{5,4},{6,7},{7,6},{8,9},{9,8},{10,11... | collective-permute-start | bytes 4718600 | tf_op jit(solution)/shard_map/ppermute | solution.py:226
  729.3 24.3 %collective-permute-start.45 = (bf16[16,32,1536]{2,1,0:T(8,128)(2,1)}, bf16[16,32,1536]{2,1,0:T(8,128)(2,1)}, u32[]{:S(2)}, u32[]{:S(2)}) collective-permute-start(bf16[16,32,1536]{2,1,0:T(8,128)(2,1)} %slice.612), channel_id=1, source_target_pairs={{0,1},{1,0},{2,3},{3,2},{4,5},{5,4},{6,7},{7,6},{8,9},{9,8},{10,11... | collective-permute-start | bytes 4718600 | tf_op jit(solution)/shard_map/ppermute | solution.py:226
  735.0 41.3 %collective-permute-start.65 = (bf16[16,128,1024]{2,1,0:T(8,128)(2,1)}, bf16[16,128,1024]{2,1,0:T(8,128)(2,1)}, u32[]{:S(2)}, u32[]{:S(2)}) collective-permute-start(bf16[16,128,1024]{2,1,0:T(8,128)(2,1)} %slice.659), channel_id=1, source_target_pairs={{0,1},{1,0},{2,3},{3,2},{4,5},{5,4},{6,7},{7,6},{8,9},{9,8},{10,11... | collective-permute-start | bytes 12582920 | tf_op jit(solution)/shard_map/ppermute | solution.py:226
  735.0 47.5 %collective-permute-start.60 = (bf16[16,32,4096]{2,1,0:T(8,128)(2,1)}, bf16[16,32,4096]{2,1,0:T(8,128)(2,1)}, u32[]{:S(2)}, u32[]{:S(2)}) collective-permute-start(bf16[16,32,4096]{2,1,0:T(8,128)(2,1)} %slice.649), channel_id=1, source_target_pairs={{0,1},{1,0},{2,3},{3,2},{4,5},{5,4},{6,7},{7,6},{8,9},{9,8},{10,11... | collective-permute-start | bytes 12582920 | tf_op jit(solution)/shard_map/ppermute | solution.py:226
  737.3 9.1 %collective-permute-start.57 = (bf16[4,32,1152]{2,1,0:T(8,128)(2,1)}, bf16[4,32,1152]{2,1,0:T(8,128)(2,1)S(1)}, u32[]{:S(2)}, u32[]{:S(2)}) collective-permute-start(bf16[4,32,1152]{2,1,0:T(8,128)(2,1)} %slice.642), channel_id=1, source_target_pairs={{0,2},{1,3},{2,0},{3,1},{4,6},{5,7},{6,4},{7,5},{8,10},{9,11},{10,... | collective-permute-start | bytes 884744 | tf_op jit(solution)/shard_map/ppermute | solution.py:226
  751.7 18.4 %collective-permute-start.51 = (bf16[8,32,1536]{2,1,0:T(8,128)(2,1)S(1)}, bf16[8,32,1536]{2,1,0:T(8,128)(2,1)S(1)}, u32[]{:S(2)}, u32[]{:S(2)}) collective-permute-start(bf16[8,32,1536]{2,1,0:T(8,128)(2,1)S(1)} %slice.625), channel_id=1, source_target_pairs={{0,2},{1,3},{2,0},{3,1},{4,6},{5,7},{6,4},{7,5},{8,10},{9,11},{10,... | collective-permute-start | bytes 2359304 | tf_op jit(solution)/shard_map/ppermute | solution.py:226
  755.6 18.9 %collective-permute-start.46 = (bf16[8,32,1536]{2,1,0:T(8,128)(2,1)S(1)}, bf16[8,32,1536]{2,1,0:T(8,128)(2,1)S(1)}, u32[]{:S(2)}, u32[]{:S(2)}) collective-permute-start(bf16[8,32,1536]{2,1,0:T(8,128)(2,1)S(1)} %slice.614), channel_id=1, source_target_pairs={{0,4},{1,5},{2,6},{3,7},{4,0},{5,1},{6,2},{7,3},{8,12},{9,13},{10,... | collective-permute-start | bytes 2359304 | tf_op jit(solution)/shard_map/ppermute | solution.py:226
  771.0 16.8 %collective-permute-start.52 = (bf16[4,32,1536]{2,1,0:T(8,128)(2,1)}, bf16[4,32,1536]{2,1,0:T(8,128)(2,1)}, u32[]{:S(2)}, u32[]{:S(2)}) collective-permute-start(bf16[4,32,1536]{2,1,0:T(8,128)(2,1)} %slice.627), channel_id=1, source_target_pairs={{0,4},{1,5},{2,6},{3,7},{4,0},{5,1},{6,2},{7,3},{8,12},{9,13},{10,... | collective-permute-start | bytes 1179656 | tf_op jit(solution)/shard_map/ppermute | solution.py:226
  775.5 14.8 %collective-permute-start.47 = (bf16[4,32,1536]{2,1,0:T(8,128)(2,1)}, bf16[4,32,1536]{2,1,0:T(8,128)(2,1)}, u32[]{:S(2)}, u32[]{:S(2)}) collective-permute-start(bf16[4,32,1536]{2,1,0:T(8,128)(2,1)} %slice.616), channel_id=1, source_target_pairs={{0,2},{1,3},{2,0},{3,1},{4,6},{5,7},{6,4},{7,5},{8,10},{9,11},{10,... | collective-permute-start | bytes 1179656 | tf_op jit(solution)/shard_map/ppermute | solution.py:226
  781.6 46.8 %collective-permute-start.66 = (bf16[8,128,1024]{2,1,0:T(8,128)(2,1)S(1)}, bf16[8,128,1024]{2,1,0:T(8,128)(2,1)S(1)}, u32[]{:S(2)}, u32[]{:S(2)}) collective-permute-start(bf16[8,128,1024]{2,1,0:T(8,128)(2,1)S(1)} %slice.661), channel_id=1, source_target_pairs={{0,2},{1,3},{2,0},{3,1},{4,6},{5,7},{6,4},{7,5},{8,10},{9,11},{10,... | collective-permute-start | bytes 6291464 | tf_op jit(solution)/shard_map/ppermute | solution.py:226
  786.5 44.0 %collective-permute-start.61 = (bf16[8,32,4096]{2,1,0:T(8,128)(2,1)S(1)}, bf16[8,32,4096]{2,1,0:T(8,128)(2,1)S(1)}, u32[]{:S(2)}, u32[]{:S(2)}) collective-permute-start(bf16[8,32,4096]{2,1,0:T(8,128)(2,1)S(1)} %slice.651), channel_id=1, source_target_pairs={{0,4},{1,5},{2,6},{3,7},{4,0},{5,1},{6,2},{7,3},{8,12},{9,13},{10,... | collective-permute-start | bytes 6291464 | tf_op jit(solution)/shard_map/ppermute | solution.py:226
  796.4 36.6 %collective-permute-start.54 = (bf16[1,32,1536]{2,1,0:T(8,128)(2,1)S(1)}, bf16[1,32,1536]{2,1,0:T(8,128)(2,1)S(1)}, u32[]{:S(2)}, u32[]{:S(2)}) collective-permute-start(bf16[1,32,1536]{2,1,0:T(8,128)(2,1)S(1)} %slice.631), channel_id=1, source_target_pairs={{0,16},{1,17},{2,18},{3,19},{4,20},{5,21},{6,22},{7,23},{8,24},{9,... | collective-permute-start | bytes 294920 | tf_op jit(solution)/shard_map/ppermute | solution.py:226
  799.8 33.2 %collective-permute-start.49 = (bf16[1,32,1536]{2,1,0:T(8,128)(2,1)S(1)}, bf16[1,32,1536]{2,1,0:T(8,128)(2,1)S(1)}, u32[]{:S(2)}, u32[]{:S(2)}) collective-permute-start(bf16[1,32,1536]{2,1,0:T(8,128)(2,1)S(1)} %slice.620), channel_id=1, source_target_pairs={{0,16},{1,17},{2,18},{3,19},{4,20},{5,21},{6,22},{7,23},{8,24},{9,... | collective-permute-start | bytes 294920 | tf_op jit(solution)/shard_map/ppermute | solution.py:226
  829.5 22.7 %collective-permute-start.67 = (bf16[4,128,1024]{2,1,0:T(8,128)(2,1)S(1)}, bf16[4,128,1024]{2,1,0:T(8,128)(2,1)S(1)}, u32[]{:S(2)}, u32[]{:S(2)}) collective-permute-start(bf16[4,128,1024]{2,1,0:T(8,128)(2,1)S(1)} %slice.663), channel_id=1, source_target_pairs={{0,4},{1,5},{2,6},{3,7},{4,0},{5,1},{6,2},{7,3},{8,12},{9,13},{10,... | collective-permute-start | bytes 3145736 | tf_op jit(solution)/shard_map/ppermute | solution.py:226
  831.5 22.3 %collective-permute-start.62 = (bf16[4,32,4096]{2,1,0:T(8,128)(2,1)S(1)}, bf16[4,32,4096]{2,1,0:T(8,128)(2,1)S(1)}, u32[]{:S(2)}, u32[]{:S(2)}) collective-permute-start(bf16[4,32,4096]{2,1,0:T(8,128)(2,1)S(1)} %slice.653), channel_id=1, source_target_pairs={{0,2},{1,3},{2,0},{3,1},{4,6},{5,7},{6,4},{7,5},{8,10},{9,11},{10,... | collective-permute-start | bytes 3145736 | tf_op jit(solution)/shard_map/ppermute | solution.py:226
  852.7 17.7 %collective-permute-start.68 = (bf16[2,128,1024]{2,1,0:T(8,128)(2,1)S(1)}, bf16[2,128,1024]{2,1,0:T(8,128)(2,1)S(1)}, u32[]{:S(2)}, u32[]{:S(2)}) collective-permute-start(bf16[2,128,1024]{2,1,0:T(8,128)(2,1)S(1)} %slice.665), channel_id=1, source_target_pairs={{0,8},{1,9},{2,10},{3,11},{4,12},{5,13},{6,14},{7,15},{8,0},{9,1},... | collective-permute-start | bytes 1572872 | tf_op jit(solution)/shard_map/ppermute | solution.py:226
  854.1 25.7 %collective-permute-start.63 = (bf16[2,32,4096]{2,1,0:T(8,128)(2,1)S(1)}, bf16[2,32,4096]{2,1,0:T(8,128)(2,1)S(1)}, u32[]{:S(2)}, u32[]{:S(2)}) collective-permute-start(bf16[2,32,4096]{2,1,0:T(8,128)(2,1)S(1)} %slice.655), channel_id=1, source_target_pairs={{0,8},{1,9},{2,10},{3,11},{4,12},{5,13},{6,14},{7,15},{8,0},{9,1},... | collective-permute-start | bytes 1572872 | tf_op jit(solution)/shard_map/ppermute | solution.py:226
  870.6 17.8 %collective-permute-start.69 = (bf16[1,128,1024]{2,1,0:T(8,128)(2,1)S(1)}, bf16[1,128,1024]{2,1,0:T(8,128)(2,1)S(1)}, u32[]{:S(2)}, u32[]{:S(2)}) collective-permute-start(bf16[1,128,1024]{2,1,0:T(8,128)(2,1)S(1)} %slice.667), channel_id=1, source_target_pairs={{0,16},{1,17},{2,18},{3,19},{4,20},{5,21},{6,22},{7,23},{8,24},{9,... | collective-permute-start | bytes 786440 | tf_op jit(solution)/shard_map/ppermute | solution.py:226
  880.0 12.3 %collective-permute-start.64 = (bf16[1,32,4096]{2,1,0:T(8,128)(2,1)S(1)}, bf16[1,32,4096]{2,1,0:T(8,128)(2,1)S(1)}, u32[]{:S(2)}, u32[]{:S(2)}) collective-permute-start(bf16[1,32,4096]{2,1,0:T(8,128)(2,1)S(1)} %slice.657), channel_id=1, source_target_pairs={{0,16},{1,17},{2,18},{3,19},{4,20},{5,21},{6,22},{7,23},{8,24},{9,... | collective-permute-start | bytes 786440 | tf_op jit(solution)/shard_map/ppermute | solution.py:226
  (96 other events, 1973.7 us)

commit v2 on v1

--- a/solution.py
+++ b/solution.py
@@ -11,6 +11,8 @@
 sharpness_divisor = 0.2
 norm_eps = 1e-05
 unit_eps = 1e-06
+root_half = 0.7071067811865476
+density_peak = 0.3989422804014327
 head_width = 64
 block_queries = 16
 masked_score = -1e30
@@ -213,65 +215,109 @@
     )(bounds,segrow,segcol,qkv,qkv,qkv,g,o,lse,qlse)
 
 
+def after(value, *earlier):
+    return lax.optimization_barrier((value, *earlier))[0]
+
+
+class Growing:
+    def __init__(self, links, shard, lane):
+        self.links, self.order, self.block = links, list(links.orders[lane]), shard.shape
+        self.held = shard.reshape((1,) * links.bits + shard.shape)
+
+    def wait(self, *earlier):
+        self.held = after(self.held, *earlier)
+
+    def step(self):
+        place = self.order.pop(0)
+        axis = self.links.bits - 1 - place
+        mine = self.links.side(place)
+        held = self.held
+        arrived = self.links.swap(held, 1 << place)
+        both = jnp.zeros(held.shape[:axis] + (2,) + held.shape[axis + 1 :], held.dtype)
+        both = lax.dynamic_update_slice_in_dim(both, held, mine, axis)
+        self.held = lax.dynamic_update_slice_in_dim(both, arrived, 1 - mine, axis)
+
+    def full(self):
+        while self.order:
+            self.step()
+        return self.held.reshape((self.links.count,) + self.block)
+
+
+class Shrinking:
+    def __init__(self, links, blocks, lane, wire):
+        self.links, self.order, self.block = links, list(links.orders[lane]), blocks.shape[1:]
+        self.wire = wire
+        self.held = blocks.astype(wire).reshape((2,) * links.bits + self.block)
+
+    def wait(self, *earlier):
+        self.held = after(self.held, *earlier)
+
+    def step(self):
+        place = self.order.pop()
+        axis = self.links.bits - 1 - place
+        mine = self.links.side(place)
+        leaving = lax.dynamic_slice_in_dim(self.held, 1 - mine, 1, axis)
+        kept = lax.dynamic_slice_in_dim(self.held, mine, 1, axis)
+        total = kept.astype(f32) + self.links.swap(leaving, 1 << place).astype(f32)
+        self.held = total.astype(self.wire) if self.order else total
+
+    def mine(self):
+        while self.order:
+            self.step()
+        return self.held.reshape(self.block)
+
+
 class Links:
     def __init__(self, dp, fsdp):
         self.dp, self.fsdp, self.count = dp, fsdp, dp * fsdp
-        low = [1 << b for b in range(fsdp.bit_length() - 1)]
-        high = [fsdp << b for b in range(dp.bit_length() - 1)]
+        self.bits = self.count.bit_length() - 1
+        inner_bits = fsdp.bit_length() - 1
+        low, high = list(range(inner_bits)), list(range(inner_bits, self.bits))
         inner, rest = low[:1], low[1:]
         near, far = high[:1], high[1:][::-1]
         self.orders = (far + rest[::-1] + near + inner, far + near + rest[::-1] + inner)
 
+    def side(self, place):
+        return (lax.axis_index(AXES) >> place) & 1
+
     def swap(self, value, bit):
         return lax.ppermute(value, AXES, [(d, d ^ bit) for d in range(self.count)])
 
-    def owners(self, order):
-        slots = jnp.arange(self.count, dtype=jnp.int32)
-        mixed = jnp.zeros_like(slots)
-        for place, bit in enumerate(order):
-            mixed = mixed + ((slots >> place) & 1) * bit
-        return mixed ^ lax.axis_index(AXES)
-
-    def places(self, order):
-        other = jnp.arange(self.count, dtype=jnp.int32) ^ lax.axis_index(AXES)
-        slots = jnp.zeros_like(other)
-        for place, bit in enumerate(order):
-            slots = slots + jnp.where((other & bit) != 0, 1 << place, 0)
-        return slots
-
-    def gather_slots(self, shard, order):
-        held = shard[None]
-        for bit in order:
-            held = jnp.concatenate([held, self.swap(held, bit)], axis=0)
-        return held
-
-    def gather(self, shard, lane=0):
-        order = self.orders[lane]
-        return jnp.take(self.gather_slots(shard, order), self.places(order), axis=0)
-
-    def scatter_sum(self, blocks, lane=0, wire=bf16):
-        order = self.orders[lane]
-        held = jnp.take(blocks.astype(wire), self.owners(order), axis=0)
-        for bit in order[::-1]:
-            half = held.shape[0] // 2
-            arrived = self.swap(held[half:], bit)
-            held = held[:half].astype(f32) + arrived.astype(f32)
-            if half > 1:
-                held = held.astype(wire)
-        return held[0]
+    def growing(self, shard, lane=0):
+        return Growing(self, shard, lane)
+
+    def shrinking(self, blocks, lane=0, wire=bf16):
+        return Shrinking(self, blocks, lane, wire)
 
     def total(self, value):
-        for bit in self.orders[0]:
-            value = value + self.swap(value, bit)
+        for place in self.orders[0]:
+            value = value + self.swap(value, 1 << place)
         return value
 
 
+class Whole:
+    def __init__(self, value):
+        self.held = value
+
+    def wait(self, *earlier):
+        pass
+
+    def step(self):
+        pass
+
+    def full(self):
+        return self.held
+
+    def mine(self):
+        return self.held
+
+
 class PlainLinks(Links):
-    def gather(self, shard, lane=0):
-        return lax.all_gather(shard, AXES, axis=0)
-
-    def scatter_sum(self, blocks, lane=0, wire=bf16):
-        return lax.psum_scatter(blocks, AXES, scatter_dimension=0, tiled=False)
+    def growing(self, shard, lane=0):
+        return Whole(lax.all_gather(shard, AXES, axis=0))
+
+    def shrinking(self, blocks, lane=0, wire=bf16):
+        return Whole(lax.psum_scatter(blocks, AXES, scatter_dimension=0, tiled=False))
 
     def total(self, value):
         return lax.psum(value, AXES)
@@ -331,7 +377,29 @@
     def rows_of(full):
         return full.reshape(full.shape[0] * full.shape[1], full.shape[2])
 
-    small_full = links.gather(small, 0).reshape(count, -1)
+    sides = []
+    for side in range(2):
+        cut = slice(side * part, (side + 1) * part)
+        shard = jnp.concatenate([w_query[:, cut], w_key[:, cut], w_value[:, cut]], axis=1)
+        sides.append(links.growing(shard, side))
+    small_part = links.growing(small, 0)
+    out_part = links.growing(jnp.concatenate([w_out, w_proj], axis=1), 0)
+    up_part = links.growing(w_up, 0)
+    down_part = links.growing(w_down, 1)
+    for hop in range(4):
+        for one in sides + [small_part]:
+            one.step()
+        for one in (out_part, up_part, down_part):
+            one.wait(sides[0].held, sides[1].held)
+            if hop < 3:
+                one.step()
+    for one in sides + [small_part]:
+        one.step()
+        one.wait(up_part.held, down_part.held)
+    for one in (out_part, up_part, down_part):
+        one.step()
+    small_full = small_part.full().reshape(count, -1)
+    full_qkv = [rows_of(one.full()) for one in sides]
     full_biases = (
         small_full[:, : 6 * shard_cols]
         .reshape(count, 6, shard_cols)
@@ -347,16 +415,6 @@
         .astype(f32)
     )
     full_upbias = small_full[:, 8 * shard_cols :].reshape(ff).astype(f32)
-
-    full_qkv = []
-    for side in range(2):
-        cut = slice(side * part, (side + 1) * part)
-        shard = jnp.concatenate([w_query[:, cut], w_key[:, cut], w_value[:, cut]], axis=1)
-        full_qkv.append(rows_of(links.gather(shard, side)))
-    out_proj = rows_of(links.gather(jnp.concatenate([w_out, w_proj], axis=1), 0))
-    full_out, full_proj = out_proj[:, :model_width], out_proj[:, model_width:]
-    full_up = rows_of(links.gather(w_up, 0))
-    full_down = rows_of(links.gather(w_down, 1))
 
     tokens = jnp.concatenate(
         [doc_hidden[0], query_hidden.reshape(query_count * span, model_width)], axis=0
@@ -376,6 +434,11 @@
         )
         contexts.append(context)
         saved.append((lse, query_lse))
+    contexts[1] = after(contexts[1], up_part.held, down_part.held)
+    out_proj = rows_of(out_part.full())
+    full_out, full_proj = out_proj[:, :model_width], out_proj[:, model_width:]
+    full_up = rows_of(up_part.full())
+    full_down = rows_of(down_part.full())
     attn_out = (
         matmul_plain(contexts[0], full_out[:part])
         + matmul_plain(contexts[1], full_out[part:])
@@ -386,7 +449,11 @@
     )
     first_low = first_out.astype(bf16)
     up_pre = matmul_plain(first_low, full_up) + full_upbias
-    gelu_out = jax.nn.gelu(up_pre, approximate=False).astype(bf16)
+    share = 0.5 * (1.0 + lax.erf(up_pre * root_half))
+    gelu_out = (up_pre * share).astype(bf16)
+    density = jnp.exp(-0.5 * up_pre * up_pre) * density_peak
+    slope = (share + up_pre * density).astype(bf16)
+    gelu_out, slope = lax.optimization_barrier((gelu_out, slope))
     ffn_out = matmul_plain(gelu_out, full_down) + full_biases[4]
     second_out, second_normed, second_scale = layer_norm_parts(
         first_out + ffn_out, full_gains[1], full_biases[5]
@@ -395,7 +462,7 @@
     vectors = matmul_plain(second_low, full_proj).astype(bf16)
     doc_vectors = vectors[:row_len]
     query_vectors = vectors[row_len:].reshape(query_count * span, proj_width)
-    every_query = links.gather(query_vectors).reshape(count * query_count, span, proj_width)
+    every_query = links.growing(query_vectors).full().reshape(count * query_count, span, proj_width)
     query_total = every_query.shape[0]
     block_count = query_total // block_queries
     levels = (proj_width, proj_width * 3 // 4, proj_width // 2)
@@ -466,7 +533,7 @@
     grad_blocks = peak_match_derivative.reshape(block_count, block_queries, 3, doc_slots)
     doc_unit_grads, query_terms = lax.scan(block_back, start_carry, (blocks, grad_blocks))
     query_terms = query_terms.reshape(count, query_count * span, proj_width)
-    query_vec_grad = links.scatter_sum(query_terms, wire=f32)
+    query_vec_grad = links.shrinking(query_terms, wire=f32).mine()
     doc_vec_grad = jnp.zeros((row_len, proj_width), f32)
     for position in range(3):
         unit_full, inv_scale = doc_prefix[position]
@@ -489,39 +556,55 @@
     )
     grad_ffn = grad_mid.astype(bf16)
     down_grad = matmul_left_t(gelu_out, grad_ffn)
-    down_shard = links.scatter_sum(spread_rows_of(down_grad), 1)
+    down_sum = links.shrinking(spread_rows_of(down_grad), 1)
+    down_sum.step()
     down_bias = jnp.sum(grad_ffn, axis=0, dtype=f32)
     grad_gelu = matmul_right_t(grad_ffn, full_down)
-    gelu_back = jax.vjp(lambda pre_act: jax.nn.gelu(pre_act, approximate=False), up_pre)[1]
-    grad_up = gelu_back(grad_gelu)[0].astype(bf16)
+    grad_up = (grad_gelu * slope.astype(f32)).astype(bf16)
     upbias_grad = jnp.sum(grad_up, axis=0, dtype=f32)
     up_grad = matmul_left_t(first_low, grad_up)
-    up_shard = links.scatter_sum(spread_rows_of(up_grad), 0)
-    grad_first = grad_mid + matmul_right_t(grad_up, full_up)
+    up_sum = links.shrinking(spread_rows_of(up_grad), 0)
+    up_sum.step()
+    grad_first = grad_mid + matmul_right_t(after(grad_up, down_sum.held), full_up)
+    down_sum.step()
     grad_res, gain_one, bias_one = layer_norm_back(
         grad_first, first_normed, first_scale, full_gains[0]
     )
-    grad_attn = grad_res.astype(bf16)
+    grad_attn = after(grad_res.astype(bf16), up_sum.held)
+    up_sum.step()
     out_bias = jnp.sum(grad_attn, axis=0, dtype=f32)
     out_grad = jnp.concatenate([matmul_left_t(c, grad_attn) for c in contexts], axis=0)
-    out_proj_shard = links.scatter_sum(
-        spread_rows_of(jnp.concatenate([out_grad, proj_grad], axis=1)), 0
-    )
+    out_sum = links.shrinking(spread_rows_of(jnp.concatenate([out_grad, proj_grad], axis=1)), 0)
+    out_sum.step()
     input_grad = grad_res
-    query_bias, value_bias, qkv_shards = [], [], []
+    query_bias, value_bias, qkv_sums = [], [], []
+    earlier = (out_sum.held,)
     for side in range(2):
         grad_context = matmul_right_t(
             grad_attn, full_out[side * part : (side + 1) * part]
         ).astype(bf16)
         grad_qkv = attention_backward(
-            qkv[side], grad_context, contexts[side], *saved[side], segrow, segcol, bounds,
-            row_len, span,
+            qkv[side], after(grad_context, *earlier), contexts[side], *saved[side], segrow, segcol,
+            bounds, row_len, span,
         )
+        if side == 0:
+            out_sum.step()
+        else:
+            grad_qkv = after(grad_qkv, up_sum.held, out_sum.held, qkv_sums[0].held)
+            up_sum.step()
+            qkv_sums[0].step()
         query_bias.append(jnp.sum(grad_qkv[:, :part], axis=0, dtype=f32))
         value_bias.append(jnp.sum(grad_qkv[:, 2 * part :], axis=0, dtype=f32))
         qkv_grad = matmul_left_t(tokens, grad_qkv)
-        qkv_shards.append(links.scatter_sum(spread_rows_of(qkv_grad), side))
+        qkv_sums.append(links.shrinking(spread_rows_of(qkv_grad), side))
+        qkv_sums[side].step()
+        earlier = (down_sum.held, qkv_sums[0].held)
+        if side == 0:
+            down_sum.step()
+            qkv_sums[0].step()
         input_grad = input_grad + matmul_right_t(grad_qkv, full_qkv[side])
+    down_shard, up_shard, out_proj_shard = down_sum.mine(), up_sum.mine(), out_sum.mine()
+    qkv_shards = [one.mine() for one in qkv_sums]
     bias_grads = jnp.stack(
         [
             jnp.concatenate(query_bias),
@@ -542,7 +625,7 @@
         ],
         axis=1,
     )
-    small_shard = links.scatter_sum(small_grads[:, None, :], 0, wire=f32)[0]
+    small_shard = links.shrinking(small_grads[:, None, :], 0, wire=f32).mine()[0]
     shards = [
         jnp.concatenate([s[:, i * part : (i + 1) * part] for s in qkv_shards], axis=1)
         for i in range(3)

time: 903 us -> 776 us (0.86)
  other arithmetic: 115 us -> 73.3 us
  local copies, waits for them, and re-layouts: 140 us -> 101 us
  matrix products: 245 us -> 213 us
  starting transfers between devices: 85.8 us -> 66.2 us
    gather x14 -> x0, local copies, waits for them, and re-layouts: 59.4 us -> none  [the longest x7 29.8 us: gather(): return jnp.take(self.gather_slots(shard, order), self.places(order), axis=0)]
    select_n x19 -> x0, other arithmetic: 45.4 us -> none  [the longest x9 23.9 us: scatter_sum(): held = jnp.take(blocks.astype(wire), self.owners(order), axis=0)]
    dynamic_update_slice x0 -> x67, local copies, waits for them, and re-layouts: none -> 38.4 us  [the longest x34 22.3 us: step(): self.held = lax.dynamic_update_slice_in_dim(both, arrived, 1 - mine, axis)]
    concatenate x14 -> x1, local copies, waits for them, and re-layouts: 27.1 us -> 0.11 us  [body(): jnp.concatenate([bias_grads.reshape(8, count, shard_cols).transpose(1, 0,...]
    dot_general x13, matrix products: 81.4 us -> 56 us  [matmul_plain(): return jnp.dot(left, right, preferred_element_type=jnp.float32)]
    ppermute x75, starting transfers between devices: 85.8 us -> 66.2 us  [swap(): return lax.ppermute(value, AXES, [(d, d ^ bit) for d in range(self.count)])]
    dynamic_slice x0 -> x34, local copies, waits for them, and re-layouts: none -> 16.1 us  [step(): leaving = lax.dynamic_slice_in_dim(self.held, 1 - mine, 1, axis)]
    convert_element_type x20 -> x21, other arithmetic: 20.3 us -> 35.3 us  [the longest x20 30.8 us: step(): self.held = total.astype(self.wire) if self.order else total]
  transfers between devices with their start and end apart: 75 -> 75, of which waited for: 42 -> 38; matrix products, arithmetic and copies ran while one was open for 19% -> 31% of each run, Pallas kernels for 5% -> 13%
where the time goes in v2:
time: 776 us; the launch traced here: 767 us
  matrix products  213 us (27%)
  waiting for transfers between devices  208 us (27%)
  local copies, waits for them, and re-layouts  101 us (13%)
  Pallas kernels  98.4 us (13%)
  other arithmetic  73.3 us (9%)
  starting transfers between devices  66.2 us (9%)
    ppermute x75, waiting for transfers between devices, swap(): return lax.ppermute(value, AXES, [(d, d ^ bit) for d in range(self.count)])  208 us
    ppermute x75, starting transfers between devices, swap(): return lax.ppermute(value, AXES, [(d, d ^ bit) for d in range(self.count)])  66.2 us
    dot_general x19, matrix products, matmul_right_t(): lax.dot_general(left, right, (((1,), (1,)), ((), ())), preferred_element_...  65.9 us
    dot_general x13, matrix products, matmul_plain(): return jnp.dot(left, right, preferred_element_type=jnp.float32)  56 us
    pallas_call x2, Pallas kernels, attention_backward(): pl.pallas_call(partial(attend_backward, row_len, qb, kb, lanes, span), ou...  54.9 us
    dot_general x13, matrix products, matmul_left_t(): lax.dot_general(left, right, (((0,), (0,)), ((), ())), preferred_element_...  53.7 us
    pallas_call x2, Pallas kernels, attention_forward(): pl.pallas_call(partial(attend_forward, row_len, qb, kb, lanes, span), out...  43.5 us
    convert_element_type x20, other arithmetic, step(): self.held = total.astype(self.wire) if self.order else total  30.8 us
  transfers between devices with their start and end apart: 75, of which 38 were waited for; matrix products, arithmetic and copies ran while one was open for 31% of the time, Pallas kernels for 13%

profile of v2, /device:TPU:0, one launch (start us, length us, event | category | flops | bytes accessed | tf_op | source)
XLA Modules:
  0.0 767.4 jit_solution(9229796282194727844)
XLA Ops:
  3.0 4.1 collective-permute-start.15
  35.2 6.9 collective-permute-done.20
  48.3 12.2 %collective-permute-done.12 = bf16[1,1,1,1,1,128,1024]{6,5,4,3,2,1,0:T(8,128)(2,1)S(1)} collective-permute-done((bf16[1,1,1,1,1,128,1024]{6,5,4,3,2,1,0:T(8,128)(2,1)S(1)}, bf16[1,1,1,1,1,128,1024]{6,5,4,3,2,1,0:T(8,128)(2,1)S(1)}, u32[]{:S(2)}, u32[]{:S(2)}) %collective-permute-start.12) | collective-permute-done | bytes 262176 | tf_op jit(solution)/shard_map/ppermute | solution.py:284
  71.4 13.1 %collective-permute-done.13 = bf16[2,1,1,1,1,128,1024]{6,5,4,3,2,1,0:T(8,128)(2,1)S(1)} collective-permute-done((bf16[2,1,1,1,1,128,1024]{6,5,4,3,2,1,0:T(8,128)(2,1)S(1)}, bf16[2,1,1,1,1,128,1024]{6,5,4,3,2,1,0:T(8,128)(2,1)S(1)}, u32[]{:S(2)}, u32[]{:S(2)}) %collective-permute-start.13) | collective-permute-done | bytes 524320 | tf_op jit(solution)/shard_map/ppermute | solution.py:284
  100.8 11.4 %collective-permute-done.14 = bf16[2,2,1,1,1,128,1024]{6,5,4,3,2,1,0:T(8,128)(2,1)S(1)} collective-permute-done((bf16[2,2,1,1,1,128,1024]{6,5,4,3,2,1,0:T(8,128)(2,1)S(1)}, bf16[2,2,1,1,1,128,1024]{6,5,4,3,2,1,0:T(8,128)(2,1)S(1)}, u32[]{:S(2)}, u32[]{:S(2)}) %collective-permute-start.14) | collective-permute-done | bytes 1048608 | tf_op jit(solution)/shard_map/ppermute | solution.py:284
  131.9 34.6 %collective-permute-done.26 = bf16[2,2,1,2,1,32,4096]{6,5,4,3,2,1,0:T(8,128)(2,1)} collective-permute-done((bf16[2,2,1,2,1,32,4096]{6,5,4,3,2,1,0:T(8,128)(2,1)S(1)}, bf16[2,2,1,2,1,32,4096]{6,5,4,3,2,1,0:T(8,128)(2,1)}, u32[]{:S(2)}, u32[]{:S(2)}) %collective-permute-start.26) | collective-permute-done | bytes 2097184 | tf_op jit(solution)/shard_map/ppermute | solution.py:284
  166.6 3.1 constant_dynamic-update-slice_fusion.16
  169.7 4.3 fusion.117.q_ref.k_ref.v_ref
  174.0 21.8 %shard_map.237 = (bf16[1056,512]{1,0:T(8,128)(2,1)S(1)}, f32[4,4,512]{2,1,0:T(4,128)S(1)}, f32[4,1,64]{2,1,0:T(1,128)S(1)}) custom-call(s32[2,4]{1,0:T(2,128)S(1)} %pad_add_fusion.bounds, s32[4,512]{1,0:T(4,128)S(1)} %constant_dynamic-update-slice_fusion.68.segrow, s32[1024,1]{1,0:T(8,128)S(1)} %copy.74.segcol, ...), custom_call_target="tpu_custom_call" | custom-call | tf_op jit(solution)/shard_map/pallas_call | solution.py:130
  196.4 6.3 fusion.118.q_ref.k_ref.v_ref
  202.7 21.8 %shard_map.238 = (bf16[1056,512]{1,0:T(8,128)(2,1)S(1)}, f32[4,4,512]{2,1,0:T(4,128)S(1)}, f32[4,1,64]{2,1,0:T(1,128)S(1)}) custom-call(s32[2,4]{1,0:T(2,128)S(1)} %pad_add_fusion.bounds, s32[4,512]{1,0:T(4,128)S(1)} %constant_dynamic-update-slice_fusion.68.segrow, s32[1024,1]{1,0:T(8,128)S(1)} %copy.74.segcol, ...), custom_call_target="tpu_custom_call" | custom-call | tf_op jit(solution)/shard_map/pallas_call | solution.py:130
  235.8 4.4 broadcast_in_dim.245
  240.1 4.7 constant_dynamic-update-slice_fusion.13
  244.8 4.7 constant_dynamic-update-slice_fusion.12
  249.4 20.9 %fusion.115 = (bf16[1056,4096]{1,0:T(8,128)(2,1)}, bf16[1056,4096]{1,0:T(8,128)(2,1)}) fusion(f32[4096]{0:T(1024)S(1)} %fusion.165, bf16[1024,4096]{1,0:T(8,128)(2,1)} %bitcast.326, f32[1056,1024]{1,0:T(8,128)S(1)} %get-tuple-element.478, f32[1024]{0:T(1024)S(1)} %add.654, f32[1024]{0:T(1024)S(1)} %mul.530, f32[1056]{0:T(1024)S(1)} %add_rsqrt_fusion.7, ...), kind=kOutput, calls=%fused_computation.141 | convolution fusion | flops 8915681280 | bytes 30048512 | tf_op jit(solution)/shard_map/dot_general | solution.py:27
  273.2 16.2 %fusion.187 = (f32[1056]{0:T(1024)S(1)}, f32[1056,1024]{1,0:T(8,128)S(1)}) fusion(f32[1024]{0:T(1024)S(1)} %add.662, bf16[1056,4096]{1,0:T(8,128)(2,1)} %get-tuple-element.249, bf16[4096,1024]{1,0:T(8,128)(2,1)S(1)} %bitcast.324, f32[1024]{0:T(1024)S(1)} %add.654, f32[1024]{0:T(1024)S(1)} %mul.530, f32[1056]{0:T(1024)S(1)} %add_rsqrt_fusion.7, ...), kind=kOutput, calls=%fused_computation.466 | convolution fusion | flops 8865938432 | bytes 25715072 | tf_op jit(solution)/shard_map/dot_general | solution.py:27
  295.5 3.7 collective-permute-done.30
  303.6 3.3 collective-permute-done.32
  312.6 18.9 %while.32 = (s32[]{:T(128)}, f32[2,16,3,8]{1,3,2,0:T(8,128)S(1)}, bf16[2,16,32,128]{3,2,1,0:T(8,128)(2,1)S(1)}, bf16[1024,128]{1,0:T(8,128)(2,1)S(1)}, bf16[1024...) while((s32[]{:T(128)}, f32[2,16,3,8]{1,3,2,0:T(8,128)S(1)}, ...), condition=%wide.region_18.19_spmd.clone, body=%wide.region_11.18_spmd.clone.sunk | while | flops 455516928 | bytes 14488185 | solution.py:490
  332.3 4.0 collective-permute-done.35
  349.1 49.4 %while.33 = (s32[]{:T(128)}, f32[1024,128]{1,0:T(8,128)S(1)}, f32[1024,96]{0,1:T(8,128)S(1)}, f32[1024,64]{0,1:T(8,128)S(1)}, f32[2,16,32,128]{3,2,1,0:T(8,128)}...) while((s32[]{:T(128)}, f32[1024,128]{1,0:T(8,128)S(1)}, ...), condition=%wide.region_29.30_spmd.clone.clone.clone, body=%wide.region_22.29_spmd.clone.clone.clone.sunk | while | flops 1217213056 | bytes 37461660 | solution.py:534
  404.3 3.9 collective-permute-done.41
  409.3 3.3 collective-permute-done.42
  418.2 3.1 collective-permute-done.44
  421.3 4.3 multiply_reduce_fusion.1
  427.1 18.8 %convolution_convert_fusion = bf16[4096,1024]{1,0:T(8,128)(2,1)} fusion(bf16[1056,4096]{1,0:T(8,128)(2,1)} %get-tuple-element.249, f32[1056,1024]{1,0:T(8,128)S(1)} %get-tuple-element.445), kind=kOutput, calls=%fused_computation.150 | convolution fusion | flops 8863645696 | bytes 21364736 | tf_op jit(solution)/shard_map/dot_general | solution.py:37
  446.2 4.8 constant_dynamic-slice_fusion.36
  451.1 17.5 %convert_reduce_fusion = (f32[4096]{0:T(1024)}, bf16[1056,4096]{1,0:T(8,128)(2,1)}) fusion(bf16[1056,4096]{1,0:T(8,128)(2,1)} %get-tuple-element.255, bf16[4096,1024]{1,0:T(8,128)(2,1)} %bitcast.325, f32[1056,1024]{1,0:T(8,128)} %copy-done.28), kind=kOutput, calls=%fused_computation.142 | convolution fusion | flops 8881074176 | bytes 30031872 | tf_op jit(solution)/shard_map/dot_general | solution.py:31
  468.6 16.1 %convolution_convert_fusion.1 = bf16[1024,4096]{1,0:T(8,128)(2,1)S(1)} fusion(bf16[1056,4096]{1,0:T(8,128)(2,1)} %get-tuple-element.256, f32[1056,1024]{1,0:T(8,128)} %copy-done.14, f32[1024]{0:T(1024)S(1)} %copy-done.72, f32[1024]{0:T(1024)S(1)} %copy-done.70, f32[1056]{0:T(1024)S(1)} %copy-done.68, f32[1056]{0:T(1024)S(1)} %copy-done.54), kind=kOutput, calls=%fused_computation.153 | convolution fusion | flops 8867971072 | bytes 21381376 | tf_op jit(solution)/shard_map/dot_general | solution.py:37
  487.0 3.9 copy-done.22
  492.3 6.0 add_convert_fusion.1
  501.8 17.4 %multiply_reduce_fusion.2 = (f32[1024]{0:T(1024)S(1)}, f32[1056]{0:T(1024)S(1)}, f32[1056]{0:T(1024)S(1)}, f32[1024]{0:T(1024)}, f32[1056,1024]{1,0:T(8,128)}) fusion(f32[1056,1024]{1,0:T(8,128)S(1)} %bitcast.306, f32[1056]{0:T(1024)S(1)} %copy-done.68, f32[1056]{0:T(1024)S(1)} %copy-done.54, f32[1024]{0:T(1024)S(1)} %copy-done.70, ...), kind=kOutput, calls=%fused_computation.163 | convolution fusion | flops 8869179392 | bytes 30044672 | tf_op jit(solution)/shard_map/dot_general | solution.py:31
  519.1 4.5 fusion.178
  523.7 7.3 add_convert_fusion
  550.2 27.4 %shard_map.239 = bf16[1056,1536]{1,0:T(8,128)(2,1)} custom-call(s32[2,4]{1,0:T(2,128)} %copy-done.10, s32[4,512]{1,0:T(4,128)} %copy-done.7, s32[1024,1]{1,0:T(8,128)} %copy-done.2, bf16[1056,1536]{1,0:T(8,128)(2,1)} %copy-done.1, bf16[1056,1536]{1,0:T(8,128)(2,1)} %copy-done.1, bf16[1056,1536]{1,0:T(8,128)(2,1)} %copy-done.1, ...), custom_call_target="tpu_custom_call" | custom-call | tf_op jit(solution)/shard_map/pallas_call | solution.py:207
  577.7 9.9 %convolution_add_fusion.10 = f32[1056,1024]{1,0:T(8,128)} fusion(f32[1056,1024]{1,0:T(8,128)} %get-tuple-element.447, bf16[1056,1536]{1,0:T(8,128)(2,1)} %shard_map.239, bf16[1024,1536]{1,0:T(8,128)(2,1)} %bitcast.345), kind=kOutput, calls=%fused_computation.160 | convolution fusion | flops 3322970112 | bytes 15040512 | tf_op jit(solution)/shard_map/dot_general | solution.py:31
  587.6 4.6 convolution_convert_fusion.3
  592.2 11.2 %collective-permute-done.51 = bf16[2,2,1,2,1,32,1152]{6,5,4,3,2,1,0:T(8,128)(2,1)S(1)} collective-permute-done((bf16[2,2,1,2,1,32,1152]{6,5,4,3,2,1,0:T(8,128)(2,1)S(1)}, bf16[2,2,1,2,1,32,1152]{6,5,4,3,2,1,0:T(8,128)(2,1)S(1)}, u32[]{:S(2)}, u32[]{:S(2)}) %collective-permute-start.51) | collective-permute-done | bytes 589856 | tf_op jit(solution)/shard_map/ppermute | solution.py:284
  605.6 5.9 collective-permute-done.61
  621.9 3.3 collective-permute-done.63
  627.9 27.4 %shard_map.240 = bf16[1056,1536]{1,0:T(8,128)(2,1)} custom-call(s32[2,4]{1,0:T(2,128)} %copy-done.10, s32[4,512]{1,0:T(4,128)} %copy-done.7, s32[1024,1]{1,0:T(8,128)} %copy-done.2, bf16[1056,1536]{1,0:T(8,128)(2,1)} %copy-done, bf16[1056,1536]{1,0:T(8,128)(2,1)} %copy-done, bf16[1056,1536]{1,0:T(8,128)(2,1)} %copy-done, ...), custom_call_target="tpu_custom_call" | custom-call | tf_op jit(solution)/shard_map/pallas_call | solution.py:207
  665.1 6.8 convolution_add_fusion.9
  674.7 6.5 convolution_convert_fusion.2
  705.5 14.2 %collective-permute-done.66 = bf16[1,1,1,1,1,32,4096]{6,5,4,3,2,1,0:T(8,128)(2,1)S(1)} collective-permute-done((bf16[1,1,1,1,1,32,4096]{6,5,4,3,2,1,0:T(8,128)(2,1)S(1)}, bf16[1,1,1,1,1,32,4096]{6,5,4,3,2,1,0:T(8,128)(2,1)S(1)}, u32[]{:S(2)}, u32[]{:S(2)}) %collective-permute-start.66) | collective-permute-done | bytes 262176 | tf_op jit(solution)/shard_map/ppermute | solution.py:284
  727.1 14.3 %collective-permute-done.57 = bf16[2,2,2,1,1,32,1536]{6,5,4,3,2,1,0:T(8,128)(2,1)S(1)} collective-permute-done((bf16[2,2,2,1,1,32,1536]{6,5,4,3,2,1,0:T(8,128)(2,1)S(1)}, bf16[2,2,2,1,1,32,1536]{6,5,4,3,2,1,0:T(8,128)(2,1)S(1)}, u32[]{:S(2)}, u32[]{:S(2)}) %collective-permute-start.57) | collective-permute-done | bytes 786464 | tf_op jit(solution)/shard_map/ppermute | solution.py:284
  743.3 8.0 %collective-permute-done.58 = bf16[2,2,1,1,1,32,1536]{6,5,4,3,2,1,0:T(8,128)(2,1)S(1)} collective-permute-done((bf16[2,2,1,1,1,32,1536]{6,5,4,3,2,1,0:T(8,128)(2,1)S(1)}, bf16[2,2,1,1,1,32,1536]{6,5,4,3,2,1,0:T(8,128)(2,1)S(1)}, u32[]{:S(2)}, u32[]{:S(2)}) %collective-permute-start.58) | collective-permute-done | bytes 393248 | tf_op jit(solution)/shard_map/ppermute | solution.py:284
  751.5 5.6 collective-permute-done.59
  757.8 6.0 collective-permute-done.60
  (715 shorter events, 297.3 us)
Async XLA Ops:
  3.0 13.8 %collective-permute-start.15 = (bf16[1,1,1,1,1,1,384]{6,4,3,2,1,0,5:T(2,128)(2,1)S(1)}, bf16[1,1,1,1,1,1,384]{6,4,3,2,1,0,5:T(2,128)(2,1)S(1)}, u32[]{:S(2)}, u32[]{:S(2)}) collective-permute-start(bf16[1,1,1,1,1,1,384]{6,4,3,2,1,0,5:T(2,128)(2,1)S(1)} %reshape_broadcast_in_dim.4), channel_id=1, source_target_pairs={{0,16},{1,17},{2,18},{3,19},{4,20},{5,21},{6,22},{7,23},{8,24},{9,... | collective-permute-start | bytes 2312 | tf_op jit(solution)/shard_map/ppermute | solution.py:284
  9.4 21.6 %collective-permute-start = (bf16[1,1,1,1,1,32,1536]{6,5,4,3,2,1,0:T(8,128)(2,1)S(1)}, bf16[1,1,1,1,1,32,1536]{6,5,4,3,2,1,0:T(8,128)(2,1)S(1)}, u32[]{:S(2)}, u32[]{:S(2)}) collective-permute-start(bf16[1,1,1,1,1,32,1536]{6,5,4,3,2,1,0:T(8,128)(2,1)S(1)} %maximum_bitcast_fusion.1), channel_id=1, source_target_pairs={{0,16},{1,17},{2,18},{3,19},{4,20},{5,21},{6,22},{7,23},{8,24},{9,... | collective-permute-start | bytes 294920 | tf_op jit(solution)/shard_map/ppermute | solution.py:284
  9.5 20.1 %collective-permute-start.5 = (bf16[1,1,1,1,1,32,1536]{6,5,4,3,2,1,0:T(8,128)(2,1)S(1)}, bf16[1,1,1,1,1,32,1536]{6,5,4,3,2,1,0:T(8,128)(2,1)S(1)}, u32[]{:S(2)}, u32[]{:S(2)}) collective-permute-start(bf16[1,1,1,1,1,32,1536]{6,5,4,3,2,1,0:T(8,128)(2,1)S(1)} %maximum_bitcast_fusion.2), channel_id=1, source_target_pairs={{0,16},{1,17},{2,18},{3,19},{4,20},{5,21},{6,22},{7,23},{8,24},{9,... | collective-permute-start | bytes 294920 | tf_op jit(solution)/shard_map/ppermute | solution.py:284
  29.6 13.5 %collective-permute-start.7 = (bf16[2,1,1,1,1,32,1536]{6,5,4,3,2,1,0:T(8,128)(2,1)S(1)}, bf16[2,1,1,1,1,32,1536]{6,5,4,3,2,1,0:T(8,128)(2,1)S(1)}, u32[]{:S(2)}, u32[]{:S(2)}) collective-permute-start(bf16[2,1,1,1,1,32,1536]{6,5,4,3,2,1,0:T(8,128)(2,1)S(1)} %constant_dynamic-update-slice_fusion.56), channel_id=1, source_target_pairs={{0,8},{1,9},{2,10},{3,11},{4,12},{5,13},{6,14},{7,15},{8,0},{9,1},... | collective-permute-start | bytes 589832 | tf_op jit(solution)/shard_map/ppermute | solution.py:284
  31.0 15.5 %collective-permute-start.1 = (bf16[2,1,1,1,1,32,1536]{6,5,4,3,2,1,0:T(8,128)(2,1)S(1)}, bf16[2,1,1,1,1,32,1536]{6,5,4,3,2,1,0:T(8,128)(2,1)S(1)}, u32[]{:S(2)}, u32[]{:S(2)}) collective-permute-start(bf16[2,1,1,1,1,32,1536]{6,5,4,3,2,1,0:T(8,128)(2,1)S(1)} %constant_dynamic-update-slice_fusion.66), channel_id=1, source_target_pairs={{0,8},{1,9},{2,10},{3,11},{4,12},{5,13},{6,14},{7,15},{8,0},{9,1},... | collective-permute-start | bytes 589832 | tf_op jit(solution)/shard_map/ppermute | solution.py:284
  31.8 10.4 %collective-permute-start.20 = (bf16[1,1,1,1,1,32,1152]{6,5,4,3,2,1,0:T(8,128)(2,1)S(1)}, bf16[1,1,1,1,1,32,1152]{6,5,4,3,2,1,0:T(8,128)(2,1)S(1)}, u32[]{:S(2)}, u32[]{:S(2)}) collective-permute-start(bf16[1,1,1,1,1,32,1152]{6,5,4,3,2,1,0:T(8,128)(2,1)S(1)} %maximum_bitcast_fusion.3), channel_id=1, source_target_pairs={{0,16},{1,17},{2,18},{3,19},{4,20},{5,21},{6,22},{7,23},{8,24},{9,... | collective-permute-start | bytes 221192 | tf_op jit(solution)/shard_map/ppermute | solution.py:284
  31.8 28.7 %collective-permute-start.6 = (bf16[1,1,1,1,1,32,4096]{6,5,4,3,2,1,0:T(8,128)(2,1)S(1)}, bf16[1,1,1,1,1,32,4096]{6,5,4,3,2,1,0:T(8,128)(2,1)S(1)}, u32[]{:S(2)}, u32[]{:S(2)}) collective-permute-start(bf16[1,1,1,1,1,32,4096]{6,5,4,3,2,1,0:T(8,128)(2,1)S(1)} %bitcast.358), channel_id=1, source_target_pairs={{0,16},{1,17},{2,18},{3,19},{4,20},{5,21},{6,22},{7,23},{8,24},{9,... | collective-permute-start | bytes 786440 | tf_op jit(solution)/shard_map/ppermute | solution.py:284
  34.8 25.7 %collective-permute-start.12 = (bf16[1,1,1,1,1,128,1024]{6,5,4,3,2,1,0:T(8,128)(2,1)S(1)}, bf16[1,1,1,1,1,128,1024]{6,5,4,3,2,1,0:T(8,128)(2,1)S(1)}, u32[]{:S(2)}, u32[]{:S(2)}) collective-permute-start(bf16[1,1,1,1,1,128,1024]{6,5,4,3,2,1,0:T(8,128)(2,1)S(1)} %bitcast.356), channel_id=1, source_target_pairs={{0,16},{1,17},{2,18},{3,19},{4,20},{5,21},{6,22},{7,23},{8,24},{9,... | collective-permute-start | bytes 786440 | tf_op jit(solution)/shard_map/ppermute | solution.py:284
  43.1 21.6 %collective-permute-start.9 = (bf16[2,2,1,1,1,32,1536]{6,5,4,3,2,1,0:T(8,128)(2,1)S(1)}, bf16[2,2,1,1,1,32,1536]{6,5,4,3,2,1,0:T(8,128)(2,1)S(1)}, u32[]{:S(2)}, u32[]{:S(2)}) collective-permute-start(bf16[2,2,1,1,1,32,1536]{6,5,4,3,2,1,0:T(8,128)(2,1)S(1)} %constant_dynamic-update-slice_fusion.52), channel_id=1, source_target_pairs={{0,4},{1,5},{2,6},{3,7},{4,0},{5,1},{6,2},{7,3},{8,12},{9,13},{10,... | collective-permute-start | bytes 1179656 | tf_op jit(solution)/shard_map/ppermute | solution.py:284
  46.5 16.6 %collective-permute-start.2 = (bf16[2,2,1,1,1,32,1536]{6,5,4,3,2,1,0:T(8,128)(2,1)S(1)}, bf16[2,2,1,1,1,32,1536]{6,5,4,3,2,1,0:T(8,128)(2,1)S(1)}, u32[]{:S(2)}, u32[]{:S(2)}) collective-permute-start(bf16[2,2,1,1,1,32,1536]{6,5,4,3,2,1,0:T(8,128)(2,1)S(1)} %constant_dynamic-update-slice_fusion.64), channel_id=1, source_target_pairs={{0,2},{1,3},{2,0},{3,1},{4,6},{5,7},{6,4},{7,5},{8,10},{9,11},{10,... | collective-permute-start | bytes 1179656 | tf_op jit(solution)/shard_map/ppermute | solution.py:284
  48.0 15.0 %collective-permute-start.21 = (bf16[2,1,1,1,1,32,1152]{6,5,4,3,2,1,0:T(8,128)(2,1)S(1)}, bf16[2,1,1,1,1,32,1152]{6,5,4,3,2,1,0:T(8,128)(2,1)S(1)}, u32[]{:S(2)}, u32[]{:S(2)}) collective-permute-start(bf16[2,1,1,1,1,32,1152]{6,5,4,3,2,1,0:T(8,128)(2,1)S(1)} %constant_dynamic-update-slice_fusion.28), channel_id=1, source_target_pairs={{0,8},{1,9},{2,10},{3,11},{4,12},{5,13},{6,14},{7,15},{8,0},{9,1},... | collective-permute-start | bytes 442376 | tf_op jit(solution)/shard_map/ppermute | solution.py:284
  60.6 24.0 %collective-permute-start.8 = (bf16[2,1,1,1,1,32,4096]{6,5,4,3,2,1,0:T(8,128)(2,1)S(1)}, bf16[2,1,1,1,1,32,4096]{6,5,4,3,2,1,0:T(8,128)(2,1)S(1)}, u32[]{:S(2)}, u32[]{:S(2)}) collective-permute-start(bf16[2,1,1,1,1,32,4096]{6,5,4,3,2,1,0:T(8,128)(2,1)S(1)} %constant_dynamic-update-slice_fusion.54), channel_id=1, source_target_pairs={{0,8},{1,9},{2,10},{3,11},{4,12},{5,13},{6,14},{7,15},{8,0},{9,1},... | collective-permute-start | bytes 1572872 | tf_op jit(solution)/shard_map/ppermute | solution.py:284
  60.7 23.8 %collective-permute-start.13 = (bf16[2,1,1,1,1,128,1024]{6,5,4,3,2,1,0:T(8,128)(2,1)S(1)}, bf16[2,1,1,1,1,128,1024]{6,5,4,3,2,1,0:T(8,128)(2,1)S(1)}, u32[]{:S(2)}, u32[]{:S(2)}) collective-permute-start(bf16[2,1,1,1,1,128,1024]{6,5,4,3,2,1,0:T(8,128)(2,1)S(1)} %constant_dynamic-update-slice_fusion.42), channel_id=1, source_target_pairs={{0,8},{1,9},{2,10},{3,11},{4,12},{5,13},{6,14},{7,15},{8,0},{9,1},... | collective-permute-start | bytes 1572872 | tf_op jit(solution)/shard_map/ppermute | solution.py:284
  63.1 29.5 %collective-permute-start.3 = (bf16[2,2,1,2,1,32,1536]{6,5,4,3,2,1,0:T(8,128)(2,1)S(1)}, bf16[2,2,1,2,1,32,1536]{6,5,4,3,2,1,0:T(8,128)(2,1)S(1)}, u32[]{:S(2)}, u32[]{:S(2)}) collective-permute-start(bf16[2,2,1,2,1,32,1536]{6,5,4,3,2,1,0:T(8,128)(2,1)S(1)} %constant_dynamic-update-slice_fusion.62), channel_id=1, source_target_pairs={{0,4},{1,5},{2,6},{3,7},{4,0},{5,1},{6,2},{7,3},{8,12},{9,13},{10,... | collective-permute-start | bytes 2359304 | tf_op jit(solution)/shard_map/ppermute | solution.py:284
  64.7 26.8 %collective-permute-start.11 = (bf16[2,2,2,1,1,32,1536]{6,5,4,3,2,1,0:T(8,128)(2,1)S(1)}, bf16[2,2,2,1,1,32,1536]{6,5,4,3,2,1,0:T(8,128)(2,1)S(1)}, u32[]{:S(2)}, u32[]{:S(2)}) collective-permute-start(bf16[2,2,2,1,1,32,1536]{6,5,4,3,2,1,0:T(8,128)(2,1)S(1)} %constant_dynamic-update-slice_fusion.48), channel_id=1, source_target_pairs={{0,2},{1,3},{2,0},{3,1},{4,6},{5,7},{6,4},{7,5},{8,10},{9,11},{10,... | collective-permute-start | bytes 2359304 | tf_op jit(solution)/shard_map/ppermute | solution.py:284
  66.3 25.2 %collective-permute-start.22 = (bf16[2,2,1,1,1,32,1152]{6,5,4,3,2,1,0:T(8,128)(2,1)S(1)}, bf16[2,2,1,1,1,32,1152]{6,5,4,3,2,1,0:T(8,128)(2,1)S(1)}, u32[]{:S(2)}, u32[]{:S(2)}) collective-permute-start(bf16[2,2,1,1,1,32,1152]{6,5,4,3,2,1,0:T(8,128)(2,1)S(1)} %constant_dynamic-update-slice_fusion.26), channel_id=1, source_target_pairs={{0,2},{1,3},{2,0},{3,1},{4,6},{5,7},{6,4},{7,5},{8,10},{9,11},{10,... | collective-permute-start | bytes 884744 | tf_op jit(solution)/shard_map/ppermute | solution.py:284
  84.6 29.0 %collective-permute-start.10 = (bf16[2,2,1,1,1,32,4096]{6,5,4,3,2,1,0:T(8,128)(2,1)S(1)}, bf16[2,2,1,1,1,32,4096]{6,5,4,3,2,1,0:T(8,128)(2,1)S(1)}, u32[]{:S(2)}, u32[]{:S(2)}) collective-permute-start(bf16[2,2,1,1,1,32,4096]{6,5,4,3,2,1,0:T(8,128)(2,1)S(1)} %constant_dynamic-update-slice_fusion.50), channel_id=1, source_target_pairs={{0,2},{1,3},{2,0},{3,1},{4,6},{5,7},{6,4},{7,5},{8,10},{9,11},{10,... | collective-permute-start | bytes 3145736 | tf_op jit(solution)/shard_map/ppermute | solution.py:284
  86.2 26.0 %collective-permute-start.14 = (bf16[2,2,1,1,1,128,1024]{6,5,4,3,2,1,0:T(8,128)(2,1)S(1)}, bf16[2,2,1,1,1,128,1024]{6,5,4,3,2,1,0:T(8,128)(2,1)S(1)}, u32[]{:S(2)}, u32[]{:S(2)}) collective-permute-start(bf16[2,2,1,1,1,128,1024]{6,5,4,3,2,1,0:T(8,128)(2,1)S(1)} %constant_dynamic-update-slice_fusion.40), channel_id=1, source_target_pairs={{0,4},{1,5},{2,6},{3,7},{4,0},{5,1},{6,2},{7,3},{8,12},{9,13},{10,... | collective-permute-start | bytes 3145736 | tf_op jit(solution)/shard_map/ppermute | solution.py:284
  92.5 37.0 %collective-permute-start.25 = (bf16[2,2,2,2,1,32,1536]{6,5,4,3,2,1,0:T(8,128)(2,1)}, bf16[2,2,2,2,1,32,1536]{6,5,4,3,2,1,0:T(8,128)(2,1)}, u32[]{:S(2)}, u32[]{:S(2)}) collective-permute-start(bf16[2,2,2,2,1,32,1536]{6,5,4,3,2,1,0:T(8,128)(2,1)} %constant_dynamic-update-slice_fusion.44), channel_id=1, source_target_pairs={{0,1},{1,0},{2,3},{3,2},{4,5},{5,4},{6,7},{7,6},{8,9},{9,8},{10,11... | collective-permute-start | bytes 4718600 | tf_op jit(solution)/shard_map/ppermute | solution.py:284
  93.5 36.1 %collective-permute-start.4 = (bf16[2,2,2,2,1,32,1536]{6,5,4,3,2,1,0:T(8,128)(2,1)}, bf16[2,2,2,2,1,32,1536]{6,5,4,3,2,1,0:T(8,128)(2,1)}, u32[]{:S(2)}, u32[]{:S(2)}) collective-permute-start(bf16[2,2,2,2,1,32,1536]{6,5,4,3,2,1,0:T(8,128)(2,1)} %constant_dynamic-update-slice_fusion.60), channel_id=1, source_target_pairs={{0,1},{1,0},{2,3},{3,2},{4,5},{5,4},{6,7},{7,6},{8,9},{9,8},{10,11... | collective-permute-start | bytes 4718600 | tf_op jit(solution)/shard_map/ppermute | solution.py:284
  94.0 31.7 %collective-permute-start.23 = (bf16[2,2,1,2,1,32,1152]{6,5,4,3,2,1,0:T(8,128)(2,1)S(1)}, bf16[2,2,1,2,1,32,1152]{6,5,4,3,2,1,0:T(8,128)(2,1)}, u32[]{:S(2)}, u32[]{:S(2)}) collective-permute-start(bf16[2,2,1,2,1,32,1152]{6,5,4,3,2,1,0:T(8,128)(2,1)S(1)} %constant_dynamic-update-slice_fusion.24), channel_id=1, source_target_pairs={{0,4},{1,5},{2,6},{3,7},{4,0},{5,1},{6,2},{7,3},{8,12},{9,13},{10,... | collective-permute-start | bytes 1769480 | tf_op jit(solution)/shard_map/ppermute | solution.py:284
  113.9 52.7 %collective-permute-start.26 = (bf16[2,2,1,2,1,32,4096]{6,5,4,3,2,1,0:T(8,128)(2,1)S(1)}, bf16[2,2,1,2,1,32,4096]{6,5,4,3,2,1,0:T(8,128)(2,1)}, u32[]{:S(2)}, u32[]{:S(2)}) collective-permute-start(bf16[2,2,1,2,1,32,4096]{6,5,4,3,2,1,0:T(8,128)(2,1)S(1)} %constant_dynamic-update-slice_fusion.46), channel_id=1, source_target_pairs={{0,4},{1,5},{2,6},{3,7},{4,0},{5,1},{6,2},{7,3},{8,12},{9,13},{10,... | collective-permute-start | bytes 6291464 | tf_op jit(solution)/shard_map/ppermute | solution.py:284
  115.4 111.0 %collective-permute-start.27 = (bf16[2,2,2,1,1,128,1024]{6,5,4,3,2,1,0:T(8,128)(2,1)}, bf16[2,2,2,1,1,128,1024]{6,5,4,3,2,1,0:T(8,128)(2,1)}, u32[]{:S(2)}, u32[]{:S(2)}) collective-permute-start(bf16[2,2,2,1,1,128,1024]{6,5,4,3,2,1,0:T(8,128)(2,1)} %copy-done.24), channel_id=1, source_target_pairs={{0,2},{1,3},{2,0},{3,1},{4,6},{5,7},{6,4},{7,5},{8,10},{9,11},{10,... | collective-permute-start | bytes 6291464 | tf_op jit(solution)/shard_map/ppermute | solution.py:284
  127.9 96.7 %collective-permute-start.24 = (bf16[2,2,2,2,1,32,1152]{6,5,4,3,2,1,0:T(8,128)(2,1)}, bf16[2,2,2,2,1,32,1152]{6,5,4,3,2,1,0:T(8,128)(2,1)}, u32[]{:S(2)}, u32[]{:S(2)}) collective-permute-start(bf16[2,2,2,2,1,32,1152]{6,5,4,3,2,1,0:T(8,128)(2,1)} %constant_dynamic-update-slice_fusion.22), channel_id=1, source_target_pairs={{0,1},{1,0},{2,3},{3,2},{4,5},{5,4},{6,7},{7,6},{8,9},{9,8},{10,11... | collective-permute-start | bytes 3538952 | tf_op jit(solution)/shard_map/ppermute | solution.py:284
  169.7 75.1 %collective-permute-start.28 = (bf16[2,2,2,2,1,32,4096]{6,5,4,3,2,1,0:T(8,128)(2,1)}, bf16[2,2,2,2,1,32,4096]{6,5,4,3,2,1,0:T(8,128)(2,1)}, u32[]{:S(2)}, u32[]{:S(2)}) collective-permute-start(bf16[2,2,2,2,1,32,4096]{6,5,4,3,2,1,0:T(8,128)(2,1)} %constant_dynamic-update-slice_fusion.16), channel_id=1, source_target_pairs={{0,1},{1,0},{2,3},{3,2},{4,5},{5,4},{6,7},{7,6},{8,9},{9,8},{10,11... | collective-permute-start | bytes 12582920 | tf_op jit(solution)/shard_map/ppermute | solution.py:284
  229.2 41.2 %collective-permute-start.29 = (bf16[2,2,2,2,1,128,1024]{6,5,4,3,2,1,0:T(8,128)(2,1)S(1)}, bf16[2,2,2,2,1,128,1024]{6,5,4,3,2,1,0:T(8,128)(2,1)}, u32[]{:S(2)}, u32[]{:S(2)}) collective-permute-start(bf16[2,2,2,2,1,128,1024]{6,5,4,3,2,1,0:T(8,128)(2,1)S(1)} %constant_dynamic-update-slice_fusion.14), channel_id=1, source_target_pairs={{0,1},{1,0},{2,3},{3,2},{4,5},{5,4},{6,7},{7,6},{8,9},{9,8},{10,11... | collective-permute-start | bytes 12582920 | tf_op jit(solution)/shard_map/ppermute | solution.py:284
  451.0 41.2 %collective-permute-start.45 = (bf16[2,2,2,2,1,128,1024]{6,5,4,3,2,1,0:T(8,128)(2,1)}, bf16[2,2,2,2,1,128,1024]{6,5,4,3,2,1,0:T(8,128)(2,1)}, u32[]{:S(2)}, u32[]{:S(2)}) collective-permute-start(bf16[2,2,2,2,1,128,1024]{6,5,4,3,2,1,0:T(8,128)(2,1)} %constant_dynamic-slice_fusion.36), channel_id=1, source_target_pairs={{0,1},{1,0},{2,3},{3,2},{4,5},{5,4},{6,7},{7,6},{8,9},{9,8},{10,11... | collective-permute-start | bytes 12582920 | tf_op jit(solution)/shard_map/ppermute | solution.py:284
  490.9 32.7 %collective-permute-start.46 = (bf16[2,2,2,2,1,32,4096]{6,5,4,3,2,1,0:T(8,128)(2,1)}, bf16[2,2,2,2,1,32,4096]{6,5,4,3,2,1,0:T(8,128)(2,1)}, u32[]{:S(2)}, u32[]{:S(2)}) collective-permute-start(bf16[2,2,2,2,1,32,4096]{6,5,4,3,2,1,0:T(8,128)(2,1)} %constant_dynamic-slice_fusion.35), channel_id=1, source_target_pairs={{0,1},{1,0},{2,3},{3,2},{4,5},{5,4},{6,7},{7,6},{8,9},{9,8},{10,11... | collective-permute-start | bytes 12582920 | tf_op jit(solution)/shard_map/ppermute | solution.py:284
  537.0 75.4 %collective-permute-start.48 = (bf16[2,2,2,1,1,128,1024]{6,5,4,3,2,1,0:T(8,128)(2,1)}, bf16[2,2,2,1,1,128,1024]{6,5,4,3,2,1,0:T(8,128)(2,1)}, u32[]{:S(2)}, u32[]{:S(2)}) collective-permute-start(bf16[2,2,2,1,1,128,1024]{6,5,4,3,2,1,0:T(8,128)(2,1)} %constant_dynamic-slice_fusion.33), channel_id=1, source_target_pairs={{0,2},{1,3},{2,0},{3,1},{4,6},{5,7},{6,4},{7,5},{8,10},{9,11},{10,... | collective-permute-start | bytes 6291464 | tf_op jit(solution)/shard_map/ppermute | solution.py:284
  540.8 8.4 %collective-permute-start.47 = (bf16[2,2,2,2,1,32,1152]{6,5,4,3,2,1,0:T(8,128)(2,1)S(1)}, bf16[2,2,2,2,1,32,1152]{6,5,4,3,2,1,0:T(8,128)(2,1)S(1)}, u32[]{:S(2)}, u32[]{:S(2)}) collective-permute-start(bf16[2,2,2,2,1,32,1152]{6,5,4,3,2,1,0:T(8,128)(2,1)S(1)} %constant_dynamic-slice_fusion.34), channel_id=1, source_target_pairs={{0,1},{1,0},{2,3},{3,2},{4,5},{5,4},{6,7},{7,6},{8,9},{9,8},{10,11... | collective-permute-start | bytes 3538952 | tf_op jit(solution)/shard_map/ppermute | solution.py:284
  543.1 73.5 %collective-permute-start.50 = (bf16[2,2,1,2,1,32,4096]{6,5,4,3,2,1,0:T(8,128)(2,1)}, bf16[2,2,1,2,1,32,4096]{6,5,4,3,2,1,0:T(8,128)(2,1)}, u32[]{:S(2)}, u32[]{:S(2)}) collective-permute-start(bf16[2,2,1,2,1,32,4096]{6,5,4,3,2,1,0:T(8,128)(2,1)} %constant_dynamic-slice_fusion.31), channel_id=1, source_target_pairs={{0,4},{1,5},{2,6},{3,7},{4,0},{5,1},{6,2},{7,3},{8,12},{9,13},{10,... | collective-permute-start | bytes 6291464 | tf_op jit(solution)/shard_map/ppermute | solution.py:284
  549.6 53.8 %collective-permute-start.51 = (bf16[2,2,1,2,1,32,1152]{6,5,4,3,2,1,0:T(8,128)(2,1)S(1)}, bf16[2,2,1,2,1,32,1152]{6,5,4,3,2,1,0:T(8,128)(2,1)S(1)}, u32[]{:S(2)}, u32[]{:S(2)}) collective-permute-start(bf16[2,2,1,2,1,32,1152]{6,5,4,3,2,1,0:T(8,128)(2,1)S(1)} %constant_dynamic-slice_fusion.30), channel_id=1, source_target_pairs={{0,4},{1,5},{2,6},{3,7},{4,0},{5,1},{6,2},{7,3},{8,12},{9,13},{10,... | collective-permute-start | bytes 1769480 | tf_op jit(solution)/shard_map/ppermute | solution.py:284
  603.5 7.9 %collective-permute-start.61 = (bf16[2,2,1,1,1,32,1152]{6,5,4,3,2,1,0:T(8,128)(2,1)S(1)}, bf16[2,2,1,1,1,32,1152]{6,5,4,3,2,1,0:T(8,128)(2,1)S(1)}, u32[]{:S(2)}, u32[]{:S(2)}) collective-permute-start(bf16[2,2,1,1,1,32,1152]{6,5,4,3,2,1,0:T(8,128)(2,1)S(1)} %constant_dynamic-slice_fusion.20), channel_id=1, source_target_pairs={{0,2},{1,3},{2,0},{3,1},{4,6},{5,7},{6,4},{7,5},{8,10},{9,11},{10,... | collective-permute-start | bytes 884744 | tf_op jit(solution)/shard_map/ppermute | solution.py:284
  605.2 21.3 %collective-permute-start.49 = (bf16[2,2,2,2,1,32,1536]{6,5,4,3,2,1,0:T(8,128)(2,1)S(1)}, bf16[2,2,2,2,1,32,1536]{6,5,4,3,2,1,0:T(8,128)(2,1)S(1)}, u32[]{:S(2)}, u32[]{:S(2)}) collective-permute-start(bf16[2,2,2,2,1,32,1536]{6,5,4,3,2,1,0:T(8,128)(2,1)S(1)} %constant_dynamic-slice_fusion.32), channel_id=1, source_target_pairs={{0,1},{1,0},{2,3},{3,2},{4,5},{5,4},{6,7},{7,6},{8,9},{9,8},{10,11... | collective-permute-start | bytes 4718600 | tf_op jit(solution)/shard_map/ppermute | solution.py:284
  611.6 7.4 collective-permute-start.62
  615.0 40.4 %collective-permute-start.67 = (bf16[2,2,1,1,1,128,1024]{6,5,4,3,2,1,0:T(8,128)(2,1)S(1)}, bf16[2,2,1,1,1,128,1024]{6,5,4,3,2,1,0:T(8,128)(2,1)}, u32[]{:S(2)}, u32[]{:S(2)}) collective-permute-start(bf16[2,2,1,1,1,128,1024]{6,5,4,3,2,1,0:T(8,128)(2,1)S(1)} %constant_dynamic-slice_fusion.14), channel_id=1, source_target_pairs={{0,4},{1,5},{2,6},{3,7},{4,0},{5,1},{6,2},{7,3},{8,12},{9,13},{10,... | collective-permute-start | bytes 3145736 | tf_op jit(solution)/shard_map/ppermute | solution.py:284
  620.5 38.7 %collective-permute-start.64 = (bf16[2,2,1,1,1,32,4096]{6,5,4,3,2,1,0:T(8,128)(2,1)S(1)}, bf16[2,2,1,1,1,32,4096]{6,5,4,3,2,1,0:T(8,128)(2,1)}, u32[]{:S(2)}, u32[]{:S(2)}) collective-permute-start(bf16[2,2,1,1,1,32,4096]{6,5,4,3,2,1,0:T(8,128)(2,1)S(1)} %constant_dynamic-slice_fusion.17), channel_id=1, source_target_pairs={{0,2},{1,3},{2,0},{3,1},{4,6},{5,7},{6,4},{7,5},{8,10},{9,11},{10,... | collective-permute-start | bytes 3145736 | tf_op jit(solution)/shard_map/ppermute | solution.py:284
  627.9 34.5 %collective-permute-start.52 = (bf16[2,2,1,2,1,32,1536]{6,5,4,3,2,1,0:T(8,128)(2,1)}, bf16[2,2,1,2,1,32,1536]{6,5,4,3,2,1,0:T(8,128)(2,1)}, u32[]{:S(2)}, u32[]{:S(2)}) collective-permute-start(bf16[2,2,1,2,1,32,1536]{6,5,4,3,2,1,0:T(8,128)(2,1)} %constant_dynamic-slice_fusion.29), channel_id=1, source_target_pairs={{0,4},{1,5},{2,6},{3,7},{4,0},{5,1},{6,2},{7,3},{8,12},{9,13},{10,... | collective-permute-start | bytes 2359304 | tf_op jit(solution)/shard_map/ppermute | solution.py:284
  658.1 43.6 %collective-permute-start.68 = (bf16[2,1,1,1,1,128,1024]{6,5,4,3,2,1,0:T(8,128)(2,1)}, bf16[2,1,1,1,1,128,1024]{6,5,4,3,2,1,0:T(8,128)(2,1)}, u32[]{:S(2)}, u32[]{:S(2)}) collective-permute-start(bf16[2,1,1,1,1,128,1024]{6,5,4,3,2,1,0:T(8,128)(2,1)} %constant_dynamic-slice_fusion.13), channel_id=1, source_target_pairs={{0,8},{1,9},{2,10},{3,11},{4,12},{5,13},{6,14},{7,15},{8,0},{9,1},... | collective-permute-start | bytes 1572872 | tf_op jit(solution)/shard_map/ppermute | solution.py:284
  661.5 38.2 %collective-permute-start.65 = (bf16[2,1,1,1,1,32,4096]{6,5,4,3,2,1,0:T(8,128)(2,1)}, bf16[2,1,1,1,1,32,4096]{6,5,4,3,2,1,0:T(8,128)(2,1)}, u32[]{:S(2)}, u32[]{:S(2)}) collective-permute-start(bf16[2,1,1,1,1,32,4096]{6,5,4,3,2,1,0:T(8,128)(2,1)} %constant_dynamic-slice_fusion.16), channel_id=1, source_target_pairs={{0,8},{1,9},{2,10},{3,11},{4,12},{5,13},{6,14},{7,15},{8,0},{9,1},... | collective-permute-start | bytes 1572872 | tf_op jit(solution)/shard_map/ppermute | solution.py:284
  691.1 34.8 %collective-permute-start.53 = (bf16[2,2,1,1,1,32,1536]{6,5,4,3,2,1,0:T(8,128)(2,1)S(1)}, bf16[2,2,1,1,1,32,1536]{6,5,4,3,2,1,0:T(8,128)(2,1)}, u32[]{:S(2)}, u32[]{:S(2)}) collective-permute-start(bf16[2,2,1,1,1,32,1536]{6,5,4,3,2,1,0:T(8,128)(2,1)S(1)} %constant_dynamic-slice_fusion.28), channel_id=1, source_target_pairs={{0,2},{1,3},{2,0},{3,1},{4,6},{5,7},{6,4},{7,5},{8,10},{9,11},{10,... | collective-permute-start | bytes 1179656 | tf_op jit(solution)/shard_map/ppermute | solution.py:284
  695.1 25.6 %collective-permute-start.56 = (bf16[2,2,2,2,1,32,1536]{6,5,4,3,2,1,0:T(8,128)(2,1)}, bf16[2,2,2,2,1,32,1536]{6,5,4,3,2,1,0:T(8,128)(2,1)}, u32[]{:S(2)}, u32[]{:S(2)}) collective-permute-start(bf16[2,2,2,2,1,32,1536]{6,5,4,3,2,1,0:T(8,128)(2,1)} %constant_dynamic-slice_fusion.25), channel_id=1, source_target_pairs={{0,1},{1,0},{2,3},{3,2},{4,5},{5,4},{6,7},{7,6},{8,9},{9,8},{10,11... | collective-permute-start | bytes 4718600 | tf_op jit(solution)/shard_map/ppermute | solution.py:284
  701.2 18.6 %collective-permute-start.66 = (bf16[1,1,1,1,1,32,4096]{6,5,4,3,2,1,0:T(8,128)(2,1)S(1)}, bf16[1,1,1,1,1,32,4096]{6,5,4,3,2,1,0:T(8,128)(2,1)S(1)}, u32[]{:S(2)}, u32[]{:S(2)}) collective-permute-start(bf16[1,1,1,1,1,32,4096]{6,5,4,3,2,1,0:T(8,128)(2,1)S(1)} %constant_dynamic-slice_fusion.15), channel_id=1, source_target_pairs={{0,16},{1,17},{2,18},{3,19},{4,20},{5,21},{6,22},{7,23},{8,24},{9,... | collective-permute-start | bytes 786440 | tf_op jit(solution)/shard_map/ppermute | solution.py:284
  703.0 22.0 %collective-permute-start.69 = (bf16[1,1,1,1,1,128,1024]{6,5,4,3,2,1,0:T(8,128)(2,1)S(1)}, bf16[1,1,1,1,1,128,1024]{6,5,4,3,2,1,0:T(8,128)(2,1)S(1)}, u32[]{:S(2)}, u32[]{:S(2)}) collective-permute-start(bf16[1,1,1,1,1,128,1024]{6,5,4,3,2,1,0:T(8,128)(2,1)S(1)} %constant_dynamic-slice_fusion.12), channel_id=1, source_target_pairs={{0,16},{1,17},{2,18},{3,19},{4,20},{5,21},{6,22},{7,23},{8,24},{9,... | collective-permute-start | bytes 786440 | tf_op jit(solution)/shard_map/ppermute | solution.py:284
  722.6 18.9 %collective-permute-start.57 = (bf16[2,2,2,1,1,32,1536]{6,5,4,3,2,1,0:T(8,128)(2,1)S(1)}, bf16[2,2,2,1,1,32,1536]{6,5,4,3,2,1,0:T(8,128)(2,1)S(1)}, u32[]{:S(2)}, u32[]{:S(2)}) collective-permute-start(bf16[2,2,2,1,1,32,1536]{6,5,4,3,2,1,0:T(8,128)(2,1)S(1)} %constant_dynamic-slice_fusion.24), channel_id=1, source_target_pairs={{0,2},{1,3},{2,0},{3,1},{4,6},{5,7},{6,4},{7,5},{8,10},{9,11},{10,... | collective-permute-start | bytes 2359304 | tf_op jit(solution)/shard_map/ppermute | solution.py:284
  727.0 16.1 %collective-permute-start.54 = (bf16[2,1,1,1,1,32,1536]{6,5,4,3,2,1,0:T(8,128)(2,1)S(1)}, bf16[2,1,1,1,1,32,1536]{6,5,4,3,2,1,0:T(8,128)(2,1)S(1)}, u32[]{:S(2)}, u32[]{:S(2)}) collective-permute-start(bf16[2,1,1,1,1,32,1536]{6,5,4,3,2,1,0:T(8,128)(2,1)S(1)} %constant_dynamic-slice_fusion.27), channel_id=1, source_target_pairs={{0,8},{1,9},{2,10},{3,11},{4,12},{5,13},{6,14},{7,15},{8,0},{9,1},... | collective-permute-start | bytes 589832 | tf_op jit(solution)/shard_map/ppermute | solution.py:284
  741.7 9.6 %collective-permute-start.58 = (bf16[2,2,1,1,1,32,1536]{6,5,4,3,2,1,0:T(8,128)(2,1)S(1)}, bf16[2,2,1,1,1,32,1536]{6,5,4,3,2,1,0:T(8,128)(2,1)S(1)}, u32[]{:S(2)}, u32[]{:S(2)}) collective-permute-start(bf16[2,2,1,1,1,32,1536]{6,5,4,3,2,1,0:T(8,128)(2,1)S(1)} %constant_dynamic-slice_fusion.23), channel_id=1, source_target_pairs={{0,4},{1,5},{2,6},{3,7},{4,0},{5,1},{6,2},{7,3},{8,12},{9,13},{10,... | collective-permute-start | bytes 1179656 | tf_op jit(solution)/shard_map/ppermute | solution.py:284
  743.2 8.3 %collective-permute-start.55 = (bf16[1,1,1,1,1,32,1536]{6,5,4,3,2,1,0:T(8,128)(2,1)S(1)}, bf16[1,1,1,1,1,32,1536]{6,5,4,3,2,1,0:T(8,128)(2,1)S(1)}, u32[]{:S(2)}, u32[]{:S(2)}) collective-permute-start(bf16[1,1,1,1,1,32,1536]{6,5,4,3,2,1,0:T(8,128)(2,1)S(1)} %constant_dynamic-slice_fusion.26), channel_id=1, source_target_pairs={{0,16},{1,17},{2,18},{3,19},{4,20},{5,21},{6,22},{7,23},{8,24},{9,... | collective-permute-start | bytes 294920 | tf_op jit(solution)/shard_map/ppermute | solution.py:284
  (108 other events, 2110.0 us)

commit v3 on v2

--- a/solution.py
+++ b/solution.py
@@ -227,19 +227,24 @@
     def wait(self, *earlier):
         self.held = after(self.held, *earlier)
 
-    def step(self):
-        place = self.order.pop(0)
-        axis = self.links.bits - 1 - place
-        mine = self.links.side(place)
+    def launch(self):
+        self.place = self.order.pop(0)
+        self.before = self.held
+        self.arrived = self.links.swap(self.held, 1 << self.place)
+
+    def merge(self, *earlier):
+        axis = self.links.bits - 1 - self.place
+        mine = self.links.side(self.place)
         held = self.held
-        arrived = self.links.swap(held, 1 << place)
+        arrived = after(self.arrived, *earlier) if earlier else self.arrived
         both = jnp.zeros(held.shape[:axis] + (2,) + held.shape[axis + 1 :], held.dtype)
         both = lax.dynamic_update_slice_in_dim(both, held, mine, axis)
         self.held = lax.dynamic_update_slice_in_dim(both, arrived, 1 - mine, axis)
 
     def full(self):
         while self.order:
-            self.step()
+            self.launch()
+            self.merge()
         return self.held.reshape((self.links.count,) + self.block)
 
 
@@ -252,18 +257,25 @@
     def wait(self, *earlier):
         self.held = after(self.held, *earlier)
 
-    def step(self):
-        place = self.order.pop()
-        axis = self.links.bits - 1 - place
-        mine = self.links.side(place)
-        leaving = lax.dynamic_slice_in_dim(self.held, 1 - mine, 1, axis)
-        kept = lax.dynamic_slice_in_dim(self.held, mine, 1, axis)
-        total = kept.astype(f32) + self.links.swap(leaving, 1 << place).astype(f32)
+    def launch(self):
+        self.place = self.order.pop()
+        axis = self.links.bits - 1 - self.place
+        self.leaving = lax.dynamic_slice_in_dim(
+            self.held, 1 - self.links.side(self.place), 1, axis
+        )
+        self.arrived = self.links.swap(self.leaving, 1 << self.place)
+
+    def merge(self, *earlier):
+        axis = self.links.bits - 1 - self.place
+        kept = lax.dynamic_slice_in_dim(self.held, self.links.side(self.place), 1, axis)
+        arrived = after(self.arrived, *earlier) if earlier else self.arrived
+        total = kept.astype(f32) + arrived.astype(f32)
         self.held = total.astype(self.wire) if self.order else total
 
     def mine(self):
         while self.order:
-            self.step()
+            self.launch()
+            self.merge()
         return self.held.reshape(self.block)
 
 
@@ -297,12 +309,15 @@
 
 class Whole:
     def __init__(self, value):
-        self.held = value
+        self.held = self.before = self.leaving = value
 
     def wait(self, *earlier):
         pass
 
-    def step(self):
+    def launch(self):
+        pass
+
+    def merge(self, *earlier):
         pass
 
     def full(self):
@@ -386,18 +401,24 @@
     out_part = links.growing(jnp.concatenate([w_out, w_proj], axis=1), 0)
     up_part = links.growing(w_up, 0)
     down_part = links.growing(w_down, 1)
-    for hop in range(4):
-        for one in sides + [small_part]:
-            one.step()
-        for one in (out_part, up_part, down_part):
-            one.wait(sides[0].held, sides[1].held)
-            if hop < 3:
-                one.step()
-    for one in sides + [small_part]:
-        one.step()
-        one.wait(up_part.held, down_part.held)
-    for one in (out_part, up_part, down_part):
-        one.step()
+    rest = (out_part, up_part, down_part)
+    for hop in range(5):
+        for one in sides:
+            one.launch()
+        if hop > 0:
+            small_part.wait(sides[0].before, sides[1].before)
+        small_part.launch()
+        for one in sides:
+            one.merge()
+        first = (sides[0].held, sides[1].held)
+        small_part.merge(*first)
+        if hop > 0 and hop < 4:
+            for one in rest:
+                one.merge(*first)
+        if hop < 4:
+            for one in rest:
+                one.wait(*first)
+                one.launch()
     small_full = small_part.full().reshape(count, -1)
     full_qkv = [rows_of(one.full()) for one in sides]
     full_biases = (
@@ -432,11 +453,20 @@
         context, lse, query_lse = attention_forward(
             qkv[side], segrow, segcol, bounds, row_len, span
         )
+        if side == 0:
+            out_part.merge(context)
+            out_part.launch()
         contexts.append(context)
         saved.append((lse, query_lse))
-    contexts[1] = after(contexts[1], up_part.held, down_part.held)
+    for one in (up_part, down_part):
+        one.merge(*contexts)
+        one.launch()
+    contexts[1] = after(contexts[1], up_part.before, down_part.before)
+    out_part.merge()
     out_proj = rows_of(out_part.full())
     full_out, full_proj = out_proj[:, :model_width], out_proj[:, model_width:]
+    up_part.merge()
+    down_part.merge()
     full_up = rows_of(up_part.full())
     full_down = rows_of(down_part.full())
     attn_out = (
@@ -557,54 +587,75 @@
     grad_ffn = grad_mid.astype(bf16)
     down_grad = matmul_left_t(gelu_out, grad_ffn)
     down_sum = links.shrinking(spread_rows_of(down_grad), 1)
-    down_sum.step()
+    down_sum.launch()
     down_bias = jnp.sum(grad_ffn, axis=0, dtype=f32)
-    grad_gelu = matmul_right_t(grad_ffn, full_down)
+    grad_gelu = matmul_right_t(after(grad_ffn, down_sum.leaving), full_down)
     grad_up = (grad_gelu * slope.astype(f32)).astype(bf16)
     upbias_grad = jnp.sum(grad_up, axis=0, dtype=f32)
     up_grad = matmul_left_t(first_low, grad_up)
     up_sum = links.shrinking(spread_rows_of(up_grad), 0)
-    up_sum.step()
-    grad_first = grad_mid + matmul_right_t(after(grad_up, down_sum.held), full_up)
-    down_sum.step()
+    up_sum.launch()
+    down_sum.merge(up_sum.leaving)
+    down_sum.launch()
+    grad_first = grad_mid + matmul_right_t(after(grad_up, down_sum.leaving), full_up)
     grad_res, gain_one, bias_one = layer_norm_back(
         grad_first, first_normed, first_scale, full_gains[0]
     )
-    grad_attn = after(grad_res.astype(bf16), up_sum.held)
-    up_sum.step()
+    up_sum.merge(grad_res)
+    up_sum.launch()
+    grad_attn = after(grad_res.astype(bf16), up_sum.leaving)
     out_bias = jnp.sum(grad_attn, axis=0, dtype=f32)
     out_grad = jnp.concatenate([matmul_left_t(c, grad_attn) for c in contexts], axis=0)
     out_sum = links.shrinking(spread_rows_of(jnp.concatenate([out_grad, proj_grad], axis=1)), 0)
-    out_sum.step()
+    out_sum.launch()
     input_grad = grad_res
     query_bias, value_bias, qkv_sums = [], [], []
-    earlier = (out_sum.held,)
+    grad_contexts = [
+        matmul_right_t(grad_attn, full_out[side * part : (side + 1) * part]).astype(bf16)
+        for side in range(2)
+    ]
+    down_sum.merge(*grad_contexts)
+    down_sum.launch()
+    earlier = (out_sum.leaving, down_sum.leaving)
     for side in range(2):
-        grad_context = matmul_right_t(
-            grad_attn, full_out[side * part : (side + 1) * part]
-        ).astype(bf16)
         grad_qkv = attention_backward(
-            qkv[side], after(grad_context, *earlier), contexts[side], *saved[side], segrow, segcol,
-            bounds, row_len, span,
+            qkv[side], after(grad_contexts[side], *earlier), contexts[side], *saved[side], segrow,
+            segcol, bounds, row_len, span,
         )
-        if side == 0:
-            out_sum.step()
-        else:
-            grad_qkv = after(grad_qkv, up_sum.held, out_sum.held, qkv_sums[0].held)
-            up_sum.step()
-            qkv_sums[0].step()
+        if side == 1:
+            up_sum.merge(grad_qkv)
+            up_sum.launch()
+            down_sum.merge(grad_qkv)
+            down_sum.launch()
+            qkv_sums[0].merge(grad_qkv)
+            qkv_sums[0].launch()
+            grad_qkv = after(grad_qkv, up_sum.leaving, down_sum.leaving, qkv_sums[0].leaving)
         query_bias.append(jnp.sum(grad_qkv[:, :part], axis=0, dtype=f32))
         value_bias.append(jnp.sum(grad_qkv[:, 2 * part :], axis=0, dtype=f32))
         qkv_grad = matmul_left_t(tokens, grad_qkv)
-        qkv_sums.append(links.shrinking(spread_rows_of(qkv_grad), side))
-        qkv_sums[side].step()
-        earlier = (down_sum.held, qkv_sums[0].held)
         if side == 0:
-            down_sum.step()
-            qkv_sums[0].step()
+            qkv_sums.append(links.shrinking(spread_rows_of(qkv_grad), side))
+        else:
+            wide = qkv_grad.shape[1] // 2
+            for lane in range(2):
+                piece = qkv_grad[:, lane * wide : (lane + 1) * wide]
+                qkv_sums.append(links.shrinking(spread_rows_of(piece), lane))
+        for one in qkv_sums[side:]:
+            one.launch()
+        if side == 0:
+            out_sum.merge(qkv_sums[0].leaving)
+            out_sum.launch()
+            earlier = (qkv_sums[0].leaving, out_sum.leaving)
+        grad_qkv = after(grad_qkv, *[one.leaving for one in qkv_sums[side:]])
         input_grad = input_grad + matmul_right_t(grad_qkv, full_qkv[side])
+    last = [one.leaving for one in qkv_sums[1:]]
+    for one in (out_sum, up_sum, down_sum, qkv_sums[0]):
+        one.merge(*last)
+    for one in qkv_sums[1:]:
+        one.merge()
     down_shard, up_shard, out_proj_shard = down_sum.mine(), up_sum.mine(), out_sum.mine()
     qkv_shards = [one.mine() for one in qkv_sums]
+    qkv_shards = [qkv_shards[0], jnp.concatenate(qkv_shards[1:], axis=-1)]
     bias_grads = jnp.stack(
         [
             jnp.concatenate(query_bias),

time: 776 us -> 738 us (0.951)
  waiting for transfers between devices: 208 us -> 144 us
  local copies, waits for them, and re-layouts: 101 us -> 131 us
    ppermute x75 -> x80, waiting for transfers between devices: 208 us -> 144 us  [swap(): return lax.ppermute(value, AXES, [(d, d ^ bit) for d in range(self.count)])]
    dynamic_update_slice x67 -> x68, local copies, waits for them, and re-layouts: 38.4 us -> 55.7 us  [the longest x35 30.5 us: merge(): self.held = lax.dynamic_update_slice_in_dim(both, arrived, 1 - mine, axis)]
    dynamic_slice x34 -> x39, local copies, waits for them, and re-layouts: 16.1 us -> 20.7 us  [launch(): lax.dynamic_slice_in_dim(self.held, 1 - self.links.side(self.place), 1, a...]
    ppermute x75 -> x80, starting transfers between devices: 66.2 us -> 68.4 us  [swap(): return lax.ppermute(value, AXES, [(d, d ^ bit) for d in range(self.count)])]
    convert_element_type x21 -> x25, other arithmetic: 35.3 us -> 36.7 us  [the longest x24 31 us: merge(): self.held = total.astype(self.wire) if self.order else total]
  transfers between devices with their start and end apart: 75 -> 80, of which waited for: 38 -> 43; matrix products, arithmetic and copies ran while one was open for 31% -> 39% of each run, Pallas kernels for 13% -> 14%
where the time goes in v3:
time: 738 us; the launch traced here: 731 us
  matrix products  207 us (28%)
  waiting for transfers between devices  144 us (20%)
  local copies, waits for them, and re-layouts  131 us (18%)
  Pallas kernels  99.4 us (13%)
  other arithmetic  74.4 us (10%)
  starting transfers between devices  68.4 us (9%)
    ppermute x80, waiting for transfers between devices, swap(): return lax.ppermute(value, AXES, [(d, d ^ bit) for d in range(self.count)])  144 us
    ppermute x80, starting transfers between devices, swap(): return lax.ppermute(value, AXES, [(d, d ^ bit) for d in range(self.count)])  68.4 us
    dot_general x13, matrix products, matmul_plain(): return jnp.dot(left, right, preferred_element_type=jnp.float32)  60.7 us
    dot_general x19, matrix products, matmul_right_t(): lax.dot_general(left, right, (((1,), (1,)), ((), ())), preferred_element_...  60.6 us
    pallas_call x2, Pallas kernels, attention_backward(): pl.pallas_call(partial(attend_backward, row_len, qb, kb, lanes, span), ou...  55.3 us
    dot_general x13, matrix products, matmul_left_t(): lax.dot_general(left, right, (((0,), (0,)), ((), ())), preferred_element_...  48 us
    pallas_call x2, Pallas kernels, attention_forward(): pl.pallas_call(partial(attend_forward, row_len, qb, kb, lanes, span), out...  44.1 us
    convert_element_type x24, other arithmetic, merge(): self.held = total.astype(self.wire) if self.order else total  31 us
  transfers between devices with their start and end apart: 80, of which 43 were waited for; matrix products, arithmetic and copies ran while one was open for 39% of the time, Pallas kernels for 14%

profile of v3, /device:TPU:0, one launch (start us, length us, event | category | flops | bytes accessed | tf_op | source)
XLA Modules:
  0.0 731.0 jit_solution(14474150528630126409)
XLA Ops:
  3.0 4.1 collective-permute-start.5
  17.2 3.8 collective-permute-done.6
  26.6 7.1 collective-permute-done.8
  39.5 8.6 %collective-permute-done.20 = bf16[1,1,1,1,1,32,4096]{6,5,4,3,2,1,0:T(8,128)(2,1)S(1)} collective-permute-done((bf16[1,1,1,1,1,32,4096]{6,5,4,3,2,1,0:T(8,128)(2,1)}, bf16[1,1,1,1,1,32,4096]{6,5,4,3,2,1,0:T(8,128)(2,1)S(1)}, u32[]{:S(2)}, u32[]{:S(2)}) %collective-permute-start.20) | collective-permute-done | bytes 262176 | tf_op jit(solution)/shard_map/ppermute | solution.py:296
  68.5 7.8 %collective-permute-done.25 = bf16[2,1,1,1,1,128,1024]{6,5,4,3,2,1,0:T(8,128)(2,1)S(1)} collective-permute-done((bf16[2,1,1,1,1,128,1024]{6,5,4,3,2,1,0:T(8,128)(2,1)S(1)}, bf16[2,1,1,1,1,128,1024]{6,5,4,3,2,1,0:T(8,128)(2,1)S(1)}, u32[]{:S(2)}, u32[]{:S(2)}) %collective-permute-start.25) | collective-permute-done | bytes 524320 | tf_op jit(solution)/shard_map/ppermute | solution.py:296
  102.4 6.9 collective-permute-done.26
  128.9 5.9 fusion.118.q_ref.k_ref.v_ref
  134.8 7.1 fusion.117.q_ref.k_ref.v_ref
  141.9 21.9 %shard_map.238 = (bf16[1056,512]{1,0:T(8,128)(2,1)S(1)}, f32[4,4,512]{2,1,0:T(4,128)S(1)}, f32[4,1,64]{2,1,0:T(1,128)S(1)}) custom-call(s32[2,4]{1,0:T(2,128)S(1)} %pad_add_fusion.bounds, s32[4,512]{1,0:T(4,128)S(1)} %constant_dynamic-update-slice_fusion.68.segrow, s32[1024,1]{1,0:T(8,128)S(1)} %copy.74.segcol, ...), custom_call_target="tpu_custom_call" | custom-call | tf_op jit(solution)/shard_map/pallas_call | solution.py:130
  163.8 22.3 %shard_map.237 = (bf16[1056,512]{1,0:T(8,128)(2,1)S(1)}, f32[4,4,512]{2,1,0:T(4,128)S(1)}, f32[4,1,64]{2,1,0:T(1,128)S(1)}) custom-call(s32[2,4]{1,0:T(2,128)S(1)} %pad_add_fusion.bounds, s32[4,512]{1,0:T(4,128)S(1)} %constant_dynamic-update-slice_fusion.68.segrow, s32[1024,1]{1,0:T(8,128)S(1)} %copy.74.segcol, ...), custom_call_target="tpu_custom_call" | custom-call | tf_op jit(solution)/shard_map/pallas_call | solution.py:130
  186.2 3.5 constant_dynamic-update-slice_fusion.22
  207.5 4.4 broadcast_in_dim.245
  211.9 4.7 constant_dynamic-update-slice_fusion.13
  225.3 5.5 constant_dynamic-update-slice_fusion.12
  230.8 21.1 %fusion.115 = (bf16[1056,4096]{1,0:T(8,128)(2,1)}, bf16[1056,4096]{1,0:T(8,128)(2,1)}) fusion(f32[4096]{0:T(1024)S(1)} %fusion.167, bf16[1024,4096]{1,0:T(8,128)(2,1)} %bitcast.331, f32[1056,1024]{1,0:T(8,128)S(1)} %get-tuple-element.542, f32[1024]{0:T(1024)S(1)} %add.368, f32[1024]{0:T(1024)S(1)} %mul.575, f32[1056]{0:T(1024)S(1)} %add_rsqrt_fusion.7, ...), kind=kOutput, calls=%fused_computation.141 | convolution fusion | flops 8915681280 | bytes 30048512 | tf_op jit(solution)/shard_map/dot_general | solution.py:27
  252.7 16.3 %fusion.187 = (f32[1056]{0:T(1024)S(1)}, f32[1056,1024]{1,0:T(8,128)S(1)}) fusion(f32[1024]{0:T(1024)S(1)} %add.376, bf16[1056,4096]{1,0:T(8,128)(2,1)} %get-tuple-element.299, bf16[4096,1024]{1,0:T(8,128)(2,1)S(1)} %bitcast.329, f32[1024]{0:T(1024)S(1)} %add.368, f32[1024]{0:T(1024)S(1)} %mul.575, f32[1056]{0:T(1024)S(1)} %add_rsqrt_fusion.7, ...), kind=kOutput, calls=%fused_computation.476 | convolution fusion | flops 8865938432 | bytes 25715072 | tf_op jit(solution)/shard_map/dot_general | solution.py:27
  274.4 3.8 collective-permute-done.30
  278.3 3.7 collective-permute-done.31
  286.0 4.2 collective-permute-done.33
  291.7 18.9 %while.32 = (s32[]{:T(128)}, f32[2,16,3,8]{1,3,2,0:T(8,128)S(1)}, bf16[2,16,32,128]{3,2,1,0:T(8,128)(2,1)S(1)}, bf16[1024,128]{1,0:T(8,128)(2,1)S(1)}, bf16[1024...) while((s32[]{:T(128)}, f32[2,16,3,8]{1,3,2,0:T(8,128)S(1)}, ...), condition=%wide.region_18.19_spmd.clone, body=%wide.region_11.18_spmd.clone.sunk | while | flops 455516928 | bytes 14488185 | solution.py:520
  310.8 4.5 collective-permute-done.35
  315.4 3.6 collective-permute-done.36
  322.6 3.6 collective-permute-done.38
  328.1 49.8 %while.33 = (s32[]{:T(128)}, f32[1024,128]{1,0:T(8,128)S(1)}, f32[1024,96]{0,1:T(8,128)S(1)}, f32[1024,64]{0,1:T(8,128)S(1)}, f32[2,16,32,128]{3,2,1,0:T(8,128)}...) while((s32[]{:T(128)}, f32[1024,128]{1,0:T(8,128)S(1)}, ...), condition=%wide.region_29.30_spmd.clone.clone.clone, body=%wide.region_22.29_spmd.clone.clone.clone.sunk | while | flops 1217213056 | bytes 37461660 | solution.py:564
  382.3 5.4 collective-permute-done.41
  397.1 3.6 collective-permute-done.44
  400.8 4.2 multiply_reduce_fusion.1
  407.9 12.0 %convolution_convert_fusion = bf16[4096,1024]{1,0:T(8,128)(2,1)S(1)} fusion(bf16[1056,4096]{1,0:T(8,128)(2,1)S(1)} %bitcast.373, bf16[1056,1024]{1,0:T(8,128)(2,1)S(1)} %get-tuple-element.305), kind=kOutput, calls=%fused_computation.150 | convolution fusion | flops 8862564352 | bytes 19202048 | tf_op jit(solution)/shard_map/dot_general | solution.py:37
  424.8 15.6 %convert_reduce_fusion = (f32[4096]{0:T(1024)S(1)}, bf16[1056,4096]{1,0:T(8,128)(2,1)}) fusion(bf16[1056,4096]{1,0:T(8,128)(2,1)} %get-tuple-element.306, bf16[1056,1024]{1,0:T(8,128)(2,1)S(1)} %get-tuple-element.305, bf16[4096,1024]{1,0:T(8,128)(2,1)} %bitcast.330), kind=kOutput, calls=%fused_computation.142 | convolution fusion | flops 8879992832 | bytes 27869184 | tf_op jit(solution)/shard_map/dot_general | solution.py:31
  440.4 15.0 %convolution_convert_fusion.1 = bf16[1024,4096]{1,0:T(8,128)(2,1)S(1)} fusion(bf16[1056,4096]{1,0:T(8,128)(2,1)} %get-tuple-element.308, f32[1056,1024]{1,0:T(8,128)S(1)} %bitcast.311, f32[1024]{0:T(1024)S(1)} %copy-done.76, f32[1024]{0:T(1024)S(1)} %copy-done.74, f32[1056]{0:T(1024)S(1)} %copy-done.72, f32[1056]{0:T(1024)S(1)} %copy-done.62), kind=kOutput, calls=%fused_computation.153 | convolution fusion | flops 8867971072 | bytes 21381376 | tf_op jit(solution)/shard_map/dot_general | solution.py:37
  461.7 6.0 add_convert_fusion.1
  472.3 17.1 %multiply_reduce_fusion.2 = (f32[1024]{0:T(1024)S(1)}, f32[1056]{0:T(1024)S(1)}, f32[1056]{0:T(1024)S(1)}, f32[1024]{0:T(1024)S(1)}, f32[1056,1024]{1,0:T(8,128)}) fusion(f32[1056,1024]{1,0:T(8,128)S(1)} %bitcast.311, f32[1056]{0:T(1024)S(1)} %copy-done.72, f32[1056]{0:T(1024)S(1)} %copy-done.62, f32[1024]{0:T(1024)S(1)} %copy-done.74, ...), kind=kOutput, calls=%fused_computation.163 | convolution fusion | flops 8869179392 | bytes 30044672 | tf_op jit(solution)/shard_map/dot_general | solution.py:31
  489.6 5.7 fusion.178
  495.3 5.8 add_convert_fusion
  509.6 3.5 convolution_convert_fusion.4.g_ref
  513.1 3.7 convolution_convert_fusion.5.g_ref
  524.3 27.4 %shard_map.239 = bf16[1056,1536]{1,0:T(8,128)(2,1)} custom-call(s32[2,4]{1,0:T(2,128)} %copy-done.10, s32[4,512]{1,0:T(4,128)} %copy-done.7, s32[1024,1]{1,0:T(8,128)} %copy-done.2, bf16[1056,1536]{1,0:T(8,128)(2,1)} %copy-done.1, bf16[1056,1536]{1,0:T(8,128)(2,1)} %copy-done.1, bf16[1056,1536]{1,0:T(8,128)(2,1)} %copy-done.1, ...), custom_call_target="tpu_custom_call" | custom-call | tf_op jit(solution)/shard_map/pallas_call | solution.py:207
  551.8 6.7 convolution_convert_fusion.3
  561.9 27.9 %shard_map.240 = bf16[1056,1536]{1,0:T(8,128)(2,1)} custom-call(s32[2,4]{1,0:T(2,128)} %copy-done.10, s32[4,512]{1,0:T(4,128)} %copy-done.7, s32[1024,1]{1,0:T(8,128)} %copy-done.2, bf16[1056,1536]{1,0:T(8,128)(2,1)} %copy-done, bf16[1056,1536]{1,0:T(8,128)(2,1)} %copy-done, bf16[1056,1536]{1,0:T(8,128)(2,1)} %copy-done, ...), custom_call_target="tpu_custom_call" | custom-call | tf_op jit(solution)/shard_map/pallas_call | solution.py:207
  603.7 5.9 convolution_convert_fusion.2
  615.1 4.0 collective-permute-done.70
  622.4 5.7 fusion.195
  628.1 5.5 fusion.121
  651.3 7.8 %collective-permute-done.79 = f32[1,1,1,1,1,1,384]{6,5,4,3,2,1,0:T(1,128)S(1)} collective-permute-done((f32[1,1,1,1,1,1,384]{6,5,4,3,2,1,0:T(1,128)S(1)}, f32[1,1,1,1,1,1,384]{6,5,4,3,2,1,0:T(1,128)S(1)}, u32[]{:S(2)}, u32[]{:S(2)}) %collective-permute-start.79) | collective-permute-done | bytes 1568 | tf_op jit(solution)/shard_map/ppermute | solution.py:296
  661.8 5.3 collective-permute-done.67
  669.7 3.8 collective-permute-done.68
  679.7 5.7 collective-permute-done.69
  707.8 3.9 collective-permute-start.63
  (753 shorter events, 342.9 us)
Async XLA Ops:
  3.0 20.1 %collective-permute-start.5 = (bf16[1,1,1,1,1,1,384]{6,4,3,2,1,0,5:T(2,128)(2,1)S(1)}, bf16[1,1,1,1,1,1,384]{6,4,3,2,1,0,5:T(2,128)(2,1)S(1)}, u32[]{:S(2)}, u32[]{:S(2)}) collective-permute-start(bf16[1,1,1,1,1,1,384]{6,4,3,2,1,0,5:T(2,128)(2,1)S(1)} %reshape_broadcast_in_dim.4), channel_id=1, source_target_pairs={{0,16},{1,17},{2,18},{3,19},{4,20},{5,21},{6,22},{7,23},{8,24},{9,... | collective-permute-start | bytes 2312 | tf_op jit(solution)/shard_map/ppermute | solution.py:296
  9.4 11.6 %collective-permute-start = (bf16[1,1,1,1,1,32,1536]{6,5,4,3,2,1,0:T(8,128)(2,1)S(1)}, bf16[1,1,1,1,1,32,1536]{6,5,4,3,2,1,0:T(8,128)(2,1)S(1)}, u32[]{:S(2)}, u32[]{:S(2)}) collective-permute-start(bf16[1,1,1,1,1,32,1536]{6,5,4,3,2,1,0:T(8,128)(2,1)S(1)} %maximum_bitcast_fusion.1), channel_id=1, source_target_pairs={{0,16},{1,17},{2,18},{3,19},{4,20},{5,21},{6,22},{7,23},{8,24},{9,... | collective-permute-start | bytes 294920 | tf_op jit(solution)/shard_map/ppermute | solution.py:296
  20.9 12.7 %collective-permute-start.8 = (bf16[2,1,1,1,1,32,1536]{6,5,4,3,2,1,0:T(8,128)(2,1)S(1)}, bf16[2,1,1,1,1,32,1536]{6,5,4,3,2,1,0:T(8,128)(2,1)S(1)}, u32[]{:S(2)}, u32[]{:S(2)}) collective-permute-start(bf16[2,1,1,1,1,32,1536]{6,5,4,3,2,1,0:T(8,128)(2,1)S(1)} %constant_dynamic-update-slice_fusion.55), channel_id=1, source_target_pairs={{0,8},{1,9},{2,10},{3,11},{4,12},{5,13},{6,14},{7,15},{8,0},{9,1},... | collective-permute-start | bytes 589832 | tf_op jit(solution)/shard_map/ppermute | solution.py:296
  21.0 14.9 %collective-permute-start.1 = (bf16[2,1,1,1,1,32,1536]{6,5,4,3,2,1,0:T(8,128)(2,1)S(1)}, bf16[2,1,1,1,1,32,1536]{6,5,4,3,2,1,0:T(8,128)(2,1)S(1)}, u32[]{:S(2)}, u32[]{:S(2)}) collective-permute-start(bf16[2,1,1,1,1,32,1536]{6,5,4,3,2,1,0:T(8,128)(2,1)S(1)} %constant_dynamic-update-slice_fusion.66), channel_id=1, source_target_pairs={{0,8},{1,9},{2,10},{3,11},{4,12},{5,13},{6,14},{7,15},{8,0},{9,1},... | collective-permute-start | bytes 589832 | tf_op jit(solution)/shard_map/ppermute | solution.py:296
  23.1 14.5 %collective-permute-start.7 = (bf16[2,1,1,1,1,1,384]{6,4,3,2,1,0,5:T(2,128)(2,1)S(1)}, bf16[2,1,1,1,1,1,384]{6,4,3,2,1,0,5:T(2,128)(2,1)S(1)}, u32[]{:S(2)}, u32[]{:S(2)}) collective-permute-start(bf16[2,1,1,1,1,1,384]{6,4,3,2,1,0,5:T(2,128)(2,1)S(1)} %constant_dynamic-update-slice_fusion.54), channel_id=1, source_target_pairs={{0,8},{1,9},{2,10},{3,11},{4,12},{5,13},{6,14},{7,15},{8,0},{9,1},... | collective-permute-start | bytes 4616 | tf_op jit(solution)/shard_map/ppermute | solution.py:296
  23.2 14.2 %collective-permute-start.15 = (bf16[1,1,1,1,1,32,1152]{6,5,4,3,2,1,0:T(8,128)(2,1)S(1)}, bf16[1,1,1,1,1,32,1152]{6,5,4,3,2,1,0:T(8,128)(2,1)S(1)}, u32[]{:S(2)}, u32[]{:S(2)}) collective-permute-start(bf16[1,1,1,1,1,32,1152]{6,5,4,3,2,1,0:T(8,128)(2,1)S(1)} %maximum_bitcast_fusion.3), channel_id=1, source_target_pairs={{0,16},{1,17},{2,18},{3,19},{4,20},{5,21},{6,22},{7,23},{8,24},{9,... | collective-permute-start | bytes 221192 | tf_op jit(solution)/shard_map/ppermute | solution.py:296
  24.9 23.1 %collective-permute-start.20 = (bf16[1,1,1,1,1,32,4096]{6,5,4,3,2,1,0:T(8,128)(2,1)}, bf16[1,1,1,1,1,32,4096]{6,5,4,3,2,1,0:T(8,128)(2,1)S(1)}, u32[]{:S(2)}, u32[]{:S(2)}) collective-permute-start(bf16[1,1,1,1,1,32,4096]{6,5,4,3,2,1,0:T(8,128)(2,1)} %bitcast.353), channel_id=1, source_target_pairs={{0,16},{1,17},{2,18},{3,19},{4,20},{5,21},{6,22},{7,23},{8,24},{9,... | collective-permute-start | bytes 786440 | tf_op jit(solution)/shard_map/ppermute | solution.py:296
  33.6 18.8 %collective-permute-start.24 = (bf16[1,1,1,1,1,128,1024]{6,5,4,3,2,1,0:T(8,128)(2,1)S(1)}, bf16[1,1,1,1,1,128,1024]{6,5,4,3,2,1,0:T(8,128)(2,1)S(1)}, u32[]{:S(2)}, u32[]{:S(2)}) collective-permute-start(bf16[1,1,1,1,1,128,1024]{6,5,4,3,2,1,0:T(8,128)(2,1)S(1)} %bitcast.356), channel_id=1, source_target_pairs={{0,16},{1,17},{2,18},{3,19},{4,20},{5,21},{6,22},{7,23},{8,24},{9,... | collective-permute-start | bytes 786440 | tf_op jit(solution)/shard_map/ppermute | solution.py:296
  35.9 20.8 %collective-permute-start.10 = (bf16[2,2,1,1,1,32,1536]{6,5,4,3,2,1,0:T(8,128)(2,1)S(1)}, bf16[2,2,1,1,1,32,1536]{6,5,4,3,2,1,0:T(8,128)(2,1)S(1)}, u32[]{:S(2)}, u32[]{:S(2)}) collective-permute-start(bf16[2,2,1,1,1,32,1536]{6,5,4,3,2,1,0:T(8,128)(2,1)S(1)} %constant_dynamic-update-slice_fusion.51), channel_id=1, source_target_pairs={{0,4},{1,5},{2,6},{3,7},{4,0},{5,1},{6,2},{7,3},{8,12},{9,13},{10,... | collective-permute-start | bytes 1179656 | tf_op jit(solution)/shard_map/ppermute | solution.py:296
  37.5 20.4 %collective-permute-start.16 = (bf16[2,1,1,1,1,32,1152]{6,5,4,3,2,1,0:T(8,128)(2,1)S(1)}, bf16[2,1,1,1,1,32,1152]{6,5,4,3,2,1,0:T(8,128)(2,1)S(1)}, u32[]{:S(2)}, u32[]{:S(2)}) collective-permute-start(bf16[2,1,1,1,1,32,1152]{6,5,4,3,2,1,0:T(8,128)(2,1)S(1)} %constant_dynamic-update-slice_fusion.38), channel_id=1, source_target_pairs={{0,8},{1,9},{2,10},{3,11},{4,12},{5,13},{6,14},{7,15},{8,0},{9,1},... | collective-permute-start | bytes 442376 | tf_op jit(solution)/shard_map/ppermute | solution.py:296
  37.7 20.2 %collective-permute-start.9 = (bf16[2,2,1,1,1,1,384]{6,4,3,2,1,0,5:T(2,128)(2,1)S(1)}, bf16[2,2,1,1,1,1,384]{6,4,3,2,1,0,5:T(2,128)(2,1)S(1)}, u32[]{:S(2)}, u32[]{:S(2)}) collective-permute-start(bf16[2,2,1,1,1,1,384]{6,4,3,2,1,0,5:T(2,128)(2,1)S(1)} %constant_dynamic-update-slice_fusion.50), channel_id=1, source_target_pairs={{0,2},{1,3},{2,0},{3,1},{4,6},{5,7},{6,4},{7,5},{8,10},{9,11},{10,... | collective-permute-start | bytes 9224 | tf_op jit(solution)/shard_map/ppermute | solution.py:296
  52.4 14.8 %collective-permute-start.21 = (bf16[2,1,1,1,1,32,4096]{6,5,4,3,2,1,0:T(8,128)(2,1)S(1)}, bf16[2,1,1,1,1,32,4096]{6,5,4,3,2,1,0:T(8,128)(2,1)S(1)}, u32[]{:S(2)}, u32[]{:S(2)}) collective-permute-start(bf16[2,1,1,1,1,32,4096]{6,5,4,3,2,1,0:T(8,128)(2,1)S(1)} %constant_dynamic-update-slice_fusion.28), channel_id=1, source_target_pairs={{0,8},{1,9},{2,10},{3,11},{4,12},{5,13},{6,14},{7,15},{8,0},{9,1},... | collective-permute-start | bytes 1572872 | tf_op jit(solution)/shard_map/ppermute | solution.py:296
  56.7 19.7 %collective-permute-start.25 = (bf16[2,1,1,1,1,128,1024]{6,5,4,3,2,1,0:T(8,128)(2,1)S(1)}, bf16[2,1,1,1,1,128,1024]{6,5,4,3,2,1,0:T(8,128)(2,1)S(1)}, u32[]{:S(2)}, u32[]{:S(2)}) collective-permute-start(bf16[2,1,1,1,1,128,1024]{6,5,4,3,2,1,0:T(8,128)(2,1)S(1)} %constant_dynamic-update-slice_fusion.20), channel_id=1, source_target_pairs={{0,8},{1,9},{2,10},{3,11},{4,12},{5,13},{6,14},{7,15},{8,0},{9,1},... | collective-permute-start | bytes 1572872 | tf_op jit(solution)/shard_map/ppermute | solution.py:296
  56.7 32.9 %collective-permute-start.3 = (bf16[2,2,1,2,1,32,1536]{6,5,4,3,2,1,0:T(8,128)(2,1)S(1)}, bf16[2,2,1,2,1,32,1536]{6,5,4,3,2,1,0:T(8,128)(2,1)S(1)}, u32[]{:S(2)}, u32[]{:S(2)}) collective-permute-start(bf16[2,2,1,2,1,32,1536]{6,5,4,3,2,1,0:T(8,128)(2,1)S(1)} %constant_dynamic-update-slice_fusion.62), channel_id=1, source_target_pairs={{0,4},{1,5},{2,6},{3,7},{4,0},{5,1},{6,2},{7,3},{8,12},{9,13},{10,... | collective-permute-start | bytes 2359304 | tf_op jit(solution)/shard_map/ppermute | solution.py:296
  57.9 33.1 %collective-permute-start.11 = (bf16[2,2,1,2,1,1,384]{6,4,3,2,1,0,5:T(2,128)(2,1)S(1)}, bf16[2,2,1,2,1,1,384]{6,4,3,2,1,0,5:T(2,128)(2,1)S(1)}, u32[]{:S(2)}, u32[]{:S(2)}) collective-permute-start(bf16[2,2,1,2,1,1,384]{6,4,3,2,1,0,5:T(2,128)(2,1)S(1)} %constant_dynamic-update-slice_fusion.46), channel_id=1, source_target_pairs={{0,4},{1,5},{2,6},{3,7},{4,0},{5,1},{6,2},{7,3},{8,12},{9,13},{10,... | collective-permute-start | bytes 18440 | tf_op jit(solution)/shard_map/ppermute | solution.py:296
  59.0 30.7 %collective-permute-start.17 = (bf16[2,2,1,1,1,32,1152]{6,5,4,3,2,1,0:T(8,128)(2,1)S(1)}, bf16[2,2,1,1,1,32,1152]{6,5,4,3,2,1,0:T(8,128)(2,1)S(1)}, u32[]{:S(2)}, u32[]{:S(2)}) collective-permute-start(bf16[2,2,1,1,1,32,1152]{6,5,4,3,2,1,0:T(8,128)(2,1)S(1)} %constant_dynamic-update-slice_fusion.36), channel_id=1, source_target_pairs={{0,2},{1,3},{2,0},{3,1},{4,6},{5,7},{6,4},{7,5},{8,10},{9,11},{10,... | collective-permute-start | bytes 884744 | tf_op jit(solution)/shard_map/ppermute | solution.py:296
  67.2 20.2 %collective-permute-start.12 = (bf16[2,2,2,1,1,32,1536]{6,5,4,3,2,1,0:T(8,128)(2,1)S(1)}, bf16[2,2,2,1,1,32,1536]{6,5,4,3,2,1,0:T(8,128)(2,1)S(1)}, u32[]{:S(2)}, u32[]{:S(2)}) collective-permute-start(bf16[2,2,2,1,1,32,1536]{6,5,4,3,2,1,0:T(8,128)(2,1)S(1)} %constant_dynamic-update-slice_fusion.47), channel_id=1, source_target_pairs={{0,2},{1,3},{2,0},{3,1},{4,6},{5,7},{6,4},{7,5},{8,10},{9,11},{10,... | collective-permute-start | bytes 2359304 | tf_op jit(solution)/shard_map/ppermute | solution.py:296
  77.2 34.4 %collective-permute-start.22 = (bf16[2,2,1,1,1,32,4096]{6,5,4,3,2,1,0:T(8,128)(2,1)S(1)}, bf16[2,2,1,1,1,32,4096]{6,5,4,3,2,1,0:T(8,128)(2,1)}, u32[]{:S(2)}, u32[]{:S(2)}) collective-permute-start(bf16[2,2,1,1,1,32,4096]{6,5,4,3,2,1,0:T(8,128)(2,1)S(1)} %constant_dynamic-update-slice_fusion.26), channel_id=1, source_target_pairs={{0,2},{1,3},{2,0},{3,1},{4,6},{5,7},{6,4},{7,5},{8,10},{9,11},{10,... | collective-permute-start | bytes 3145736 | tf_op jit(solution)/shard_map/ppermute | solution.py:296
  87.4 21.9 %collective-permute-start.26 = (bf16[2,2,1,1,1,128,1024]{6,5,4,3,2,1,0:T(8,128)(2,1)}, bf16[2,2,1,1,1,128,1024]{6,5,4,3,2,1,0:T(8,128)(2,1)}, u32[]{:S(2)}, u32[]{:S(2)}) collective-permute-start(bf16[2,2,1,1,1,128,1024]{6,5,4,3,2,1,0:T(8,128)(2,1)} %constant_dynamic-update-slice_fusion.18), channel_id=1, source_target_pairs={{0,4},{1,5},{2,6},{3,7},{4,0},{5,1},{6,2},{7,3},{8,12},{9,13},{10,... | collective-permute-start | bytes 3145736 | tf_op jit(solution)/shard_map/ppermute | solution.py:296
  89.6 35.9 %collective-permute-start.14 = (bf16[2,2,2,2,1,32,1536]{6,5,4,3,2,1,0:T(8,128)(2,1)}, bf16[2,2,2,2,1,32,1536]{6,5,4,3,2,1,0:T(8,128)(2,1)}, u32[]{:S(2)}, u32[]{:S(2)}) collective-permute-start(bf16[2,2,2,2,1,32,1536]{6,5,4,3,2,1,0:T(8,128)(2,1)} %constant_dynamic-update-slice_fusion.43), channel_id=1, source_target_pairs={{0,1},{1,0},{2,3},{3,2},{4,5},{5,4},{6,7},{7,6},{8,9},{9,8},{10,11... | collective-permute-start | bytes 4718600 | tf_op jit(solution)/shard_map/ppermute | solution.py:296
  89.7 32.1 %collective-permute-start.4 = (bf16[2,2,2,2,1,32,1536]{6,5,4,3,2,1,0:T(8,128)(2,1)S(1)}, bf16[2,2,2,2,1,32,1536]{6,5,4,3,2,1,0:T(8,128)(2,1)}, u32[]{:S(2)}, u32[]{:S(2)}) collective-permute-start(bf16[2,2,2,2,1,32,1536]{6,5,4,3,2,1,0:T(8,128)(2,1)S(1)} %constant_dynamic-update-slice_fusion.60), channel_id=1, source_target_pairs={{0,1},{1,0},{2,3},{3,2},{4,5},{5,4},{6,7},{7,6},{8,9},{9,8},{10,11... | collective-permute-start | bytes 4718600 | tf_op jit(solution)/shard_map/ppermute | solution.py:296
  91.0 37.2 %collective-permute-start.13 = (bf16[2,2,2,2,1,1,384]{6,4,3,2,1,0,5:T(2,128)(2,1)S(1)}, bf16[2,2,2,2,1,1,384]{6,4,3,2,1,0,5:T(2,128)(2,1)S(1)}, u32[]{:S(2)}, u32[]{:S(2)}) collective-permute-start(bf16[2,2,2,2,1,1,384]{6,4,3,2,1,0,5:T(2,128)(2,1)S(1)} %constant_dynamic-update-slice_fusion.42), channel_id=1, source_target_pairs={{0,1},{1,0},{2,3},{3,2},{4,5},{5,4},{6,7},{7,6},{8,9},{9,8},{10,11... | collective-permute-start | bytes 36872 | tf_op jit(solution)/shard_map/ppermute | solution.py:296
  109.3 85.0 %collective-permute-start.18 = (bf16[2,2,1,2,1,32,1152]{6,5,4,3,2,1,0:T(8,128)(2,1)}, bf16[2,2,1,2,1,32,1152]{6,5,4,3,2,1,0:T(8,128)(2,1)}, u32[]{:S(2)}, u32[]{:S(2)}) collective-permute-start(bf16[2,2,1,2,1,32,1152]{6,5,4,3,2,1,0:T(8,128)(2,1)} %constant_dynamic-update-slice_fusion.34), channel_id=1, source_target_pairs={{0,4},{1,5},{2,6},{3,7},{4,0},{5,1},{6,2},{7,3},{8,12},{9,13},{10,... | collective-permute-start | bytes 1769480 | tf_op jit(solution)/shard_map/ppermute | solution.py:296
  116.2 70.0 %collective-permute-start.23 = (bf16[2,2,1,2,1,32,4096]{6,5,4,3,2,1,0:T(8,128)(2,1)}, bf16[2,2,1,2,1,32,4096]{6,5,4,3,2,1,0:T(8,128)(2,1)}, u32[]{:S(2)}, u32[]{:S(2)}) collective-permute-start(bf16[2,2,1,2,1,32,4096]{6,5,4,3,2,1,0:T(8,128)(2,1)} %constant_dynamic-update-slice_fusion.24), channel_id=1, source_target_pairs={{0,4},{1,5},{2,6},{3,7},{4,0},{5,1},{6,2},{7,3},{8,12},{9,13},{10,... | collective-permute-start | bytes 6291464 | tf_op jit(solution)/shard_map/ppermute | solution.py:296
  121.8 79.8 %collective-permute-start.27 = (bf16[2,2,2,1,1,128,1024]{6,5,4,3,2,1,0:T(8,128)(2,1)}, bf16[2,2,2,1,1,128,1024]{6,5,4,3,2,1,0:T(8,128)(2,1)}, u32[]{:S(2)}, u32[]{:S(2)}) collective-permute-start(bf16[2,2,2,1,1,128,1024]{6,5,4,3,2,1,0:T(8,128)(2,1)} %constant_dynamic-update-slice_fusion.16), channel_id=1, source_target_pairs={{0,2},{1,3},{2,0},{3,1},{4,6},{5,7},{6,4},{7,5},{8,10},{9,11},{10,... | collective-permute-start | bytes 6291464 | tf_op jit(solution)/shard_map/ppermute | solution.py:296
  189.7 35.6 %collective-permute-start.28 = (bf16[2,2,2,2,1,32,4096]{6,5,4,3,2,1,0:T(8,128)(2,1)}, bf16[2,2,2,2,1,32,4096]{6,5,4,3,2,1,0:T(8,128)(2,1)}, u32[]{:S(2)}, u32[]{:S(2)}) collective-permute-start(bf16[2,2,2,2,1,32,4096]{6,5,4,3,2,1,0:T(8,128)(2,1)} %constant_dynamic-update-slice_fusion.22), channel_id=1, source_target_pairs={{0,1},{1,0},{2,3},{3,2},{4,5},{5,4},{6,7},{7,6},{8,9},{9,8},{10,11... | collective-permute-start | bytes 12582920 | tf_op jit(solution)/shard_map/ppermute | solution.py:296
  196.2 20.4 %collective-permute-start.19 = (bf16[2,2,2,2,1,32,1152]{6,5,4,3,2,1,0:T(8,128)(2,1)}, bf16[2,2,2,2,1,32,1152]{6,5,4,3,2,1,0:T(8,128)(2,1)}, u32[]{:S(2)}, u32[]{:S(2)}) collective-permute-start(bf16[2,2,2,2,1,32,1152]{6,5,4,3,2,1,0:T(8,128)(2,1)} %constant_dynamic-update-slice_fusion.32), channel_id=1, source_target_pairs={{0,1},{1,0},{2,3},{3,2},{4,5},{5,4},{6,7},{7,6},{8,9},{9,8},{10,11... | collective-permute-start | bytes 3538952 | tf_op jit(solution)/shard_map/ppermute | solution.py:296
  204.7 47.2 %collective-permute-start.29 = (bf16[2,2,2,2,1,128,1024]{6,5,4,3,2,1,0:T(8,128)(2,1)}, bf16[2,2,2,2,1,128,1024]{6,5,4,3,2,1,0:T(8,128)(2,1)S(1)}, u32[]{:S(2)}, u32[]{:S(2)}) collective-permute-start(bf16[2,2,2,2,1,128,1024]{6,5,4,3,2,1,0:T(8,128)(2,1)} %constant_dynamic-update-slice_fusion.14), channel_id=1, source_target_pairs={{0,1},{1,0},{2,3},{3,2},{4,5},{5,4},{6,7},{7,6},{8,9},{9,8},{10,11... | collective-permute-start | bytes 12582920 | tf_op jit(solution)/shard_map/ppermute | solution.py:296
  424.5 37.2 %collective-permute-start.45 = (bf16[2,2,2,2,1,128,1024]{6,5,4,3,2,1,0:T(8,128)(2,1)}, bf16[2,2,2,2,1,128,1024]{6,5,4,3,2,1,0:T(8,128)(2,1)}, u32[]{:S(2)}, u32[]{:S(2)}) collective-permute-start(bf16[2,2,2,2,1,128,1024]{6,5,4,3,2,1,0:T(8,128)(2,1)} %constant_dynamic-slice_fusion.41), channel_id=1, source_target_pairs={{0,1},{1,0},{2,3},{3,2},{4,5},{5,4},{6,7},{7,6},{8,9},{9,8},{10,11... | collective-permute-start | bytes 12582920 | tf_op jit(solution)/shard_map/ppermute | solution.py:296
  460.3 35.1 %collective-permute-start.46 = (bf16[2,2,2,2,1,32,4096]{6,5,4,3,2,1,0:T(8,128)(2,1)}, bf16[2,2,2,2,1,32,4096]{6,5,4,3,2,1,0:T(8,128)(2,1)}, u32[]{:S(2)}, u32[]{:S(2)}) collective-permute-start(bf16[2,2,2,2,1,32,4096]{6,5,4,3,2,1,0:T(8,128)(2,1)} %constant_dynamic-slice_fusion.40), channel_id=1, source_target_pairs={{0,1},{1,0},{2,3},{3,2},{4,5},{5,4},{6,7},{7,6},{8,9},{9,8},{10,11... | collective-permute-start | bytes 12582920 | tf_op jit(solution)/shard_map/ppermute | solution.py:296
  471.2 47.9 %collective-permute-start.47 = (bf16[2,2,2,1,1,128,1024]{6,5,4,3,2,1,0:T(8,128)(2,1)}, bf16[2,2,2,1,1,128,1024]{6,5,4,3,2,1,0:T(8,128)(2,1)}, u32[]{:S(2)}, u32[]{:S(2)}) collective-permute-start(bf16[2,2,2,1,1,128,1024]{6,5,4,3,2,1,0:T(8,128)(2,1)} %constant_dynamic-slice_fusion.39), channel_id=1, source_target_pairs={{0,2},{1,3},{2,0},{3,1},{4,6},{5,7},{6,4},{7,5},{8,10},{9,11},{10,... | collective-permute-start | bytes 6291464 | tf_op jit(solution)/shard_map/ppermute | solution.py:296
  502.6 87.2 %collective-permute-start.49 = (bf16[2,2,1,2,1,32,4096]{6,5,4,3,2,1,0:T(8,128)(2,1)}, bf16[2,2,1,2,1,32,4096]{6,5,4,3,2,1,0:T(8,128)(2,1)}, u32[]{:S(2)}, u32[]{:S(2)}) collective-permute-start(bf16[2,2,1,2,1,32,4096]{6,5,4,3,2,1,0:T(8,128)(2,1)} %constant_dynamic-slice_fusion.38), channel_id=1, source_target_pairs={{0,4},{1,5},{2,6},{3,7},{4,0},{5,1},{6,2},{7,3},{8,12},{9,13},{10,... | collective-permute-start | bytes 6291464 | tf_op jit(solution)/shard_map/ppermute | solution.py:296
  509.5 50.4 %collective-permute-start.48 = (bf16[2,2,2,2,1,32,1152]{6,5,4,3,2,1,0:T(8,128)(2,1)S(1)}, bf16[2,2,2,2,1,32,1152]{6,5,4,3,2,1,0:T(8,128)(2,1)S(1)}, u32[]{:S(2)}, u32[]{:S(2)}) collective-permute-start(bf16[2,2,2,2,1,32,1152]{6,5,4,3,2,1,0:T(8,128)(2,1)S(1)} %constant_dynamic-slice_fusion.37), channel_id=1, source_target_pairs={{0,1},{1,0},{2,3},{3,2},{4,5},{5,4},{6,7},{7,6},{8,9},{9,8},{10,11... | collective-permute-start | bytes 3538952 | tf_op jit(solution)/shard_map/ppermute | solution.py:296
  524.1 71.0 %collective-permute-start.50 = (bf16[2,2,1,1,1,128,1024]{6,5,4,3,2,1,0:T(8,128)(2,1)}, bf16[2,2,1,1,1,128,1024]{6,5,4,3,2,1,0:T(8,128)(2,1)}, u32[]{:S(2)}, u32[]{:S(2)}) collective-permute-start(bf16[2,2,1,1,1,128,1024]{6,5,4,3,2,1,0:T(8,128)(2,1)} %constant_dynamic-slice_fusion.36), channel_id=1, source_target_pairs={{0,4},{1,5},{2,6},{3,7},{4,0},{5,1},{6,2},{7,3},{8,12},{9,13},{10,... | collective-permute-start | bytes 3145736 | tf_op jit(solution)/shard_map/ppermute | solution.py:296
  561.6 59.2 %collective-permute-start.66 = (bf16[2,2,1,2,1,32,1152]{6,5,4,3,2,1,0:T(8,128)(2,1)}, bf16[2,2,1,2,1,32,1152]{6,5,4,3,2,1,0:T(8,128)(2,1)}, u32[]{:S(2)}, u32[]{:S(2)}) collective-permute-start(bf16[2,2,1,2,1,32,1152]{6,5,4,3,2,1,0:T(8,128)(2,1)} %constant_dynamic-slice_fusion.34), channel_id=1, source_target_pairs={{0,4},{1,5},{2,6},{3,7},{4,0},{5,1},{6,2},{7,3},{8,12},{9,13},{10,... | collective-permute-start | bytes 1769480 | tf_op jit(solution)/shard_map/ppermute | solution.py:296
  561.6 36.2 %collective-permute-start.51 = (bf16[2,2,2,2,1,32,1536]{6,5,4,3,2,1,0:T(8,128)(2,1)}, bf16[2,2,2,2,1,32,1536]{6,5,4,3,2,1,0:T(8,128)(2,1)}, u32[]{:S(2)}, u32[]{:S(2)}) collective-permute-start(bf16[2,2,2,2,1,32,1536]{6,5,4,3,2,1,0:T(8,128)(2,1)} %constant_dynamic-slice_fusion.35), channel_id=1, source_target_pairs={{0,1},{1,0},{2,3},{3,2},{4,5},{5,4},{6,7},{7,6},{8,9},{9,8},{10,11... | collective-permute-start | bytes 4718600 | tf_op jit(solution)/shard_map/ppermute | solution.py:296
  593.5 25.6 %collective-permute-start.70 = (bf16[2,2,1,1,1,32,4096]{6,5,4,3,2,1,0:T(8,128)(2,1)}, bf16[2,2,1,1,1,32,4096]{6,5,4,3,2,1,0:T(8,128)(2,1)}, u32[]{:S(2)}, u32[]{:S(2)}) collective-permute-start(bf16[2,2,1,1,1,32,4096]{6,5,4,3,2,1,0:T(8,128)(2,1)} %constant_dynamic-slice_fusion.33), channel_id=1, source_target_pairs={{0,2},{1,3},{2,0},{3,1},{4,6},{5,7},{6,4},{7,5},{8,10},{9,11},{10,... | collective-permute-start | bytes 3145736 | tf_op jit(solution)/shard_map/ppermute | solution.py:296
  597.6 17.3 %collective-permute-start.73 = (bf16[2,1,1,1,1,128,1024]{6,5,4,3,2,1,0:T(8,128)(2,1)}, bf16[2,1,1,1,1,128,1024]{6,5,4,3,2,1,0:T(8,128)(2,1)}, u32[]{:S(2)}, u32[]{:S(2)}) collective-permute-start(bf16[2,1,1,1,1,128,1024]{6,5,4,3,2,1,0:T(8,128)(2,1)} %constant_dynamic-slice_fusion.32), channel_id=1, source_target_pairs={{0,8},{1,9},{2,10},{3,11},{4,12},{5,13},{6,14},{7,15},{8,0},{9,1},... | collective-permute-start | bytes 1572872 | tf_op jit(solution)/shard_map/ppermute | solution.py:296
  602.1 88.2 %collective-permute-start.52 = (bf16[2,2,1,2,1,32,1536]{6,5,4,3,2,1,0:T(8,128)(2,1)}, bf16[2,2,1,2,1,32,1536]{6,5,4,3,2,1,0:T(8,128)(2,1)}, u32[]{:S(2)}, u32[]{:S(2)}) collective-permute-start(bf16[2,2,1,2,1,32,1536]{6,5,4,3,2,1,0:T(8,128)(2,1)} %constant_dynamic-slice_fusion.31), channel_id=1, source_target_pairs={{0,4},{1,5},{2,6},{3,7},{4,0},{5,1},{6,2},{7,3},{8,12},{9,13},{10,... | collective-permute-start | bytes 2359304 | tf_op jit(solution)/shard_map/ppermute | solution.py:296
  613.6 78.9 %collective-permute-start.61 = (bf16[2,2,2,2,1,32,768]{6,5,4,3,2,1,0:T(8,128)(2,1)}, bf16[2,2,2,2,1,32,768]{6,5,4,3,2,1,0:T(8,128)(2,1)}, u32[]{:S(2)}, u32[]{:S(2)}) collective-permute-start(bf16[2,2,2,2,1,32,768]{6,5,4,3,2,1,0:T(8,128)(2,1)} %constant_dynamic-slice_fusion.29), channel_id=1, source_target_pairs={{0,1},{1,0},{2,3},{3,2},{4,5},{5,4},{6,7},{7,6},{8,9},{9,8},{10,11... | collective-permute-start | bytes 2359304 | tf_op jit(solution)/shard_map/ppermute | solution.py:296
  614.8 80.4 %collective-permute-start.56 = (bf16[2,2,2,2,1,32,768]{6,5,4,3,2,1,0:T(8,128)(2,1)}, bf16[2,2,2,2,1,32,768]{6,5,4,3,2,1,0:T(8,128)(2,1)}, u32[]{:S(2)}, u32[]{:S(2)}) collective-permute-start(bf16[2,2,2,2,1,32,768]{6,5,4,3,2,1,0:T(8,128)(2,1)} %constant_dynamic-slice_fusion.30), channel_id=1, source_target_pairs={{0,1},{1,0},{2,3},{3,2},{4,5},{5,4},{6,7},{7,6},{8,9},{9,8},{10,11... | collective-permute-start | bytes 2359304 | tf_op jit(solution)/shard_map/ppermute | solution.py:296
  619.1 18.3 %collective-permute-start.75 = (f32[2,2,2,2,1,1,384]{6,5,4,3,2,1,0:T(1,128)S(1)}, f32[2,2,2,2,1,1,384]{6,5,4,3,2,1,0:T(1,128)S(1)}, u32[]{:S(2)}, u32[]{:S(2)}) collective-permute-start(f32[2,2,2,2,1,1,384]{6,5,4,3,2,1,0:T(1,128)S(1)} %fusion.159), channel_id=1, source_target_pairs={{0,1},{1,0},{2,3},{3,2},{4,5},{5,4},{6,7},{7,6},{8,9},{9,8},{10,11... | collective-permute-start | bytes 73736 | tf_op jit(solution)/shard_map/ppermute | solution.py:296
  645.8 28.6 %collective-permute-start.74 = (bf16[1,1,1,1,1,128,1024]{6,5,4,3,2,1,0:T(8,128)(2,1)}, bf16[1,1,1,1,1,128,1024]{6,5,4,3,2,1,0:T(8,128)(2,1)}, u32[]{:S(2)}, u32[]{:S(2)}) collective-permute-start(bf16[1,1,1,1,1,128,1024]{6,5,4,3,2,1,0:T(8,128)(2,1)} %constant_dynamic-slice_fusion.12), channel_id=1, source_target_pairs={{0,16},{1,17},{2,18},{3,19},{4,20},{5,21},{6,22},{7,23},{8,24},{9,... | collective-permute-start | bytes 786440 | tf_op jit(solution)/shard_map/ppermute | solution.py:296
  673.4 13.2 %collective-permute-start.71 = (bf16[2,1,1,1,1,32,4096]{6,5,4,3,2,1,0:T(8,128)(2,1)}, bf16[2,1,1,1,1,32,4096]{6,5,4,3,2,1,0:T(8,128)(2,1)S(1)}, u32[]{:S(2)}, u32[]{:S(2)}) collective-permute-start(bf16[2,1,1,1,1,32,4096]{6,5,4,3,2,1,0:T(8,128)(2,1)} %constant_dynamic-slice_fusion.14), channel_id=1, source_target_pairs={{0,8},{1,9},{2,10},{3,11},{4,12},{5,13},{6,14},{7,15},{8,0},{9,1},... | collective-permute-start | bytes 1572872 | tf_op jit(solution)/shard_map/ppermute | solution.py:296
  686.8 13.1 %collective-permute-start.72 = (bf16[1,1,1,1,1,32,4096]{6,5,4,3,2,1,0:T(8,128)(2,1)S(1)}, bf16[1,1,1,1,1,32,4096]{6,5,4,3,2,1,0:T(8,128)(2,1)S(1)}, u32[]{:S(2)}, u32[]{:S(2)}) collective-permute-start(bf16[1,1,1,1,1,32,4096]{6,5,4,3,2,1,0:T(8,128)(2,1)S(1)} %constant_dynamic-slice_fusion.13), channel_id=1, source_target_pairs={{0,16},{1,17},{2,18},{3,19},{4,20},{5,21},{6,22},{7,23},{8,24},{9,... | collective-permute-start | bytes 786440 | tf_op jit(solution)/shard_map/ppermute | solution.py:296
  691.7 11.8 %collective-permute-start.53 = (bf16[2,2,1,1,1,32,1536]{6,5,4,3,2,1,0:T(8,128)(2,1)S(1)}, bf16[2,2,1,1,1,32,1536]{6,5,4,3,2,1,0:T(8,128)(2,1)S(1)}, u32[]{:S(2)}, u32[]{:S(2)}) collective-permute-start(bf16[2,2,1,1,1,32,1536]{6,5,4,3,2,1,0:T(8,128)(2,1)S(1)} %constant_dynamic-slice_fusion.28), channel_id=1, source_target_pairs={{0,2},{1,3},{2,0},{3,1},{4,6},{5,7},{6,4},{7,5},{8,10},{9,11},{10,... | collective-permute-start | bytes 1179656 | tf_op jit(solution)/shard_map/ppermute | solution.py:296
  693.9 13.7 %collective-permute-start.62 = (bf16[2,2,2,1,1,32,768]{6,5,4,3,2,1,0:T(8,128)(2,1)S(1)}, bf16[2,2,2,1,1,32,768]{6,5,4,3,2,1,0:T(8,128)(2,1)S(1)}, u32[]{:S(2)}, u32[]{:S(2)}) collective-permute-start(bf16[2,2,2,1,1,32,768]{6,5,4,3,2,1,0:T(8,128)(2,1)S(1)} %constant_dynamic-slice_fusion.21), channel_id=1, source_target_pairs={{0,2},{1,3},{2,0},{3,1},{4,6},{5,7},{6,4},{7,5},{8,10},{9,11},{10,... | collective-permute-start | bytes 1179656 | tf_op jit(solution)/shard_map/ppermute | solution.py:296
  696.7 15.0 %collective-permute-start.57 = (bf16[2,2,1,2,1,32,768]{6,5,4,3,2,1,0:T(8,128)(2,1)S(1)}, bf16[2,2,1,2,1,32,768]{6,5,4,3,2,1,0:T(8,128)(2,1)S(1)}, u32[]{:S(2)}, u32[]{:S(2)}) collective-permute-start(bf16[2,2,1,2,1,32,768]{6,5,4,3,2,1,0:T(8,128)(2,1)S(1)} %constant_dynamic-slice_fusion.25), channel_id=1, source_target_pairs={{0,4},{1,5},{2,6},{3,7},{4,0},{5,1},{6,2},{7,3},{8,12},{9,13},{10,... | collective-permute-start | bytes 1179656 | tf_op jit(solution)/shard_map/ppermute | solution.py:296
  (120 other events, 1756.2 us)

commit v4 on v3

--- a/solution.py
+++ b/solution.py
@@ -14,7 +14,7 @@
 root_half = 0.7071067811865476
 density_peak = 0.3989422804014327
 head_width = 64
-block_queries = 16
+block_queries = 8
 masked_score = -1e30
 rate = 0.125 * 1.4426950408889634
 q_rows = 256
@@ -53,12 +53,6 @@
     mean_proj = jnp.mean(grad_norm * normed, axis=-1, keepdims=True)
     grad_in = inv_scale * (grad_norm - mean_grad - normed * mean_proj)
     return (grad_in, jnp.sum(grad_out * normed, axis=0), jnp.sum(grad_out, axis=0))
-
-
-def unit_prefix(vectors, level_width):
-    part_cols = vectors[..., :level_width].astype(jnp.float32)
-    inv_scale = lax.rsqrt(jnp.sum(part_cols * part_cols, axis=-1, keepdims=True) + unit_eps)
-    return (part_cols * inv_scale, inv_scale)
 
 
 def dot_nt(a,b): return lax.dot_general(a,b,(((1,),(1,)),((),())),preferred_element_type=f32)
@@ -215,6 +209,141 @@
     )(bounds,segrow,segcol,qkv,qkv,qkv,g,o,lse,qlse)
 
 
+def level_units(values, width):
+    lanes = lax.broadcasted_iota(jnp.int32, values.shape, 1)
+    part_cols = jnp.where(lanes < width, values, 0.0)
+    inv_scale = lax.rsqrt(jnp.sum(part_cols * part_cols, axis=-1, keepdims=True) + unit_eps)
+    return part_cols * inv_scale, inv_scale
+
+
+def three_parts(values):
+    top = values.astype(bf16)
+    rest = values - top.astype(f32)
+    middle = rest.astype(bf16)
+    return top, middle, (rest - middle.astype(f32)).astype(bf16)
+
+
+def exact_dot(values, marks):
+    return sum(dot_nn(part, marks) for part in three_parts(values))
+
+
+def keep_doc_units(levels, doc_ref, low_ref):
+    @pl.when(pl.program_id(0) == 0)
+    def _():
+        docs = doc_ref[...].astype(f32)
+        for position, width in enumerate(levels):
+            low_ref[position] = level_units(docs, width)[0].astype(bf16)
+
+
+def interact_forward(levels, span, doc_ref, member_ref, query_ref, logit_ref, sums_ref, low_ref):
+    keep_doc_units(levels, doc_ref, low_ref)
+    queries = query_ref[...].astype(f32)
+    member = member_ref[...]
+    for position, width in enumerate(levels):
+        unit_rows = level_units(queries, width)[0].astype(bf16)
+        powers = jnp.exp(dot_nt(unit_rows, low_ref[position]) / softness)
+        doc_sums = exact_dot(powers, member)
+        sums_ref[position] = doc_sums
+        logs = (softness * jnp.log(doc_sums)).reshape(-1, span, doc_sums.shape[1])
+        logit_ref[position] = jnp.sum(logs, axis=1) / (span * sharpness_divisor)
+
+
+def interact_backward(
+    levels, span, doc_ref, member_t_ref, query_ref, sums_ref, grad_ref, query_grad_ref,
+    doc_grad_ref, low_ref, held_ref,
+):
+    keep_doc_units(levels, doc_ref, low_ref)
+
+    @pl.when(pl.program_id(0) == 0)
+    def _():
+        held_ref[...] = jnp.zeros_like(held_ref)
+
+    queries = query_ref[...].astype(f32)
+    member_t = member_t_ref[...]
+    total = jnp.zeros(queries.shape, f32)
+    for position, width in enumerate(levels):
+        unit_full, inv_scale = level_units(queries, width)
+        unit_rows = unit_full.astype(bf16)
+        powers = jnp.exp(dot_nt(unit_rows, low_ref[position]) / softness)
+        grads = grad_ref[position]
+        rows = jnp.broadcast_to(grads[:, None, :], (grads.shape[0], span, grads.shape[1]))
+        rows = rows.reshape(-1, grads.shape[1]) / sums_ref[position]
+        grad_scores = (powers * exact_dot(rows, member_t)).astype(bf16)
+        grad_unit = dot_nn(grad_scores, low_ref[position])
+        held_ref[position] += matmul_left_t(grad_scores, unit_rows)
+        total = total + inv_scale * (
+            grad_unit - unit_full * jnp.sum(grad_unit * unit_full, axis=-1, keepdims=True)
+        )
+    query_grad_ref[...] = total
+
+    @pl.when(pl.program_id(0) == pl.num_programs(0) - 1)
+    def _():
+        docs = doc_ref[...].astype(f32)
+        doc_total = jnp.zeros(docs.shape, f32)
+        for position, width in enumerate(levels):
+            unit_full, inv_scale = level_units(docs, width)
+            grad_unit = held_ref[position]
+            doc_total = doc_total + inv_scale * (
+                grad_unit - unit_full * jnp.sum(grad_unit * unit_full, axis=-1, keepdims=True)
+            )
+        doc_grad_ref[...] = doc_total
+
+
+def interaction_logits(levels, span, docs, member, queries):
+    tokens, width = queries.shape
+    row_len, slots = member.shape
+    rows = block_queries * span
+    return pl.pallas_call(
+        partial(interact_forward, levels, span),
+        grid=(tokens // rows,),
+        out_shape=(
+            jax.ShapeDtypeStruct((3, tokens // span, slots), f32),
+            jax.ShapeDtypeStruct((3, tokens, slots), f32),
+        ),
+        in_specs=[
+            pl.BlockSpec((row_len, width), lambda i: (0, 0)),
+            pl.BlockSpec((row_len, slots), lambda i: (0, 0)),
+            pl.BlockSpec((rows, width), lambda i: (i, 0)),
+        ],
+        out_specs=(
+            pl.BlockSpec((3, block_queries, slots), lambda i: (0, i, 0)),
+            pl.BlockSpec((3, rows, slots), lambda i: (0, i, 0)),
+        ),
+        scratch_shapes=[pltpu.VMEM((3, row_len, width), bf16)],
+        compiler_params=pltpu.CompilerParams(vmem_limit_bytes=40 << 20),
+    )(docs, member, queries)
+
+
+def interaction_grads(levels, span, docs, member_t, queries, sums, grads):
+    tokens, width = queries.shape
+    slots, row_len = member_t.shape
+    rows = block_queries * span
+    return pl.pallas_call(
+        partial(interact_backward, levels, span),
+        grid=(tokens // rows,),
+        out_shape=(
+            jax.ShapeDtypeStruct((tokens, width), f32),
+            jax.ShapeDtypeStruct((row_len, width), f32),
+        ),
+        in_specs=[
+            pl.BlockSpec((row_len, width), lambda i: (0, 0)),
+            pl.BlockSpec((slots, row_len), lambda i: (0, 0)),
+            pl.BlockSpec((rows, width), lambda i: (i, 0)),
+            pl.BlockSpec((3, rows, slots), lambda i: (0, i, 0)),
+            pl.BlockSpec((3, block_queries, slots), lambda i: (0, i, 0)),
+        ],
+        out_specs=(
+            pl.BlockSpec((rows, width), lambda i: (i, 0)),
+            pl.BlockSpec((row_len, width), lambda i: (0, 0)),
+        ),
+        scratch_shapes=[
+            pltpu.VMEM((3, row_len, width), bf16),
+            pltpu.VMEM((3, row_len, width), f32),
+        ],
+        compiler_params=pltpu.CompilerParams(vmem_limit_bytes=40 << 20),
+    )(docs, member_t, queries, sums, grads)
+
+
 def after(value, *earlier):
     return lax.optimization_barrier((value, *earlier))[0]
 
@@ -237,9 +366,9 @@
         mine = self.links.side(self.place)
         held = self.held
         arrived = after(self.arrived, *earlier) if earlier else self.arrived
-        both = jnp.zeros(held.shape[:axis] + (2,) + held.shape[axis + 1 :], held.dtype)
-        both = lax.dynamic_update_slice_in_dim(both, held, mine, axis)
-        self.held = lax.dynamic_update_slice_in_dim(both, arrived, 1 - mine, axis)
+        shape = held.shape[:axis] + (2,) + held.shape[axis + 1 :]
+        own = lax.broadcasted_iota(jnp.int32, shape, axis) == mine
+        self.held = jnp.where(own, held, arrived)
 
     def full(self):
         while self.order:
@@ -258,6 +387,8 @@
         self.held = after(self.held, *earlier)
 
     def launch(self):
+        if not self.order:
+            return
         self.place = self.order.pop()
         axis = self.links.bits - 1 - self.place
         self.leaving = lax.dynamic_slice_in_dim(
@@ -266,11 +397,14 @@
         self.arrived = self.links.swap(self.leaving, 1 << self.place)
 
     def merge(self, *earlier):
+        if self.arrived is None:
+            return
         axis = self.links.bits - 1 - self.place
         kept = lax.dynamic_slice_in_dim(self.held, self.links.side(self.place), 1, axis)
         arrived = after(self.arrived, *earlier) if earlier else self.arrived
         total = kept.astype(f32) + arrived.astype(f32)
         self.held = total.astype(self.wire) if self.order else total
+        self.arrived = None
 
     def mine(self):
         while self.order:
@@ -492,32 +626,11 @@
     vectors = matmul_plain(second_low, full_proj).astype(bf16)
     doc_vectors = vectors[:row_len]
     query_vectors = vectors[row_len:].reshape(query_count * span, proj_width)
-    every_query = links.growing(query_vectors).full().reshape(count * query_count, span, proj_width)
-    query_total = every_query.shape[0]
-    block_count = query_total // block_queries
+    every_query = links.growing(query_vectors).full().reshape(count * query_count * span, proj_width)
+    query_total = count * query_count
     levels = (proj_width, proj_width * 3 // 4, proj_width // 2)
-    doc_prefix = tuple((unit_prefix(doc_vectors, level_width) for level_width in levels))
-    doc_lows = tuple((prefix_pair[0].astype(bf16) for prefix_pair in doc_prefix))
-
-    def block_logits(one_block):
-        row_total = one_block.shape[0] * span
-        piled_entries = []
-        for position in range(3):
-            level_width = levels[position]
-            unit_rows = (
-                unit_prefix(one_block, level_width)[0].astype(bf16).reshape(row_total, level_width)
-            )
-            scores = matmul_right_t(unit_rows, doc_lows[position])
-            doc_sums = jnp.dot(jnp.exp(scores / softness), member, precision=lax.Precision.HIGHEST)
-            peak_match_score = jnp.sum(
-                (softness * jnp.log(doc_sums)).reshape(one_block.shape[0], span, doc_slots),
-                axis=1,
-            )
-            piled_entries.append(peak_match_score / (span * sharpness_divisor))
-        return jnp.stack(piled_entries, axis=1)
-
-    blocks = every_query.reshape(block_count, block_queries, span, proj_width)
-    logits = lax.map(block_logits, blocks).reshape(query_total, 3, doc_slots)
+    logits, doc_sums = interaction_logits(levels, span, doc_vectors, member.astype(bf16), every_query)
+    logits = logits.transpose(1, 0, 2)
     powers = jnp.exp(logits)
     local_sum = jnp.sum(powers, axis=-1)
     my_row = lax.axis_index(AXES)
@@ -529,51 +642,12 @@
     score_derivative = (powers / all_sums[:, :, None] - chosen[:, None, :]) / query_total
     peak_match_derivative = score_derivative / (span * sharpness_divisor)
 
-    def block_back(carry, inputs):
-        one_block, grad_block = inputs
-        block_size = one_block.shape[0]
-        row_total = block_size * span
-        grad_vectors = jnp.zeros((block_size, span, proj_width), f32)
-        new_carry = []
-        for position in range(3):
-            level_width = levels[position]
-            unit_full, inv_scale = unit_prefix(one_block, level_width)
-            unit_rows = unit_full.astype(bf16).reshape(row_total, level_width)
-            scores = matmul_right_t(unit_rows, doc_lows[position])
-            score_powers = jnp.exp(scores / softness)
-            doc_sums = jnp.dot(score_powers, member, precision=lax.Precision.HIGHEST)
-            grad_rows = jnp.broadcast_to(
-                grad_block[:, None, position, :], (block_size, span, doc_slots)
-            ).reshape(row_total, doc_slots)
-            spread_rows = jnp.dot(grad_rows / doc_sums, member_t, precision=lax.Precision.HIGHEST)
-            grad_scores = (score_powers * spread_rows).astype(bf16)
-            grad_unit = matmul_plain(grad_scores, doc_lows[position]).reshape(
-                block_size, span, level_width
-            )
-            new_carry.append(carry[position] + matmul_left_t(grad_scores, unit_rows))
-            grad_part = inv_scale * (
-                grad_unit - unit_full * jnp.sum(grad_unit * unit_full, axis=-1, keepdims=True)
-            )
-            grad_vectors = grad_vectors + jnp.pad(
-                grad_part, ((0, 0), (0, 0), (0, proj_width - level_width))
-            )
-        return (tuple(new_carry), grad_vectors)
-
-    start_carry = tuple((jnp.zeros((row_len, level_width), f32) for level_width in levels))
-    grad_blocks = peak_match_derivative.reshape(block_count, block_queries, 3, doc_slots)
-    doc_unit_grads, query_terms = lax.scan(block_back, start_carry, (blocks, grad_blocks))
+    query_terms, doc_vec_grad = interaction_grads(
+        levels, span, doc_vectors, member_t.astype(bf16), every_query, doc_sums,
+        peak_match_derivative.transpose(1, 0, 2),
+    )
     query_terms = query_terms.reshape(count, query_count * span, proj_width)
     query_vec_grad = links.shrinking(query_terms, wire=f32).mine()
-    doc_vec_grad = jnp.zeros((row_len, proj_width), f32)
-    for position in range(3):
-        unit_full, inv_scale = doc_prefix[position]
-        grad_unit = doc_unit_grads[position]
-        grad_part = inv_scale * (
-            grad_unit - unit_full * jnp.sum(grad_unit * unit_full, axis=-1, keepdims=True)
-        )
-        doc_vec_grad = doc_vec_grad + jnp.pad(
-            grad_part, ((0, 0), (0, proj_width - levels[position]))
-        )
     grad_vectors = jnp.concatenate([doc_vec_grad, query_vec_grad], axis=0).astype(bf16)
 
     def spread_rows_of(full):
@@ -645,17 +719,11 @@
         if side == 0:
             out_sum.merge(qkv_sums[0].leaving)
             out_sum.launch()
-            earlier = (qkv_sums[0].leaving, out_sum.leaving)
+            up_sum.merge(qkv_sums[0].leaving)
+            up_sum.launch()
+            earlier = (qkv_sums[0].leaving, out_sum.leaving, up_sum.leaving)
         grad_qkv = after(grad_qkv, *[one.leaving for one in qkv_sums[side:]])
         input_grad = input_grad + matmul_right_t(grad_qkv, full_qkv[side])
-    last = [one.leaving for one in qkv_sums[1:]]
-    for one in (out_sum, up_sum, down_sum, qkv_sums[0]):
-        one.merge(*last)
-    for one in qkv_sums[1:]:
-        one.merge()
-    down_shard, up_shard, out_proj_shard = down_sum.mine(), up_sum.mine(), out_sum.mine()
-    qkv_shards = [one.mine() for one in qkv_sums]
-    qkv_shards = [qkv_shards[0], jnp.concatenate(qkv_shards[1:], axis=-1)]
     bias_grads = jnp.stack(
         [
             jnp.concatenate(query_bias),
@@ -676,7 +744,22 @@
         ],
         axis=1,
     )
-    small_shard = links.shrinking(small_grads[:, None, :], 0, wire=f32).mine()[0]
+    small_sum = links.shrinking(small_grads[:, None, :], 0, wire=f32)
+    small_sum.launch()
+    first, others = qkv_sums[1:], [small_sum, qkv_sums[0], out_sum, up_sum, down_sum]
+    last = [one.leaving for one in first]
+    for hop in range(links.bits):
+        for one in first:
+            one.merge()
+        for one in others:
+            one.merge(*last)
+        for one in first + others:
+            one.launch()
+        last = [one.leaving for one in first]
+    down_shard, up_shard, out_proj_shard = down_sum.mine(), up_sum.mine(), out_sum.mine()
+    qkv_shards = [one.mine() for one in qkv_sums]
+    qkv_shards = [qkv_shards[0], jnp.concatenate(qkv_shards[1:], axis=-1)]
+    small_shard = small_sum.mine()[0]
     shards = [
         jnp.concatenate([s[:, i * part : (i + 1) * part] for s in qkv_shards], axis=1)
         for i in range(3)

time: 738 us -> 644 us (0.87)
  local copies, waits for them, and re-layouts: 131 us -> 64.3 us
  matrix products: 207 us -> 152 us
  Pallas kernels: 99.4 us -> 122 us
  other arithmetic: 74.4 us -> 91.1 us
  waiting for transfers between devices: 144 us -> 135 us
    dynamic_update_slice x68 -> x0, local copies, waits for them, and re-layouts: 55.7 us -> none  [the longest x35 30.5 us: merge(): self.held = lax.dynamic_update_slice_in_dim(both, arrived, 1 - mine, axis)]
    select_n x0 -> x45, other arithmetic: none -> 38.7 us  [merge(): self.held = jnp.where(own, held, arrived)]
    dot_general x18 -> x0, matrix products: 38 us -> none  [the longest x6 12.9 us: block_logits(): jnp.dot(jnp.exp(scores / softness), member, precision=lax.Precision.HIGHEST)]
    pallas_call x0 -> x2, Pallas kernels: none -> 23.4 us  [the longest x1 13.6 us: interaction_grads(): pl.pallas_call(partial(interact_backward, levels, span), grid=(tokens //...]
    broadcast_in_dim x35 -> x4, local copies, waits for them, and re-layouts: 17.4 us -> 2.09 us  [merge(): self.held = jnp.where(own, held, arrived)]
    mul x6 -> x0, other arithmetic: 12.1 us -> none  [the longest x4 10.7 us: block_back(): unit_full * jnp.sum(grad_unit * unit_full, axis=-1, keepdims=True)]
    dot_general x13 -> x7, matrix products: 60.7 us -> 51.9 us  [matmul_plain(): return jnp.dot(left, right, preferred_element_type=jnp.float32)]
    ppermute x80, waiting for transfers between devices: 144 us -> 135 us  [swap(): return lax.ppermute(value, AXES, [(d, d ^ bit) for d in range(self.count)])]
  transfers between devices with their start and end apart: 80 -> 80, of which waited for: 43 -> 31; matrix products, arithmetic and copies ran while one was open for 39% -> 38% of each run, Pallas kernels for 14% -> 15%
where the time goes in v4:
time: 644 us; the launch traced here: 637 us
  matrix products  152 us (24%)
  waiting for transfers between devices  135 us (21%)
  Pallas kernels  122 us (19%)
  other arithmetic  91.1 us (14%)
  starting transfers between devices  68.3 us (11%)
  local copies, waits for them, and re-layouts  64.3 us (10%)
    ppermute x80, waiting for transfers between devices, swap(): return lax.ppermute(value, AXES, [(d, d ^ bit) for d in range(self.count)])  135 us
    ppermute x80, starting transfers between devices, swap(): return lax.ppermute(value, AXES, [(d, d ^ bit) for d in range(self.count)])  68.3 us
    dot_general x7, matrix products, matmul_right_t(): lax.dot_general(left, right, (((1,), (1,)), ((), ())), preferred_element_...  54.8 us
    pallas_call x2, Pallas kernels, attention_backward(): pl.pallas_call(partial(attend_backward, row_len, qb, kb, lanes, span), ou...  54.7 us
    dot_general x7, matrix products, matmul_plain(): return jnp.dot(left, right, preferred_element_type=jnp.float32)  51.9 us
    dot_general x7, matrix products, matmul_left_t(): lax.dot_general(left, right, (((0,), (0,)), ((), ())), preferred_element_...  45 us
    pallas_call x2, Pallas kernels, attention_forward(): pl.pallas_call(partial(attend_forward, row_len, qb, kb, lanes, span), out...  43.6 us
    select_n x45, other arithmetic, merge(): self.held = jnp.where(own, held, arrived)  38.7 us
  transfers between devices with their start and end apart: 80, of which 31 were waited for; matrix products, arithmetic and copies ran while one was open for 38% of the time, Pallas kernels for 15%

profile of v4, /device:TPU:0, one launch (start us, length us, event | category | flops | bytes accessed | tf_op | source)
XLA Modules:
  0.0 637.4 jit_solution(6340520061211204039)
XLA Ops:
  3.0 4.1 collective-permute-start.5
  9.5 3.0 collective-permute-start
  26.3 7.7 %collective-permute-done.8 = bf16[2,1,1,1,1,32,1536]{6,5,0,4,3,2,1:T(8,128)(2,1)S(1)} collective-permute-done((bf16[2,1,1,1,1,32,1536]{6,5,0,4,3,2,1:T(8,128)(2,1)S(1)}, bf16[2,1,1,1,1,32,1536]{6,5,0,4,3,2,1:T(8,128)(2,1)S(1)}, u32[]{:S(2)}, u32[]{:S(2)}) %collective-permute-start.8) | collective-permute-done | bytes 196640 | tf_op jit(solution)/shard_map/ppermute | solution.py:430
  40.4 7.6 %collective-permute-done.20 = bf16[1,1,1,1,1,32,4096]{6,5,4,3,2,1,0:T(8,128)(2,1)S(1)} collective-permute-done((bf16[1,1,1,1,1,32,4096]{6,5,4,3,2,1,0:T(8,128)(2,1)S(1)}, bf16[1,1,1,1,1,32,4096]{6,5,4,3,2,1,0:T(8,128)(2,1)S(1)}, u32[]{:S(2)}, u32[]{:S(2)}) %collective-permute-start.20) | collective-permute-done | bytes 262176 | tf_op jit(solution)/shard_map/ppermute | solution.py:430
  48.1 4.4 collective-permute-done.24
  58.8 8.6 %collective-permute-done.25 = bf16[2,1,1,1,1,128,1024]{6,5,0,4,3,2,1:T(8,128)(2,1)S(1)} collective-permute-done((bf16[2,1,1,1,1,128,1024]{6,5,0,4,3,2,1:T(8,128)(2,1)S(1)}, bf16[2,1,1,1,1,128,1024]{6,5,0,4,3,2,1:T(8,128)(2,1)S(1)}, u32[]{:S(2)}, u32[]{:S(2)}) %collective-permute-start.25) | collective-permute-done | bytes 524320 | tf_op jit(solution)/shard_map/ppermute | solution.py:430
  68.9 9.1 %collective-permute-done.21 = bf16[2,1,1,1,1,32,4096]{6,5,0,4,3,2,1:T(8,128)(2,1)S(1)} collective-permute-done((bf16[2,1,1,1,1,32,4096]{6,5,0,4,3,2,1:T(8,128)(2,1)S(1)}, bf16[2,1,1,1,1,32,4096]{6,5,0,4,3,2,1:T(8,128)(2,1)S(1)}, u32[]{:S(2)}, u32[]{:S(2)}) %collective-permute-start.21) | collective-permute-done | bytes 524320 | tf_op jit(solution)/shard_map/ppermute | solution.py:430
  88.5 3.9 collective-permute-done.13
  116.4 3.9 bitcast_select_fusion.2
  121.9 4.0 fusion.7.q_ref.k_ref.v_ref
  125.9 21.8 %shard_map.238 = (bf16[1056,512]{1,0:T(8,128)(2,1)S(1)}, f32[4,4,512]{2,1,0:T(4,128)S(1)}, f32[4,1,64]{2,1,0:T(1,128)S(1)}) custom-call(s32[2,4]{1,0:T(2,128)S(1)} %pad_add_fusion.bounds, s32[4,512]{1,0:T(4,128)S(1)} %constant_dynamic-update-slice_fusion.segrow, s32[1024,1]{1,0:T(8,128)S(1)} %copy.41.segcol, bf16[1056,1536]{1,0:T(8,128)(2,1)S(1)} %fusion.7.q_ref.k_ref.v_ref, ...), custom_call_target="tpu_custom_call" | custom-call | tf_op jit(solution)/shard_map/pallas_call | solution.py:124
  147.8 6.4 %fusion.6.q_ref.k_ref.v_ref = bf16[1056,1536]{1,0:T(8,128)(2,1)S(1)} fusion(bf16[1024,1536]{1,0:T(8,128)(2,1)} %get-tuple-element.224, f32[1536]{0:T(1024)S(1)} %copy-done.64, bf16[32,1024]{1,0:T(8,128)(2,1)S(1)} %bitcast.262, bf16[1024,1024]{1,0:T(8,128)(2,1)} %bitcast.221), kind=kOutput, calls=%fused_computation.19 | convolution fusion | flops 3329458176 | bytes 8558592 | tf_op jit(solution)/shard_map/dot_general | solution.py:27
  154.3 21.8 %shard_map.237 = (bf16[1056,512]{1,0:T(8,128)(2,1)S(1)}, f32[4,4,512]{2,1,0:T(4,128)S(1)}, f32[4,1,64]{2,1,0:T(1,128)S(1)}) custom-call(s32[2,4]{1,0:T(2,128)S(1)} %pad_add_fusion.bounds, s32[4,512]{1,0:T(4,128)S(1)} %constant_dynamic-update-slice_fusion.segrow, s32[1024,1]{1,0:T(8,128)S(1)} %copy.41.segcol, bf16[1056,1536]{1,0:T(8,128)(2,1)S(1)} %fusion.6.q_ref.k_ref.v_ref, ...), custom_call_target="tpu_custom_call" | custom-call | tf_op jit(solution)/shard_map/pallas_call | solution.py:124
  193.3 7.4 %bitcast_select_fusion.1 = bf16[1024,4096]{1,0:T(8,128)(2,1)} fusion(pred[1024]{0:T(1024)(128)(4,1)S(1)} %copy-done.60, bf16[2,2,2,2,32,4096]{5,4,3,2,1,0:T(8,128)(2,1)} %bitcast.70, bf16[2,2,2,2,32,4096]{5,4,3,2,1,0:T(8,128)(2,1)S(1)} %broadcast_select_fusion.1), kind=kLoop, calls=%fused_computation.15 | loop fusion | flops 4194304 | bytes 16778240 | tf_op jit(solution)/shard_map/jit(_where)/select_n | solution.py:371
  200.7 20.9 %fusion.4 = (bf16[1056,4096]{1,0:T(8,128)(2,1)}, bf16[1056,4096]{1,0:T(8,128)(2,1)}) fusion(f32[4096]{0:T(1024)S(1)} %fusion.31, bf16[1024,4096]{1,0:T(8,128)(2,1)} %bitcast_select_fusion.1, f32[1056,1024]{1,0:T(8,128)S(1)} %get-tuple-element.234, f32[1024]{0:T(1024)S(1)} %copy-done.66, f32[1024]{0:T(1024)S(1)} %copy-done.61, f32[1056]{0:T(1024)S(1)} %add_rsqrt_fusion.1, ...), kind=kOutput, calls=%fused_computation.7 | convolution fusion | flops 8915681280 | bytes 30048512 | tf_op jit(solution)/shard_map/dot_general | solution.py:27
  221.6 3.4 bitcast_select_fusion
  225.1 16.1 %fusion.52 = (f32[1056]{0:T(1024)S(1)}, f32[1056,1024]{1,0:T(8,128)S(1)}) fusion(f32[1024]{0:T(1024)S(1)} %copy-done.67, bf16[1056,4096]{1,0:T(8,128)(2,1)} %get-tuple-element.126, bf16[4096,1024]{1,0:T(8,128)(2,1)S(1)} %bitcast_select_fusion, f32[1024]{0:T(1024)S(1)} %copy-done.66, f32[1024]{0:T(1024)S(1)} %copy-done.61, f32[1056]{0:T(1024)S(1)} %add_rsqrt_fusion.1, ...), kind=kOutput, calls=%fused_computation.302 | convolution fusion | flops 8865938432 | bytes 25715072 | tf_op jit(solution)/shard_map/dot_general | solution.py:27
  244.1 4.4 collective-permute-done.30
  248.7 3.6 collective-permute-done.31
  257.3 3.4 collective-permute-done.33
  262.4 9.8 %shard_map.239 = (f32[3,32,8]{2,1,0:T(8,128)S(1)}, f32[3,1024,8]{2,1,0:T(8,128)S(1)}) custom-call(bf16[1024,128]{1,0:T(8,128)(2,1)S(1)} %slice.227.doc_ref, bf16[1024,8]{1,0:T(8,128)(2,1)S(1)} %convert_convert_fusion.member_ref, bf16[1024,128]{1,0:T(8,128)(2,1)S(1)} %bitcast_select_fusion.5.query_ref), custom_call_target="tpu_custom_call" | custom-call | tf_op jit(solution)/shard_map/pallas_call | solution.py:296
  272.8 4.1 collective-permute-done.35
  277.0 3.6 collective-permute-done.36
  289.7 13.6 %shard_map.240 = (f32[1024,128]{1,0:T(8,128)S(1)}, f32[1024,128]{1,0:T(8,128)S(1)}) custom-call(bf16[1024,128]{1,0:T(8,128)(2,1)S(1)} %slice.227.doc_ref, bf16[8,1024]{1,0:T(8,128)(2,1)S(1)} %convert_convert_fusion.1.member_t_ref, bf16[1024,128]{1,0:T(8,128)(2,1)S(1)} %bitcast_select_fusion.5.query_ref, f32[3,1024,8]{2,1,0:T(8,128)S(1)} %get-tuple-element.128.sums_ref, ...), custom_call_target="tpu_custom_call" | custom-call | tf_op jit(solution)/shard_map/pallas_call | solution.py:321
  305.8 4.8 collective-permute-done.41
  315.2 3.9 collective-permute-done.43
  320.2 3.5 collective-permute-done.44
  323.8 4.1 multiply_reduce_fusion
  330.9 12.0 %convolution_convert_fusion = bf16[4096,1024]{1,0:T(8,128)(2,1)S(1)} fusion(bf16[1056,4096]{1,0:T(8,128)(2,1)S(1)} %bitcast.290, bf16[1056,1024]{1,0:T(8,128)(2,1)S(1)} %get-tuple-element.131), kind=kOutput, calls=%fused_computation.18 | convolution fusion | flops 8862564352 | bytes 19202048 | tf_op jit(solution)/shard_map/dot_general | solution.py:37
  342.9 3.1 constant_dynamic-slice_fusion.37
  347.6 15.6 %convert_reduce_fusion = (f32[4096]{0:T(1024)S(1)}, bf16[1056,4096]{1,0:T(8,128)(2,1)}) fusion(bf16[1056,4096]{1,0:T(8,128)(2,1)} %get-tuple-element.132, bf16[1056,1024]{1,0:T(8,128)(2,1)S(1)} %get-tuple-element.131, bf16[4096,1024]{1,0:T(8,128)(2,1)} %copy-done.26), kind=kOutput, calls=%fused_computation.8 | convolution fusion | flops 8879992832 | bytes 27869184 | tf_op jit(solution)/shard_map/dot_general | solution.py:31
  363.2 14.7 %convolution_convert_fusion.1 = bf16[1024,4096]{1,0:T(8,128)(2,1)S(1)} fusion(bf16[1056,4096]{1,0:T(8,128)(2,1)} %get-tuple-element.134, f32[1056,1024]{1,0:T(8,128)S(1)} %bitcast.188, f32[1024]{0:T(1024)S(1)} %copy-done.66, f32[1024]{0:T(1024)S(1)} %copy-done.61, f32[1056]{0:T(1024)S(1)} %add_rsqrt_fusion.1, f32[1056]{0:T(1024)S(1)} %broadcast_multiply_fusion.5), kind=kOutput, calls=%fused_computation.21 | convolution fusion | flops 8867971072 | bytes 21381376 | tf_op jit(solution)/shard_map/dot_general | solution.py:37
  384.1 6.0 add_convert_fusion.1
  395.2 16.9 %multiply_reduce_fusion.1 = (f32[1024]{0:T(1024)S(1)}, f32[1056]{0:T(1024)S(1)}, f32[1056]{0:T(1024)S(1)}, f32[1024]{0:T(1024)S(1)}, f32[1056,1024]{1,0:T(8,128)}) fusion(f32[1056,1024]{1,0:T(8,128)S(1)} %bitcast.188, f32[1056]{0:T(1024)S(1)} %add_rsqrt_fusion.1, f32[1056]{0:T(1024)S(1)} %broadcast_multiply_fusion.5, f32[1024]{0:T(1024)S(1)} %copy-done.61, ...), kind=kOutput, calls=%fused_computation.31 | convolution fusion | flops 8869179392 | bytes 30044672 | tf_op jit(solution)/shard_map/dot_general | solution.py:31
  412.3 5.8 fusion.43
  418.1 5.8 add_convert_fusion
  427.0 3.3 convolution_convert_fusion.7
  445.9 27.5 %shard_map.241 = bf16[1056,1536]{1,0:T(8,128)(2,1)} custom-call(s32[2,4]{1,0:T(2,128)} %copy-done.10, s32[4,512]{1,0:T(4,128)} %copy-done.7, s32[1024,1]{1,0:T(8,128)} %copy-done.2, bf16[1056,1536]{1,0:T(8,128)(2,1)} %copy-done.1, bf16[1056,1536]{1,0:T(8,128)(2,1)} %copy-done.1, bf16[1056,1536]{1,0:T(8,128)(2,1)} %copy-done.1, ...), custom_call_target="tpu_custom_call" | custom-call | tf_op jit(solution)/shard_map/pallas_call | solution.py:201
  473.5 7.0 %convolution_convert_fusion.3 = bf16[1024,1536]{1,0:T(8,128)(2,1)S(1)} fusion(bf16[1056,1536]{1,0:T(8,128)(2,1)} %shard_map.241, bf16[32,1024]{1,0:T(8,128)(2,1)S(1)} %bitcast.264, bf16[1024,1024]{1,0:T(8,128)(2,1)} %bitcast.222), kind=kOutput, calls=%fused_computation.55 | convolution fusion | flops 3327787008 | bytes 8552448 | tf_op jit(solution)/shard_map/dot_general | solution.py:37
  493.8 27.2 %shard_map.242 = bf16[1056,1536]{1,0:T(8,128)(2,1)} custom-call(s32[2,4]{1,0:T(2,128)} %copy-done.10, s32[4,512]{1,0:T(4,128)} %copy-done.7, s32[1024,1]{1,0:T(8,128)} %copy-done.2, bf16[1056,1536]{1,0:T(8,128)(2,1)} %copy-done, bf16[1056,1536]{1,0:T(8,128)(2,1)} %copy-done, bf16[1056,1536]{1,0:T(8,128)(2,1)} %copy-done, ...), custom_call_target="tpu_custom_call" | custom-call | tf_op jit(solution)/shard_map/pallas_call | solution.py:201
  521.0 7.9 %convolution_add_fusion.7 = f32[1056,1024]{1,0:T(8,128)} fusion(f32[1056,1024]{1,0:T(8,128)} %get-tuple-element.195, bf16[1056,1536]{1,0:T(8,128)(2,1)S(1)} %copy-done.21, bf16[1024,1536]{1,0:T(8,128)(2,1)} %get-tuple-element.224), kind=kOutput, calls=%fused_computation.28 | convolution fusion | flops 3322970112 | bytes 15040512 | tf_op jit(solution)/shard_map/dot_general | solution.py:31
  539.6 5.7 convolution_convert_fusion.2
  548.3 7.5 %collective-permute-done.71 = bf16[2,1,1,1,1,32,4096]{6,5,4,3,2,1,0:T(8,128)(2,1)} collective-permute-done((bf16[2,1,1,1,1,32,4096]{6,5,4,3,2,1,0:T(8,128)(2,1)}, bf16[2,1,1,1,1,32,4096]{6,5,4,3,2,1,0:T(8,128)(2,1)}, u32[]{:S(2)}, u32[]{:S(2)}) %collective-permute-start.71) | collective-permute-done | bytes 524320 | tf_op jit(solution)/shard_map/ppermute | solution.py:430
  558.2 5.7 convolution_add_fusion.6
  575.9 19.2 %collective-permute-done.72 = bf16[1,1,1,1,1,32,4096]{6,5,4,3,2,1,0:T(8,128)(2,1)S(1)} collective-permute-done((bf16[1,1,1,1,1,32,4096]{6,5,4,3,2,1,0:T(8,128)(2,1)S(1)}, bf16[1,1,1,1,1,32,4096]{6,5,4,3,2,1,0:T(8,128)(2,1)S(1)}, u32[]{:S(2)}, u32[]{:S(2)}) %collective-permute-start.72) | collective-permute-done | bytes 262176 | tf_op jit(solution)/shard_map/ppermute | solution.py:430
  602.8 6.4 %collective-permute-done.54 = bf16[2,2,1,1,1,32,1536]{6,5,4,3,2,1,0:T(8,128)(2,1)S(1)} collective-permute-done((bf16[2,2,1,1,1,32,1536]{6,5,4,3,2,1,0:T(8,128)(2,1)S(1)}, bf16[2,2,1,1,1,32,1536]{6,5,4,3,2,1,0:T(8,128)(2,1)S(1)}, u32[]{:S(2)}, u32[]{:S(2)}) %collective-permute-start.54) | collective-permute-done | bytes 393248 | tf_op jit(solution)/shard_map/ppermute | solution.py:430
  615.7 3.7 collective-permute-done.70
  630.4 3.4 collective-permute-done.64
  (540 shorter events, 215.1 us)
Async XLA Ops:
  3.0 20.3 %collective-permute-start.5 = (bf16[1,1,1,1,1,1,384]{6,5,4,3,2,1,0:T(2,128)(2,1)S(1)}, bf16[1,1,1,1,1,1,384]{6,5,4,3,2,1,0:T(2,128)(2,1)S(1)}, u32[]{:S(2)}, u32[]{:S(2)}) collective-permute-start(bf16[1,1,1,1,1,1,384]{6,5,4,3,2,1,0:T(2,128)(2,1)S(1)} %reshape_broadcast_in_dim.4), channel_id=1, source_target_pairs={{0,16},{1,17},{2,18},{3,19},{4,20},{5,21},{6,22},{7,23},{8,24},{9,... | collective-permute-start | bytes 2312 | tf_op jit(solution)/shard_map/ppermute | solution.py:430
  9.5 11.4 %collective-permute-start = (bf16[1,1,1,1,1,32,1536]{6,5,4,3,2,1,0:T(8,128)(2,1)S(1)}, bf16[1,1,1,1,1,32,1536]{6,5,4,3,2,1,0:T(8,128)(2,1)S(1)}, u32[]{:S(2)}, u32[]{:S(2)}) collective-permute-start(bf16[1,1,1,1,1,32,1536]{6,5,4,3,2,1,0:T(8,128)(2,1)S(1)} %get-tuple-element.208), channel_id=1, source_target_pairs={{0,16},{1,17},{2,18},{3,19},{4,20},{5,21},{6,22},{7,23},{8,24},{9,... | collective-permute-start | bytes 294920 | tf_op jit(solution)/shard_map/ppermute | solution.py:430
  21.1 12.9 %collective-permute-start.8 = (bf16[2,1,1,1,1,32,1536]{6,5,0,4,3,2,1:T(8,128)(2,1)S(1)}, bf16[2,1,1,1,1,32,1536]{6,5,0,4,3,2,1:T(8,128)(2,1)S(1)}, u32[]{:S(2)}, u32[]{:S(2)}) collective-permute-start(bf16[2,1,1,1,1,32,1536]{6,5,0,4,3,2,1:T(8,128)(2,1)S(1)} %get-tuple-element.231), channel_id=1, source_target_pairs={{0,8},{1,9},{2,10},{3,11},{4,12},{5,13},{6,14},{7,15},{8,0},{9,1},... | collective-permute-start | bytes 589832 | tf_op jit(solution)/shard_map/ppermute | solution.py:430
  21.2 15.1 %collective-permute-start.1 = (bf16[2,1,1,1,1,32,1536]{6,5,0,4,3,2,1:T(8,128)(2,1)S(1)}, bf16[2,1,1,1,1,32,1536]{6,5,0,4,3,2,1:T(8,128)(2,1)S(1)}, u32[]{:S(2)}, u32[]{:S(2)}) collective-permute-start(bf16[2,1,1,1,1,32,1536]{6,5,0,4,3,2,1:T(8,128)(2,1)S(1)} %get-tuple-element.232), channel_id=1, source_target_pairs={{0,8},{1,9},{2,10},{3,11},{4,12},{5,13},{6,14},{7,15},{8,0},{9,1},... | collective-permute-start | bytes 589832 | tf_op jit(solution)/shard_map/ppermute | solution.py:430
  23.3 16.3 %collective-permute-start.7 = (bf16[2,1,1,1,1,1,384]{6,0,5,4,3,2,1:T(2,128)(2,1)S(1)}, bf16[2,1,1,1,1,1,384]{6,0,5,4,3,2,1:T(2,128)(2,1)S(1)}, u32[]{:S(2)}, u32[]{:S(2)}) collective-permute-start(bf16[2,1,1,1,1,1,384]{6,0,5,4,3,2,1:T(2,128)(2,1)S(1)} %broadcast_select_fusion.43), channel_id=1, source_target_pairs={{0,8},{1,9},{2,10},{3,11},{4,12},{5,13},{6,14},{7,15},{8,0},{9,1},... | collective-permute-start | bytes 4616 | tf_op jit(solution)/shard_map/ppermute | solution.py:430
  23.4 14.7 %collective-permute-start.14 = (bf16[1,1,1,1,1,32,1152]{6,5,4,3,2,1,0:T(8,128)(2,1)S(1)}, bf16[1,1,1,1,1,32,1152]{6,5,4,3,2,1,0:T(8,128)(2,1)S(1)}, u32[]{:S(2)}, u32[]{:S(2)}) collective-permute-start(bf16[1,1,1,1,1,32,1152]{6,5,4,3,2,1,0:T(8,128)(2,1)S(1)} %maximum_bitcast_fusion), channel_id=1, source_target_pairs={{0,16},{1,17},{2,18},{3,19},{4,20},{5,21},{6,22},{7,23},{8,24},{9,... | collective-permute-start | bytes 221192 | tf_op jit(solution)/shard_map/ppermute | solution.py:430
  25.1 22.9 %collective-permute-start.20 = (bf16[1,1,1,1,1,32,4096]{6,5,4,3,2,1,0:T(8,128)(2,1)S(1)}, bf16[1,1,1,1,1,32,4096]{6,5,4,3,2,1,0:T(8,128)(2,1)S(1)}, u32[]{:S(2)}, u32[]{:S(2)}) collective-permute-start(bf16[1,1,1,1,1,32,4096]{6,5,4,3,2,1,0:T(8,128)(2,1)S(1)} %bitcast.248), channel_id=1, source_target_pairs={{0,16},{1,17},{2,18},{3,19},{4,20},{5,21},{6,22},{7,23},{8,24},{9,... | collective-permute-start | bytes 786440 | tf_op jit(solution)/shard_map/ppermute | solution.py:430
  34.1 18.4 %collective-permute-start.24 = (bf16[1,1,1,1,1,128,1024]{6,5,4,3,2,1,0:T(8,128)(2,1)S(1)}, bf16[1,1,1,1,1,128,1024]{6,5,4,3,2,1,0:T(8,128)(2,1)S(1)}, u32[]{:S(2)}, u32[]{:S(2)}) collective-permute-start(bf16[1,1,1,1,1,128,1024]{6,5,4,3,2,1,0:T(8,128)(2,1)S(1)} %bitcast.249), channel_id=1, source_target_pairs={{0,16},{1,17},{2,18},{3,19},{4,20},{5,21},{6,22},{7,23},{8,24},{9,... | collective-permute-start | bytes 786440 | tf_op jit(solution)/shard_map/ppermute | solution.py:430
  36.5 18.5 %collective-permute-start.10 = (bf16[2,2,1,1,1,32,1536]{6,5,1,0,4,3,2:T(8,128)(2,1)S(1)}, bf16[2,2,1,1,1,32,1536]{6,5,1,0,4,3,2:T(8,128)(2,1)S(1)}, u32[]{:S(2)}, u32[]{:S(2)}) collective-permute-start(bf16[2,2,1,1,1,32,1536]{6,5,1,0,4,3,2:T(8,128)(2,1)S(1)} %get-tuple-element.227), channel_id=1, source_target_pairs={{0,4},{1,5},{2,6},{3,7},{4,0},{5,1},{6,2},{7,3},{8,12},{9,13},{10,... | collective-permute-start | bytes 1179656 | tf_op jit(solution)/shard_map/ppermute | solution.py:430
  38.1 14.6 %collective-permute-start.2 = (bf16[2,2,1,1,1,32,1536]{6,5,1,0,4,3,2:T(8,128)(2,1)S(1)}, bf16[2,2,1,1,1,32,1536]{6,5,1,0,4,3,2:T(8,128)(2,1)S(1)}, u32[]{:S(2)}, u32[]{:S(2)}) collective-permute-start(bf16[2,2,1,1,1,32,1536]{6,5,1,0,4,3,2:T(8,128)(2,1)S(1)} %get-tuple-element.228), channel_id=1, source_target_pairs={{0,2},{1,3},{2,0},{3,1},{4,6},{5,7},{6,4},{7,5},{8,10},{9,11},{10,... | collective-permute-start | bytes 1179656 | tf_op jit(solution)/shard_map/ppermute | solution.py:430
  39.7 18.5 %collective-permute-start.9 = (bf16[2,2,1,1,1,1,384]{6,1,0,5,4,3,2:T(2,128)(2,1)S(1)}, bf16[2,2,1,1,1,1,384]{6,1,0,5,4,3,2:T(2,128)(2,1)S(1)}, u32[]{:S(2)}, u32[]{:S(2)}) collective-permute-start(bf16[2,2,1,1,1,1,384]{6,1,0,5,4,3,2:T(2,128)(2,1)S(1)} %broadcast_select_fusion.42), channel_id=1, source_target_pairs={{0,2},{1,3},{2,0},{3,1},{4,6},{5,7},{6,4},{7,5},{8,10},{9,11},{10,... | collective-permute-start | bytes 9224 | tf_op jit(solution)/shard_map/ppermute | solution.py:430
  52.6 14.9 %collective-permute-start.25 = (bf16[2,1,1,1,1,128,1024]{6,5,0,4,3,2,1:T(8,128)(2,1)S(1)}, bf16[2,1,1,1,1,128,1024]{6,5,0,4,3,2,1:T(8,128)(2,1)S(1)}, u32[]{:S(2)}, u32[]{:S(2)}) collective-permute-start(bf16[2,1,1,1,1,128,1024]{6,5,0,4,3,2,1:T(8,128)(2,1)S(1)} %broadcast_select_fusion.19), channel_id=1, source_target_pairs={{0,8},{1,9},{2,10},{3,11},{4,12},{5,13},{6,14},{7,15},{8,0},{9,1},... | collective-permute-start | bytes 1572872 | tf_op jit(solution)/shard_map/ppermute | solution.py:430
  52.7 25.3 %collective-permute-start.21 = (bf16[2,1,1,1,1,32,4096]{6,5,0,4,3,2,1:T(8,128)(2,1)S(1)}, bf16[2,1,1,1,1,32,4096]{6,5,0,4,3,2,1:T(8,128)(2,1)S(1)}, u32[]{:S(2)}, u32[]{:S(2)}) collective-permute-start(bf16[2,1,1,1,1,32,4096]{6,5,0,4,3,2,1:T(8,128)(2,1)S(1)} %broadcast_select_fusion.20), channel_id=1, source_target_pairs={{0,8},{1,9},{2,10},{3,11},{4,12},{5,13},{6,14},{7,15},{8,0},{9,1},... | collective-permute-start | bytes 1572872 | tf_op jit(solution)/shard_map/ppermute | solution.py:430
  55.3 28.5 %collective-permute-start.12 = (bf16[2,2,2,1,1,32,1536]{6,5,2,1,0,4,3:T(8,128)(2,1)S(1)}, bf16[2,2,2,1,1,32,1536]{6,5,2,1,0,4,3:T(8,128)(2,1)S(1)}, u32[]{:S(2)}, u32[]{:S(2)}) collective-permute-start(bf16[2,2,2,1,1,32,1536]{6,5,2,1,0,4,3:T(8,128)(2,1)S(1)} %broadcast_select_fusion.15), channel_id=1, source_target_pairs={{0,2},{1,3},{2,0},{3,1},{4,6},{5,7},{6,4},{7,5},{8,10},{9,11},{10,... | collective-permute-start | bytes 2359304 | tf_op jit(solution)/shard_map/ppermute | solution.py:430
  56.6 22.9 %collective-permute-start.3 = (bf16[2,2,1,2,1,32,1536]{6,5,3,1,0,4,2:T(8,128)(2,1)S(1)}, bf16[2,2,1,2,1,32,1536]{6,5,3,1,0,4,2:T(8,128)(2,1)S(1)}, u32[]{:S(2)}, u32[]{:S(2)}) collective-permute-start(bf16[2,2,1,2,1,32,1536]{6,5,3,1,0,4,2:T(8,128)(2,1)S(1)} %broadcast_select_fusion.16), channel_id=1, source_target_pairs={{0,4},{1,5},{2,6},{3,7},{4,0},{5,1},{6,2},{7,3},{8,12},{9,13},{10,... | collective-permute-start | bytes 2359304 | tf_op jit(solution)/shard_map/ppermute | solution.py:430
  58.3 28.7 %collective-permute-start.11 = (bf16[2,2,1,2,1,1,384]{6,3,1,0,5,4,2:T(2,128)(2,1)S(1)}, bf16[2,2,1,2,1,1,384]{6,3,1,0,5,4,2:T(2,128)(2,1)S(1)}, u32[]{:S(2)}, u32[]{:S(2)}) collective-permute-start(bf16[2,2,1,2,1,1,384]{6,3,1,0,5,4,2:T(2,128)(2,1)S(1)} %broadcast_select_fusion.41), channel_id=1, source_target_pairs={{0,4},{1,5},{2,6},{3,7},{4,0},{5,1},{6,2},{7,3},{8,12},{9,13},{10,... | collective-permute-start | bytes 18440 | tf_op jit(solution)/shard_map/ppermute | solution.py:430
  67.5 19.0 %collective-permute-start.16 = (bf16[2,2,1,1,1,32,1152]{6,5,1,0,4,3,2:T(8,128)(2,1)S(1)}, bf16[2,2,1,1,1,32,1152]{6,5,1,0,4,3,2:T(8,128)(2,1)S(1)}, u32[]{:S(2)}, u32[]{:S(2)}) collective-permute-start(bf16[2,2,1,1,1,32,1152]{6,5,1,0,4,3,2:T(8,128)(2,1)S(1)} %broadcast_select_fusion.25), channel_id=1, source_target_pairs={{0,2},{1,3},{2,0},{3,1},{4,6},{5,7},{6,4},{7,5},{8,10},{9,11},{10,... | collective-permute-start | bytes 884744 | tf_op jit(solution)/shard_map/ppermute | solution.py:430
  78.2 34.5 %collective-permute-start.22 = (bf16[2,2,1,1,1,32,4096]{6,5,1,0,4,3,2:T(8,128)(2,1)S(1)}, bf16[2,2,1,1,1,32,4096]{6,5,1,0,4,3,2:T(8,128)(2,1)}, u32[]{:S(2)}, u32[]{:S(2)}) collective-permute-start(bf16[2,2,1,1,1,32,4096]{6,5,1,0,4,3,2:T(8,128)(2,1)S(1)} %broadcast_select_fusion.13), channel_id=1, source_target_pairs={{0,2},{1,3},{2,0},{3,1},{4,6},{5,7},{6,4},{7,5},{8,10},{9,11},{10,... | collective-permute-start | bytes 3145736 | tf_op jit(solution)/shard_map/ppermute | solution.py:430
  79.5 31.4 %collective-permute-start.26 = (bf16[2,2,1,1,1,128,1024]{6,5,1,0,4,3,2:T(8,128)(2,1)S(1)}, bf16[2,2,1,1,1,128,1024]{6,5,1,0,4,3,2:T(8,128)(2,1)}, u32[]{:S(2)}, u32[]{:S(2)}) collective-permute-start(bf16[2,2,1,1,1,128,1024]{6,5,1,0,4,3,2:T(8,128)(2,1)S(1)} %broadcast_select_fusion.12), channel_id=1, source_target_pairs={{0,4},{1,5},{2,6},{3,7},{4,0},{5,1},{6,2},{7,3},{8,12},{9,13},{10,... | collective-permute-start | bytes 3145736 | tf_op jit(solution)/shard_map/ppermute | solution.py:430
  86.5 29.9 %collective-permute-start.19 = (bf16[2,2,2,2,1,32,1536]{6,5,3,2,1,0,4:T(8,128)(2,1)}, bf16[2,2,2,2,1,32,1536]{6,5,3,2,1,0,4:T(8,128)(2,1)}, u32[]{:S(2)}, u32[]{:S(2)}) collective-permute-start(bf16[2,2,2,2,1,32,1536]{6,5,3,2,1,0,4:T(8,128)(2,1)} %broadcast_select_fusion.7), channel_id=1, source_target_pairs={{0,1},{1,0},{2,3},{3,2},{4,5},{5,4},{6,7},{7,6},{8,9},{9,8},{10,11... | collective-permute-start | bytes 4718600 | tf_op jit(solution)/shard_map/ppermute | solution.py:430
  86.5 29.8 %collective-permute-start.4 = (bf16[2,2,2,2,1,32,1536]{6,5,3,2,1,0,4:T(8,128)(2,1)}, bf16[2,2,2,2,1,32,1536]{6,5,3,2,1,0,4:T(8,128)(2,1)}, u32[]{:S(2)}, u32[]{:S(2)}) collective-permute-start(bf16[2,2,2,2,1,32,1536]{6,5,3,2,1,0,4:T(8,128)(2,1)} %broadcast_select_fusion.8), channel_id=1, source_target_pairs={{0,1},{1,0},{2,3},{3,2},{4,5},{5,4},{6,7},{7,6},{8,9},{9,8},{10,11... | collective-permute-start | bytes 4718600 | tf_op jit(solution)/shard_map/ppermute | solution.py:430
  92.5 83.7 %collective-permute-start.17 = (bf16[2,2,1,2,1,32,1152]{6,5,3,1,0,4,2:T(8,128)(2,1)S(1)}, bf16[2,2,1,2,1,32,1152]{6,5,3,1,0,4,2:T(8,128)(2,1)}, u32[]{:S(2)}, u32[]{:S(2)}) collective-permute-start(bf16[2,2,1,2,1,32,1152]{6,5,3,1,0,4,2:T(8,128)(2,1)S(1)} %broadcast_select_fusion.18), channel_id=1, source_target_pairs={{0,4},{1,5},{2,6},{3,7},{4,0},{5,1},{6,2},{7,3},{8,12},{9,13},{10,... | collective-permute-start | bytes 1769480 | tf_op jit(solution)/shard_map/ppermute | solution.py:430
  114.2 63.7 %collective-permute-start.23 = (bf16[2,2,1,2,1,32,4096]{6,5,3,1,0,4,2:T(8,128)(2,1)S(1)}, bf16[2,2,1,2,1,32,4096]{6,5,3,1,0,4,2:T(8,128)(2,1)S(1)}, u32[]{:S(2)}, u32[]{:S(2)}) collective-permute-start(bf16[2,2,1,2,1,32,4096]{6,5,3,1,0,4,2:T(8,128)(2,1)S(1)} %broadcast_select_fusion.5), channel_id=1, source_target_pairs={{0,4},{1,5},{2,6},{3,7},{4,0},{5,1},{6,2},{7,3},{8,12},{9,13},{10,... | collective-permute-start | bytes 6291464 | tf_op jit(solution)/shard_map/ppermute | solution.py:430
  115.8 66.4 %collective-permute-start.27 = (bf16[2,2,2,1,1,128,1024]{6,5,2,1,0,4,3:T(8,128)(2,1)S(1)}, bf16[2,2,2,1,1,128,1024]{6,5,2,1,0,4,3:T(8,128)(2,1)S(1)}, u32[]{:S(2)}, u32[]{:S(2)}) collective-permute-start(bf16[2,2,2,1,1,128,1024]{6,5,2,1,0,4,3:T(8,128)(2,1)S(1)} %broadcast_select_fusion.4), channel_id=1, source_target_pairs={{0,2},{1,3},{2,0},{3,1},{4,6},{5,7},{6,4},{7,5},{8,10},{9,11},{10,... | collective-permute-start | bytes 6291464 | tf_op jit(solution)/shard_map/ppermute | solution.py:430
  180.4 12.8 %collective-permute-start.28 = (bf16[2,2,2,2,1,32,4096]{6,5,4,3,2,1,0:T(8,128)(2,1)}, bf16[2,2,2,2,1,32,4096]{6,5,4,3,2,1,0:T(8,128)(2,1)}, u32[]{:S(2)}, u32[]{:S(2)}) collective-permute-start(bf16[2,2,2,2,1,32,4096]{6,5,4,3,2,1,0:T(8,128)(2,1)} %broadcast_select_fusion.3), channel_id=1, source_target_pairs={{0,1},{1,0},{2,3},{3,2},{4,5},{5,4},{6,7},{7,6},{8,9},{9,8},{10,11... | collective-permute-start | bytes 12582920 | tf_op jit(solution)/shard_map/ppermute | solution.py:430
  186.8 34.7 %collective-permute-start.29 = (bf16[2,2,2,2,1,128,1024]{6,5,4,3,2,1,0:T(8,128)(2,1)}, bf16[2,2,2,2,1,128,1024]{6,5,4,3,2,1,0:T(8,128)(2,1)}, u32[]{:S(2)}, u32[]{:S(2)}) collective-permute-start(bf16[2,2,2,2,1,128,1024]{6,5,4,3,2,1,0:T(8,128)(2,1)} %broadcast_select_fusion.2), channel_id=1, source_target_pairs={{0,1},{1,0},{2,3},{3,2},{4,5},{5,4},{6,7},{7,6},{8,9},{9,8},{10,11... | collective-permute-start | bytes 12582920 | tf_op jit(solution)/shard_map/ppermute | solution.py:430
  347.3 36.8 %collective-permute-start.45 = (bf16[2,2,2,2,1,128,1024]{6,5,4,3,2,1,0:T(8,128)(2,1)}, bf16[2,2,2,2,1,128,1024]{6,5,4,3,2,1,0:T(8,128)(2,1)}, u32[]{:S(2)}, u32[]{:S(2)}) collective-permute-start(bf16[2,2,2,2,1,128,1024]{6,5,4,3,2,1,0:T(8,128)(2,1)} %constant_dynamic-slice_fusion.37), channel_id=1, source_target_pairs={{0,1},{1,0},{2,3},{3,2},{4,5},{5,4},{6,7},{7,6},{8,9},{9,8},{10,11... | collective-permute-start | bytes 12582920 | tf_op jit(solution)/shard_map/ppermute | solution.py:430
  382.7 35.4 %collective-permute-start.46 = (bf16[2,2,2,2,1,32,4096]{6,5,4,3,2,1,0:T(8,128)(2,1)}, bf16[2,2,2,2,1,32,4096]{6,5,4,3,2,1,0:T(8,128)(2,1)}, u32[]{:S(2)}, u32[]{:S(2)}) collective-permute-start(bf16[2,2,2,2,1,32,4096]{6,5,4,3,2,1,0:T(8,128)(2,1)} %constant_dynamic-slice_fusion.36), channel_id=1, source_target_pairs={{0,1},{1,0},{2,3},{3,2},{4,5},{5,4},{6,7},{7,6},{8,9},{9,8},{10,11... | collective-permute-start | bytes 12582920 | tf_op jit(solution)/shard_map/ppermute | solution.py:430
  393.7 47.9 %collective-permute-start.47 = (bf16[2,2,2,1,1,128,1024]{6,5,4,3,2,1,0:T(8,128)(2,1)}, bf16[2,2,2,1,1,128,1024]{6,5,4,3,2,1,0:T(8,128)(2,1)}, u32[]{:S(2)}, u32[]{:S(2)}) collective-permute-start(bf16[2,2,2,1,1,128,1024]{6,5,4,3,2,1,0:T(8,128)(2,1)} %constant_dynamic-slice_fusion.35), channel_id=1, source_target_pairs={{0,2},{1,3},{2,0},{3,1},{4,6},{5,7},{6,4},{7,5},{8,10},{9,11},{10,... | collective-permute-start | bytes 6291464 | tf_op jit(solution)/shard_map/ppermute | solution.py:430
  425.4 56.4 %collective-permute-start.49 = (bf16[2,2,1,2,1,32,4096]{6,5,4,3,2,1,0:T(8,128)(2,1)}, bf16[2,2,1,2,1,32,4096]{6,5,4,3,2,1,0:T(8,128)(2,1)}, u32[]{:S(2)}, u32[]{:S(2)}) collective-permute-start(bf16[2,2,1,2,1,32,4096]{6,5,4,3,2,1,0:T(8,128)(2,1)} %constant_dynamic-slice_fusion.34), channel_id=1, source_target_pairs={{0,4},{1,5},{2,6},{3,7},{4,0},{5,1},{6,2},{7,3},{8,12},{9,13},{10,... | collective-permute-start | bytes 6291464 | tf_op jit(solution)/shard_map/ppermute | solution.py:430
  437.0 49.7 %collective-permute-start.48 = (bf16[2,2,2,2,1,32,1152]{6,5,4,3,2,1,0:T(8,128)(2,1)}, bf16[2,2,2,2,1,32,1152]{6,5,4,3,2,1,0:T(8,128)(2,1)}, u32[]{:S(2)}, u32[]{:S(2)}) collective-permute-start(bf16[2,2,2,2,1,32,1152]{6,5,4,3,2,1,0:T(8,128)(2,1)} %constant_dynamic-slice_fusion.33), channel_id=1, source_target_pairs={{0,1},{1,0},{2,3},{3,2},{4,5},{5,4},{6,7},{7,6},{8,9},{9,8},{10,11... | collective-permute-start | bytes 3538952 | tf_op jit(solution)/shard_map/ppermute | solution.py:430
  445.2 83.8 %collective-permute-start.51 = (bf16[2,2,1,1,1,128,1024]{6,5,4,3,2,1,0:T(8,128)(2,1)}, bf16[2,2,1,1,1,128,1024]{6,5,4,3,2,1,0:T(8,128)(2,1)}, u32[]{:S(2)}, u32[]{:S(2)}) collective-permute-start(bf16[2,2,1,1,1,128,1024]{6,5,4,3,2,1,0:T(8,128)(2,1)} %constant_dynamic-slice_fusion.32), channel_id=1, source_target_pairs={{0,4},{1,5},{2,6},{3,7},{4,0},{5,1},{6,2},{7,3},{8,12},{9,13},{10,... | collective-permute-start | bytes 3145736 | tf_op jit(solution)/shard_map/ppermute | solution.py:430
  490.0 66.9 %collective-permute-start.67 = (bf16[2,2,1,2,1,32,1152]{6,5,4,3,2,1,0:T(8,128)(2,1)}, bf16[2,2,1,2,1,32,1152]{6,5,4,3,2,1,0:T(8,128)(2,1)}, u32[]{:S(2)}, u32[]{:S(2)}) collective-permute-start(bf16[2,2,1,2,1,32,1152]{6,5,4,3,2,1,0:T(8,128)(2,1)} %constant_dynamic-slice_fusion.30), channel_id=1, source_target_pairs={{0,4},{1,5},{2,6},{3,7},{4,0},{5,1},{6,2},{7,3},{8,12},{9,13},{10,... | collective-permute-start | bytes 1769480 | tf_op jit(solution)/shard_map/ppermute | solution.py:430
  492.3 39.3 %collective-permute-start.50 = (bf16[2,2,1,1,1,32,4096]{6,5,4,3,2,1,0:T(8,128)(2,1)}, bf16[2,2,1,1,1,32,4096]{6,5,4,3,2,1,0:T(8,128)(2,1)}, u32[]{:S(2)}, u32[]{:S(2)}) collective-permute-start(bf16[2,2,1,1,1,32,4096]{6,5,4,3,2,1,0:T(8,128)(2,1)} %constant_dynamic-slice_fusion.29), channel_id=1, source_target_pairs={{0,2},{1,3},{2,0},{3,1},{4,6},{5,7},{6,4},{7,5},{8,10},{9,11},{10,... | collective-permute-start | bytes 3145736 | tf_op jit(solution)/shard_map/ppermute | solution.py:430
  493.8 42.2 %collective-permute-start.52 = (bf16[2,2,2,2,1,32,1536]{6,5,4,3,2,1,0:T(8,128)(2,1)}, bf16[2,2,2,2,1,32,1536]{6,5,4,3,2,1,0:T(8,128)(2,1)S(1)}, u32[]{:S(2)}, u32[]{:S(2)}) collective-permute-start(bf16[2,2,2,2,1,32,1536]{6,5,4,3,2,1,0:T(8,128)(2,1)} %constant_dynamic-slice_fusion.31), channel_id=1, source_target_pairs={{0,1},{1,0},{2,3},{3,2},{4,5},{5,4},{6,7},{7,6},{8,9},{9,8},{10,11... | collective-permute-start | bytes 4718600 | tf_op jit(solution)/shard_map/ppermute | solution.py:430
  531.6 36.2 %collective-permute-start.73 = (bf16[2,1,1,1,1,128,1024]{6,5,4,3,2,1,0:T(8,128)(2,1)}, bf16[2,1,1,1,1,128,1024]{6,5,4,3,2,1,0:T(8,128)(2,1)}, u32[]{:S(2)}, u32[]{:S(2)}) collective-permute-start(bf16[2,1,1,1,1,128,1024]{6,5,4,3,2,1,0:T(8,128)(2,1)} %constant_dynamic-slice_fusion.27), channel_id=1, source_target_pairs={{0,8},{1,9},{2,10},{3,11},{4,12},{5,13},{6,14},{7,15},{8,0},{9,1},... | collective-permute-start | bytes 1572872 | tf_op jit(solution)/shard_map/ppermute | solution.py:430
  534.7 21.1 %collective-permute-start.71 = (bf16[2,1,1,1,1,32,4096]{6,5,4,3,2,1,0:T(8,128)(2,1)}, bf16[2,1,1,1,1,32,4096]{6,5,4,3,2,1,0:T(8,128)(2,1)}, u32[]{:S(2)}, u32[]{:S(2)}) collective-permute-start(bf16[2,1,1,1,1,32,4096]{6,5,4,3,2,1,0:T(8,128)(2,1)} %constant_dynamic-slice_fusion.28), channel_id=1, source_target_pairs={{0,8},{1,9},{2,10},{3,11},{4,12},{5,13},{6,14},{7,15},{8,0},{9,1},... | collective-permute-start | bytes 1572872 | tf_op jit(solution)/shard_map/ppermute | solution.py:430
  538.7 33.4 %collective-permute-start.53 = (bf16[2,2,1,2,1,32,1536]{6,5,4,3,2,1,0:T(8,128)(2,1)}, bf16[2,2,1,2,1,32,1536]{6,5,4,3,2,1,0:T(8,128)(2,1)}, u32[]{:S(2)}, u32[]{:S(2)}) collective-permute-start(bf16[2,2,1,2,1,32,1536]{6,5,4,3,2,1,0:T(8,128)(2,1)} %constant_dynamic-slice_fusion.26), channel_id=1, source_target_pairs={{0,4},{1,5},{2,6},{3,7},{4,0},{5,1},{6,2},{7,3},{8,12},{9,13},{10,... | collective-permute-start | bytes 2359304 | tf_op jit(solution)/shard_map/ppermute | solution.py:430
  548.1 24.1 %collective-permute-start.56 = (bf16[2,2,2,2,1,32,768]{6,5,4,3,2,1,0:T(8,128)(2,1)S(1)}, bf16[2,2,2,2,1,32,768]{6,5,4,3,2,1,0:T(8,128)(2,1)S(1)}, u32[]{:S(2)}, u32[]{:S(2)}) collective-permute-start(bf16[2,2,2,2,1,32,768]{6,5,4,3,2,1,0:T(8,128)(2,1)S(1)} %constant_dynamic-slice_fusion.24), channel_id=1, source_target_pairs={{0,1},{1,0},{2,3},{3,2},{4,5},{5,4},{6,7},{7,6},{8,9},{9,8},{10,11... | collective-permute-start | bytes 2359304 | tf_op jit(solution)/shard_map/ppermute | solution.py:430
  555.8 19.7 %collective-permute-start.55 = (bf16[2,2,2,2,1,32,768]{6,5,4,3,2,1,0:T(8,128)(2,1)S(1)}, bf16[2,2,2,2,1,32,768]{6,5,4,3,2,1,0:T(8,128)(2,1)S(1)}, u32[]{:S(2)}, u32[]{:S(2)}) collective-permute-start(bf16[2,2,2,2,1,32,768]{6,5,4,3,2,1,0:T(8,128)(2,1)S(1)} %constant_dynamic-slice_fusion.25), channel_id=1, source_target_pairs={{0,1},{1,0},{2,3},{3,2},{4,5},{5,4},{6,7},{7,6},{8,9},{9,8},{10,11... | collective-permute-start | bytes 2359304 | tf_op jit(solution)/shard_map/ppermute | solution.py:430
  569.0 31.1 %collective-permute-start.74 = (bf16[1,1,1,1,1,128,1024]{6,5,4,3,2,1,0:T(8,128)(2,1)S(1)}, bf16[1,1,1,1,1,128,1024]{6,5,4,3,2,1,0:T(8,128)(2,1)S(1)}, u32[]{:S(2)}, u32[]{:S(2)}) collective-permute-start(bf16[1,1,1,1,1,128,1024]{6,5,4,3,2,1,0:T(8,128)(2,1)S(1)} %constant_dynamic-slice_fusion.8), channel_id=1, source_target_pairs={{0,16},{1,17},{2,18},{3,19},{4,20},{5,21},{6,22},{7,23},{8,24},{9,... | collective-permute-start | bytes 786440 | tf_op jit(solution)/shard_map/ppermute | solution.py:430
  571.3 23.9 %collective-permute-start.72 = (bf16[1,1,1,1,1,32,4096]{6,5,4,3,2,1,0:T(8,128)(2,1)S(1)}, bf16[1,1,1,1,1,32,4096]{6,5,4,3,2,1,0:T(8,128)(2,1)S(1)}, u32[]{:S(2)}, u32[]{:S(2)}) collective-permute-start(bf16[1,1,1,1,1,32,4096]{6,5,4,3,2,1,0:T(8,128)(2,1)S(1)} %constant_dynamic-slice_fusion.9), channel_id=1, source_target_pairs={{0,16},{1,17},{2,18},{3,19},{4,20},{5,21},{6,22},{7,23},{8,24},{9,... | collective-permute-start | bytes 786440 | tf_op jit(solution)/shard_map/ppermute | solution.py:430
  572.1 28.1 %collective-permute-start.68 = (bf16[2,2,1,1,1,32,1152]{6,5,4,3,2,1,0:T(8,128)(2,1)S(1)}, bf16[2,2,1,1,1,32,1152]{6,5,4,3,2,1,0:T(8,128)(2,1)S(1)}, u32[]{:S(2)}, u32[]{:S(2)}) collective-permute-start(bf16[2,2,1,1,1,32,1152]{6,5,4,3,2,1,0:T(8,128)(2,1)S(1)} %constant_dynamic-slice_fusion.12), channel_id=1, source_target_pairs={{0,2},{1,3},{2,0},{3,1},{4,6},{5,7},{6,4},{7,5},{8,10},{9,11},{10,... | collective-permute-start | bytes 884744 | tf_op jit(solution)/shard_map/ppermute | solution.py:430
  572.3 25.1 %collective-permute-start.76 = (f32[2,2,1,2,1,1,384]{6,5,4,3,2,1,0:T(1,128)S(1)}, f32[2,2,1,2,1,1,384]{6,5,4,3,2,1,0:T(1,128)S(1)}, u32[]{:S(2)}, u32[]{:S(2)}) collective-permute-start(f32[2,2,1,2,1,1,384]{6,5,4,3,2,1,0:T(1,128)S(1)} %constant_dynamic-slice_fusion.6), channel_id=1, source_target_pairs={{0,4},{1,5},{2,6},{3,7},{4,0},{5,1},{6,2},{7,3},{8,12},{9,13},{10,... | collective-permute-start | bytes 36872 | tf_op jit(solution)/shard_map/ppermute | solution.py:430
  575.5 25.9 %collective-permute-start.59 = (bf16[2,2,2,1,1,32,768]{6,5,4,3,2,1,0:T(8,128)(2,1)S(1)}, bf16[2,2,2,1,1,32,768]{6,5,4,3,2,1,0:T(8,128)(2,1)S(1)}, u32[]{:S(2)}, u32[]{:S(2)}) collective-permute-start(bf16[2,2,2,1,1,32,768]{6,5,4,3,2,1,0:T(8,128)(2,1)S(1)} %constant_dynamic-slice_fusion.21), channel_id=1, source_target_pairs={{0,2},{1,3},{2,0},{3,1},{4,6},{5,7},{6,4},{7,5},{8,10},{9,11},{10,... | collective-permute-start | bytes 1179656 | tf_op jit(solution)/shard_map/ppermute | solution.py:430
  595.1 14.4 %collective-permute-start.58 = (bf16[2,2,1,2,1,32,768]{6,5,4,3,2,1,0:T(8,128)(2,1)S(1)}, bf16[2,2,1,2,1,32,768]{6,5,4,3,2,1,0:T(8,128)(2,1)S(1)}, u32[]{:S(2)}, u32[]{:S(2)}) collective-permute-start(bf16[2,2,1,2,1,32,768]{6,5,4,3,2,1,0:T(8,128)(2,1)S(1)} %constant_dynamic-slice_fusion.22), channel_id=1, source_target_pairs={{0,4},{1,5},{2,6},{3,7},{4,0},{5,1},{6,2},{7,3},{8,12},{9,13},{10,... | collective-permute-start | bytes 1179656 | tf_op jit(solution)/shard_map/ppermute | solution.py:430
  597.4 11.8 %collective-permute-start.54 = (bf16[2,2,1,1,1,32,1536]{6,5,4,3,2,1,0:T(8,128)(2,1)S(1)}, bf16[2,2,1,1,1,32,1536]{6,5,4,3,2,1,0:T(8,128)(2,1)S(1)}, u32[]{:S(2)}, u32[]{:S(2)}) collective-permute-start(bf16[2,2,1,1,1,32,1536]{6,5,4,3,2,1,0:T(8,128)(2,1)S(1)} %constant_dynamic-slice_fusion.23), channel_id=1, source_target_pairs={{0,2},{1,3},{2,0},{3,1},{4,6},{5,7},{6,4},{7,5},{8,10},{9,11},{10,... | collective-permute-start | bytes 1179656 | tf_op jit(solution)/shard_map/ppermute | solution.py:430
  601.5 12.1 %collective-permute-start.62 = (bf16[2,2,1,1,1,32,768]{6,5,4,3,2,1,0:T(8,128)(2,1)S(1)}, bf16[2,2,1,1,1,32,768]{6,5,4,3,2,1,0:T(8,128)(2,1)S(1)}, u32[]{:S(2)}, u32[]{:S(2)}) collective-permute-start(bf16[2,2,1,1,1,32,768]{6,5,4,3,2,1,0:T(8,128)(2,1)S(1)} %constant_dynamic-slice_fusion.18), channel_id=1, source_target_pairs={{0,4},{1,5},{2,6},{3,7},{4,0},{5,1},{6,2},{7,3},{8,12},{9,13},{10,... | collective-permute-start | bytes 589832 | tf_op jit(solution)/shard_map/ppermute | solution.py:430
  (110 other events, 1404.6 us)

commit v5 on v4

--- a/solution.py
+++ b/solution.py
@@ -546,12 +546,12 @@
             one.merge()
         first = (sides[0].held, sides[1].held)
         small_part.merge(*first)
-        if hop > 0 and hop < 4:
-            for one in rest:
+        for one in rest:
+            if hop == 0:
+                one.wait(*first)
+                one.launch()
+            if hop == 2 or hop == 3:
                 one.merge(*first)
-        if hop < 4:
-            for one in rest:
-                one.wait(*first)
                 one.launch()
     small_full = small_part.full().reshape(count, -1)
     full_qkv = [rows_of(one.full()) for one in sides]
@@ -584,6 +584,11 @@
         cut = slice(side * part, (side + 1) * part)
         bias = jnp.concatenate([full_biases[0, cut], zero_row, full_biases[1, cut]])
         qkv.append((matmul_plain(tokens, full_qkv[side]) + bias).astype(bf16))
+    for one in rest:
+        one.merge(*qkv)
+        one.launch()
+    for side in range(2):
+        qkv[side] = after(qkv[side], *[one.before for one in rest])
         context, lse, query_lse = attention_forward(
             qkv[side], segrow, segcol, bounds, row_len, span
         )
@@ -746,7 +751,7 @@
     )
     small_sum = links.shrinking(small_grads[:, None, :], 0, wire=f32)
     small_sum.launch()
-    first, others = qkv_sums[1:], [small_sum, qkv_sums[0], out_sum, up_sum, down_sum]
+    first, others, slow = qkv_sums[1:], [small_sum, qkv_sums[0], out_sum], [up_sum, down_sum]
     last = [one.leaving for one in first]
     for hop in range(links.bits):
         for one in first:
@@ -755,6 +760,11 @@
             one.merge(*last)
         for one in first + others:
             one.launch()
+        last = [one.held for one in first]
+        if hop == 0 or hop == 3:
+            for one in slow:
+                one.merge(*last)
+                one.launch()
         last = [one.leaving for one in first]
     down_shard, up_shard, out_proj_shard = down_sum.mine(), up_sum.mine(), out_sum.mine()
     qkv_shards = [one.mine() for one in qkv_sums]

time: 644 us -> 646 us (level)
  other arithmetic: 91.1 us -> 102 us
    select_n x45 -> x54, other arithmetic: 38.7 us -> 51.1 us  [merge(): self.held = jnp.where(own, held, arrived)]
    unnamed x157 -> x151, local copies, waits for them, and re-layouts: 14.9 us -> 11.8 us
  transfers between devices with their start and end apart: 80 -> 80, of which waited for: 31 -> 34; matrix products, arithmetic and copies ran while one was open for 38% -> 39% of each run, Pallas kernels for 15% -> 15%
where the time goes in v5:
time: 646 us; the launch traced here: 639 us
  matrix products  154 us (24%)
  waiting for transfers between devices  129 us (20%)
  Pallas kernels  122 us (19%)
  other arithmetic  102 us (16%)
  starting transfers between devices  67.5 us (10%)
  local copies, waits for them, and re-layouts  59.5 us (9%)
    ppermute x80, waiting for transfers between devices, swap(): return lax.ppermute(value, AXES, [(d, d ^ bit) for d in range(self.count)])  129 us
    ppermute x80, starting transfers between devices, swap(): return lax.ppermute(value, AXES, [(d, d ^ bit) for d in range(self.count)])  67.5 us
    dot_general x7, matrix products, matmul_right_t(): lax.dot_general(left, right, (((1,), (1,)), ((), ())), preferred_element_...  54.9 us
    pallas_call x2, Pallas kernels, attention_backward(): pl.pallas_call(partial(attend_backward, row_len, qb, kb, lanes, span), ou...  54.7 us
    dot_general x7, matrix products, matmul_plain(): return jnp.dot(left, right, preferred_element_type=jnp.float32)  54.3 us
    select_n x54, other arithmetic, merge(): self.held = jnp.where(own, held, arrived)  51.1 us
    dot_general x7, matrix products, matmul_left_t(): lax.dot_general(left, right, (((0,), (0,)), ((), ())), preferred_element_...  44.8 us
    pallas_call x2, Pallas kernels, attention_forward(): pl.pallas_call(partial(attend_forward, row_len, qb, kb, lanes, span), out...  43.8 us
  transfers between devices with their start and end apart: 80, of which 34 were waited for; matrix products, arithmetic and copies ran while one was open for 39% of the time, Pallas kernels for 15%

profile of v5, /device:TPU:0, one launch (start us, length us, event | category | flops | bytes accessed | tf_op | source)
XLA Modules:
  0.0 639.2 jit_solution(2918708646401224771)
XLA Ops:
  3.0 4.1 collective-permute-start.5
  26.3 7.7 %collective-permute-done.8 = bf16[2,1,1,1,1,32,1536]{6,5,0,4,3,2,1:T(8,128)(2,1)S(1)} collective-permute-done((bf16[2,1,1,1,1,32,1536]{6,5,0,4,3,2,1:T(8,128)(2,1)S(1)}, bf16[2,1,1,1,1,32,1536]{6,5,0,4,3,2,1:T(8,128)(2,1)S(1)}, u32[]{:S(2)}, u32[]{:S(2)}) %collective-permute-start.8) | collective-permute-done | bytes 196640 | tf_op jit(solution)/shard_map/ppermute | solution.py:430
  39.8 7.2 %collective-permute-done.2 = bf16[2,2,1,1,1,32,1536]{6,5,1,0,4,3,2:T(8,128)(2,1)S(1)} collective-permute-done((bf16[2,2,1,1,1,32,1536]{6,5,1,0,4,3,2:T(8,128)(2,1)S(1)}, bf16[2,2,1,1,1,32,1536]{6,5,1,0,4,3,2:T(8,128)(2,1)S(1)}, u32[]{:S(2)}, u32[]{:S(2)}) %collective-permute-start.2) | collective-permute-done | bytes 393248 | tf_op jit(solution)/shard_map/ppermute | solution.py:430
  58.4 13.4 %collective-permute-done.3 = bf16[2,2,1,2,1,32,1536]{6,5,3,1,0,4,2:T(8,128)(2,1)S(1)} collective-permute-done((bf16[2,2,1,2,1,32,1536]{6,5,3,1,0,4,2:T(8,128)(2,1)S(1)}, bf16[2,2,1,2,1,32,1536]{6,5,3,1,0,4,2:T(8,128)(2,1)S(1)}, u32[]{:S(2)}, u32[]{:S(2)}) %collective-permute-start.3) | collective-permute-done | bytes 786464 | tf_op jit(solution)/shard_map/ppermute | solution.py:430
  75.8 7.3 %collective-permute-done.19 = bf16[2,1,1,1,1,32,4096]{6,5,0,4,3,2,1:T(8,128)(2,1)S(1)} collective-permute-done((bf16[2,1,1,1,1,32,4096]{6,5,0,4,3,2,1:T(8,128)(2,1)S(1)}, bf16[2,1,1,1,1,32,4096]{6,5,0,4,3,2,1:T(8,128)(2,1)S(1)}, u32[]{:S(2)}, u32[]{:S(2)}) %collective-permute-start.19) | collective-permute-done | bytes 524320 | tf_op jit(solution)/shard_map/ppermute | solution.py:430
  110.0 3.6 bitcast_select_fusion.2
  113.6 4.0 fusion.7.q_ref.k_ref.v_ref
  117.7 4.0 fusion.6.q_ref.k_ref.v_ref
  134.6 21.8 %shard_map.237 = (bf16[1056,512]{1,0:T(8,128)(2,1)S(1)}, f32[4,4,512]{2,1,0:T(4,128)S(1)}, f32[4,1,64]{2,1,0:T(1,128)S(1)}) custom-call(s32[2,4]{1,0:T(2,128)S(1)} %pad_add_fusion.bounds, s32[4,512]{1,0:T(4,128)S(1)} %constant_dynamic-update-slice_fusion.segrow, s32[1024,1]{1,0:T(8,128)S(1)} %copy.41.segcol, bf16[1056,1536]{1,0:T(8,128)(2,1)S(1)} %fusion.6.q_ref.k_ref.v_ref, ...), custom_call_target="tpu_custom_call" | custom-call | tf_op jit(solution)/shard_map/pallas_call | solution.py:124
  157.8 22.0 %shard_map.238 = (bf16[1056,512]{1,0:T(8,128)(2,1)S(1)}, f32[4,4,512]{2,1,0:T(4,128)S(1)}, f32[4,1,64]{2,1,0:T(1,128)S(1)}) custom-call(s32[2,4]{1,0:T(2,128)S(1)} %pad_add_fusion.bounds, s32[4,512]{1,0:T(4,128)S(1)} %constant_dynamic-update-slice_fusion.segrow, s32[1024,1]{1,0:T(8,128)S(1)} %copy.41.segcol, bf16[1056,1536]{1,0:T(8,128)(2,1)S(1)} %fusion.7.q_ref.k_ref.v_ref, ...), custom_call_target="tpu_custom_call" | custom-call | tf_op jit(solution)/shard_map/pallas_call | solution.py:124
  179.9 3.3 collective-permute-done.26
  183.2 4.1 broadcast_select_fusion.3
  189.1 3.3 fusion.15
  195.4 3.9 fusion.51
  202.9 6.2 bitcast_select_fusion.1
  209.1 20.9 %fusion.4 = (bf16[1056,4096]{1,0:T(8,128)(2,1)}, bf16[1056,4096]{1,0:T(8,128)(2,1)}) fusion(f32[4096]{0:T(1024)S(1)} %fusion.31, bf16[1024,4096]{1,0:T(8,128)(2,1)} %bitcast_select_fusion.1, f32[1056,1024]{1,0:T(8,128)S(1)} %get-tuple-element.220, f32[1024]{0:T(1024)S(1)} %copy-done.63, f32[1024]{0:T(1024)S(1)} %copy-done.59, f32[1056]{0:T(1024)S(1)} %add_rsqrt_fusion.1, ...), kind=kOutput, calls=%fused_computation.7 | convolution fusion | flops 8915681280 | bytes 30048512 | tf_op jit(solution)/shard_map/dot_general | solution.py:27
  230.1 6.2 bitcast_select_fusion
  236.3 16.1 %fusion.52 = (f32[1056]{0:T(1024)S(1)}, f32[1056,1024]{1,0:T(8,128)S(1)}) fusion(f32[1024]{0:T(1024)S(1)} %copy-done.64, bf16[1056,4096]{1,0:T(8,128)(2,1)} %get-tuple-element.112, bf16[4096,1024]{1,0:T(8,128)(2,1)} %bitcast_select_fusion, f32[1024]{0:T(1024)S(1)} %copy-done.63, f32[1024]{0:T(1024)S(1)} %copy-done.59, f32[1056]{0:T(1024)S(1)} %add_rsqrt_fusion.1, ...), kind=kOutput, calls=%fused_computation.311 | convolution fusion | flops 8865938432 | bytes 25715072 | tf_op jit(solution)/shard_map/dot_general | solution.py:27
  256.5 4.4 collective-permute-done.30
  261.4 3.4 collective-permute-done.31
  274.9 9.6 %shard_map.239 = (f32[3,32,8]{2,1,0:T(8,128)S(1)}, f32[3,1024,8]{2,1,0:T(8,128)S(1)}) custom-call(bf16[1024,128]{1,0:T(8,128)(2,1)S(1)} %slice.227.doc_ref, bf16[1024,8]{1,0:T(8,128)(2,1)S(1)} %convert_convert_fusion.member_ref, bf16[1024,128]{1,0:T(8,128)(2,1)S(1)} %bitcast_select_fusion.5.query_ref), custom_call_target="tpu_custom_call" | custom-call | tf_op jit(solution)/shard_map/pallas_call | solution.py:296
  284.7 4.5 collective-permute-done.35
  289.6 3.3 collective-permute-done.36
  302.0 13.8 %shard_map.240 = (f32[1024,128]{1,0:T(8,128)S(1)}, f32[1024,128]{1,0:T(8,128)S(1)}) custom-call(bf16[1024,128]{1,0:T(8,128)(2,1)S(1)} %slice.227.doc_ref, bf16[8,1024]{1,0:T(8,128)(2,1)S(1)} %convert_convert_fusion.1.member_t_ref, bf16[1024,128]{1,0:T(8,128)(2,1)S(1)} %bitcast_select_fusion.5.query_ref, f32[3,1024,8]{2,1,0:T(8,128)S(1)} %get-tuple-element.114.sums_ref, ...), custom_call_target="tpu_custom_call" | custom-call | tf_op jit(solution)/shard_map/pallas_call | solution.py:321
  318.6 4.5 collective-permute-done.41
  324.1 3.4 collective-permute-done.42
  327.9 3.6 collective-permute-done.43
  332.3 4.0 collective-permute-done.44
  336.3 4.1 multiply_reduce_fusion
  343.4 11.8 %convolution_convert_fusion = bf16[4096,1024]{1,0:T(8,128)(2,1)S(1)} fusion(bf16[1056,4096]{1,0:T(8,128)(2,1)S(1)} %bitcast.278, bf16[1056,1024]{1,0:T(8,128)(2,1)S(1)} %get-tuple-element.117), kind=kOutput, calls=%fused_computation.18 | convolution fusion | flops 8862564352 | bytes 19202048 | tf_op jit(solution)/shard_map/dot_general | solution.py:37
  359.9 15.8 %convert_reduce_fusion = (f32[4096]{0:T(1024)S(1)}, bf16[1056,4096]{1,0:T(8,128)(2,1)}) fusion(bf16[1056,4096]{1,0:T(8,128)(2,1)} %get-tuple-element.118, bf16[1056,1024]{1,0:T(8,128)(2,1)S(1)} %get-tuple-element.117, bf16[4096,1024]{1,0:T(8,128)(2,1)} %bitcast_select_fusion), kind=kOutput, calls=%fused_computation.8 | convolution fusion | flops 8879992832 | bytes 27869184 | tf_op jit(solution)/shard_map/dot_general | solution.py:31
  375.7 14.7 %convolution_convert_fusion.1 = bf16[1024,4096]{1,0:T(8,128)(2,1)S(1)} fusion(bf16[1056,4096]{1,0:T(8,128)(2,1)} %get-tuple-element.120, f32[1056,1024]{1,0:T(8,128)S(1)} %bitcast.179, f32[1024]{0:T(1024)S(1)} %copy-done.63, f32[1024]{0:T(1024)S(1)} %copy-done.59, f32[1056]{0:T(1024)S(1)} %add_rsqrt_fusion.1, f32[1056]{0:T(1024)S(1)} %broadcast_multiply_fusion.5), kind=kOutput, calls=%fused_computation.21 | convolution fusion | flops 8867971072 | bytes 21381376 | tf_op jit(solution)/shard_map/dot_general | solution.py:37
  396.6 6.0 add_convert_fusion.1
  407.1 16.8 %multiply_reduce_fusion.1 = (f32[1024]{0:T(1024)S(1)}, f32[1056]{0:T(1024)S(1)}, f32[1056]{0:T(1024)S(1)}, f32[1024]{0:T(1024)S(1)}, f32[1056,1024]{1,0:T(8,128)}) fusion(f32[1056,1024]{1,0:T(8,128)S(1)} %bitcast.179, f32[1056]{0:T(1024)S(1)} %add_rsqrt_fusion.1, f32[1056]{0:T(1024)S(1)} %broadcast_multiply_fusion.5, f32[1024]{0:T(1024)S(1)} %copy-done.59, ...), kind=kOutput, calls=%fused_computation.31 | convolution fusion | flops 8869179392 | bytes 30044672 | tf_op jit(solution)/shard_map/dot_general | solution.py:31
  424.1 5.7 fusion.43
  429.8 5.8 add_convert_fusion
  439.0 3.3 convolution_convert_fusion.7
  458.8 27.5 %shard_map.241 = bf16[1056,1536]{1,0:T(8,128)(2,1)} custom-call(s32[2,4]{1,0:T(2,128)} %copy-done.10, s32[4,512]{1,0:T(4,128)} %copy-done.7, s32[1024,1]{1,0:T(8,128)} %copy-done.2, bf16[1056,1536]{1,0:T(8,128)(2,1)} %copy-done.1, bf16[1056,1536]{1,0:T(8,128)(2,1)} %copy-done.1, bf16[1056,1536]{1,0:T(8,128)(2,1)} %copy-done.1, ...), custom_call_target="tpu_custom_call" | custom-call | tf_op jit(solution)/shard_map/pallas_call | solution.py:201
  486.3 7.0 %convolution_convert_fusion.3 = bf16[1024,1536]{1,0:T(8,128)(2,1)S(1)} fusion(bf16[1056,1536]{1,0:T(8,128)(2,1)} %shard_map.241, bf16[32,1024]{1,0:T(8,128)(2,1)S(1)} %bitcast.250, bf16[1024,1024]{1,0:T(8,128)(2,1)} %bitcast.206), kind=kOutput, calls=%fused_computation.55 | convolution fusion | flops 3327787008 | bytes 8552448 | tf_op jit(solution)/shard_map/dot_general | solution.py:37
  505.7 27.2 %shard_map.242 = bf16[1056,1536]{1,0:T(8,128)(2,1)} custom-call(s32[2,4]{1,0:T(2,128)} %copy-done.10, s32[4,512]{1,0:T(4,128)} %copy-done.7, s32[1024,1]{1,0:T(8,128)} %copy-done.2, bf16[1056,1536]{1,0:T(8,128)(2,1)} %copy-done, bf16[1056,1536]{1,0:T(8,128)(2,1)} %copy-done, bf16[1056,1536]{1,0:T(8,128)(2,1)} %copy-done, ...), custom_call_target="tpu_custom_call" | custom-call | tf_op jit(solution)/shard_map/pallas_call | solution.py:201
  532.9 7.9 %convolution_add_fusion.7 = f32[1056,1024]{1,0:T(8,128)} fusion(f32[1056,1024]{1,0:T(8,128)} %get-tuple-element.181, bf16[1056,1536]{1,0:T(8,128)(2,1)S(1)} %copy-done.22, bf16[1024,1536]{1,0:T(8,128)(2,1)} %copy-done.43), kind=kOutput, calls=%fused_computation.28 | convolution fusion | flops 3322970112 | bytes 15040512 | tf_op jit(solution)/shard_map/dot_general | solution.py:31
  552.3 5.7 convolution_convert_fusion.2
  562.9 5.7 convolution_add_fusion.6
  584.8 5.5 collective-permute-done.54
  591.3 7.1 %collective-permute-done.59 = bf16[2,2,2,1,1,32,768]{6,5,4,3,2,1,0:T(8,128)(2,1)S(1)} collective-permute-done((bf16[2,2,2,1,1,32,768]{6,5,4,3,2,1,0:T(8,128)(2,1)S(1)}, bf16[2,2,2,1,1,32,768]{6,5,4,3,2,1,0:T(8,128)(2,1)S(1)}, u32[]{:S(2)}, u32[]{:S(2)}) %collective-permute-start.59) | collective-permute-done | bytes 393248 | tf_op jit(solution)/shard_map/ppermute | solution.py:430
  601.2 7.8 %collective-permute-done.69 = bf16[2,1,1,1,1,32,1152]{6,5,4,3,2,1,0:T(8,128)(2,1)S(1)} collective-permute-done((bf16[2,1,1,1,1,32,1152]{6,5,4,3,2,1,0:T(8,128)(2,1)S(1)}, bf16[2,1,1,1,1,32,1152]{6,5,4,3,2,1,0:T(8,128)(2,1)S(1)}, u32[]{:S(2)}, u32[]{:S(2)}) %collective-permute-start.69) | collective-permute-done | bytes 147488 | tf_op jit(solution)/shard_map/ppermute | solution.py:430
  611.4 6.0 collective-permute-done.70
  624.4 3.2 collective-permute-done.60
  (543 shorter events, 226.1 us)
Async XLA Ops:
  3.0 20.3 %collective-permute-start.5 = (bf16[1,1,1,1,1,1,384]{6,5,4,3,2,1,0:T(2,128)(2,1)S(1)}, bf16[1,1,1,1,1,1,384]{6,5,4,3,2,1,0:T(2,128)(2,1)S(1)}, u32[]{:S(2)}, u32[]{:S(2)}) collective-permute-start(bf16[1,1,1,1,1,1,384]{6,5,4,3,2,1,0:T(2,128)(2,1)S(1)} %reshape_broadcast_in_dim.4), channel_id=1, source_target_pairs={{0,16},{1,17},{2,18},{3,19},{4,20},{5,21},{6,22},{7,23},{8,24},{9,... | collective-permute-start | bytes 2312 | tf_op jit(solution)/shard_map/ppermute | solution.py:430
  9.5 11.4 %collective-permute-start = (bf16[1,1,1,1,1,32,1536]{6,5,4,3,2,1,0:T(8,128)(2,1)S(1)}, bf16[1,1,1,1,1,32,1536]{6,5,4,3,2,1,0:T(8,128)(2,1)S(1)}, u32[]{:S(2)}, u32[]{:S(2)}) collective-permute-start(bf16[1,1,1,1,1,32,1536]{6,5,4,3,2,1,0:T(8,128)(2,1)S(1)} %get-tuple-element.194), channel_id=1, source_target_pairs={{0,16},{1,17},{2,18},{3,19},{4,20},{5,21},{6,22},{7,23},{8,24},{9,... | collective-permute-start | bytes 294920 | tf_op jit(solution)/shard_map/ppermute | solution.py:430
  21.1 12.9 %collective-permute-start.8 = (bf16[2,1,1,1,1,32,1536]{6,5,0,4,3,2,1:T(8,128)(2,1)S(1)}, bf16[2,1,1,1,1,32,1536]{6,5,0,4,3,2,1:T(8,128)(2,1)S(1)}, u32[]{:S(2)}, u32[]{:S(2)}) collective-permute-start(bf16[2,1,1,1,1,32,1536]{6,5,0,4,3,2,1:T(8,128)(2,1)S(1)} %get-tuple-element.217), channel_id=1, source_target_pairs={{0,8},{1,9},{2,10},{3,11},{4,12},{5,13},{6,14},{7,15},{8,0},{9,1},... | collective-permute-start | bytes 589832 | tf_op jit(solution)/shard_map/ppermute | solution.py:430
  21.2 15.1 %collective-permute-start.1 = (bf16[2,1,1,1,1,32,1536]{6,5,0,4,3,2,1:T(8,128)(2,1)S(1)}, bf16[2,1,1,1,1,32,1536]{6,5,0,4,3,2,1:T(8,128)(2,1)S(1)}, u32[]{:S(2)}, u32[]{:S(2)}) collective-permute-start(bf16[2,1,1,1,1,32,1536]{6,5,0,4,3,2,1:T(8,128)(2,1)S(1)} %get-tuple-element.218), channel_id=1, source_target_pairs={{0,8},{1,9},{2,10},{3,11},{4,12},{5,13},{6,14},{7,15},{8,0},{9,1},... | collective-permute-start | bytes 589832 | tf_op jit(solution)/shard_map/ppermute | solution.py:430
  23.3 14.7 %collective-permute-start.7 = (bf16[2,1,1,1,1,1,384]{6,0,5,4,3,2,1:T(2,128)(2,1)S(1)}, bf16[2,1,1,1,1,1,384]{6,0,5,4,3,2,1:T(2,128)(2,1)S(1)}, u32[]{:S(2)}, u32[]{:S(2)}) collective-permute-start(bf16[2,1,1,1,1,1,384]{6,0,5,4,3,2,1:T(2,128)(2,1)S(1)} %broadcast_select_fusion.52), channel_id=1, source_target_pairs={{0,8},{1,9},{2,10},{3,11},{4,12},{5,13},{6,14},{7,15},{8,0},{9,1},... | collective-permute-start | bytes 4616 | tf_op jit(solution)/shard_map/ppermute | solution.py:430
  23.4 25.6 %collective-permute-start.14 = (bf16[1,1,1,1,1,32,1152]{6,5,4,3,2,1,0:T(8,128)(2,1)S(1)}, bf16[1,1,1,1,1,32,1152]{6,5,4,3,2,1,0:T(8,128)(2,1)S(1)}, u32[]{:S(2)}, u32[]{:S(2)}) collective-permute-start(bf16[1,1,1,1,1,32,1152]{6,5,4,3,2,1,0:T(8,128)(2,1)S(1)} %maximum_bitcast_fusion), channel_id=1, source_target_pairs={{0,16},{1,17},{2,18},{3,19},{4,20},{5,21},{6,22},{7,23},{8,24},{9,... | collective-permute-start | bytes 221192 | tf_op jit(solution)/shard_map/ppermute | solution.py:430
  25.1 30.4 %collective-permute-start.18 = (bf16[1,1,1,1,1,32,4096]{6,5,4,3,2,1,0:T(8,128)(2,1)S(1)}, bf16[1,1,1,1,1,32,4096]{6,5,4,3,2,1,0:T(8,128)(2,1)S(1)}, u32[]{:S(2)}, u32[]{:S(2)}) collective-permute-start(bf16[1,1,1,1,1,32,4096]{6,5,4,3,2,1,0:T(8,128)(2,1)S(1)} %bitcast.218), channel_id=1, source_target_pairs={{0,16},{1,17},{2,18},{3,19},{4,20},{5,21},{6,22},{7,23},{8,24},{9,... | collective-permute-start | bytes 786440 | tf_op jit(solution)/shard_map/ppermute | solution.py:430
  34.1 18.3 %collective-permute-start.21 = (bf16[1,1,1,1,1,128,1024]{6,5,4,3,2,1,0:T(8,128)(2,1)S(1)}, bf16[1,1,1,1,1,128,1024]{6,5,4,3,2,1,0:T(8,128)(2,1)S(1)}, u32[]{:S(2)}, u32[]{:S(2)}) collective-permute-start(bf16[1,1,1,1,1,128,1024]{6,5,4,3,2,1,0:T(8,128)(2,1)S(1)} %bitcast.217), channel_id=1, source_target_pairs={{0,16},{1,17},{2,18},{3,19},{4,20},{5,21},{6,22},{7,23},{8,24},{9,... | collective-permute-start | bytes 786440 | tf_op jit(solution)/shard_map/ppermute | solution.py:430
  36.5 12.2 %collective-permute-start.10 = (bf16[2,2,1,1,1,32,1536]{6,5,1,0,4,3,2:T(8,128)(2,1)S(1)}, bf16[2,2,1,1,1,32,1536]{6,5,1,0,4,3,2:T(8,128)(2,1)S(1)}, u32[]{:S(2)}, u32[]{:S(2)}) collective-permute-start(bf16[2,2,1,1,1,32,1536]{6,5,1,0,4,3,2:T(8,128)(2,1)S(1)} %get-tuple-element.213), channel_id=1, source_target_pairs={{0,4},{1,5},{2,6},{3,7},{4,0},{5,1},{6,2},{7,3},{8,12},{9,13},{10,... | collective-permute-start | bytes 1179656 | tf_op jit(solution)/shard_map/ppermute | solution.py:430
  52.6 21.8 %collective-permute-start.12 = (bf16[2,2,2,1,1,32,1536]{6,5,2,1,0,4,3:T(8,128)(2,1)S(1)}, bf16[2,2,2,1,1,32,1536]{6,5,2,1,0,4,3:T(8,128)(2,1)S(1)}, u32[]{:S(2)}, u32[]{:S(2)}) collective-permute-start(bf16[2,2,2,1,1,32,1536]{6,5,2,1,0,4,3:T(8,128)(2,1)S(1)} %broadcast_select_fusion.19), channel_id=1, source_target_pairs={{0,2},{1,3},{2,0},{3,1},{4,6},{5,7},{6,4},{7,5},{8,10},{9,11},{10,... | collective-permute-start | bytes 2359304 | tf_op jit(solution)/shard_map/ppermute | solution.py:430
  54.0 17.8 %collective-permute-start.3 = (bf16[2,2,1,2,1,32,1536]{6,5,3,1,0,4,2:T(8,128)(2,1)S(1)}, bf16[2,2,1,2,1,32,1536]{6,5,3,1,0,4,2:T(8,128)(2,1)S(1)}, u32[]{:S(2)}, u32[]{:S(2)}) collective-permute-start(bf16[2,2,1,2,1,32,1536]{6,5,3,1,0,4,2:T(8,128)(2,1)S(1)} %broadcast_select_fusion.20), channel_id=1, source_target_pairs={{0,4},{1,5},{2,6},{3,7},{4,0},{5,1},{6,2},{7,3},{8,12},{9,13},{10,... | collective-permute-start | bytes 2359304 | tf_op jit(solution)/shard_map/ppermute | solution.py:430
  55.6 31.5 %collective-permute-start.11 = (bf16[2,2,1,2,1,1,384]{6,3,1,0,5,4,2:T(2,128)(2,1)S(1)}, bf16[2,2,1,2,1,1,384]{6,3,1,0,5,4,2:T(2,128)(2,1)S(1)}, u32[]{:S(2)}, u32[]{:S(2)}) collective-permute-start(bf16[2,2,1,2,1,1,384]{6,3,1,0,5,4,2:T(2,128)(2,1)S(1)} %broadcast_select_fusion.50), channel_id=1, source_target_pairs={{0,4},{1,5},{2,6},{3,7},{4,0},{5,1},{6,2},{7,3},{8,12},{9,13},{10,... | collective-permute-start | bytes 18440 | tf_op jit(solution)/shard_map/ppermute | solution.py:430
  56.1 29.6 %collective-permute-start.15 = (bf16[2,1,1,1,1,32,1152]{6,5,0,4,3,2,1:T(8,128)(2,1)S(1)}, bf16[2,1,1,1,1,32,1152]{6,5,0,4,3,2,1:T(8,128)(2,1)S(1)}, u32[]{:S(2)}, u32[]{:S(2)}) collective-permute-start(bf16[2,1,1,1,1,32,1152]{6,5,0,4,3,2,1:T(8,128)(2,1)S(1)} %broadcast_select_fusion.38), channel_id=1, source_target_pairs={{0,8},{1,9},{2,10},{3,11},{4,12},{5,13},{6,14},{7,15},{8,0},{9,1},... | collective-permute-start | bytes 442376 | tf_op jit(solution)/shard_map/ppermute | solution.py:430
  56.1 31.0 %collective-permute-start.22 = (bf16[2,1,1,1,1,128,1024]{6,5,0,4,3,2,1:T(8,128)(2,1)S(1)}, bf16[2,1,1,1,1,128,1024]{6,5,0,4,3,2,1:T(8,128)(2,1)S(1)}, u32[]{:S(2)}, u32[]{:S(2)}) collective-permute-start(bf16[2,1,1,1,1,128,1024]{6,5,0,4,3,2,1:T(8,128)(2,1)S(1)} %broadcast_select_fusion.24), channel_id=1, source_target_pairs={{0,8},{1,9},{2,10},{3,11},{4,12},{5,13},{6,14},{7,15},{8,0},{9,1},... | collective-permute-start | bytes 1572872 | tf_op jit(solution)/shard_map/ppermute | solution.py:430
  71.8 11.2 %collective-permute-start.19 = (bf16[2,1,1,1,1,32,4096]{6,5,0,4,3,2,1:T(8,128)(2,1)S(1)}, bf16[2,1,1,1,1,32,4096]{6,5,0,4,3,2,1:T(8,128)(2,1)S(1)}, u32[]{:S(2)}, u32[]{:S(2)}) collective-permute-start(bf16[2,1,1,1,1,32,4096]{6,5,0,4,3,2,1:T(8,128)(2,1)S(1)} %broadcast_select_fusion.26), channel_id=1, source_target_pairs={{0,8},{1,9},{2,10},{3,11},{4,12},{5,13},{6,14},{7,15},{8,0},{9,1},... | collective-permute-start | bytes 1572872 | tf_op jit(solution)/shard_map/ppermute | solution.py:430
  86.6 23.3 %collective-permute-start.17 = (bf16[2,2,2,2,1,32,1536]{6,5,3,2,1,0,4:T(8,128)(2,1)}, bf16[2,2,2,2,1,32,1536]{6,5,3,2,1,0,4:T(8,128)(2,1)}, u32[]{:S(2)}, u32[]{:S(2)}) collective-permute-start(bf16[2,2,2,2,1,32,1536]{6,5,3,2,1,0,4:T(8,128)(2,1)} %broadcast_select_fusion.9), channel_id=1, source_target_pairs={{0,1},{1,0},{2,3},{3,2},{4,5},{5,4},{6,7},{7,6},{8,9},{9,8},{10,11... | collective-permute-start | bytes 4718600 | tf_op jit(solution)/shard_map/ppermute | solution.py:430
  86.6 23.3 %collective-permute-start.4 = (bf16[2,2,2,2,1,32,1536]{6,5,3,2,1,0,4:T(8,128)(2,1)}, bf16[2,2,2,2,1,32,1536]{6,5,3,2,1,0,4:T(8,128)(2,1)}, u32[]{:S(2)}, u32[]{:S(2)}) collective-permute-start(bf16[2,2,2,2,1,32,1536]{6,5,3,2,1,0,4:T(8,128)(2,1)} %broadcast_select_fusion.10), channel_id=1, source_target_pairs={{0,1},{1,0},{2,3},{3,2},{4,5},{5,4},{6,7},{7,6},{8,9},{9,8},{10,11... | collective-permute-start | bytes 4718600 | tf_op jit(solution)/shard_map/ppermute | solution.py:430
  88.8 33.0 %collective-permute-start.16 = (bf16[2,2,1,1,1,32,1152]{6,5,1,0,4,3,2:T(8,128)(2,1)}, bf16[2,2,1,1,1,32,1152]{6,5,1,0,4,3,2:T(8,128)(2,1)S(1)}, u32[]{:S(2)}, u32[]{:S(2)}) collective-permute-start(bf16[2,2,1,1,1,32,1152]{6,5,1,0,4,3,2:T(8,128)(2,1)} %broadcast_select_fusion.32), channel_id=1, source_target_pairs={{0,2},{1,3},{2,0},{3,1},{4,6},{5,7},{6,4},{7,5},{8,10},{9,11},{10,... | collective-permute-start | bytes 884744 | tf_op jit(solution)/shard_map/ppermute | solution.py:430
  90.1 31.6 %collective-permute-start.23 = (bf16[2,2,1,1,1,128,1024]{6,5,1,0,4,3,2:T(8,128)(2,1)}, bf16[2,2,1,1,1,128,1024]{6,5,1,0,4,3,2:T(8,128)(2,1)}, u32[]{:S(2)}, u32[]{:S(2)}) collective-permute-start(bf16[2,2,1,1,1,128,1024]{6,5,1,0,4,3,2:T(8,128)(2,1)} %broadcast_select_fusion.14), channel_id=1, source_target_pairs={{0,4},{1,5},{2,6},{3,7},{4,0},{5,1},{6,2},{7,3},{8,12},{9,13},{10,... | collective-permute-start | bytes 3145736 | tf_op jit(solution)/shard_map/ppermute | solution.py:430
  92.6 29.1 %collective-permute-start.20 = (bf16[2,2,1,1,1,32,4096]{6,5,1,0,4,3,2:T(8,128)(2,1)}, bf16[2,2,1,1,1,32,4096]{6,5,1,0,4,3,2:T(8,128)(2,1)}, u32[]{:S(2)}, u32[]{:S(2)}) collective-permute-start(bf16[2,2,1,1,1,32,4096]{6,5,1,0,4,3,2:T(8,128)(2,1)} %broadcast_select_fusion.16), channel_id=1, source_target_pairs={{0,2},{1,3},{2,0},{3,1},{4,6},{5,7},{6,4},{7,5},{8,10},{9,11},{10,... | collective-permute-start | bytes 3145736 | tf_op jit(solution)/shard_map/ppermute | solution.py:430
  122.9 33.6 %collective-permute-start.24 = (bf16[2,2,1,2,1,32,1152]{6,5,4,3,2,1,0:T(8,128)(2,1)}, bf16[2,2,1,2,1,32,1152]{6,5,4,3,2,1,0:T(8,128)(2,1)S(1)}, u32[]{:S(2)}, u32[]{:S(2)}) collective-permute-start(bf16[2,2,1,2,1,32,1152]{6,5,4,3,2,1,0:T(8,128)(2,1)} %broadcast_select_fusion.23), channel_id=1, source_target_pairs={{0,4},{1,5},{2,6},{3,7},{4,0},{5,1},{6,2},{7,3},{8,12},{9,13},{10,... | collective-permute-start | bytes 1769480 | tf_op jit(solution)/shard_map/ppermute | solution.py:430
  126.6 56.7 %collective-permute-start.26 = (bf16[2,2,1,2,1,32,4096]{6,5,4,3,2,1,0:T(8,128)(2,1)}, bf16[2,2,1,2,1,32,4096]{6,5,4,3,2,1,0:T(8,128)(2,1)}, u32[]{:S(2)}, u32[]{:S(2)}) collective-permute-start(bf16[2,2,1,2,1,32,4096]{6,5,4,3,2,1,0:T(8,128)(2,1)} %broadcast_select_fusion.7), channel_id=1, source_target_pairs={{0,4},{1,5},{2,6},{3,7},{4,0},{5,1},{6,2},{7,3},{8,12},{9,13},{10,... | collective-permute-start | bytes 6291464 | tf_op jit(solution)/shard_map/ppermute | solution.py:430
  133.7 58.7 %collective-permute-start.27 = (bf16[2,2,2,1,1,128,1024]{6,5,4,3,2,1,0:T(8,128)(2,1)}, bf16[2,2,2,1,1,128,1024]{6,5,4,3,2,1,0:T(8,128)(2,1)S(1)}, u32[]{:S(2)}, u32[]{:S(2)}) collective-permute-start(bf16[2,2,2,1,1,128,1024]{6,5,4,3,2,1,0:T(8,128)(2,1)} %broadcast_select_fusion.6), channel_id=1, source_target_pairs={{0,2},{1,3},{2,0},{3,1},{4,6},{5,7},{6,4},{7,5},{8,10},{9,11},{10,... | collective-permute-start | bytes 6291464 | tf_op jit(solution)/shard_map/ppermute | solution.py:430
  157.8 29.7 %collective-permute-start.25 = (bf16[2,2,2,2,1,32,1152]{6,5,3,2,1,0,4:T(8,128)(2,1)}, bf16[2,2,2,2,1,32,1152]{6,5,3,2,1,0,4:T(8,128)(2,1)}, u32[]{:S(2)}, u32[]{:S(2)}) collective-permute-start(bf16[2,2,2,2,1,32,1152]{6,5,3,2,1,0,4:T(8,128)(2,1)} %broadcast_select_fusion.12), channel_id=1, source_target_pairs={{0,1},{1,0},{2,3},{3,2},{4,5},{5,4},{6,7},{7,6},{8,9},{9,8},{10,11... | collective-permute-start | bytes 3538952 | tf_op jit(solution)/shard_map/ppermute | solution.py:430
  187.3 15.6 %collective-permute-start.28 = (bf16[2,2,2,2,1,32,4096]{6,5,4,3,2,1,0:T(8,128)(2,1)}, bf16[2,2,2,2,1,32,4096]{6,5,4,3,2,1,0:T(8,128)(2,1)}, u32[]{:S(2)}, u32[]{:S(2)}) collective-permute-start(bf16[2,2,2,2,1,32,4096]{6,5,4,3,2,1,0:T(8,128)(2,1)} %broadcast_select_fusion.3), channel_id=1, source_target_pairs={{0,1},{1,0},{2,3},{3,2},{4,5},{5,4},{6,7},{7,6},{8,9},{9,8},{10,11... | collective-permute-start | bytes 12582920 | tf_op jit(solution)/shard_map/ppermute | solution.py:430
  194.9 35.1 %collective-permute-start.29 = (bf16[2,2,2,2,1,128,1024]{6,5,4,3,2,1,0:T(8,128)(2,1)}, bf16[2,2,2,2,1,128,1024]{6,5,4,3,2,1,0:T(8,128)(2,1)}, u32[]{:S(2)}, u32[]{:S(2)}) collective-permute-start(bf16[2,2,2,2,1,128,1024]{6,5,4,3,2,1,0:T(8,128)(2,1)} %broadcast_select_fusion.2), channel_id=1, source_target_pairs={{0,1},{1,0},{2,3},{3,2},{4,5},{5,4},{6,7},{7,6},{8,9},{9,8},{10,11... | collective-permute-start | bytes 12582920 | tf_op jit(solution)/shard_map/ppermute | solution.py:430
  359.6 37.0 %collective-permute-start.45 = (bf16[2,2,2,2,1,128,1024]{6,5,4,3,2,1,0:T(8,128)(2,1)}, bf16[2,2,2,2,1,128,1024]{6,5,4,3,2,1,0:T(8,128)(2,1)}, u32[]{:S(2)}, u32[]{:S(2)}) collective-permute-start(bf16[2,2,2,2,1,128,1024]{6,5,4,3,2,1,0:T(8,128)(2,1)} %constant_dynamic-slice_fusion.37), channel_id=1, source_target_pairs={{0,1},{1,0},{2,3},{3,2},{4,5},{5,4},{6,7},{7,6},{8,9},{9,8},{10,11... | collective-permute-start | bytes 12582920 | tf_op jit(solution)/shard_map/ppermute | solution.py:430
  395.3 34.6 %collective-permute-start.46 = (bf16[2,2,2,2,1,32,4096]{6,5,4,3,2,1,0:T(8,128)(2,1)}, bf16[2,2,2,2,1,32,4096]{6,5,4,3,2,1,0:T(8,128)(2,1)}, u32[]{:S(2)}, u32[]{:S(2)}) collective-permute-start(bf16[2,2,2,2,1,32,4096]{6,5,4,3,2,1,0:T(8,128)(2,1)} %constant_dynamic-slice_fusion.36), channel_id=1, source_target_pairs={{0,1},{1,0},{2,3},{3,2},{4,5},{5,4},{6,7},{7,6},{8,9},{9,8},{10,11... | collective-permute-start | bytes 12582920 | tf_op jit(solution)/shard_map/ppermute | solution.py:430
  406.2 47.9 %collective-permute-start.47 = (bf16[2,2,2,1,1,128,1024]{6,5,4,3,2,1,0:T(8,128)(2,1)}, bf16[2,2,2,1,1,128,1024]{6,5,4,3,2,1,0:T(8,128)(2,1)}, u32[]{:S(2)}, u32[]{:S(2)}) collective-permute-start(bf16[2,2,2,1,1,128,1024]{6,5,4,3,2,1,0:T(8,128)(2,1)} %constant_dynamic-slice_fusion.35), channel_id=1, source_target_pairs={{0,2},{1,3},{2,0},{3,1},{4,6},{5,7},{6,4},{7,5},{8,10},{9,11},{10,... | collective-permute-start | bytes 6291464 | tf_op jit(solution)/shard_map/ppermute | solution.py:430
  437.2 57.5 %collective-permute-start.49 = (bf16[2,2,1,2,1,32,4096]{6,5,4,3,2,1,0:T(8,128)(2,1)}, bf16[2,2,1,2,1,32,4096]{6,5,4,3,2,1,0:T(8,128)(2,1)}, u32[]{:S(2)}, u32[]{:S(2)}) collective-permute-start(bf16[2,2,1,2,1,32,4096]{6,5,4,3,2,1,0:T(8,128)(2,1)} %constant_dynamic-slice_fusion.34), channel_id=1, source_target_pairs={{0,4},{1,5},{2,6},{3,7},{4,0},{5,1},{6,2},{7,3},{8,12},{9,13},{10,... | collective-permute-start | bytes 6291464 | tf_op jit(solution)/shard_map/ppermute | solution.py:430
  449.0 50.6 %collective-permute-start.48 = (bf16[2,2,2,2,1,32,1152]{6,5,4,3,2,1,0:T(8,128)(2,1)}, bf16[2,2,2,2,1,32,1152]{6,5,4,3,2,1,0:T(8,128)(2,1)}, u32[]{:S(2)}, u32[]{:S(2)}) collective-permute-start(bf16[2,2,2,2,1,32,1152]{6,5,4,3,2,1,0:T(8,128)(2,1)} %constant_dynamic-slice_fusion.33), channel_id=1, source_target_pairs={{0,1},{1,0},{2,3},{3,2},{4,5},{5,4},{6,7},{7,6},{8,9},{9,8},{10,11... | collective-permute-start | bytes 3538952 | tf_op jit(solution)/shard_map/ppermute | solution.py:430
  457.7 83.1 %collective-permute-start.51 = (bf16[2,2,1,1,1,128,1024]{6,5,4,3,2,1,0:T(8,128)(2,1)}, bf16[2,2,1,1,1,128,1024]{6,5,4,3,2,1,0:T(8,128)(2,1)}, u32[]{:S(2)}, u32[]{:S(2)}) collective-permute-start(bf16[2,2,1,1,1,128,1024]{6,5,4,3,2,1,0:T(8,128)(2,1)} %constant_dynamic-slice_fusion.32), channel_id=1, source_target_pairs={{0,4},{1,5},{2,6},{3,7},{4,0},{5,1},{6,2},{7,3},{8,12},{9,13},{10,... | collective-permute-start | bytes 3145736 | tf_op jit(solution)/shard_map/ppermute | solution.py:430
  502.9 58.1 %collective-permute-start.67 = (bf16[2,2,1,2,1,32,1152]{6,5,4,3,2,1,0:T(8,128)(2,1)}, bf16[2,2,1,2,1,32,1152]{6,5,4,3,2,1,0:T(8,128)(2,1)}, u32[]{:S(2)}, u32[]{:S(2)}) collective-permute-start(bf16[2,2,1,2,1,32,1152]{6,5,4,3,2,1,0:T(8,128)(2,1)} %constant_dynamic-slice_fusion.30), channel_id=1, source_target_pairs={{0,4},{1,5},{2,6},{3,7},{4,0},{5,1},{6,2},{7,3},{8,12},{9,13},{10,... | collective-permute-start | bytes 1769480 | tf_op jit(solution)/shard_map/ppermute | solution.py:430
  504.9 38.6 %collective-permute-start.50 = (bf16[2,2,1,1,1,32,4096]{6,5,4,3,2,1,0:T(8,128)(2,1)}, bf16[2,2,1,1,1,32,4096]{6,5,4,3,2,1,0:T(8,128)(2,1)}, u32[]{:S(2)}, u32[]{:S(2)}) collective-permute-start(bf16[2,2,1,1,1,32,4096]{6,5,4,3,2,1,0:T(8,128)(2,1)} %constant_dynamic-slice_fusion.29), channel_id=1, source_target_pairs={{0,2},{1,3},{2,0},{3,1},{4,6},{5,7},{6,4},{7,5},{8,10},{9,11},{10,... | collective-permute-start | bytes 3145736 | tf_op jit(solution)/shard_map/ppermute | solution.py:430
  505.7 42.1 %collective-permute-start.52 = (bf16[2,2,2,2,1,32,1536]{6,5,4,3,2,1,0:T(8,128)(2,1)}, bf16[2,2,2,2,1,32,1536]{6,5,4,3,2,1,0:T(8,128)(2,1)S(1)}, u32[]{:S(2)}, u32[]{:S(2)}) collective-permute-start(bf16[2,2,2,2,1,32,1536]{6,5,4,3,2,1,0:T(8,128)(2,1)} %constant_dynamic-slice_fusion.31), channel_id=1, source_target_pairs={{0,1},{1,0},{2,3},{3,2},{4,5},{5,4},{6,7},{7,6},{8,9},{9,8},{10,11... | collective-permute-start | bytes 4718600 | tf_op jit(solution)/shard_map/ppermute | solution.py:430
  543.5 33.2 %collective-permute-start.73 = (bf16[2,1,1,1,1,128,1024]{6,5,4,3,2,1,0:T(8,128)(2,1)}, bf16[2,1,1,1,1,128,1024]{6,5,4,3,2,1,0:T(8,128)(2,1)}, u32[]{:S(2)}, u32[]{:S(2)}) collective-permute-start(bf16[2,1,1,1,1,128,1024]{6,5,4,3,2,1,0:T(8,128)(2,1)} %constant_dynamic-slice_fusion.27), channel_id=1, source_target_pairs={{0,8},{1,9},{2,10},{3,11},{4,12},{5,13},{6,14},{7,15},{8,0},{9,1},... | collective-permute-start | bytes 1572872 | tf_op jit(solution)/shard_map/ppermute | solution.py:430
  546.5 32.7 %collective-permute-start.71 = (bf16[2,1,1,1,1,32,4096]{6,5,4,3,2,1,0:T(8,128)(2,1)}, bf16[2,1,1,1,1,32,4096]{6,5,4,3,2,1,0:T(8,128)(2,1)}, u32[]{:S(2)}, u32[]{:S(2)}) collective-permute-start(bf16[2,1,1,1,1,32,4096]{6,5,4,3,2,1,0:T(8,128)(2,1)} %constant_dynamic-slice_fusion.28), channel_id=1, source_target_pairs={{0,8},{1,9},{2,10},{3,11},{4,12},{5,13},{6,14},{7,15},{8,0},{9,1},... | collective-permute-start | bytes 1572872 | tf_op jit(solution)/shard_map/ppermute | solution.py:430
  550.5 22.6 %collective-permute-start.53 = (bf16[2,2,1,2,1,32,1536]{6,5,4,3,2,1,0:T(8,128)(2,1)}, bf16[2,2,1,2,1,32,1536]{6,5,4,3,2,1,0:T(8,128)(2,1)}, u32[]{:S(2)}, u32[]{:S(2)}) collective-permute-start(bf16[2,2,1,2,1,32,1536]{6,5,4,3,2,1,0:T(8,128)(2,1)} %constant_dynamic-slice_fusion.26), channel_id=1, source_target_pairs={{0,4},{1,5},{2,6},{3,7},{4,0},{5,1},{6,2},{7,3},{8,12},{9,13},{10,... | collective-permute-start | bytes 2359304 | tf_op jit(solution)/shard_map/ppermute | solution.py:430
  560.8 11.1 %collective-permute-start.56 = (bf16[2,2,2,2,1,32,768]{6,5,4,3,2,1,0:T(8,128)(2,1)S(1)}, bf16[2,2,2,2,1,32,768]{6,5,4,3,2,1,0:T(8,128)(2,1)S(1)}, u32[]{:S(2)}, u32[]{:S(2)}) collective-permute-start(bf16[2,2,2,2,1,32,768]{6,5,4,3,2,1,0:T(8,128)(2,1)S(1)} %constant_dynamic-slice_fusion.24), channel_id=1, source_target_pairs={{0,1},{1,0},{2,3},{3,2},{4,5},{5,4},{6,7},{7,6},{8,9},{9,8},{10,11... | collective-permute-start | bytes 2359304 | tf_op jit(solution)/shard_map/ppermute | solution.py:430
  561.0 10.8 %collective-permute-start.75 = (f32[2,2,2,2,1,1,384]{6,5,4,3,2,1,0:T(1,128)S(1)}, f32[2,2,2,2,1,1,384]{6,5,4,3,2,1,0:T(1,128)S(1)}, u32[]{:S(2)}, u32[]{:S(2)}) collective-permute-start(f32[2,2,2,2,1,1,384]{6,5,4,3,2,1,0:T(1,128)S(1)} %fusion.21), channel_id=1, source_target_pairs={{0,1},{1,0},{2,3},{3,2},{4,5},{5,4},{6,7},{7,6},{8,9},{9,8},{10,11... | collective-permute-start | bytes 73736 | tf_op jit(solution)/shard_map/ppermute | solution.py:430
  575.5 14.8 %collective-permute-start.54 = (bf16[2,2,1,1,1,32,1536]{6,5,4,3,2,1,0:T(8,128)(2,1)S(1)}, bf16[2,2,1,1,1,32,1536]{6,5,4,3,2,1,0:T(8,128)(2,1)S(1)}, u32[]{:S(2)}, u32[]{:S(2)}) collective-permute-start(bf16[2,2,1,1,1,32,1536]{6,5,4,3,2,1,0:T(8,128)(2,1)S(1)} %constant_dynamic-slice_fusion.23), channel_id=1, source_target_pairs={{0,2},{1,3},{2,0},{3,1},{4,6},{5,7},{6,4},{7,5},{8,10},{9,11},{10,... | collective-permute-start | bytes 1179656 | tf_op jit(solution)/shard_map/ppermute | solution.py:430
  576.7 21.6 %collective-permute-start.59 = (bf16[2,2,2,1,1,32,768]{6,5,4,3,2,1,0:T(8,128)(2,1)S(1)}, bf16[2,2,2,1,1,32,768]{6,5,4,3,2,1,0:T(8,128)(2,1)S(1)}, u32[]{:S(2)}, u32[]{:S(2)}) collective-permute-start(bf16[2,2,2,1,1,32,768]{6,5,4,3,2,1,0:T(8,128)(2,1)S(1)} %constant_dynamic-slice_fusion.21), channel_id=1, source_target_pairs={{0,2},{1,3},{2,0},{3,1},{4,6},{5,7},{6,4},{7,5},{8,10},{9,11},{10,... | collective-permute-start | bytes 1179656 | tf_op jit(solution)/shard_map/ppermute | solution.py:430
  580.4 48.0 %collective-permute-start.74 = (bf16[1,1,1,1,1,128,1024]{6,5,4,3,2,1,0:T(8,128)(2,1)S(1)}, bf16[1,1,1,1,1,128,1024]{6,5,4,3,2,1,0:T(8,128)(2,1)S(1)}, u32[]{:S(2)}, u32[]{:S(2)}) collective-permute-start(bf16[1,1,1,1,1,128,1024]{6,5,4,3,2,1,0:T(8,128)(2,1)S(1)} %constant_dynamic-slice_fusion.8), channel_id=1, source_target_pairs={{0,16},{1,17},{2,18},{3,19},{4,20},{5,21},{6,22},{7,23},{8,24},{9,... | collective-permute-start | bytes 786440 | tf_op jit(solution)/shard_map/ppermute | solution.py:430
  580.5 18.6 %collective-permute-start.58 = (bf16[2,2,1,2,1,32,768]{6,5,4,3,2,1,0:T(8,128)(2,1)S(1)}, bf16[2,2,1,2,1,32,768]{6,5,4,3,2,1,0:T(8,128)(2,1)S(1)}, u32[]{:S(2)}, u32[]{:S(2)}) collective-permute-start(bf16[2,2,1,2,1,32,768]{6,5,4,3,2,1,0:T(8,128)(2,1)S(1)} %constant_dynamic-slice_fusion.22), channel_id=1, source_target_pairs={{0,4},{1,5},{2,6},{3,7},{4,0},{5,1},{6,2},{7,3},{8,12},{9,13},{10,... | collective-permute-start | bytes 1179656 | tf_op jit(solution)/shard_map/ppermute | solution.py:430
  581.9 47.5 %collective-permute-start.72 = (bf16[1,1,1,1,1,32,4096]{6,5,4,3,2,1,0:T(8,128)(2,1)S(1)}, bf16[1,1,1,1,1,32,4096]{6,5,4,3,2,1,0:T(8,128)(2,1)S(1)}, u32[]{:S(2)}, u32[]{:S(2)}) collective-permute-start(bf16[1,1,1,1,1,32,4096]{6,5,4,3,2,1,0:T(8,128)(2,1)S(1)} %constant_dynamic-slice_fusion.9), channel_id=1, source_target_pairs={{0,16},{1,17},{2,18},{3,19},{4,20},{5,21},{6,22},{7,23},{8,24},{9,... | collective-permute-start | bytes 786440 | tf_op jit(solution)/shard_map/ppermute | solution.py:430
  598.3 10.7 %collective-permute-start.69 = (bf16[2,1,1,1,1,32,1152]{6,5,4,3,2,1,0:T(8,128)(2,1)S(1)}, bf16[2,1,1,1,1,32,1152]{6,5,4,3,2,1,0:T(8,128)(2,1)S(1)}, u32[]{:S(2)}, u32[]{:S(2)}) collective-permute-start(bf16[2,1,1,1,1,32,1152]{6,5,4,3,2,1,0:T(8,128)(2,1)S(1)} %constant_dynamic-slice_fusion.11), channel_id=1, source_target_pairs={{0,8},{1,9},{2,10},{3,11},{4,12},{5,13},{6,14},{7,15},{8,0},{9,1},... | collective-permute-start | bytes 442376 | tf_op jit(solution)/shard_map/ppermute | solution.py:430
  600.0 11.2 %collective-permute-start.61 = (bf16[2,2,1,1,1,32,768]{6,5,4,3,2,1,0:T(8,128)(2,1)S(1)}, bf16[2,2,1,1,1,32,768]{6,5,4,3,2,1,0:T(8,128)(2,1)S(1)}, u32[]{:S(2)}, u32[]{:S(2)}) collective-permute-start(bf16[2,2,1,1,1,32,768]{6,5,4,3,2,1,0:T(8,128)(2,1)S(1)} %constant_dynamic-slice_fusion.19), channel_id=1, source_target_pairs={{0,2},{1,3},{2,0},{3,1},{4,6},{5,7},{6,4},{7,5},{8,10},{9,11},{10,... | collective-permute-start | bytes 589832 | tf_op jit(solution)/shard_map/ppermute | solution.py:430
  609.1 11.7 %collective-permute-start.78 = (f32[2,1,1,1,1,1,384]{6,5,4,3,2,1,0:T(1,128)S(1)}, f32[2,1,1,1,1,1,384]{6,5,4,3,2,1,0:T(1,128)S(1)}, u32[]{:S(2)}, u32[]{:S(2)}) collective-permute-start(f32[2,1,1,1,1,1,384]{6,5,4,3,2,1,0:T(1,128)S(1)} %constant_dynamic-slice_fusion.2), channel_id=1, source_target_pairs={{0,8},{1,9},{2,10},{3,11},{4,12},{5,13},{6,14},{7,15},{8,0},{9,1},... | collective-permute-start | bytes 9224 | tf_op jit(solution)/shard_map/ppermute | solution.py:430
  (107 other events, 1317.9 us)

commit v6 on v5

--- a/solution.py
+++ b/solution.py
@@ -348,6 +348,69 @@
     return lax.optimization_barrier((value, *earlier))[0]
 
 
+def exchange(dp, fsdp, scatter, add, mine_ref, out_ref, held, send_sem, recv_sem):
+    count = dp * fsdp
+    me = lax.axis_index("dp") * fsdp + lax.axis_index("fsdp")
+
+    def device(other):
+        return (other // fsdp, other % fsdp)
+
+    def copy(step, other, place):
+        return pltpu.make_async_remote_copy(
+            src_ref=mine_ref.at[other] if scatter else mine_ref,
+            dst_ref=held.at[place],
+            send_sem=send_sem.at[step],
+            recv_sem=recv_sem.at[step],
+            device_id=device(other),
+            device_id_type=pl.DeviceIdType.MESH,
+        )
+
+    barrier = pltpu.get_barrier_semaphore()
+
+    @pl.loop(1, count)
+    def _(step):
+        pl.semaphore_signal(
+            barrier, inc=1, device_id=device((me + step) % count),
+            device_id_type=pl.DeviceIdType.MESH,
+        )
+
+    pl.semaphore_wait(barrier, count - 1)
+
+    @pl.loop(1, count)
+    def _(step):
+        copy(step, (me + step) % count, me).start()
+
+    held[me] = mine_ref[me] if scatter else mine_ref[...]
+
+    @pl.loop(1, count)
+    def _(step):
+        arriving = copy(step, (me + step) % count, (me + count - step) % count)
+        arriving.wait_send()
+        arriving.wait_recv()
+
+    if add:
+        out_ref[...] = jnp.sum(held[...].astype(f32), axis=0)
+    else:
+        out_ref[...] = held[...]
+
+
+def exchanged(links, value, scatter, add, name):
+    block = value.shape[1:] if scatter else value.shape
+    whole = (links.count,) + block
+    return pl.pallas_call(
+        partial(exchange, links.dp, links.fsdp, scatter, add),
+        out_shape=jax.ShapeDtypeStruct(block if add else whole, f32 if add else value.dtype),
+        in_specs=[pl.BlockSpec(memory_space=pltpu.VMEM)],
+        out_specs=pl.BlockSpec(memory_space=pltpu.VMEM),
+        scratch_shapes=[
+            pltpu.VMEM(whole, value.dtype),
+            pltpu.SemaphoreType.DMA((links.count,)),
+            pltpu.SemaphoreType.DMA((links.count,)),
+        ],
+        compiler_params=pltpu.CompilerParams(collective_id=name, has_side_effects=True),
+    )(value)
+
+
 class Growing:
     def __init__(self, links, shard, lane):
         self.links, self.order, self.block = links, list(links.orders[lane]), shard.shape
@@ -368,7 +431,7 @@
         arrived = after(self.arrived, *earlier) if earlier else self.arrived
         shape = held.shape[:axis] + (2,) + held.shape[axis + 1 :]
         own = lax.broadcasted_iota(jnp.int32, shape, axis) == mine
-        self.held = jnp.where(own, held, arrived)
+        self.held = lax.optimization_barrier(jnp.where(own, held, arrived))
 
     def full(self):
         while self.order:
@@ -436,9 +499,15 @@
         return Shrinking(self, blocks, lane, wire)
 
     def total(self, value):
-        for place in self.orders[0]:
-            value = value + self.swap(value, 1 << place)
-        return value
+        high, wide = value.shape
+        padded = jnp.pad(value, ((0, -high % 8), (0, -wide % 128)))
+        return exchanged(self, padded, False, True, 0)[:high, :wide]
+
+    def everyone(self, value):
+        return exchanged(self, value, False, False, 1)
+
+    def owners_sum(self, blocks):
+        return exchanged(self, blocks.astype(bf16), True, True, 2)
 
 
 class Whole:
@@ -470,6 +539,12 @@
 
     def total(self, value):
         return lax.psum(value, AXES)
+
+    def everyone(self, value):
+        return lax.all_gather(value, AXES, axis=0)
+
+    def owners_sum(self, blocks):
+        return lax.psum_scatter(blocks, AXES, scatter_dimension=0, tiled=False)
 
 
 def make_links(mesh):
@@ -631,7 +706,7 @@
     vectors = matmul_plain(second_low, full_proj).astype(bf16)
     doc_vectors = vectors[:row_len]
     query_vectors = vectors[row_len:].reshape(query_count * span, proj_width)
-    every_query = links.growing(query_vectors).full().reshape(count * query_count * span, proj_width)
+    every_query = links.everyone(query_vectors).reshape(count * query_count * span, proj_width)
     query_total = count * query_count
     levels = (proj_width, proj_width * 3 // 4, proj_width // 2)
     logits, doc_sums = interaction_logits(levels, span, doc_vectors, member.astype(bf16), every_query)
@@ -641,7 +716,7 @@
     my_row = lax.axis_index(AXES)
     chosen = ((positives - my_row * doc_slots)[:, None] == slot_ids[None, :]).astype(f32)
     local_pick = jnp.sum(logits * chosen[:, None, :], axis=-1)
-    both = links.total(jnp.concatenate([local_sum, local_pick], axis=1))
+    both = links.total(jnp.concatenate([local_sum, local_pick], axis=1).T).T
     all_sums, picked = both[:, :3], both[:, 3:]
     loss = jnp.sum(jnp.log(all_sums) - picked) / query_total
     score_derivative = (powers / all_sums[:, :, None] - chosen[:, None, :]) / query_total
@@ -652,7 +727,7 @@
         peak_match_derivative.transpose(1, 0, 2),
     )
     query_terms = query_terms.reshape(count, query_count * span, proj_width)
-    query_vec_grad = links.shrinking(query_terms, wire=f32).mine()
+    query_vec_grad = links.owners_sum(query_terms)
     grad_vectors = jnp.concatenate([doc_vec_grad, query_vec_grad], axis=0).astype(bf16)
 
     def spread_rows_of(full):

time: 646 us -> 674 us (1.043)
  Pallas kernels: 122 us -> 156 us
  waiting for transfers between devices: 129 us -> 142 us
    pallas_call x0 -> x3, Pallas kernels: none -> 34.2 us  [exchanged(): pl.pallas_call(partial(exchange, links.dp, links.fsdp, scatter, add), out...]
    ppermute x80 -> x65, waiting for transfers between devices: 129 us -> 142 us  [swap(): return lax.ppermute(value, AXES, [(d, d ^ bit) for d in range(self.count)])]
    select_n x54 -> x27, other arithmetic: 51.1 us -> 42 us  [merge(): self.held = lax.optimization_barrier(jnp.where(own, held, arrived))]
    unnamed x151 -> x165, local copies, waits for them, and re-layouts: 11.8 us -> 18.9 us
    ppermute x80 -> x65, starting transfers between devices: 67.5 us -> 68.4 us  [swap(): return lax.ppermute(value, AXES, [(d, d ^ bit) for d in range(self.count)])]
    dynamic_slice x39 -> x34, local copies, waits for them, and re-layouts: 17.1 us -> 17.1 us  [launch(): lax.dynamic_slice_in_dim(self.held, 1 - self.links.side(self.place), 1, a...]
  transfers between devices with their start and end apart: 80 -> 65, of which waited for: 34 -> 20; matrix products, arithmetic and copies ran while one was open for 39% -> 30% of each run, Pallas kernels for 15% -> 15%
where the time goes in v6:
time: 674 us; the launch traced here: 669 us
  Pallas kernels  156 us (23%)
  matrix products  149 us (22%)
  waiting for transfers between devices  142 us (21%)
  other arithmetic  95.5 us (14%)
  starting transfers between devices  68.4 us (10%)
  local copies, waits for them, and re-layouts  54.4 us (8%)
    ppermute x65, waiting for transfers between devices, swap(): return lax.ppermute(value, AXES, [(d, d ^ bit) for d in range(self.count)])  142 us
    ppermute x65, starting transfers between devices, swap(): return lax.ppermute(value, AXES, [(d, d ^ bit) for d in range(self.count)])  68.4 us
    pallas_call x2, Pallas kernels, attention_backward(): pl.pallas_call(partial(attend_backward, row_len, qb, kb, lanes, span), ou...  54.7 us
    dot_general x7, matrix products, matmul_right_t(): lax.dot_general(left, right, (((1,), (1,)), ((), ())), preferred_element_...  54.3 us
    dot_general x7, matrix products, matmul_plain(): return jnp.dot(left, right, preferred_element_type=jnp.float32)  49.7 us
    dot_general x7, matrix products, matmul_left_t(): lax.dot_general(left, right, (((0,), (0,)), ((), ())), preferred_element_...  44.9 us
    pallas_call x2, Pallas kernels, attention_forward(): pl.pallas_call(partial(attend_forward, row_len, qb, kb, lanes, span), out...  43.7 us
    select_n x27, other arithmetic, merge(): self.held = lax.optimization_barrier(jnp.where(own, held, arrived))  42 us
  transfers between devices with their start and end apart: 65, of which 20 were waited for; matrix products, arithmetic and copies ran while one was open for 30% of the time, Pallas kernels for 15%

profile of v6, /device:TPU:0, one launch (start us, length us, event | category | flops | bytes accessed | tf_op | source)
XLA Modules:
  0.0 669.5 jit_solution(1370843110105344220)
XLA Ops:
  3.0 4.1 collective-permute-start.5
  9.5 3.0 collective-permute-start
  16.3 3.5 collective-permute-done.6
  23.2 5.7 collective-permute-done.1
  42.1 4.8 collective-permute-done.10
  52.5 8.7 %collective-permute-done.21 = bf16[1,1,1,1,1,128,1024]{6,5,4,3,2,1,0:T(8,128)(2,1)S(1)} collective-permute-done((bf16[1,1,1,1,1,128,1024]{6,5,4,3,2,1,0:T(8,128)(2,1)}, bf16[1,1,1,1,1,128,1024]{6,5,4,3,2,1,0:T(8,128)(2,1)S(1)}, u32[]{:S(2)}, u32[]{:S(2)}) %collective-permute-start.21) | collective-permute-done | bytes 262176 | tf_op jit(solution)/shard_map/ppermute | solution.py:493
  66.2 10.2 %collective-permute-done.22 = bf16[2,1,1,1,1,128,1024]{6,5,0,4,3,2,1:T(8,128)(2,1)S(1)} collective-permute-done((bf16[2,1,1,1,1,128,1024]{6,5,0,4,3,2,1:T(8,128)(2,1)S(1)}, bf16[2,1,1,1,1,128,1024]{6,5,0,4,3,2,1:T(8,128)(2,1)S(1)}, u32[]{:S(2)}, u32[]{:S(2)}) %collective-permute-start.22) | collective-permute-done | bytes 524320 | tf_op jit(solution)/shard_map/ppermute | solution.py:493
  76.4 11.1 %collective-permute-done.19 = bf16[2,1,1,1,1,32,4096]{6,5,0,4,3,2,1:T(8,128)(2,1)S(1)} collective-permute-done((bf16[2,1,1,1,1,32,4096]{6,5,0,4,3,2,1:T(8,128)(2,1)S(1)}, bf16[2,1,1,1,1,32,4096]{6,5,0,4,3,2,1:T(8,128)(2,1)S(1)}, u32[]{:S(2)}, u32[]{:S(2)}) %collective-permute-start.19) | collective-permute-done | bytes 524320 | tf_op jit(solution)/shard_map/ppermute | solution.py:493
  92.1 3.1 broadcast_select_fusion.4
  96.2 6.2 fusion.7.q_ref.k_ref.v_ref
  102.4 5.2 fusion.6.q_ref.k_ref.v_ref
  107.7 9.0 %collective-permute-done.23 = bf16[2,2,1,1,1,128,1024]{6,5,1,0,4,3,2:T(8,128)(2,1)} collective-permute-done((bf16[2,2,1,1,1,128,1024]{6,5,1,0,4,3,2:T(8,128)(2,1)}, bf16[2,2,1,1,1,128,1024]{6,5,1,0,4,3,2:T(8,128)(2,1)}, u32[]{:S(2)}, u32[]{:S(2)}) %collective-permute-start.23) | collective-permute-done | bytes 1048608 | tf_op jit(solution)/shard_map/ppermute | solution.py:493
  116.7 3.1 broadcast_select_fusion.7
  119.9 3.1 broadcast_select_fusion.8
  126.1 50.9 %collective-permute-done.17 = bf16[2,2,1,1,1,32,1152]{6,5,1,0,4,3,2:T(8,128)(2,1)S(1)} collective-permute-done((bf16[2,2,1,1,1,32,1152]{6,5,1,0,4,3,2:T(8,128)(2,1)S(1)}, bf16[2,2,1,1,1,32,1152]{6,5,1,0,4,3,2:T(8,128)(2,1)S(1)}, u32[]{:S(2)}, u32[]{:S(2)}) %collective-permute-start.17) | collective-permute-done | bytes 294944 | tf_op jit(solution)/shard_map/ppermute | solution.py:493
  184.4 21.8 %shard_map.237 = (bf16[1056,512]{1,0:T(8,128)(2,1)S(1)}, f32[4,4,512]{2,1,0:T(4,128)S(1)}, f32[4,1,64]{2,1,0:T(1,128)S(1)}) custom-call(s32[2,4]{1,0:T(2,128)S(1)} %pad_add_fusion.bounds, s32[4,512]{1,0:T(4,128)S(1)} %constant_dynamic-update-slice_fusion.segrow, s32[1024,1]{1,0:T(8,128)S(1)} %copy-done.2, bf16[1056,1536]{1,0:T(8,128)(2,1)S(1)} %copy-done.1, ...), custom_call_target="tpu_custom_call" | custom-call | tf_op jit(solution)/shard_map/pallas_call | solution.py:124
  209.2 22.0 %shard_map.238 = (bf16[1056,512]{1,0:T(8,128)(2,1)S(1)}, f32[4,4,512]{2,1,0:T(4,128)S(1)}, f32[4,1,64]{2,1,0:T(1,128)S(1)}) custom-call(s32[2,4]{1,0:T(2,128)S(1)} %pad_add_fusion.bounds, s32[4,512]{1,0:T(4,128)S(1)} %constant_dynamic-update-slice_fusion.segrow, s32[1024,1]{1,0:T(8,128)S(1)} %copy-done.2, bf16[1056,1536]{1,0:T(8,128)(2,1)S(1)} %fusion.7.q_ref.k_ref.v_ref, ...), custom_call_target="tpu_custom_call" | custom-call | tf_op jit(solution)/shard_map/pallas_call | solution.py:124
  231.3 4.9 broadcast_select_fusion.2
  236.7 4.7 broadcast_select_fusion.3
  250.0 5.2 broadcast_select_fusion
  255.2 7.3 %broadcast_select_fusion.1 = bf16[2,2,2,2,2,32,4096]{6,5,4,3,2,1,0:T(8,128)(2,1)S(1)} fusion(pred[2]{0:T(512)(128)(4,1)S(1)} %copy-done.65, bf16[2,2,2,2,32,4096]{5,4,3,2,1,0:T(8,128)(2,1)} %bitcast.76, bf16[2,2,2,2,32,4096]{5,4,3,2,1,0:T(8,128)(2,1)} %bitcast.75), kind=kLoop, calls=%fused_computation.17 | loop fusion | flops 4194304 | bytes 16777218 | tf_op jit(solution)/shard_map/jit(_where)/select_n | solution.py:434
  262.6 20.1 %fusion.4 = (bf16[1056,4096]{1,0:T(8,128)(2,1)}, bf16[1056,4096]{1,0:T(8,128)(2,1)}) fusion(f32[4096]{0:T(1024)S(1)} %fusion.28, bf16[1024,4096]{1,0:T(8,128)(2,1)S(1)} %bitcast.183, f32[1056,1024]{1,0:T(8,128)S(1)} %get-tuple-element.216, f32[1024]{0:T(1024)S(1)} %add.206, f32[1024]{0:T(1024)S(1)} %mul.85, f32[1056]{0:T(1024)S(1)} %add_rsqrt_fusion.1, ...), kind=kOutput, calls=%fused_computation.7 | convolution fusion | flops 8915681280 | bytes 30048512 | tf_op jit(solution)/shard_map/dot_general | solution.py:27
  282.7 13.1 %fusion.47 = (f32[1056]{0:T(1024)S(1)}, f32[1056,1024]{1,0:T(8,128)S(1)}) fusion(f32[1024]{0:T(1024)S(1)} %add.214, bf16[1056,4096]{1,0:T(8,128)(2,1)} %get-tuple-element.114, bf16[4096,1024]{1,0:T(8,128)(2,1)S(1)} %bitcast.187, f32[1024]{0:T(1024)S(1)} %add.206, f32[1024]{0:T(1024)S(1)} %mul.85, f32[1056]{0:T(1024)S(1)} %add_rsqrt_fusion.1, ...), kind=kOutput, calls=%fused_computation.267 | convolution fusion | flops 8865938432 | bytes 25715072 | tf_op jit(solution)/shard_map/dot_general | solution.py:27
  300.3 10.0 %shard_map.239 = bf16[32,32,128]{2,1,0:T(8,128)(2,1)} custom-call(bf16[32,128]{1,0:T(8,128)(2,1)} %slice.232.mine_ref), custom_call_target="tpu_custom_call" | custom-call | tf_op jit(solution)/shard_map/pallas_call | solution.py:400
  311.2 9.6 %shard_map.240 = (f32[3,32,8]{2,1,0:T(8,128)S(1)}, f32[3,1024,8]{2,1,0:T(8,128)S(1)}) custom-call(bf16[1024,128]{1,0:T(8,128)(2,1)S(1)} %slice.231.doc_ref, bf16[1024,8]{1,0:T(8,128)(2,1)S(1)} %convert_convert_fusion.member_ref, bf16[1024,128]{1,0:T(8,128)(2,1)S(1)} %bitcast.173), custom_call_target="tpu_custom_call" | custom-call | tf_op jit(solution)/shard_map/pallas_call | solution.py:296
  321.6 11.5 %shard_map.241 = f32[8,128]{1,0:T(8,128)} custom-call(f32[8,128]{1,0:T(8,128)} %pad.4.mine_ref), custom_call_target="tpu_custom_call" | custom-call | tf_op jit(solution)/shard_map/pallas_call | solution.py:400
  335.4 13.8 %shard_map.242 = (f32[1024,128]{1,0:T(8,128)S(1)}, f32[1024,128]{1,0:T(8,128)S(1)}) custom-call(bf16[1024,128]{1,0:T(8,128)(2,1)S(1)} %slice.231.doc_ref, bf16[8,1024]{1,0:T(8,128)(2,1)S(1)} %convert_convert_fusion.1.member_t_ref, bf16[1024,128]{1,0:T(8,128)(2,1)S(1)} %bitcast.174, f32[3,1024,8]{2,1,0:T(8,128)S(1)} %get-tuple-element.116.sums_ref, ...), custom_call_target="tpu_custom_call" | custom-call | tf_op jit(solution)/shard_map/pallas_call | solution.py:321
  350.0 12.7 %shard_map.243 = f32[32,128]{1,0:T(8,128)} custom-call(bf16[32,32,128]{2,1,0:T(8,128)(2,1)} %bitcast.225), custom_call_target="tpu_custom_call" | custom-call | tf_op jit(solution)/shard_map/pallas_call | solution.py:400
  363.4 4.1 multiply_reduce_fusion
  370.4 11.8 %convolution_convert_fusion = bf16[4096,1024]{1,0:T(8,128)(2,1)S(1)} fusion(bf16[1056,4096]{1,0:T(8,128)(2,1)S(1)} %bitcast.277, bf16[1056,1024]{1,0:T(8,128)(2,1)S(1)} %get-tuple-element.119), kind=kOutput, calls=%fused_computation.18 | convolution fusion | flops 8862564352 | bytes 19202048 | tf_op jit(solution)/shard_map/dot_general | solution.py:37
  382.2 3.0 constant_dynamic-slice_fusion.37
  387.3 15.8 %convert_reduce_fusion = (f32[4096]{0:T(1024)S(1)}, bf16[1056,4096]{1,0:T(8,128)(2,1)}) fusion(bf16[1056,4096]{1,0:T(8,128)(2,1)} %get-tuple-element.120, bf16[1056,1024]{1,0:T(8,128)(2,1)S(1)} %get-tuple-element.119, bf16[4096,1024]{1,0:T(8,128)(2,1)} %bitcast.188), kind=kOutput, calls=%fused_computation.8 | convolution fusion | flops 8879992832 | bytes 27869184 | tf_op jit(solution)/shard_map/dot_general | solution.py:31
  403.1 14.7 %convolution_convert_fusion.1 = bf16[1024,4096]{1,0:T(8,128)(2,1)S(1)} fusion(bf16[1056,4096]{1,0:T(8,128)(2,1)} %get-tuple-element.122, f32[1056,1024]{1,0:T(8,128)S(1)} %bitcast.178, f32[1024]{0:T(1024)S(1)} %add.206, f32[1024]{0:T(1024)S(1)} %mul.85, f32[1056]{0:T(1024)S(1)} %add_rsqrt_fusion.1, f32[1056]{0:T(1024)S(1)} %broadcast_multiply_fusion.5), kind=kOutput, calls=%fused_computation.21 | convolution fusion | flops 8867971072 | bytes 21381376 | tf_op jit(solution)/shard_map/dot_general | solution.py:37
  424.6 6.1 add_convert_fusion.1
  436.4 16.2 %multiply_reduce_fusion.1 = (f32[1024]{0:T(1024)S(1)}, f32[1056]{0:T(1024)S(1)}, f32[1056]{0:T(1024)S(1)}, f32[1024]{0:T(1024)S(1)}, f32[1056,1024]{1,0:T(8,128)}) fusion(f32[1056,1024]{1,0:T(8,128)S(1)} %bitcast.180, f32[1056]{0:T(1024)S(1)} %add_rsqrt_fusion.1, f32[1056]{0:T(1024)S(1)} %broadcast_multiply_fusion.5, f32[1024]{0:T(1024)S(1)} %mul.85, ...), kind=kOutput, calls=%fused_computation.31 | convolution fusion | flops 8869179392 | bytes 30044672 | tf_op jit(solution)/shard_map/dot_general | solution.py:31
  452.8 5.8 fusion.39
  458.6 5.8 add_convert_fusion
  470.4 3.3 convolution_convert_fusion.7
  488.2 27.5 %shard_map.244 = bf16[1056,1536]{1,0:T(8,128)(2,1)} custom-call(s32[2,4]{1,0:T(2,128)} %copy-done.14, s32[4,512]{1,0:T(4,128)} %copy-done.11, s32[1024,1]{1,0:T(8,128)} %copy.41.segcol, bf16[1056,1536]{1,0:T(8,128)(2,1)} %fusion.6.q_ref.k_ref.v_ref, bf16[1056,1536]{1,0:T(8,128)(2,1)} %fusion.6.q_ref.k_ref.v_ref, bf16[1056,1536]{1,0:T(8,128)(2,1)} %fusion.6.q_ref.k_ref.v_ref, ...), custom_call_target="tpu_custom_call" | custom-call | tf_op jit(solution)/shard_map/pallas_call | solution.py:201
  515.7 7.0 %convolution_convert_fusion.3 = bf16[1024,1536]{1,0:T(8,128)(2,1)S(1)} fusion(bf16[1056,1536]{1,0:T(8,128)(2,1)} %shard_map.244, bf16[32,1024]{1,0:T(8,128)(2,1)S(1)} %bitcast.255, bf16[1024,1024]{1,0:T(8,128)(2,1)} %bitcast.216), kind=kOutput, calls=%fused_computation.53 | convolution fusion | flops 3327787008 | bytes 8552448 | tf_op jit(solution)/shard_map/dot_general | solution.py:37
  534.2 27.2 %shard_map.245 = bf16[1056,1536]{1,0:T(8,128)(2,1)} custom-call(s32[2,4]{1,0:T(2,128)} %copy-done.14, s32[4,512]{1,0:T(4,128)} %copy-done.11, s32[1024,1]{1,0:T(8,128)} %copy.41.segcol, bf16[1056,1536]{1,0:T(8,128)(2,1)} %copy-done, bf16[1056,1536]{1,0:T(8,128)(2,1)} %copy-done, bf16[1056,1536]{1,0:T(8,128)(2,1)} %copy-done, ...), custom_call_target="tpu_custom_call" | custom-call | tf_op jit(solution)/shard_map/pallas_call | solution.py:201
  561.3 7.9 %convolution_add_fusion.7 = f32[1056,1024]{1,0:T(8,128)} fusion(f32[1056,1024]{1,0:T(8,128)} %get-tuple-element.183, bf16[1056,1536]{1,0:T(8,128)(2,1)S(1)} %copy-done.24, bf16[1024,1536]{1,0:T(8,128)(2,1)} %bitcast.209), kind=kOutput, calls=%fused_computation.28 | convolution fusion | flops 3322970112 | bytes 15040512 | tf_op jit(solution)/shard_map/dot_general | solution.py:31
  582.9 5.7 convolution_convert_fusion.2
  593.5 5.7 convolution_add_fusion.6
  615.5 5.7 collective-permute-done.39
  622.0 7.0 %collective-permute-done.44 = bf16[2,2,2,1,1,32,768]{6,5,4,3,2,1,0:T(8,128)(2,1)S(1)} collective-permute-done((bf16[2,2,2,1,1,32,768]{6,5,4,3,2,1,0:T(8,128)(2,1)S(1)}, bf16[2,2,2,1,1,32,768]{6,5,4,3,2,1,0:T(8,128)(2,1)S(1)}, u32[]{:S(2)}, u32[]{:S(2)}) %collective-permute-start.44) | collective-permute-done | bytes 393248 | tf_op jit(solution)/shard_map/ppermute | solution.py:493
  631.5 7.6 %collective-permute-done.54 = bf16[2,1,1,1,1,32,1152]{6,5,4,3,2,1,0:T(8,128)(2,1)S(1)} collective-permute-done((bf16[2,1,1,1,1,32,1152]{6,5,4,3,2,1,0:T(8,128)(2,1)S(1)}, bf16[2,1,1,1,1,32,1152]{6,5,4,3,2,1,0:T(8,128)(2,1)S(1)}, u32[]{:S(2)}, u32[]{:S(2)}) %collective-permute-start.54) | collective-permute-done | bytes 147488 | tf_op jit(solution)/shard_map/ppermute | solution.py:493
  642.7 4.5 collective-permute-done.55
  (484 shorter events, 184.2 us)
Async XLA Ops:
  3.0 20.2 %collective-permute-start.5 = (bf16[1,1,1,1,1,1,384]{6,5,4,3,2,1,0:T(2,128)(2,1)S(1)}, bf16[1,1,1,1,1,1,384]{6,5,4,3,2,1,0:T(2,128)(2,1)S(1)}, u32[]{:S(2)}, u32[]{:S(2)}) collective-permute-start(bf16[1,1,1,1,1,1,384]{6,5,4,3,2,1,0:T(2,128)(2,1)S(1)} %reshape_broadcast_in_dim.4), channel_id=1, source_target_pairs={{0,16},{1,17},{2,18},{3,19},{4,20},{5,21},{6,22},{7,23},{8,24},{9,... | collective-permute-start | bytes 2312 | tf_op jit(solution)/shard_map/ppermute | solution.py:493
  9.4 10.5 %collective-permute-start.6 = (bf16[1,1,1,1,1,32,1536]{6,5,4,3,2,1,0:T(8,128)(2,1)S(1)}, bf16[1,1,1,1,1,32,1536]{6,5,4,3,2,1,0:T(8,128)(2,1)S(1)}, u32[]{:S(2)}, u32[]{:S(2)}) collective-permute-start(bf16[1,1,1,1,1,32,1536]{6,5,4,3,2,1,0:T(8,128)(2,1)S(1)} %get-tuple-element.192), channel_id=1, source_target_pairs={{0,16},{1,17},{2,18},{3,19},{4,20},{5,21},{6,22},{7,23},{8,24},{9,... | collective-permute-start | bytes 294920 | tf_op jit(solution)/shard_map/ppermute | solution.py:493
  9.5 11.4 %collective-permute-start = (bf16[1,1,1,1,1,32,1536]{6,5,4,3,2,1,0:T(8,128)(2,1)S(1)}, bf16[1,1,1,1,1,32,1536]{6,5,4,3,2,1,0:T(8,128)(2,1)S(1)}, u32[]{:S(2)}, u32[]{:S(2)}) collective-permute-start(bf16[1,1,1,1,1,32,1536]{6,5,4,3,2,1,0:T(8,128)(2,1)S(1)} %get-tuple-element.194), channel_id=1, source_target_pairs={{0,16},{1,17},{2,18},{3,19},{4,20},{5,21},{6,22},{7,23},{8,24},{9,... | collective-permute-start | bytes 294920 | tf_op jit(solution)/shard_map/ppermute | solution.py:493
  33.2 17.7 %collective-permute-start.15 = (bf16[1,1,1,1,1,32,1152]{6,5,4,3,2,1,0:T(8,128)(2,1)S(1)}, bf16[1,1,1,1,1,32,1152]{6,5,4,3,2,1,0:T(8,128)(2,1)S(1)}, u32[]{:S(2)}, u32[]{:S(2)}) collective-permute-start(bf16[1,1,1,1,1,32,1152]{6,5,4,3,2,1,0:T(8,128)(2,1)S(1)} %maximum_bitcast_fusion), channel_id=1, source_target_pairs={{0,16},{1,17},{2,18},{3,19},{4,20},{5,21},{6,22},{7,23},{8,24},{9,... | collective-permute-start | bytes 221192 | tf_op jit(solution)/shard_map/ppermute | solution.py:493
  35.5 25.8 %collective-permute-start.18 = (bf16[1,1,1,1,1,32,4096]{6,5,4,3,2,1,0:T(8,128)(2,1)}, bf16[1,1,1,1,1,32,4096]{6,5,4,3,2,1,0:T(8,128)(2,1)S(1)}, u32[]{:S(2)}, u32[]{:S(2)}) collective-permute-start(bf16[1,1,1,1,1,32,4096]{6,5,4,3,2,1,0:T(8,128)(2,1)} %bitcast.240), channel_id=1, source_target_pairs={{0,16},{1,17},{2,18},{3,19},{4,20},{5,21},{6,22},{7,23},{8,24},{9,... | collective-permute-start | bytes 786440 | tf_op jit(solution)/shard_map/ppermute | solution.py:493
  36.1 25.1 %collective-permute-start.21 = (bf16[1,1,1,1,1,128,1024]{6,5,4,3,2,1,0:T(8,128)(2,1)}, bf16[1,1,1,1,1,128,1024]{6,5,4,3,2,1,0:T(8,128)(2,1)S(1)}, u32[]{:S(2)}, u32[]{:S(2)}) collective-permute-start(bf16[1,1,1,1,1,128,1024]{6,5,4,3,2,1,0:T(8,128)(2,1)} %bitcast.241), channel_id=1, source_target_pairs={{0,16},{1,17},{2,18},{3,19},{4,20},{5,21},{6,22},{7,23},{8,24},{9,... | collective-permute-start | bytes 786440 | tf_op jit(solution)/shard_map/ppermute | solution.py:493
  40.5 20.7 %collective-permute-start.9 = (bf16[2,2,1,1,1,1,384]{6,1,0,5,4,3,2:T(2,128)(2,1)S(1)}, bf16[2,2,1,1,1,1,384]{6,1,0,5,4,3,2:T(2,128)(2,1)S(1)}, u32[]{:S(2)}, u32[]{:S(2)}) collective-permute-start(bf16[2,2,1,1,1,1,384]{6,1,0,5,4,3,2:T(2,128)(2,1)S(1)} %broadcast_select_fusion.28), channel_id=1, source_target_pairs={{0,2},{1,3},{2,0},{3,1},{4,6},{5,7},{6,4},{7,5},{8,10},{9,11},{10,... | collective-permute-start | bytes 9224 | tf_op jit(solution)/shard_map/ppermute | solution.py:493
  47.0 16.6 %collective-permute-start.12 = (bf16[2,2,2,1,1,32,1536]{6,5,2,1,0,4,3:T(8,128)(2,1)S(1)}, bf16[2,2,2,1,1,32,1536]{6,5,2,1,0,4,3:T(8,128)(2,1)S(1)}, u32[]{:S(2)}, u32[]{:S(2)}) collective-permute-start(bf16[2,2,2,1,1,32,1536]{6,5,2,1,0,4,3:T(8,128)(2,1)S(1)} %broadcast_select_fusion.14), channel_id=1, source_target_pairs={{0,2},{1,3},{2,0},{3,1},{4,6},{5,7},{6,4},{7,5},{8,10},{9,11},{10,... | collective-permute-start | bytes 2359304 | tf_op jit(solution)/shard_map/ppermute | solution.py:493
  50.9 13.3 %collective-permute-start.3 = (bf16[2,2,1,2,1,32,1536]{6,5,3,1,0,4,2:T(8,128)(2,1)S(1)}, bf16[2,2,1,2,1,32,1536]{6,5,3,1,0,4,2:T(8,128)(2,1)S(1)}, u32[]{:S(2)}, u32[]{:S(2)}) collective-permute-start(bf16[2,2,1,2,1,32,1536]{6,5,3,1,0,4,2:T(8,128)(2,1)S(1)} %broadcast_select_fusion.15), channel_id=1, source_target_pairs={{0,4},{1,5},{2,6},{3,7},{4,0},{5,1},{6,2},{7,3},{8,12},{9,13},{10,... | collective-permute-start | bytes 2359304 | tf_op jit(solution)/shard_map/ppermute | solution.py:493
  61.5 14.9 %collective-permute-start.22 = (bf16[2,1,1,1,1,128,1024]{6,5,0,4,3,2,1:T(8,128)(2,1)S(1)}, bf16[2,1,1,1,1,128,1024]{6,5,0,4,3,2,1:T(8,128)(2,1)S(1)}, u32[]{:S(2)}, u32[]{:S(2)}) collective-permute-start(bf16[2,1,1,1,1,128,1024]{6,5,0,4,3,2,1:T(8,128)(2,1)S(1)} %broadcast_select_fusion.17), channel_id=1, source_target_pairs={{0,8},{1,9},{2,10},{3,11},{4,12},{5,13},{6,14},{7,15},{8,0},{9,1},... | collective-permute-start | bytes 1572872 | tf_op jit(solution)/shard_map/ppermute | solution.py:493
  61.6 25.9 %collective-permute-start.19 = (bf16[2,1,1,1,1,32,4096]{6,5,0,4,3,2,1:T(8,128)(2,1)S(1)}, bf16[2,1,1,1,1,32,4096]{6,5,0,4,3,2,1:T(8,128)(2,1)S(1)}, u32[]{:S(2)}, u32[]{:S(2)}) collective-permute-start(bf16[2,1,1,1,1,32,4096]{6,5,0,4,3,2,1:T(8,128)(2,1)S(1)} %broadcast_select_fusion.18), channel_id=1, source_target_pairs={{0,8},{1,9},{2,10},{3,11},{4,12},{5,13},{6,14},{7,15},{8,0},{9,1},... | collective-permute-start | bytes 1572872 | tf_op jit(solution)/shard_map/ppermute | solution.py:493
  64.4 27.7 %collective-permute-start.4 = (bf16[2,2,2,2,1,32,1536]{6,5,3,2,1,0,4:T(8,128)(2,1)S(1)}, bf16[2,2,2,2,1,32,1536]{6,5,3,2,1,0,4:T(8,128)(2,1)S(1)}, u32[]{:S(2)}, u32[]{:S(2)}) collective-permute-start(bf16[2,2,2,2,1,32,1536]{6,5,3,2,1,0,4:T(8,128)(2,1)S(1)} %broadcast_select_fusion.10), channel_id=1, source_target_pairs={{0,1},{1,0},{2,3},{3,2},{4,5},{5,4},{6,7},{7,6},{8,9},{9,8},{10,11... | collective-permute-start | bytes 4718600 | tf_op jit(solution)/shard_map/ppermute | solution.py:493
  64.5 27.6 %collective-permute-start.14 = (bf16[2,2,2,2,1,32,1536]{6,5,3,2,1,0,4:T(8,128)(2,1)S(1)}, bf16[2,2,2,2,1,32,1536]{6,5,3,2,1,0,4:T(8,128)(2,1)S(1)}, u32[]{:S(2)}, u32[]{:S(2)}) collective-permute-start(bf16[2,2,2,2,1,32,1536]{6,5,3,2,1,0,4:T(8,128)(2,1)S(1)} %broadcast_select_fusion.9), channel_id=1, source_target_pairs={{0,1},{1,0},{2,3},{3,2},{4,5},{5,4},{6,7},{7,6},{8,9},{9,8},{10,11... | collective-permute-start | bytes 4718600 | tf_op jit(solution)/shard_map/ppermute | solution.py:493
  65.0 24.8 %collective-permute-start.11 = (bf16[2,2,1,2,1,1,384]{6,3,1,0,5,4,2:T(2,128)(2,1)S(1)}, bf16[2,2,1,2,1,1,384]{6,3,1,0,5,4,2:T(2,128)(2,1)S(1)}, u32[]{:S(2)}, u32[]{:S(2)}) collective-permute-start(bf16[2,2,1,2,1,1,384]{6,3,1,0,5,4,2:T(2,128)(2,1)S(1)} %broadcast_select_fusion.27), channel_id=1, source_target_pairs={{0,4},{1,5},{2,6},{3,7},{4,0},{5,1},{6,2},{7,3},{8,12},{9,13},{10,... | collective-permute-start | bytes 18440 | tf_op jit(solution)/shard_map/ppermute | solution.py:493
  76.4 13.4 %collective-permute-start.16 = (bf16[2,1,1,1,1,32,1152]{6,5,0,4,3,2,1:T(8,128)(2,1)S(1)}, bf16[2,1,1,1,1,32,1152]{6,5,0,4,3,2,1:T(8,128)(2,1)S(1)}, u32[]{:S(2)}, u32[]{:S(2)}) collective-permute-start(bf16[2,1,1,1,1,32,1152]{6,5,0,4,3,2,1:T(8,128)(2,1)S(1)} %broadcast_select_fusion.24), channel_id=1, source_target_pairs={{0,8},{1,9},{2,10},{3,11},{4,12},{5,13},{6,14},{7,15},{8,0},{9,1},... | collective-permute-start | bytes 442376 | tf_op jit(solution)/shard_map/ppermute | solution.py:493
  90.0 29.9 %collective-permute-start.20 = (bf16[2,2,1,1,1,32,4096]{6,5,1,0,4,3,2:T(8,128)(2,1)}, bf16[2,2,1,1,1,32,4096]{6,5,1,0,4,3,2:T(8,128)(2,1)}, u32[]{:S(2)}, u32[]{:S(2)}) collective-permute-start(bf16[2,2,1,1,1,32,4096]{6,5,1,0,4,3,2:T(8,128)(2,1)} %broadcast_select_fusion.13), channel_id=1, source_target_pairs={{0,2},{1,3},{2,0},{3,1},{4,6},{5,7},{6,4},{7,5},{8,10},{9,11},{10,... | collective-permute-start | bytes 3145736 | tf_op jit(solution)/shard_map/ppermute | solution.py:493
  91.2 25.5 %collective-permute-start.23 = (bf16[2,2,1,1,1,128,1024]{6,5,1,0,4,3,2:T(8,128)(2,1)}, bf16[2,2,1,1,1,128,1024]{6,5,1,0,4,3,2:T(8,128)(2,1)}, u32[]{:S(2)}, u32[]{:S(2)}) collective-permute-start(bf16[2,2,1,1,1,128,1024]{6,5,1,0,4,3,2:T(8,128)(2,1)} %broadcast_select_fusion.12), channel_id=1, source_target_pairs={{0,4},{1,5},{2,6},{3,7},{4,0},{5,1},{6,2},{7,3},{8,12},{9,13},{10,... | collective-permute-start | bytes 3145736 | tf_op jit(solution)/shard_map/ppermute | solution.py:493
  122.9 108.3 %collective-permute-start.26 = (bf16[2,2,1,2,1,32,4096]{6,5,4,3,2,1,0:T(8,128)(2,1)}, bf16[2,2,1,2,1,32,4096]{6,5,4,3,2,1,0:T(8,128)(2,1)}, u32[]{:S(2)}, u32[]{:S(2)}) collective-permute-start(bf16[2,2,1,2,1,32,4096]{6,5,4,3,2,1,0:T(8,128)(2,1)} %broadcast_select_fusion.8), channel_id=1, source_target_pairs={{0,4},{1,5},{2,6},{3,7},{4,0},{5,1},{6,2},{7,3},{8,12},{9,13},{10,... | collective-permute-start | bytes 6291464 | tf_op jit(solution)/shard_map/ppermute | solution.py:493
  123.9 107.4 %collective-permute-start.27 = (bf16[2,2,2,1,1,128,1024]{6,5,4,3,2,1,0:T(8,128)(2,1)}, bf16[2,2,2,1,1,128,1024]{6,5,4,3,2,1,0:T(8,128)(2,1)}, u32[]{:S(2)}, u32[]{:S(2)}) collective-permute-start(bf16[2,2,2,1,1,128,1024]{6,5,4,3,2,1,0:T(8,128)(2,1)} %broadcast_select_fusion.7), channel_id=1, source_target_pairs={{0,2},{1,3},{2,0},{3,1},{4,6},{5,7},{6,4},{7,5},{8,10},{9,11},{10,... | collective-permute-start | bytes 6291464 | tf_op jit(solution)/shard_map/ppermute | solution.py:493
  125.5 51.5 %collective-permute-start.17 = (bf16[2,2,1,1,1,32,1152]{6,5,1,0,4,3,2:T(8,128)(2,1)S(1)}, bf16[2,2,1,1,1,32,1152]{6,5,1,0,4,3,2:T(8,128)(2,1)S(1)}, u32[]{:S(2)}, u32[]{:S(2)}) collective-permute-start(bf16[2,2,1,1,1,32,1152]{6,5,1,0,4,3,2:T(8,128)(2,1)S(1)} %broadcast_select_fusion.21), channel_id=1, source_target_pairs={{0,2},{1,3},{2,0},{3,1},{4,6},{5,7},{6,4},{7,5},{8,10},{9,11},{10,... | collective-permute-start | bytes 884744 | tf_op jit(solution)/shard_map/ppermute | solution.py:493
  178.6 27.6 %collective-permute-start.24 = (bf16[2,2,1,2,1,32,1152]{6,5,4,3,2,1,0:T(8,128)(2,1)}, bf16[2,2,1,2,1,32,1152]{6,5,4,3,2,1,0:T(8,128)(2,1)}, u32[]{:S(2)}, u32[]{:S(2)}) collective-permute-start(bf16[2,2,1,2,1,32,1152]{6,5,4,3,2,1,0:T(8,128)(2,1)} %broadcast_select_fusion.16), channel_id=1, source_target_pairs={{0,4},{1,5},{2,6},{3,7},{4,0},{5,1},{6,2},{7,3},{8,12},{9,13},{10,... | collective-permute-start | bytes 1769480 | tf_op jit(solution)/shard_map/ppermute | solution.py:493
  209.1 33.6 %collective-permute-start.25 = (bf16[2,2,2,2,1,32,1152]{6,5,3,2,1,0,4:T(8,128)(2,1)}, bf16[2,2,2,2,1,32,1152]{6,5,3,2,1,0,4:T(8,128)(2,1)}, u32[]{:S(2)}, u32[]{:S(2)}) collective-permute-start(bf16[2,2,2,2,1,32,1152]{6,5,3,2,1,0,4:T(8,128)(2,1)} %broadcast_select_fusion.11), channel_id=1, source_target_pairs={{0,1},{1,0},{2,3},{3,2},{4,5},{5,4},{6,7},{7,6},{8,9},{9,8},{10,11... | collective-permute-start | bytes 3538952 | tf_op jit(solution)/shard_map/ppermute | solution.py:493
  236.2 13.7 %collective-permute-start.29 = (bf16[2,2,2,2,1,128,1024]{6,5,4,3,2,1,0:T(8,128)(2,1)}, bf16[2,2,2,2,1,128,1024]{6,5,4,3,2,1,0:T(8,128)(2,1)}, u32[]{:S(2)}, u32[]{:S(2)}) collective-permute-start(bf16[2,2,2,2,1,128,1024]{6,5,4,3,2,1,0:T(8,128)(2,1)} %broadcast_select_fusion.2), channel_id=1, source_target_pairs={{0,1},{1,0},{2,3},{3,2},{4,5},{5,4},{6,7},{7,6},{8,9},{9,8},{10,11... | collective-permute-start | bytes 12582920 | tf_op jit(solution)/shard_map/ppermute | solution.py:493
  241.5 13.7 %collective-permute-start.28 = (bf16[2,2,2,2,1,32,4096]{6,5,4,3,2,1,0:T(8,128)(2,1)}, bf16[2,2,2,2,1,32,4096]{6,5,4,3,2,1,0:T(8,128)(2,1)}, u32[]{:S(2)}, u32[]{:S(2)}) collective-permute-start(bf16[2,2,2,2,1,32,4096]{6,5,4,3,2,1,0:T(8,128)(2,1)} %broadcast_select_fusion.3), channel_id=1, source_target_pairs={{0,1},{1,0},{2,3},{3,2},{4,5},{5,4},{6,7},{7,6},{8,9},{9,8},{10,11... | collective-permute-start | bytes 12582920 | tf_op jit(solution)/shard_map/ppermute | solution.py:493
  386.9 37.7 %collective-permute-start.30 = (bf16[2,2,2,2,1,128,1024]{6,5,4,3,2,1,0:T(8,128)(2,1)}, bf16[2,2,2,2,1,128,1024]{6,5,4,3,2,1,0:T(8,128)(2,1)}, u32[]{:S(2)}, u32[]{:S(2)}) collective-permute-start(bf16[2,2,2,2,1,128,1024]{6,5,4,3,2,1,0:T(8,128)(2,1)} %constant_dynamic-slice_fusion.37), channel_id=1, source_target_pairs={{0,1},{1,0},{2,3},{3,2},{4,5},{5,4},{6,7},{7,6},{8,9},{9,8},{10,11... | collective-permute-start | bytes 12582920 | tf_op jit(solution)/shard_map/ppermute | solution.py:493
  422.6 36.0 %collective-permute-start.31 = (bf16[2,2,2,2,1,32,4096]{6,5,4,3,2,1,0:T(8,128)(2,1)}, bf16[2,2,2,2,1,32,4096]{6,5,4,3,2,1,0:T(8,128)(2,1)}, u32[]{:S(2)}, u32[]{:S(2)}) collective-permute-start(bf16[2,2,2,2,1,32,4096]{6,5,4,3,2,1,0:T(8,128)(2,1)} %constant_dynamic-slice_fusion.36), channel_id=1, source_target_pairs={{0,1},{1,0},{2,3},{3,2},{4,5},{5,4},{6,7},{7,6},{8,9},{9,8},{10,11... | collective-permute-start | bytes 12582920 | tf_op jit(solution)/shard_map/ppermute | solution.py:493
  434.3 48.3 %collective-permute-start.32 = (bf16[2,2,2,1,1,128,1024]{6,5,4,3,2,1,0:T(8,128)(2,1)}, bf16[2,2,2,1,1,128,1024]{6,5,4,3,2,1,0:T(8,128)(2,1)}, u32[]{:S(2)}, u32[]{:S(2)}) collective-permute-start(bf16[2,2,2,1,1,128,1024]{6,5,4,3,2,1,0:T(8,128)(2,1)} %constant_dynamic-slice_fusion.35), channel_id=1, source_target_pairs={{0,2},{1,3},{2,0},{3,1},{4,6},{5,7},{6,4},{7,5},{8,10},{9,11},{10,... | collective-permute-start | bytes 6291464 | tf_op jit(solution)/shard_map/ppermute | solution.py:493
  467.9 57.7 %collective-permute-start.34 = (bf16[2,2,1,2,1,32,4096]{6,5,4,3,2,1,0:T(8,128)(2,1)}, bf16[2,2,1,2,1,32,4096]{6,5,4,3,2,1,0:T(8,128)(2,1)}, u32[]{:S(2)}, u32[]{:S(2)}) collective-permute-start(bf16[2,2,1,2,1,32,4096]{6,5,4,3,2,1,0:T(8,128)(2,1)} %constant_dynamic-slice_fusion.34), channel_id=1, source_target_pairs={{0,4},{1,5},{2,6},{3,7},{4,0},{5,1},{6,2},{7,3},{8,12},{9,13},{10,... | collective-permute-start | bytes 6291464 | tf_op jit(solution)/shard_map/ppermute | solution.py:493
  478.9 47.1 %collective-permute-start.33 = (bf16[2,2,2,2,1,32,1152]{6,5,4,3,2,1,0:T(8,128)(2,1)}, bf16[2,2,2,2,1,32,1152]{6,5,4,3,2,1,0:T(8,128)(2,1)}, u32[]{:S(2)}, u32[]{:S(2)}) collective-permute-start(bf16[2,2,2,2,1,32,1152]{6,5,4,3,2,1,0:T(8,128)(2,1)} %constant_dynamic-slice_fusion.33), channel_id=1, source_target_pairs={{0,1},{1,0},{2,3},{3,2},{4,5},{5,4},{6,7},{7,6},{8,9},{9,8},{10,11... | collective-permute-start | bytes 3538952 | tf_op jit(solution)/shard_map/ppermute | solution.py:493
  486.2 83.1 %collective-permute-start.36 = (bf16[2,2,1,1,1,128,1024]{6,5,4,3,2,1,0:T(8,128)(2,1)}, bf16[2,2,1,1,1,128,1024]{6,5,4,3,2,1,0:T(8,128)(2,1)}, u32[]{:S(2)}, u32[]{:S(2)}) collective-permute-start(bf16[2,2,1,1,1,128,1024]{6,5,4,3,2,1,0:T(8,128)(2,1)} %constant_dynamic-slice_fusion.32), channel_id=1, source_target_pairs={{0,4},{1,5},{2,6},{3,7},{4,0},{5,1},{6,2},{7,3},{8,12},{9,13},{10,... | collective-permute-start | bytes 3145736 | tf_op jit(solution)/shard_map/ppermute | solution.py:493
  528.9 63.0 %collective-permute-start.52 = (bf16[2,2,1,2,1,32,1152]{6,5,4,3,2,1,0:T(8,128)(2,1)}, bf16[2,2,1,2,1,32,1152]{6,5,4,3,2,1,0:T(8,128)(2,1)}, u32[]{:S(2)}, u32[]{:S(2)}) collective-permute-start(bf16[2,2,1,2,1,32,1152]{6,5,4,3,2,1,0:T(8,128)(2,1)} %constant_dynamic-slice_fusion.30), channel_id=1, source_target_pairs={{0,4},{1,5},{2,6},{3,7},{4,0},{5,1},{6,2},{7,3},{8,12},{9,13},{10,... | collective-permute-start | bytes 1769480 | tf_op jit(solution)/shard_map/ppermute | solution.py:493
  532.4 41.5 %collective-permute-start.35 = (bf16[2,2,1,1,1,32,4096]{6,5,4,3,2,1,0:T(8,128)(2,1)}, bf16[2,2,1,1,1,32,4096]{6,5,4,3,2,1,0:T(8,128)(2,1)}, u32[]{:S(2)}, u32[]{:S(2)}) collective-permute-start(bf16[2,2,1,1,1,32,4096]{6,5,4,3,2,1,0:T(8,128)(2,1)} %constant_dynamic-slice_fusion.29), channel_id=1, source_target_pairs={{0,2},{1,3},{2,0},{3,1},{4,6},{5,7},{6,4},{7,5},{8,10},{9,11},{10,... | collective-permute-start | bytes 3145736 | tf_op jit(solution)/shard_map/ppermute | solution.py:493
  534.2 42.2 %collective-permute-start.37 = (bf16[2,2,2,2,1,32,1536]{6,5,4,3,2,1,0:T(8,128)(2,1)}, bf16[2,2,2,2,1,32,1536]{6,5,4,3,2,1,0:T(8,128)(2,1)}, u32[]{:S(2)}, u32[]{:S(2)}) collective-permute-start(bf16[2,2,2,2,1,32,1536]{6,5,4,3,2,1,0:T(8,128)(2,1)} %constant_dynamic-slice_fusion.31), channel_id=1, source_target_pairs={{0,1},{1,0},{2,3},{3,2},{4,5},{5,4},{6,7},{7,6},{8,9},{9,8},{10,11... | collective-permute-start | bytes 4718600 | tf_op jit(solution)/shard_map/ppermute | solution.py:493
  572.0 35.3 %collective-permute-start.58 = (bf16[2,1,1,1,1,128,1024]{6,5,4,3,2,1,0:T(8,128)(2,1)}, bf16[2,1,1,1,1,128,1024]{6,5,4,3,2,1,0:T(8,128)(2,1)}, u32[]{:S(2)}, u32[]{:S(2)}) collective-permute-start(bf16[2,1,1,1,1,128,1024]{6,5,4,3,2,1,0:T(8,128)(2,1)} %constant_dynamic-slice_fusion.27), channel_id=1, source_target_pairs={{0,8},{1,9},{2,10},{3,11},{4,12},{5,13},{6,14},{7,15},{8,0},{9,1},... | collective-permute-start | bytes 1572872 | tf_op jit(solution)/shard_map/ppermute | solution.py:493
  576.2 31.6 %collective-permute-start.56 = (bf16[2,1,1,1,1,32,4096]{6,5,4,3,2,1,0:T(8,128)(2,1)}, bf16[2,1,1,1,1,32,4096]{6,5,4,3,2,1,0:T(8,128)(2,1)}, u32[]{:S(2)}, u32[]{:S(2)}) collective-permute-start(bf16[2,1,1,1,1,32,4096]{6,5,4,3,2,1,0:T(8,128)(2,1)} %constant_dynamic-slice_fusion.28), channel_id=1, source_target_pairs={{0,8},{1,9},{2,10},{3,11},{4,12},{5,13},{6,14},{7,15},{8,0},{9,1},... | collective-permute-start | bytes 1572872 | tf_op jit(solution)/shard_map/ppermute | solution.py:493
  581.2 21.6 %collective-permute-start.38 = (bf16[2,2,1,2,1,32,1536]{6,5,4,3,2,1,0:T(8,128)(2,1)}, bf16[2,2,1,2,1,32,1536]{6,5,4,3,2,1,0:T(8,128)(2,1)}, u32[]{:S(2)}, u32[]{:S(2)}) collective-permute-start(bf16[2,2,1,2,1,32,1536]{6,5,4,3,2,1,0:T(8,128)(2,1)} %constant_dynamic-slice_fusion.26), channel_id=1, source_target_pairs={{0,4},{1,5},{2,6},{3,7},{4,0},{5,1},{6,2},{7,3},{8,12},{9,13},{10,... | collective-permute-start | bytes 2359304 | tf_op jit(solution)/shard_map/ppermute | solution.py:493
  591.5 12.1 %collective-permute-start.41 = (bf16[2,2,2,2,1,32,768]{6,5,4,3,2,1,0:T(8,128)(2,1)S(1)}, bf16[2,2,2,2,1,32,768]{6,5,4,3,2,1,0:T(8,128)(2,1)S(1)}, u32[]{:S(2)}, u32[]{:S(2)}) collective-permute-start(bf16[2,2,2,2,1,32,768]{6,5,4,3,2,1,0:T(8,128)(2,1)S(1)} %constant_dynamic-slice_fusion.24), channel_id=1, source_target_pairs={{0,1},{1,0},{2,3},{3,2},{4,5},{5,4},{6,7},{7,6},{8,9},{9,8},{10,11... | collective-permute-start | bytes 2359304 | tf_op jit(solution)/shard_map/ppermute | solution.py:493
  591.9 10.5 %collective-permute-start.60 = (f32[2,2,2,2,1,1,384]{6,5,4,3,2,1,0:T(1,128)S(1)}, f32[2,2,2,2,1,1,384]{6,5,4,3,2,1,0:T(1,128)S(1)}, u32[]{:S(2)}, u32[]{:S(2)}) collective-permute-start(f32[2,2,2,2,1,1,384]{6,5,4,3,2,1,0:T(1,128)S(1)} %fusion.21), channel_id=1, source_target_pairs={{0,1},{1,0},{2,3},{3,2},{4,5},{5,4},{6,7},{7,6},{8,9},{9,8},{10,11... | collective-permute-start | bytes 73736 | tf_op jit(solution)/shard_map/ppermute | solution.py:493
  602.8 11.4 %collective-permute-start.53 = (bf16[2,2,1,1,1,32,1152]{6,5,4,3,2,1,0:T(8,128)(2,1)S(1)}, bf16[2,2,1,1,1,32,1152]{6,5,4,3,2,1,0:T(8,128)(2,1)S(1)}, u32[]{:S(2)}, u32[]{:S(2)}) collective-permute-start(bf16[2,2,1,1,1,32,1152]{6,5,4,3,2,1,0:T(8,128)(2,1)S(1)} %constant_dynamic-slice_fusion.12), channel_id=1, source_target_pairs={{0,2},{1,3},{2,0},{3,1},{4,6},{5,7},{6,4},{7,5},{8,10},{9,11},{10,... | collective-permute-start | bytes 884744 | tf_op jit(solution)/shard_map/ppermute | solution.py:493
  605.3 15.8 %collective-permute-start.39 = (bf16[2,2,1,1,1,32,1536]{6,5,4,3,2,1,0:T(8,128)(2,1)S(1)}, bf16[2,2,1,1,1,32,1536]{6,5,4,3,2,1,0:T(8,128)(2,1)S(1)}, u32[]{:S(2)}, u32[]{:S(2)}) collective-permute-start(bf16[2,2,1,1,1,32,1536]{6,5,4,3,2,1,0:T(8,128)(2,1)S(1)} %constant_dynamic-slice_fusion.23), channel_id=1, source_target_pairs={{0,2},{1,3},{2,0},{3,1},{4,6},{5,7},{6,4},{7,5},{8,10},{9,11},{10,... | collective-permute-start | bytes 1179656 | tf_op jit(solution)/shard_map/ppermute | solution.py:493
  607.4 21.6 %collective-permute-start.44 = (bf16[2,2,2,1,1,32,768]{6,5,4,3,2,1,0:T(8,128)(2,1)S(1)}, bf16[2,2,2,1,1,32,768]{6,5,4,3,2,1,0:T(8,128)(2,1)S(1)}, u32[]{:S(2)}, u32[]{:S(2)}) collective-permute-start(bf16[2,2,2,1,1,32,768]{6,5,4,3,2,1,0:T(8,128)(2,1)S(1)} %constant_dynamic-slice_fusion.21), channel_id=1, source_target_pairs={{0,2},{1,3},{2,0},{3,1},{4,6},{5,7},{6,4},{7,5},{8,10},{9,11},{10,... | collective-permute-start | bytes 1179656 | tf_op jit(solution)/shard_map/ppermute | solution.py:493
  610.2 49.0 %collective-permute-start.59 = (bf16[1,1,1,1,1,128,1024]{6,5,4,3,2,1,0:T(8,128)(2,1)S(1)}, bf16[1,1,1,1,1,128,1024]{6,5,4,3,2,1,0:T(8,128)(2,1)S(1)}, u32[]{:S(2)}, u32[]{:S(2)}) collective-permute-start(bf16[1,1,1,1,1,128,1024]{6,5,4,3,2,1,0:T(8,128)(2,1)S(1)} %constant_dynamic-slice_fusion.8), channel_id=1, source_target_pairs={{0,16},{1,17},{2,18},{3,19},{4,20},{5,21},{6,22},{7,23},{8,24},{9,... | collective-permute-start | bytes 786440 | tf_op jit(solution)/shard_map/ppermute | solution.py:493
  612.4 18.0 %collective-permute-start.43 = (bf16[2,2,1,2,1,32,768]{6,5,4,3,2,1,0:T(8,128)(2,1)S(1)}, bf16[2,2,1,2,1,32,768]{6,5,4,3,2,1,0:T(8,128)(2,1)S(1)}, u32[]{:S(2)}, u32[]{:S(2)}) collective-permute-start(bf16[2,2,1,2,1,32,768]{6,5,4,3,2,1,0:T(8,128)(2,1)S(1)} %constant_dynamic-slice_fusion.22), channel_id=1, source_target_pairs={{0,4},{1,5},{2,6},{3,7},{4,0},{5,1},{6,2},{7,3},{8,12},{9,13},{10,... | collective-permute-start | bytes 1179656 | tf_op jit(solution)/shard_map/ppermute | solution.py:493
  614.2 45.9 %collective-permute-start.57 = (bf16[1,1,1,1,1,32,4096]{6,5,4,3,2,1,0:T(8,128)(2,1)S(1)}, bf16[1,1,1,1,1,32,4096]{6,5,4,3,2,1,0:T(8,128)(2,1)S(1)}, u32[]{:S(2)}, u32[]{:S(2)}) collective-permute-start(bf16[1,1,1,1,1,32,4096]{6,5,4,3,2,1,0:T(8,128)(2,1)S(1)} %constant_dynamic-slice_fusion.9), channel_id=1, source_target_pairs={{0,16},{1,17},{2,18},{3,19},{4,20},{5,21},{6,22},{7,23},{8,24},{9,... | collective-permute-start | bytes 786440 | tf_op jit(solution)/shard_map/ppermute | solution.py:493
  628.9 10.1 %collective-permute-start.54 = (bf16[2,1,1,1,1,32,1152]{6,5,4,3,2,1,0:T(8,128)(2,1)S(1)}, bf16[2,1,1,1,1,32,1152]{6,5,4,3,2,1,0:T(8,128)(2,1)S(1)}, u32[]{:S(2)}, u32[]{:S(2)}) collective-permute-start(bf16[2,1,1,1,1,32,1152]{6,5,4,3,2,1,0:T(8,128)(2,1)S(1)} %constant_dynamic-slice_fusion.11), channel_id=1, source_target_pairs={{0,8},{1,9},{2,10},{3,11},{4,12},{5,13},{6,14},{7,15},{8,0},{9,1},... | collective-permute-start | bytes 442376 | tf_op jit(solution)/shard_map/ppermute | solution.py:493
  631.0 10.3 %collective-permute-start.46 = (bf16[2,2,1,1,1,32,768]{6,5,4,3,2,1,0:T(8,128)(2,1)S(1)}, bf16[2,2,1,1,1,32,768]{6,5,4,3,2,1,0:T(8,128)(2,1)S(1)}, u32[]{:S(2)}, u32[]{:S(2)}) collective-permute-start(bf16[2,2,1,1,1,32,768]{6,5,4,3,2,1,0:T(8,128)(2,1)S(1)} %constant_dynamic-slice_fusion.19), channel_id=1, source_target_pairs={{0,2},{1,3},{2,0},{3,1},{4,6},{5,7},{6,4},{7,5},{8,10},{9,11},{10,... | collective-permute-start | bytes 589832 | tf_op jit(solution)/shard_map/ppermute | solution.py:493
  639.1 11.2 %collective-permute-start.42 = (bf16[2,1,1,1,1,32,1536]{6,5,4,3,2,1,0:T(8,128)(2,1)S(1)}, bf16[2,1,1,1,1,32,1536]{6,5,4,3,2,1,0:T(8,128)(2,1)S(1)}, u32[]{:S(2)}, u32[]{:S(2)}) collective-permute-start(bf16[2,1,1,1,1,32,1536]{6,5,4,3,2,1,0:T(8,128)(2,1)S(1)} %constant_dynamic-slice_fusion.20), channel_id=1, source_target_pairs={{0,8},{1,9},{2,10},{3,11},{4,12},{5,13},{6,14},{7,15},{8,0},{9,1},... | collective-permute-start | bytes 589832 | tf_op jit(solution)/shard_map/ppermute | solution.py:493
  639.2 11.4 %collective-permute-start.63 = (f32[2,1,1,1,1,1,384]{6,5,4,3,2,1,0:T(1,128)S(1)}, f32[2,1,1,1,1,1,384]{6,5,4,3,2,1,0:T(1,128)S(1)}, u32[]{:S(2)}, u32[]{:S(2)}) collective-permute-start(f32[2,1,1,1,1,1,384]{6,5,4,3,2,1,0:T(1,128)S(1)} %constant_dynamic-slice_fusion.2), channel_id=1, source_target_pairs={{0,8},{1,9},{2,10},{3,11},{4,12},{5,13},{6,14},{7,15},{8,0},{9,1},... | collective-permute-start | bytes 9224 | tf_op jit(solution)/shard_map/ppermute | solution.py:493
  (99 other events, 1498.8 us)

commit v7 on v6

--- a/solution.py
+++ b/solution.py
@@ -610,7 +610,7 @@
     out_part = links.growing(jnp.concatenate([w_out, w_proj], axis=1), 0)
     up_part = links.growing(w_up, 0)
     down_part = links.growing(w_down, 1)
-    rest = (out_part, up_part, down_part)
+    near = (out_part, up_part)
     for hop in range(5):
         for one in sides:
             one.launch()
@@ -621,13 +621,19 @@
             one.merge()
         first = (sides[0].held, sides[1].held)
         small_part.merge(*first)
-        for one in rest:
+        for one in near:
             if hop == 0:
                 one.wait(*first)
+            elif hop < 4:
+                one.merge(*first)
+            if hop < 4:
                 one.launch()
-            if hop == 2 or hop == 3:
-                one.merge(*first)
-                one.launch()
+        if hop == 1:
+            down_part.wait(*first)
+        elif hop == 2 or hop == 3:
+            down_part.merge(*first)
+        if hop > 0 and hop < 4:
+            down_part.launch()
     small_full = small_part.full().reshape(count, -1)
     full_qkv = [rows_of(one.full()) for one in sides]
     full_biases = (
@@ -659,30 +665,25 @@
         cut = slice(side * part, (side + 1) * part)
         bias = jnp.concatenate([full_biases[0, cut], zero_row, full_biases[1, cut]])
         qkv.append((matmul_plain(tokens, full_qkv[side]) + bias).astype(bf16))
-    for one in rest:
-        one.merge(*qkv)
-        one.launch()
     for side in range(2):
-        qkv[side] = after(qkv[side], *[one.before for one in rest])
+        qkv[side] = after(qkv[side], (up_part, down_part)[side].before)
         context, lse, query_lse = attention_forward(
             qkv[side], segrow, segcol, bounds, row_len, span
         )
         if side == 0:
-            out_part.merge(context)
-            out_part.launch()
+            for one in (out_part, down_part):
+                one.merge(context)
+                one.launch()
         contexts.append(context)
         saved.append((lse, query_lse))
-    for one in (up_part, down_part):
-        one.merge(*contexts)
-        one.launch()
-    contexts[1] = after(contexts[1], up_part.before, down_part.before)
+    up_part.merge(*contexts)
+    up_part.launch()
+    contexts[1] = after(contexts[1], up_part.before)
     out_part.merge()
     out_proj = rows_of(out_part.full())
     full_out, full_proj = out_proj[:, :model_width], out_proj[:, model_width:]
     up_part.merge()
-    down_part.merge()
     full_up = rows_of(up_part.full())
-    full_down = rows_of(down_part.full())
     attn_out = (
         matmul_plain(contexts[0], full_out[:part])
         + matmul_plain(contexts[1], full_out[part:])
@@ -692,12 +693,17 @@
         tokens.astype(f32) + attn_out, full_gains[0], full_biases[3]
     )
     first_low = first_out.astype(bf16)
+    down_part.merge(first_low)
+    down_part.launch()
+    first_low = after(first_low, down_part.before)
     up_pre = matmul_plain(first_low, full_up) + full_upbias
     share = 0.5 * (1.0 + lax.erf(up_pre * root_half))
     gelu_out = (up_pre * share).astype(bf16)
     density = jnp.exp(-0.5 * up_pre * up_pre) * density_peak
     slope = (share + up_pre * density).astype(bf16)
     gelu_out, slope = lax.optimization_barrier((gelu_out, slope))
+    down_part.merge()
+    full_down = rows_of(down_part.full())
     ffn_out = matmul_plain(gelu_out, full_down) + full_biases[4]
     second_out, second_normed, second_scale = layer_norm_parts(
         first_out + ffn_out, full_gains[1], full_biases[5]

time: 674 us -> 635 us (0.942)
  waiting for transfers between devices: 142 us -> 126 us
  other arithmetic: 95.5 us -> 81.1 us
    ppermute x65, waiting for transfers between devices: 142 us -> 126 us  [swap(): return lax.ppermute(value, AXES, [(d, d ^ bit) for d in range(self.count)])]
    select_n x27, other arithmetic: 42 us -> 27.2 us  [merge(): self.held = lax.optimization_barrier(jnp.where(own, held, arrived))]
    unnamed x165 -> x141, local copies, waits for them, and re-layouts: 18.9 us -> 15.6 us
  transfers between devices with their start and end apart: 65 -> 65, of which waited for: 20 -> 22; matrix products, arithmetic and copies ran while one was open for 30% -> 34% of each run, Pallas kernels for 15% -> 16%
where the time goes in v7:
time: 635 us; the launch traced here: 630 us
  Pallas kernels  158 us (25%)
  matrix products  148 us (23%)
  waiting for transfers between devices  126 us (20%)
  other arithmetic  81.1 us (13%)
  starting transfers between devices  62.6 us (10%)
  local copies, waits for them, and re-layouts  49.7 us (8%)
    ppermute x65, waiting for transfers between devices, swap(): return lax.ppermute(value, AXES, [(d, d ^ bit) for d in range(self.count)])  126 us
    ppermute x65, starting transfers between devices, swap(): return lax.ppermute(value, AXES, [(d, d ^ bit) for d in range(self.count)])  62.6 us
    pallas_call x2, Pallas kernels, attention_backward(): pl.pallas_call(partial(attend_backward, row_len, qb, kb, lanes, span), ou...  54.9 us
    dot_general x7, matrix products, matmul_right_t(): lax.dot_general(left, right, (((1,), (1,)), ((), ())), preferred_element_...  54.6 us
    dot_general x7, matrix products, matmul_plain(): return jnp.dot(left, right, preferred_element_type=jnp.float32)  49.7 us
    dot_general x7, matrix products, matmul_left_t(): lax.dot_general(left, right, (((0,), (0,)), ((), ())), preferred_element_...  43.8 us
    pallas_call x2, Pallas kernels, attention_forward(): pl.pallas_call(partial(attend_forward, row_len, qb, kb, lanes, span), out...  43.6 us
    pallas_call x3, Pallas kernels, exchanged(): pl.pallas_call(partial(exchange, links.dp, links.fsdp, scatter, add), out...  36.2 us
  transfers between devices with their start and end apart: 65, of which 22 were waited for; matrix products, arithmetic and copies ran while one was open for 34% of the time, Pallas kernels for 16%

profile of v7, /device:TPU:0, one launch (start us, length us, event | category | flops | bytes accessed | tf_op | source)
XLA Modules:
  0.0 630.3 jit_solution(9367353466697264862)
XLA Ops:
  3.0 4.1 collective-permute-start.5
  9.5 3.0 collective-permute-start
  16.6 3.3 collective-permute-done.6
  26.2 7.5 %collective-permute-done.1 = bf16[2,1,1,1,1,32,1536]{6,5,0,4,3,2,1:T(8,128)(2,1)S(1)} collective-permute-done((bf16[2,1,1,1,1,32,1536]{6,5,0,4,3,2,1:T(8,128)(2,1)S(1)}, bf16[2,1,1,1,1,32,1536]{6,5,0,4,3,2,1:T(8,128)(2,1)S(1)}, u32[]{:S(2)}, u32[]{:S(2)}) %collective-permute-start.1) | collective-permute-done | bytes 196640 | tf_op jit(solution)/shard_map/ppermute | solution.py:493
  49.0 4.9 collective-permute-done.23
  56.8 5.2 collective-permute-done.16
  62.1 5.1 collective-permute-done.12
  68.2 5.3 collective-permute-done.20
  76.0 16.0 %collective-permute-done.17 = bf16[2,2,1,1,1,32,4096]{6,5,1,0,4,3,2:T(8,128)(2,1)S(1)} collective-permute-done((bf16[2,2,1,1,1,32,4096]{6,5,1,0,4,3,2:T(8,128)(2,1)S(1)}, bf16[2,2,1,1,1,32,4096]{6,5,1,0,4,3,2:T(8,128)(2,1)S(1)}, u32[]{:S(2)}, u32[]{:S(2)}) %collective-permute-start.17) | collective-permute-done | bytes 1048608 | tf_op jit(solution)/shard_map/ppermute | solution.py:493
  95.6 3.1 broadcast_select_fusion.4
  100.2 6.1 fusion.6.q_ref.k_ref.v_ref
  106.3 21.8 %shard_map.237 = (bf16[1056,512]{1,0:T(8,128)(2,1)S(1)}, f32[4,4,512]{2,1,0:T(4,128)S(1)}, f32[4,1,64]{2,1,0:T(1,128)S(1)}) custom-call(s32[2,4]{1,0:T(2,128)S(1)} %pad_add_fusion.bounds, s32[4,512]{1,0:T(4,128)S(1)} %constant_dynamic-update-slice_fusion.segrow, s32[1024,1]{1,0:T(8,128)S(1)} %copy.41.segcol, bf16[1056,1536]{1,0:T(8,128)(2,1)S(1)} %fusion.6.q_ref.k_ref.v_ref, ...), custom_call_target="tpu_custom_call" | custom-call | tf_op jit(solution)/shard_map/pallas_call | solution.py:124
  128.1 3.3 broadcast_select_fusion.7
  131.4 4.1 fusion.7.q_ref.k_ref.v_ref
  138.3 21.8 %shard_map.238 = (bf16[1056,512]{1,0:T(8,128)(2,1)S(1)}, f32[4,4,512]{2,1,0:T(4,128)S(1)}, f32[4,1,64]{2,1,0:T(1,128)S(1)}) custom-call(s32[2,4]{1,0:T(2,128)S(1)} %pad_add_fusion.bounds, s32[4,512]{1,0:T(4,128)S(1)} %constant_dynamic-update-slice_fusion.segrow, s32[1024,1]{1,0:T(8,128)S(1)} %copy.41.segcol, bf16[1056,1536]{1,0:T(8,128)(2,1)S(1)} %fusion.7.q_ref.k_ref.v_ref, ...), custom_call_target="tpu_custom_call" | custom-call | tf_op jit(solution)/shard_map/pallas_call | solution.py:124
  160.2 5.0 broadcast_select_fusion.3
  175.3 38.4 %collective-permute-done.27 = bf16[2,2,2,1,1,128,1024]{6,5,4,3,2,1,0:T(8,128)(2,1)} collective-permute-done((bf16[2,2,2,1,1,128,1024]{6,5,4,3,2,1,0:T(8,128)(2,1)}, bf16[2,2,2,1,1,128,1024]{6,5,4,3,2,1,0:T(8,128)(2,1)}, u32[]{:S(2)}, u32[]{:S(2)}) %collective-permute-start.27) | collective-permute-done | bytes 2097184 | tf_op jit(solution)/shard_map/ppermute | solution.py:493
  216.0 4.4 broadcast_select_fusion.1
  220.3 17.7 %fusion.4 = (bf16[1056,4096]{1,0:T(8,128)(2,1)}, bf16[1056,4096]{1,0:T(8,128)(2,1)}) fusion(f32[4096]{0:T(1024)S(1)} %fusion.28, bf16[1056,1024]{1,0:T(8,128)(2,1)S(1)} %fusion.11, bf16[1024,4096]{1,0:T(8,128)(2,1)S(1)} %bitcast.184), kind=kOutput, calls=%fused_computation.7 | convolution fusion | flops 8910274560 | bytes 27869184 | tf_op jit(solution)/shard_map/dot_general | solution.py:27
  239.1 16.4 %fusion.45 = (f32[1056]{0:T(1024)S(1)}, f32[1056,1024]{1,0:T(8,128)S(1)}) fusion(f32[1024]{0:T(1024)S(1)} %add.214, bf16[1056,4096]{1,0:T(8,128)(2,1)} %get-tuple-element.116, bf16[4096,1024]{1,0:T(8,128)(2,1)S(1)} %bitcast.188, f32[1024]{0:T(1024)S(1)} %add.206, f32[1024]{0:T(1024)S(1)} %mul.85, f32[1056]{0:T(1024)S(1)} %add_rsqrt_fusion.1, ...), kind=kOutput, calls=%fused_computation.267 | convolution fusion | flops 8865938432 | bytes 25715072 | tf_op jit(solution)/shard_map/dot_general | solution.py:27
  259.9 12.3 %shard_map.239 = bf16[32,32,128]{2,1,0:T(8,128)(2,1)} custom-call(bf16[32,128]{1,0:T(8,128)(2,1)} %slice.232.mine_ref), custom_call_target="tpu_custom_call" | custom-call | tf_op jit(solution)/shard_map/pallas_call | solution.py:400
  273.2 9.6 %shard_map.240 = (f32[3,32,8]{2,1,0:T(8,128)S(1)}, f32[3,1024,8]{2,1,0:T(8,128)S(1)}) custom-call(bf16[1024,128]{1,0:T(8,128)(2,1)S(1)} %slice.231.doc_ref, bf16[1024,8]{1,0:T(8,128)(2,1)S(1)} %convert_convert_fusion.member_ref, bf16[1024,128]{1,0:T(8,128)(2,1)S(1)} %bitcast.175), custom_call_target="tpu_custom_call" | custom-call | tf_op jit(solution)/shard_map/pallas_call | solution.py:296
  283.5 11.3 %shard_map.241 = f32[8,128]{1,0:T(8,128)} custom-call(f32[8,128]{1,0:T(8,128)} %pad.4.mine_ref), custom_call_target="tpu_custom_call" | custom-call | tf_op jit(solution)/shard_map/pallas_call | solution.py:400
  297.1 13.8 %shard_map.242 = (f32[1024,128]{1,0:T(8,128)S(1)}, f32[1024,128]{1,0:T(8,128)S(1)}) custom-call(bf16[1024,128]{1,0:T(8,128)(2,1)S(1)} %slice.231.doc_ref, bf16[8,1024]{1,0:T(8,128)(2,1)S(1)} %convert_convert_fusion.1.member_t_ref, bf16[1024,128]{1,0:T(8,128)(2,1)S(1)} %bitcast.176, f32[3,1024,8]{2,1,0:T(8,128)S(1)} %get-tuple-element.118.sums_ref, ...), custom_call_target="tpu_custom_call" | custom-call | tf_op jit(solution)/shard_map/pallas_call | solution.py:321
  311.7 12.6 %shard_map.243 = f32[32,128]{1,0:T(8,128)} custom-call(bf16[32,32,128]{2,1,0:T(8,128)(2,1)} %bitcast.232), custom_call_target="tpu_custom_call" | custom-call | tf_op jit(solution)/shard_map/pallas_call | solution.py:400
  325.0 4.1 multiply_reduce_fusion
  329.2 2.8 convert_reduce_fusion.1
  332.1 11.8 %convolution_convert_fusion = bf16[4096,1024]{1,0:T(8,128)(2,1)S(1)} fusion(bf16[1056,4096]{1,0:T(8,128)(2,1)S(1)} %bitcast.284, bf16[1056,1024]{1,0:T(8,128)(2,1)S(1)} %get-tuple-element.121), kind=kOutput, calls=%fused_computation.18 | convolution fusion | flops 8862564352 | bytes 19202048 | tf_op jit(solution)/shard_map/dot_general | solution.py:37
  343.9 3.0 constant_dynamic-slice_fusion.37
  349.0 16.0 %convert_reduce_fusion = (f32[4096]{0:T(1024)S(1)}, bf16[1056,4096]{1,0:T(8,128)(2,1)}) fusion(bf16[1056,4096]{1,0:T(8,128)(2,1)} %get-tuple-element.122, bf16[1056,1024]{1,0:T(8,128)(2,1)S(1)} %get-tuple-element.121, bf16[4096,1024]{1,0:T(8,128)(2,1)} %bitcast.189), kind=kOutput, calls=%fused_computation.8 | convolution fusion | flops 8879992832 | bytes 27869184 | tf_op jit(solution)/shard_map/dot_general | solution.py:31
  365.0 13.7 %convolution_convert_fusion.1 = bf16[1024,4096]{1,0:T(8,128)(2,1)S(1)} fusion(bf16[1056,1024]{1,0:T(8,128)(2,1)S(1)} %copy-done.45, bf16[1056,4096]{1,0:T(8,128)(2,1)} %get-tuple-element.124), kind=kOutput, calls=%fused_computation.21 | convolution fusion | flops 8862564352 | bytes 19202048 | tf_op jit(solution)/shard_map/dot_general | solution.py:37
  385.4 6.1 add_convert_fusion.1
  397.0 16.3 %multiply_reduce_fusion.1 = (f32[1024]{0:T(1024)S(1)}, f32[1056]{0:T(1024)S(1)}, f32[1056]{0:T(1024)S(1)}, f32[1024]{0:T(1024)S(1)}, f32[1056,1024]{1,0:T(8,128)}) fusion(f32[1056,1024]{1,0:T(8,128)S(1)} %bitcast.178, f32[1056]{0:T(1024)S(1)} %add_rsqrt_fusion.1, f32[1056]{0:T(1024)S(1)} %broadcast_multiply_fusion.5, f32[1024]{0:T(1024)S(1)} %mul.85, ...), kind=kOutput, calls=%fused_computation.31 | convolution fusion | flops 8869179392 | bytes 30044672 | tf_op jit(solution)/shard_map/dot_general | solution.py:31
  413.5 5.7 fusion.37
  419.2 5.8 add_convert_fusion
  428.9 3.3 convolution_convert_fusion.7
  449.1 27.7 %shard_map.244 = bf16[1056,1536]{1,0:T(8,128)(2,1)} custom-call(s32[2,4]{1,0:T(2,128)} %copy-done.12, s32[4,512]{1,0:T(4,128)} %copy-done.9, s32[1024,1]{1,0:T(8,128)} %copy-done.2, bf16[1056,1536]{1,0:T(8,128)(2,1)} %copy-done.1, bf16[1056,1536]{1,0:T(8,128)(2,1)} %copy-done.1, bf16[1056,1536]{1,0:T(8,128)(2,1)} %copy-done.1, ...), custom_call_target="tpu_custom_call" | custom-call | tf_op jit(solution)/shard_map/pallas_call | solution.py:201
  476.8 7.0 %convolution_convert_fusion.3 = bf16[1024,1536]{1,0:T(8,128)(2,1)S(1)} fusion(bf16[1056,1536]{1,0:T(8,128)(2,1)} %shard_map.244, bf16[32,1024]{1,0:T(8,128)(2,1)S(1)} %bitcast.262, bf16[1024,1024]{1,0:T(8,128)(2,1)} %bitcast.222), kind=kOutput, calls=%fused_computation.53 | convolution fusion | flops 3327787008 | bytes 8552448 | tf_op jit(solution)/shard_map/dot_general | solution.py:37
  494.9 27.2 %shard_map.245 = bf16[1056,1536]{1,0:T(8,128)(2,1)} custom-call(s32[2,4]{1,0:T(2,128)} %copy-done.12, s32[4,512]{1,0:T(4,128)} %copy-done.9, s32[1024,1]{1,0:T(8,128)} %copy-done.2, bf16[1056,1536]{1,0:T(8,128)(2,1)} %copy-done, bf16[1056,1536]{1,0:T(8,128)(2,1)} %copy-done, bf16[1056,1536]{1,0:T(8,128)(2,1)} %copy-done, ...), custom_call_target="tpu_custom_call" | custom-call | tf_op jit(solution)/shard_map/pallas_call | solution.py:201
  522.1 7.8 %convolution_add_fusion.7 = f32[1056,1024]{1,0:T(8,128)} fusion(f32[1056,1024]{1,0:T(8,128)} %get-tuple-element.185, bf16[1056,1536]{1,0:T(8,128)(2,1)S(1)} %copy-done.22, bf16[1024,1536]{1,0:T(8,128)(2,1)} %bitcast.215), kind=kOutput, calls=%fused_computation.28 | convolution fusion | flops 3322970112 | bytes 15040512 | tf_op jit(solution)/shard_map/dot_general | solution.py:31
  543.5 5.7 convolution_convert_fusion.2
  554.1 5.7 convolution_add_fusion.6
  576.0 5.5 collective-permute-done.39
  582.2 7.3 %collective-permute-done.44 = bf16[2,2,2,1,1,32,768]{6,5,4,3,2,1,0:T(8,128)(2,1)S(1)} collective-permute-done((bf16[2,2,2,1,1,32,768]{6,5,4,3,2,1,0:T(8,128)(2,1)S(1)}, bf16[2,2,2,1,1,32,768]{6,5,4,3,2,1,0:T(8,128)(2,1)S(1)}, u32[]{:S(2)}, u32[]{:S(2)}) %collective-permute-start.44) | collective-permute-done | bytes 393248 | tf_op jit(solution)/shard_map/ppermute | solution.py:493
  591.9 7.5 %collective-permute-done.54 = bf16[2,1,1,1,1,32,1152]{6,5,4,3,2,1,0:T(8,128)(2,1)S(1)} collective-permute-done((bf16[2,1,1,1,1,32,1152]{6,5,4,3,2,1,0:T(8,128)(2,1)S(1)}, bf16[2,1,1,1,1,32,1152]{6,5,4,3,2,1,0:T(8,128)(2,1)S(1)}, u32[]{:S(2)}, u32[]{:S(2)}) %collective-permute-start.54) | collective-permute-done | bytes 147488 | tf_op jit(solution)/shard_map/ppermute | solution.py:493
  603.6 3.5 collective-permute-done.55
  607.1 2.8 collective-permute-start.50
  624.1 2.9 collective-permute-done.49
  (460 shorter events, 170.9 us)
Async XLA Ops:
  3.0 20.2 %collective-permute-start.5 = (bf16[1,1,1,1,1,1,384]{6,5,4,3,2,1,0:T(2,128)(2,1)S(1)}, bf16[1,1,1,1,1,1,384]{6,5,4,3,2,1,0:T(2,128)(2,1)S(1)}, u32[]{:S(2)}, u32[]{:S(2)}) collective-permute-start(bf16[1,1,1,1,1,1,384]{6,5,4,3,2,1,0:T(2,128)(2,1)S(1)} %reshape_broadcast_in_dim.4), channel_id=1, source_target_pairs={{0,16},{1,17},{2,18},{3,19},{4,20},{5,21},{6,22},{7,23},{8,24},{9,... | collective-permute-start | bytes 2312 | tf_op jit(solution)/shard_map/ppermute | solution.py:493
  9.4 10.5 %collective-permute-start.6 = (bf16[1,1,1,1,1,32,1536]{6,5,4,3,2,1,0:T(8,128)(2,1)S(1)}, bf16[1,1,1,1,1,32,1536]{6,5,4,3,2,1,0:T(8,128)(2,1)S(1)}, u32[]{:S(2)}, u32[]{:S(2)}) collective-permute-start(bf16[1,1,1,1,1,32,1536]{6,5,4,3,2,1,0:T(8,128)(2,1)S(1)} %get-tuple-element.194), channel_id=1, source_target_pairs={{0,16},{1,17},{2,18},{3,19},{4,20},{5,21},{6,22},{7,23},{8,24},{9,... | collective-permute-start | bytes 294920 | tf_op jit(solution)/shard_map/ppermute | solution.py:493
  9.5 11.4 %collective-permute-start = (bf16[1,1,1,1,1,32,1536]{6,5,4,3,2,1,0:T(8,128)(2,1)S(1)}, bf16[1,1,1,1,1,32,1536]{6,5,4,3,2,1,0:T(8,128)(2,1)S(1)}, u32[]{:S(2)}, u32[]{:S(2)}) collective-permute-start(bf16[1,1,1,1,1,32,1536]{6,5,4,3,2,1,0:T(8,128)(2,1)S(1)} %get-tuple-element.196), channel_id=1, source_target_pairs={{0,16},{1,17},{2,18},{3,19},{4,20},{5,21},{6,22},{7,23},{8,24},{9,... | collective-permute-start | bytes 294920 | tf_op jit(solution)/shard_map/ppermute | solution.py:493
  21.0 12.7 %collective-permute-start.1 = (bf16[2,1,1,1,1,32,1536]{6,5,0,4,3,2,1:T(8,128)(2,1)S(1)}, bf16[2,1,1,1,1,32,1536]{6,5,0,4,3,2,1:T(8,128)(2,1)S(1)}, u32[]{:S(2)}, u32[]{:S(2)}) collective-permute-start(bf16[2,1,1,1,1,32,1536]{6,5,0,4,3,2,1:T(8,128)(2,1)S(1)} %get-tuple-element.216), channel_id=1, source_target_pairs={{0,8},{1,9},{2,10},{3,11},{4,12},{5,13},{6,14},{7,15},{8,0},{9,1},... | collective-permute-start | bytes 589832 | tf_op jit(solution)/shard_map/ppermute | solution.py:493
  21.1 14.9 %collective-permute-start.8 = (bf16[2,1,1,1,1,32,1536]{6,5,0,4,3,2,1:T(8,128)(2,1)S(1)}, bf16[2,1,1,1,1,32,1536]{6,5,0,4,3,2,1:T(8,128)(2,1)S(1)}, u32[]{:S(2)}, u32[]{:S(2)}) collective-permute-start(bf16[2,1,1,1,1,32,1536]{6,5,0,4,3,2,1:T(8,128)(2,1)S(1)} %get-tuple-element.215), channel_id=1, source_target_pairs={{0,8},{1,9},{2,10},{3,11},{4,12},{5,13},{6,14},{7,15},{8,0},{9,1},... | collective-permute-start | bytes 589832 | tf_op jit(solution)/shard_map/ppermute | solution.py:493
  23.2 16.1 %collective-permute-start.7 = (bf16[2,1,1,1,1,1,384]{6,0,5,4,3,2,1:T(2,128)(2,1)S(1)}, bf16[2,1,1,1,1,1,384]{6,0,5,4,3,2,1:T(2,128)(2,1)S(1)}, u32[]{:S(2)}, u32[]{:S(2)}) collective-permute-start(bf16[2,1,1,1,1,1,384]{6,0,5,4,3,2,1:T(2,128)(2,1)S(1)} %broadcast_select_fusion.29), channel_id=1, source_target_pairs={{0,8},{1,9},{2,10},{3,11},{4,12},{5,13},{6,14},{7,15},{8,0},{9,1},... | collective-permute-start | bytes 4616 | tf_op jit(solution)/shard_map/ppermute | solution.py:493
  23.3 15.9 %collective-permute-start.18 = (bf16[1,1,1,1,1,32,1152]{6,5,4,3,2,1,0:T(8,128)(2,1)S(1)}, bf16[1,1,1,1,1,32,1152]{6,5,4,3,2,1,0:T(8,128)(2,1)S(1)}, u32[]{:S(2)}, u32[]{:S(2)}) collective-permute-start(bf16[1,1,1,1,1,32,1152]{6,5,4,3,2,1,0:T(8,128)(2,1)S(1)} %maximum_bitcast_fusion), channel_id=1, source_target_pairs={{0,16},{1,17},{2,18},{3,19},{4,20},{5,21},{6,22},{7,23},{8,24},{9,... | collective-permute-start | bytes 221192 | tf_op jit(solution)/shard_map/ppermute | solution.py:493
  25.0 16.3 %collective-permute-start.15 = (bf16[1,1,1,1,1,32,4096]{6,5,4,3,2,1,0:T(8,128)(2,1)}, bf16[1,1,1,1,1,32,4096]{6,5,4,3,2,1,0:T(8,128)(2,1)S(1)}, u32[]{:S(2)}, u32[]{:S(2)}) collective-permute-start(bf16[1,1,1,1,1,32,4096]{6,5,4,3,2,1,0:T(8,128)(2,1)} %bitcast.247), channel_id=1, source_target_pairs={{0,16},{1,17},{2,18},{3,19},{4,20},{5,21},{6,22},{7,23},{8,24},{9,... | collective-permute-start | bytes 786440 | tf_op jit(solution)/shard_map/ppermute | solution.py:493
  39.4 14.4 %collective-permute-start.9 = (bf16[2,2,1,1,1,1,384]{6,1,0,5,4,3,2:T(2,128)(2,1)S(1)}, bf16[2,2,1,1,1,1,384]{6,1,0,5,4,3,2:T(2,128)(2,1)S(1)}, u32[]{:S(2)}, u32[]{:S(2)}) collective-permute-start(bf16[2,2,1,1,1,1,384]{6,1,0,5,4,3,2:T(2,128)(2,1)S(1)} %broadcast_select_fusion.28), channel_id=1, source_target_pairs={{0,2},{1,3},{2,0},{3,1},{4,6},{5,7},{6,4},{7,5},{8,10},{9,11},{10,... | collective-permute-start | bytes 9224 | tf_op jit(solution)/shard_map/ppermute | solution.py:493
  41.3 12.5 %collective-permute-start.23 = (bf16[1,1,1,1,1,128,1024]{6,5,4,3,2,1,0:T(8,128)(2,1)S(1)}, bf16[1,1,1,1,1,128,1024]{6,5,4,3,2,1,0:T(8,128)(2,1)S(1)}, u32[]{:S(2)}, u32[]{:S(2)}) collective-permute-start(bf16[1,1,1,1,1,128,1024]{6,5,4,3,2,1,0:T(8,128)(2,1)S(1)} %bitcast.248), channel_id=1, source_target_pairs={{0,16},{1,17},{2,18},{3,19},{4,20},{5,21},{6,22},{7,23},{8,24},{9,... | collective-permute-start | bytes 786440 | tf_op jit(solution)/shard_map/ppermute | solution.py:493
  45.4 16.6 %collective-permute-start.16 = (bf16[2,1,1,1,1,32,4096]{6,5,0,4,3,2,1:T(8,128)(2,1)S(1)}, bf16[2,1,1,1,1,32,4096]{6,5,0,4,3,2,1:T(8,128)(2,1)S(1)}, u32[]{:S(2)}, u32[]{:S(2)}) collective-permute-start(bf16[2,1,1,1,1,32,4096]{6,5,0,4,3,2,1:T(8,128)(2,1)S(1)} %broadcast_select_fusion.18), channel_id=1, source_target_pairs={{0,8},{1,9},{2,10},{3,11},{4,12},{5,13},{6,14},{7,15},{8,0},{9,1},... | collective-permute-start | bytes 1572872 | tf_op jit(solution)/shard_map/ppermute | solution.py:493
  46.7 20.5 %collective-permute-start.12 = (bf16[2,2,2,1,1,32,1536]{6,5,2,1,0,4,3:T(8,128)(2,1)S(1)}, bf16[2,2,2,1,1,32,1536]{6,5,2,1,0,4,3:T(8,128)(2,1)S(1)}, u32[]{:S(2)}, u32[]{:S(2)}) collective-permute-start(bf16[2,2,2,1,1,32,1536]{6,5,2,1,0,4,3:T(8,128)(2,1)S(1)} %broadcast_select_fusion.14), channel_id=1, source_target_pairs={{0,2},{1,3},{2,0},{3,1},{4,6},{5,7},{6,4},{7,5},{8,10},{9,11},{10,... | collective-permute-start | bytes 2359304 | tf_op jit(solution)/shard_map/ppermute | solution.py:493
  47.4 20.5 %collective-permute-start.3 = (bf16[2,2,1,2,1,32,1536]{6,5,3,1,0,4,2:T(8,128)(2,1)S(1)}, bf16[2,2,1,2,1,32,1536]{6,5,3,1,0,4,2:T(8,128)(2,1)S(1)}, u32[]{:S(2)}, u32[]{:S(2)}) collective-permute-start(bf16[2,2,1,2,1,32,1536]{6,5,3,1,0,4,2:T(8,128)(2,1)S(1)} %broadcast_select_fusion.15), channel_id=1, source_target_pairs={{0,4},{1,5},{2,6},{3,7},{4,0},{5,1},{6,2},{7,3},{8,12},{9,13},{10,... | collective-permute-start | bytes 2359304 | tf_op jit(solution)/shard_map/ppermute | solution.py:493
  53.9 20.5 %collective-permute-start.11 = (bf16[2,2,1,2,1,1,384]{6,3,1,0,5,4,2:T(2,128)(2,1)S(1)}, bf16[2,2,1,2,1,1,384]{6,3,1,0,5,4,2:T(2,128)(2,1)S(1)}, u32[]{:S(2)}, u32[]{:S(2)}) collective-permute-start(bf16[2,2,1,2,1,1,384]{6,3,1,0,5,4,2:T(2,128)(2,1)S(1)} %broadcast_select_fusion.27), channel_id=1, source_target_pairs={{0,4},{1,5},{2,6},{3,7},{4,0},{5,1},{6,2},{7,3},{8,12},{9,13},{10,... | collective-permute-start | bytes 18440 | tf_op jit(solution)/shard_map/ppermute | solution.py:493
  55.2 18.3 %collective-permute-start.20 = (bf16[2,2,1,1,1,32,1152]{6,5,1,0,4,3,2:T(8,128)(2,1)S(1)}, bf16[2,2,1,1,1,32,1152]{6,5,1,0,4,3,2:T(8,128)(2,1)S(1)}, u32[]{:S(2)}, u32[]{:S(2)}) collective-permute-start(bf16[2,2,1,1,1,32,1152]{6,5,1,0,4,3,2:T(8,128)(2,1)S(1)} %broadcast_select_fusion.21), channel_id=1, source_target_pairs={{0,2},{1,3},{2,0},{3,1},{4,6},{5,7},{6,4},{7,5},{8,10},{9,11},{10,... | collective-permute-start | bytes 884744 | tf_op jit(solution)/shard_map/ppermute | solution.py:493
  62.0 12.3 %collective-permute-start.24 = (bf16[2,1,1,1,1,128,1024]{6,5,0,4,3,2,1:T(8,128)(2,1)S(1)}, bf16[2,1,1,1,1,128,1024]{6,5,0,4,3,2,1:T(8,128)(2,1)S(1)}, u32[]{:S(2)}, u32[]{:S(2)}) collective-permute-start(bf16[2,1,1,1,1,128,1024]{6,5,0,4,3,2,1:T(8,128)(2,1)S(1)} %broadcast_select_fusion.17), channel_id=1, source_target_pairs={{0,8},{1,9},{2,10},{3,11},{4,12},{5,13},{6,14},{7,15},{8,0},{9,1},... | collective-permute-start | bytes 1572872 | tf_op jit(solution)/shard_map/ppermute | solution.py:493
  67.2 24.8 %collective-permute-start.17 = (bf16[2,2,1,1,1,32,4096]{6,5,1,0,4,3,2:T(8,128)(2,1)S(1)}, bf16[2,2,1,1,1,32,4096]{6,5,1,0,4,3,2:T(8,128)(2,1)S(1)}, u32[]{:S(2)}, u32[]{:S(2)}) collective-permute-start(bf16[2,2,1,1,1,32,4096]{6,5,1,0,4,3,2:T(8,128)(2,1)S(1)} %broadcast_select_fusion.13), channel_id=1, source_target_pairs={{0,2},{1,3},{2,0},{3,1},{4,6},{5,7},{6,4},{7,5},{8,10},{9,11},{10,... | collective-permute-start | bytes 3145736 | tf_op jit(solution)/shard_map/ppermute | solution.py:493
  68.1 26.9 %collective-permute-start.4 = (bf16[2,2,2,2,1,32,1536]{6,5,3,2,1,0,4:T(8,128)(2,1)S(1)}, bf16[2,2,2,2,1,32,1536]{6,5,3,2,1,0,4:T(8,128)(2,1)S(1)}, u32[]{:S(2)}, u32[]{:S(2)}) collective-permute-start(bf16[2,2,2,2,1,32,1536]{6,5,3,2,1,0,4:T(8,128)(2,1)S(1)} %broadcast_select_fusion.10), channel_id=1, source_target_pairs={{0,1},{1,0},{2,3},{3,2},{4,5},{5,4},{6,7},{7,6},{8,9},{9,8},{10,11... | collective-permute-start | bytes 4718600 | tf_op jit(solution)/shard_map/ppermute | solution.py:493
  73.5 22.1 %collective-permute-start.14 = (bf16[2,2,2,2,1,32,1536]{6,5,3,2,1,0,4:T(8,128)(2,1)S(1)}, bf16[2,2,2,2,1,32,1536]{6,5,3,2,1,0,4:T(8,128)(2,1)S(1)}, u32[]{:S(2)}, u32[]{:S(2)}) collective-permute-start(bf16[2,2,2,2,1,32,1536]{6,5,3,2,1,0,4:T(8,128)(2,1)S(1)} %broadcast_select_fusion.9), channel_id=1, source_target_pairs={{0,1},{1,0},{2,3},{3,2},{4,5},{5,4},{6,7},{7,6},{8,9},{9,8},{10,11... | collective-permute-start | bytes 4718600 | tf_op jit(solution)/shard_map/ppermute | solution.py:493
  74.5 24.2 %collective-permute-start.13 = (bf16[2,2,2,2,1,1,384]{6,3,2,1,0,5,4:T(2,128)(2,1)S(1)}, bf16[2,2,2,2,1,1,384]{6,3,2,1,0,5,4:T(2,128)(2,1)S(1)}, u32[]{:S(2)}, u32[]{:S(2)}) collective-permute-start(bf16[2,2,2,2,1,1,384]{6,3,2,1,0,5,4:T(2,128)(2,1)S(1)} %broadcast_select_fusion.26), channel_id=1, source_target_pairs={{0,1},{1,0},{2,3},{3,2},{4,5},{5,4},{6,7},{7,6},{8,9},{9,8},{10,11... | collective-permute-start | bytes 36872 | tf_op jit(solution)/shard_map/ppermute | solution.py:493
  74.6 60.9 %collective-permute-start.21 = (bf16[2,2,1,2,1,32,1152]{6,5,3,1,0,4,2:T(8,128)(2,1)S(1)}, bf16[2,2,1,2,1,32,1152]{6,5,3,1,0,4,2:T(8,128)(2,1)}, u32[]{:S(2)}, u32[]{:S(2)}) collective-permute-start(bf16[2,2,1,2,1,32,1152]{6,5,3,1,0,4,2:T(8,128)(2,1)S(1)} %broadcast_select_fusion.16), channel_id=1, source_target_pairs={{0,4},{1,5},{2,6},{3,7},{4,0},{5,1},{6,2},{7,3},{8,12},{9,13},{10,... | collective-permute-start | bytes 1769480 | tf_op jit(solution)/shard_map/ppermute | solution.py:493
  92.0 36.1 %collective-permute-start.25 = (bf16[2,2,1,1,1,128,1024]{6,5,1,0,4,3,2:T(8,128)(2,1)S(1)}, bf16[2,2,1,1,1,128,1024]{6,5,1,0,4,3,2:T(8,128)(2,1)}, u32[]{:S(2)}, u32[]{:S(2)}) collective-permute-start(bf16[2,2,1,1,1,128,1024]{6,5,1,0,4,3,2:T(8,128)(2,1)S(1)} %broadcast_select_fusion.12), channel_id=1, source_target_pairs={{0,4},{1,5},{2,6},{3,7},{4,0},{5,1},{6,2},{7,3},{8,12},{9,13},{10,... | collective-permute-start | bytes 3145736 | tf_op jit(solution)/shard_map/ppermute | solution.py:493
  95.1 65.1 %collective-permute-start.26 = (bf16[2,2,1,2,1,32,4096]{6,5,4,3,2,1,0:T(8,128)(2,1)}, bf16[2,2,1,2,1,32,4096]{6,5,4,3,2,1,0:T(8,128)(2,1)}, u32[]{:S(2)}, u32[]{:S(2)}) collective-permute-start(bf16[2,2,1,2,1,32,4096]{6,5,4,3,2,1,0:T(8,128)(2,1)} %broadcast_select_fusion.8), channel_id=1, source_target_pairs={{0,4},{1,5},{2,6},{3,7},{4,0},{5,1},{6,2},{7,3},{8,12},{9,13},{10,... | collective-permute-start | bytes 6291464 | tf_op jit(solution)/shard_map/ppermute | solution.py:493
  165.2 50.7 %collective-permute-start.28 = (bf16[2,2,2,2,1,32,4096]{6,5,4,3,2,1,0:T(8,128)(2,1)}, bf16[2,2,2,2,1,32,4096]{6,5,4,3,2,1,0:T(8,128)(2,1)}, u32[]{:S(2)}, u32[]{:S(2)}) collective-permute-start(bf16[2,2,2,2,1,32,4096]{6,5,4,3,2,1,0:T(8,128)(2,1)} %broadcast_select_fusion.3), channel_id=1, source_target_pairs={{0,1},{1,0},{2,3},{3,2},{4,5},{5,4},{6,7},{7,6},{8,9},{9,8},{10,11... | collective-permute-start | bytes 12582920 | tf_op jit(solution)/shard_map/ppermute | solution.py:493
  165.5 48.2 %collective-permute-start.27 = (bf16[2,2,2,1,1,128,1024]{6,5,4,3,2,1,0:T(8,128)(2,1)}, bf16[2,2,2,1,1,128,1024]{6,5,4,3,2,1,0:T(8,128)(2,1)}, u32[]{:S(2)}, u32[]{:S(2)}) collective-permute-start(bf16[2,2,2,1,1,128,1024]{6,5,4,3,2,1,0:T(8,128)(2,1)} %broadcast_select_fusion.7), channel_id=1, source_target_pairs={{0,2},{1,3},{2,0},{3,1},{4,6},{5,7},{6,4},{7,5},{8,10},{9,11},{10,... | collective-permute-start | bytes 6291464 | tf_op jit(solution)/shard_map/ppermute | solution.py:493
  215.9 22.2 %collective-permute-start.29 = (bf16[2,2,2,2,1,128,1024]{6,5,4,3,2,1,0:T(8,128)(2,1)S(1)}, bf16[2,2,2,2,1,128,1024]{6,5,4,3,2,1,0:T(8,128)(2,1)S(1)}, u32[]{:S(2)}, u32[]{:S(2)}) collective-permute-start(bf16[2,2,2,2,1,128,1024]{6,5,4,3,2,1,0:T(8,128)(2,1)S(1)} %broadcast_select_fusion.2), channel_id=1, source_target_pairs={{0,1},{1,0},{2,3},{3,2},{4,5},{5,4},{6,7},{7,6},{8,9},{9,8},{10,11... | collective-permute-start | bytes 12582920 | tf_op jit(solution)/shard_map/ppermute | solution.py:493
  348.5 36.9 %collective-permute-start.30 = (bf16[2,2,2,2,1,128,1024]{6,5,4,3,2,1,0:T(8,128)(2,1)}, bf16[2,2,2,2,1,128,1024]{6,5,4,3,2,1,0:T(8,128)(2,1)}, u32[]{:S(2)}, u32[]{:S(2)}) collective-permute-start(bf16[2,2,2,2,1,128,1024]{6,5,4,3,2,1,0:T(8,128)(2,1)} %constant_dynamic-slice_fusion.37), channel_id=1, source_target_pairs={{0,1},{1,0},{2,3},{3,2},{4,5},{5,4},{6,7},{7,6},{8,9},{9,8},{10,11... | collective-permute-start | bytes 12582920 | tf_op jit(solution)/shard_map/ppermute | solution.py:493
  383.5 35.7 %collective-permute-start.31 = (bf16[2,2,2,2,1,32,4096]{6,5,4,3,2,1,0:T(8,128)(2,1)}, bf16[2,2,2,2,1,32,4096]{6,5,4,3,2,1,0:T(8,128)(2,1)}, u32[]{:S(2)}, u32[]{:S(2)}) collective-permute-start(bf16[2,2,2,2,1,32,4096]{6,5,4,3,2,1,0:T(8,128)(2,1)} %constant_dynamic-slice_fusion.36), channel_id=1, source_target_pairs={{0,1},{1,0},{2,3},{3,2},{4,5},{5,4},{6,7},{7,6},{8,9},{9,8},{10,11... | collective-permute-start | bytes 12582920 | tf_op jit(solution)/shard_map/ppermute | solution.py:493
  395.2 48.0 %collective-permute-start.32 = (bf16[2,2,2,1,1,128,1024]{6,5,4,3,2,1,0:T(8,128)(2,1)}, bf16[2,2,2,1,1,128,1024]{6,5,4,3,2,1,0:T(8,128)(2,1)}, u32[]{:S(2)}, u32[]{:S(2)}) collective-permute-start(bf16[2,2,2,1,1,128,1024]{6,5,4,3,2,1,0:T(8,128)(2,1)} %constant_dynamic-slice_fusion.35), channel_id=1, source_target_pairs={{0,2},{1,3},{2,0},{3,1},{4,6},{5,7},{6,4},{7,5},{8,10},{9,11},{10,... | collective-permute-start | bytes 6291464 | tf_op jit(solution)/shard_map/ppermute | solution.py:493
  426.5 60.2 %collective-permute-start.34 = (bf16[2,2,1,2,1,32,4096]{6,5,4,3,2,1,0:T(8,128)(2,1)}, bf16[2,2,1,2,1,32,4096]{6,5,4,3,2,1,0:T(8,128)(2,1)}, u32[]{:S(2)}, u32[]{:S(2)}) collective-permute-start(bf16[2,2,1,2,1,32,4096]{6,5,4,3,2,1,0:T(8,128)(2,1)} %constant_dynamic-slice_fusion.34), channel_id=1, source_target_pairs={{0,4},{1,5},{2,6},{3,7},{4,0},{5,1},{6,2},{7,3},{8,12},{9,13},{10,... | collective-permute-start | bytes 6291464 | tf_op jit(solution)/shard_map/ppermute | solution.py:493
  438.9 48.1 %collective-permute-start.33 = (bf16[2,2,2,2,1,32,1152]{6,5,4,3,2,1,0:T(8,128)(2,1)}, bf16[2,2,2,2,1,32,1152]{6,5,4,3,2,1,0:T(8,128)(2,1)}, u32[]{:S(2)}, u32[]{:S(2)}) collective-permute-start(bf16[2,2,2,2,1,32,1152]{6,5,4,3,2,1,0:T(8,128)(2,1)} %constant_dynamic-slice_fusion.33), channel_id=1, source_target_pairs={{0,1},{1,0},{2,3},{3,2},{4,5},{5,4},{6,7},{7,6},{8,9},{9,8},{10,11... | collective-permute-start | bytes 3538952 | tf_op jit(solution)/shard_map/ppermute | solution.py:493
  446.8 83.2 %collective-permute-start.36 = (bf16[2,2,1,1,1,128,1024]{6,5,4,3,2,1,0:T(8,128)(2,1)}, bf16[2,2,1,1,1,128,1024]{6,5,4,3,2,1,0:T(8,128)(2,1)}, u32[]{:S(2)}, u32[]{:S(2)}) collective-permute-start(bf16[2,2,1,1,1,128,1024]{6,5,4,3,2,1,0:T(8,128)(2,1)} %constant_dynamic-slice_fusion.32), channel_id=1, source_target_pairs={{0,4},{1,5},{2,6},{3,7},{4,0},{5,1},{6,2},{7,3},{8,12},{9,13},{10,... | collective-permute-start | bytes 3145736 | tf_op jit(solution)/shard_map/ppermute | solution.py:493
  490.0 62.2 %collective-permute-start.52 = (bf16[2,2,1,2,1,32,1152]{6,5,4,3,2,1,0:T(8,128)(2,1)}, bf16[2,2,1,2,1,32,1152]{6,5,4,3,2,1,0:T(8,128)(2,1)}, u32[]{:S(2)}, u32[]{:S(2)}) collective-permute-start(bf16[2,2,1,2,1,32,1152]{6,5,4,3,2,1,0:T(8,128)(2,1)} %constant_dynamic-slice_fusion.30), channel_id=1, source_target_pairs={{0,4},{1,5},{2,6},{3,7},{4,0},{5,1},{6,2},{7,3},{8,12},{9,13},{10,... | collective-permute-start | bytes 1769480 | tf_op jit(solution)/shard_map/ppermute | solution.py:493
  493.5 39.0 %collective-permute-start.35 = (bf16[2,2,1,1,1,32,4096]{6,5,4,3,2,1,0:T(8,128)(2,1)}, bf16[2,2,1,1,1,32,4096]{6,5,4,3,2,1,0:T(8,128)(2,1)}, u32[]{:S(2)}, u32[]{:S(2)}) collective-permute-start(bf16[2,2,1,1,1,32,4096]{6,5,4,3,2,1,0:T(8,128)(2,1)} %constant_dynamic-slice_fusion.29), channel_id=1, source_target_pairs={{0,2},{1,3},{2,0},{3,1},{4,6},{5,7},{6,4},{7,5},{8,10},{9,11},{10,... | collective-permute-start | bytes 3145736 | tf_op jit(solution)/shard_map/ppermute | solution.py:493
  494.9 42.0 %collective-permute-start.37 = (bf16[2,2,2,2,1,32,1536]{6,5,4,3,2,1,0:T(8,128)(2,1)}, bf16[2,2,2,2,1,32,1536]{6,5,4,3,2,1,0:T(8,128)(2,1)}, u32[]{:S(2)}, u32[]{:S(2)}) collective-permute-start(bf16[2,2,2,2,1,32,1536]{6,5,4,3,2,1,0:T(8,128)(2,1)} %constant_dynamic-slice_fusion.31), channel_id=1, source_target_pairs={{0,1},{1,0},{2,3},{3,2},{4,5},{5,4},{6,7},{7,6},{8,9},{9,8},{10,11... | collective-permute-start | bytes 4718600 | tf_op jit(solution)/shard_map/ppermute | solution.py:493
  532.5 35.5 %collective-permute-start.58 = (bf16[2,1,1,1,1,128,1024]{6,5,4,3,2,1,0:T(8,128)(2,1)}, bf16[2,1,1,1,1,128,1024]{6,5,4,3,2,1,0:T(8,128)(2,1)}, u32[]{:S(2)}, u32[]{:S(2)}) collective-permute-start(bf16[2,1,1,1,1,128,1024]{6,5,4,3,2,1,0:T(8,128)(2,1)} %constant_dynamic-slice_fusion.27), channel_id=1, source_target_pairs={{0,8},{1,9},{2,10},{3,11},{4,12},{5,13},{6,14},{7,15},{8,0},{9,1},... | collective-permute-start | bytes 1572872 | tf_op jit(solution)/shard_map/ppermute | solution.py:493
  535.5 33.1 %collective-permute-start.56 = (bf16[2,1,1,1,1,32,4096]{6,5,4,3,2,1,0:T(8,128)(2,1)}, bf16[2,1,1,1,1,32,4096]{6,5,4,3,2,1,0:T(8,128)(2,1)}, u32[]{:S(2)}, u32[]{:S(2)}) collective-permute-start(bf16[2,1,1,1,1,32,4096]{6,5,4,3,2,1,0:T(8,128)(2,1)} %constant_dynamic-slice_fusion.28), channel_id=1, source_target_pairs={{0,8},{1,9},{2,10},{3,11},{4,12},{5,13},{6,14},{7,15},{8,0},{9,1},... | collective-permute-start | bytes 1572872 | tf_op jit(solution)/shard_map/ppermute | solution.py:493
  541.2 22.0 %collective-permute-start.38 = (bf16[2,2,1,2,1,32,1536]{6,5,4,3,2,1,0:T(8,128)(2,1)}, bf16[2,2,1,2,1,32,1536]{6,5,4,3,2,1,0:T(8,128)(2,1)}, u32[]{:S(2)}, u32[]{:S(2)}) collective-permute-start(bf16[2,2,1,2,1,32,1536]{6,5,4,3,2,1,0:T(8,128)(2,1)} %constant_dynamic-slice_fusion.26), channel_id=1, source_target_pairs={{0,4},{1,5},{2,6},{3,7},{4,0},{5,1},{6,2},{7,3},{8,12},{9,13},{10,... | collective-permute-start | bytes 2359304 | tf_op jit(solution)/shard_map/ppermute | solution.py:493
  552.0 11.8 %collective-permute-start.41 = (bf16[2,2,2,2,1,32,768]{6,5,4,3,2,1,0:T(8,128)(2,1)S(1)}, bf16[2,2,2,2,1,32,768]{6,5,4,3,2,1,0:T(8,128)(2,1)S(1)}, u32[]{:S(2)}, u32[]{:S(2)}) collective-permute-start(bf16[2,2,2,2,1,32,768]{6,5,4,3,2,1,0:T(8,128)(2,1)S(1)} %constant_dynamic-slice_fusion.24), channel_id=1, source_target_pairs={{0,1},{1,0},{2,3},{3,2},{4,5},{5,4},{6,7},{7,6},{8,9},{9,8},{10,11... | collective-permute-start | bytes 2359304 | tf_op jit(solution)/shard_map/ppermute | solution.py:493
  552.2 10.8 %collective-permute-start.60 = (f32[2,2,2,2,1,1,384]{6,5,4,3,2,1,0:T(1,128)S(1)}, f32[2,2,2,2,1,1,384]{6,5,4,3,2,1,0:T(1,128)S(1)}, u32[]{:S(2)}, u32[]{:S(2)}) collective-permute-start(f32[2,2,2,2,1,1,384]{6,5,4,3,2,1,0:T(1,128)S(1)} %fusion.21), channel_id=1, source_target_pairs={{0,1},{1,0},{2,3},{3,2},{4,5},{5,4},{6,7},{7,6},{8,9},{9,8},{10,11... | collective-permute-start | bytes 73736 | tf_op jit(solution)/shard_map/ppermute | solution.py:493
  563.1 12.2 %collective-permute-start.53 = (bf16[2,2,1,1,1,32,1152]{6,5,4,3,2,1,0:T(8,128)(2,1)S(1)}, bf16[2,2,1,1,1,32,1152]{6,5,4,3,2,1,0:T(8,128)(2,1)S(1)}, u32[]{:S(2)}, u32[]{:S(2)}) collective-permute-start(bf16[2,2,1,1,1,32,1152]{6,5,4,3,2,1,0:T(8,128)(2,1)S(1)} %constant_dynamic-slice_fusion.12), channel_id=1, source_target_pairs={{0,2},{1,3},{2,0},{3,1},{4,6},{5,7},{6,4},{7,5},{8,10},{9,11},{10,... | collective-permute-start | bytes 884744 | tf_op jit(solution)/shard_map/ppermute | solution.py:493
  566.2 15.3 %collective-permute-start.39 = (bf16[2,2,1,1,1,32,1536]{6,5,4,3,2,1,0:T(8,128)(2,1)S(1)}, bf16[2,2,1,1,1,32,1536]{6,5,4,3,2,1,0:T(8,128)(2,1)S(1)}, u32[]{:S(2)}, u32[]{:S(2)}) collective-permute-start(bf16[2,2,1,1,1,32,1536]{6,5,4,3,2,1,0:T(8,128)(2,1)S(1)} %constant_dynamic-slice_fusion.23), channel_id=1, source_target_pairs={{0,2},{1,3},{2,0},{3,1},{4,6},{5,7},{6,4},{7,5},{8,10},{9,11},{10,... | collective-permute-start | bytes 1179656 | tf_op jit(solution)/shard_map/ppermute | solution.py:493
  568.0 21.6 %collective-permute-start.44 = (bf16[2,2,2,1,1,32,768]{6,5,4,3,2,1,0:T(8,128)(2,1)S(1)}, bf16[2,2,2,1,1,32,768]{6,5,4,3,2,1,0:T(8,128)(2,1)S(1)}, u32[]{:S(2)}, u32[]{:S(2)}) collective-permute-start(bf16[2,2,2,1,1,32,768]{6,5,4,3,2,1,0:T(8,128)(2,1)S(1)} %constant_dynamic-slice_fusion.21), channel_id=1, source_target_pairs={{0,2},{1,3},{2,0},{3,1},{4,6},{5,7},{6,4},{7,5},{8,10},{9,11},{10,... | collective-permute-start | bytes 1179656 | tf_op jit(solution)/shard_map/ppermute | solution.py:493
  571.1 49.1 %collective-permute-start.59 = (bf16[1,1,1,1,1,128,1024]{6,5,4,3,2,1,0:T(8,128)(2,1)S(1)}, bf16[1,1,1,1,1,128,1024]{6,5,4,3,2,1,0:T(8,128)(2,1)S(1)}, u32[]{:S(2)}, u32[]{:S(2)}) collective-permute-start(bf16[1,1,1,1,1,128,1024]{6,5,4,3,2,1,0:T(8,128)(2,1)S(1)} %constant_dynamic-slice_fusion.8), channel_id=1, source_target_pairs={{0,16},{1,17},{2,18},{3,19},{4,20},{5,21},{6,22},{7,23},{8,24},{9,... | collective-permute-start | bytes 786440 | tf_op jit(solution)/shard_map/ppermute | solution.py:493
  573.6 16.9 %collective-permute-start.43 = (bf16[2,2,1,2,1,32,768]{6,5,4,3,2,1,0:T(8,128)(2,1)S(1)}, bf16[2,2,1,2,1,32,768]{6,5,4,3,2,1,0:T(8,128)(2,1)S(1)}, u32[]{:S(2)}, u32[]{:S(2)}) collective-permute-start(bf16[2,2,1,2,1,32,768]{6,5,4,3,2,1,0:T(8,128)(2,1)S(1)} %constant_dynamic-slice_fusion.22), channel_id=1, source_target_pairs={{0,4},{1,5},{2,6},{3,7},{4,0},{5,1},{6,2},{7,3},{8,12},{9,13},{10,... | collective-permute-start | bytes 1179656 | tf_op jit(solution)/shard_map/ppermute | solution.py:493
  575.4 45.7 %collective-permute-start.57 = (bf16[1,1,1,1,1,32,4096]{6,5,4,3,2,1,0:T(8,128)(2,1)S(1)}, bf16[1,1,1,1,1,32,4096]{6,5,4,3,2,1,0:T(8,128)(2,1)S(1)}, u32[]{:S(2)}, u32[]{:S(2)}) collective-permute-start(bf16[1,1,1,1,1,32,4096]{6,5,4,3,2,1,0:T(8,128)(2,1)S(1)} %constant_dynamic-slice_fusion.9), channel_id=1, source_target_pairs={{0,16},{1,17},{2,18},{3,19},{4,20},{5,21},{6,22},{7,23},{8,24},{9,... | collective-permute-start | bytes 786440 | tf_op jit(solution)/shard_map/ppermute | solution.py:493
  599.4 11.8 %collective-permute-start.42 = (bf16[2,1,1,1,1,32,1536]{6,5,4,3,2,1,0:T(8,128)(2,1)S(1)}, bf16[2,1,1,1,1,32,1536]{6,5,4,3,2,1,0:T(8,128)(2,1)S(1)}, u32[]{:S(2)}, u32[]{:S(2)}) collective-permute-start(bf16[2,1,1,1,1,32,1536]{6,5,4,3,2,1,0:T(8,128)(2,1)S(1)} %constant_dynamic-slice_fusion.20), channel_id=1, source_target_pairs={{0,8},{1,9},{2,10},{3,11},{4,12},{5,13},{6,14},{7,15},{8,0},{9,1},... | collective-permute-start | bytes 589832 | tf_op jit(solution)/shard_map/ppermute | solution.py:493
  599.5 11.8 %collective-permute-start.63 = (f32[2,1,1,1,1,1,384]{6,5,4,3,2,1,0:T(1,128)S(1)}, f32[2,1,1,1,1,1,384]{6,5,4,3,2,1,0:T(1,128)S(1)}, u32[]{:S(2)}, u32[]{:S(2)}) collective-permute-start(f32[2,1,1,1,1,1,384]{6,5,4,3,2,1,0:T(1,128)S(1)} %constant_dynamic-slice_fusion.2), channel_id=1, source_target_pairs={{0,8},{1,9},{2,10},{3,11},{4,12},{5,13},{6,14},{7,15},{8,0},{9,1},... | collective-permute-start | bytes 9224 | tf_op jit(solution)/shard_map/ppermute | solution.py:493
  (87 other events, 1189.0 us)

commit v8 on v7

--- a/solution.py
+++ b/solution.py
@@ -676,9 +676,10 @@
                 one.launch()
         contexts.append(context)
         saved.append((lse, query_lse))
-    up_part.merge(*contexts)
-    up_part.launch()
-    contexts[1] = after(contexts[1], up_part.before)
+    for one in (up_part, down_part):
+        one.merge(*contexts)
+        one.launch()
+    contexts[1] = after(contexts[1], up_part.before, down_part.before)
     out_part.merge()
     out_proj = rows_of(out_part.full())
     full_out, full_proj = out_proj[:, :model_width], out_proj[:, model_width:]
@@ -693,9 +694,6 @@
         tokens.astype(f32) + attn_out, full_gains[0], full_biases[3]
     )
     first_low = first_out.astype(bf16)
-    down_part.merge(first_low)
-    down_part.launch()
-    first_low = after(first_low, down_part.before)
     up_pre = matmul_plain(first_low, full_up) + full_upbias
     share = 0.5 * (1.0 + lax.erf(up_pre * root_half))
     gelu_out = (up_pre * share).astype(bf16)

time: 635 us -> 604 us (0.951)
  waiting for transfers between devices: 126 us -> 95 us
    ppermute x65, waiting for transfers between devices: 126 us -> 95 us  [swap(): return lax.ppermute(value, AXES, [(d, d ^ bit) for d in range(self.count)])]
    unnamed x141 -> x127, local copies, waits for them, and re-layouts: 15.6 us -> 14.8 us
  transfers between devices with their start and end apart: 65 -> 65, of which waited for: 22 -> 23; matrix products, arithmetic and copies ran while one was open for 34% -> 36% of each run, Pallas kernels for 16% -> 16%
where the time goes in v8:
time: 604 us; the launch traced here: 599 us
  Pallas kernels  159 us (26%)
  matrix products  150 us (25%)
  waiting for transfers between devices  95 us (16%)
  other arithmetic  80.3 us (13%)
  starting transfers between devices  62.7 us (10%)
  local copies, waits for them, and re-layouts  48.7 us (8%)
    ppermute x65, waiting for transfers between devices, swap(): return lax.ppermute(value, AXES, [(d, d ^ bit) for d in range(self.count)])  95 us
    ppermute x65, starting transfers between devices, swap(): return lax.ppermute(value, AXES, [(d, d ^ bit) for d in range(self.count)])  62.7 us
    pallas_call x2, Pallas kernels, attention_backward(): pl.pallas_call(partial(attend_backward, row_len, qb, kb, lanes, span), ou...  54.7 us
    dot_general x7, matrix products, matmul_right_t(): lax.dot_general(left, right, (((1,), (1,)), ((), ())), preferred_element_...  54.4 us
    dot_general x7, matrix products, matmul_plain(): return jnp.dot(left, right, preferred_element_type=jnp.float32)  50.4 us
    dot_general x7, matrix products, matmul_left_t(): lax.dot_general(left, right, (((0,), (0,)), ((), ())), preferred_element_...  44.8 us
    pallas_call x2, Pallas kernels, attention_forward(): pl.pallas_call(partial(attend_forward, row_len, qb, kb, lanes, span), out...  43.6 us
    pallas_call x3, Pallas kernels, exchanged(): pl.pallas_call(partial(exchange, links.dp, links.fsdp, scatter, add), out...  36.9 us
  transfers between devices with their start and end apart: 65, of which 23 were waited for; matrix products, arithmetic and copies ran while one was open for 36% of the time, Pallas kernels for 16%

profile of v8, /device:TPU:0, one launch (start us, length us, event | category | flops | bytes accessed | tf_op | source)
XLA Modules:
  0.0 599.3 jit_solution(3441042378369650328)
XLA Ops:
  3.0 4.1 collective-permute-start.5
  9.5 3.0 collective-permute-start
  16.4 3.5 collective-permute-done.6
  26.2 7.5 %collective-permute-done.1 = bf16[2,1,1,1,1,32,1536]{6,5,0,4,3,2,1:T(8,128)(2,1)S(1)} collective-permute-done((bf16[2,1,1,1,1,32,1536]{6,5,0,4,3,2,1:T(8,128)(2,1)S(1)}, bf16[2,1,1,1,1,32,1536]{6,5,0,4,3,2,1:T(8,128)(2,1)S(1)}, u32[]{:S(2)}, u32[]{:S(2)}) %collective-permute-start.1) | collective-permute-done | bytes 196640 | tf_op jit(solution)/shard_map/ppermute | solution.py:493
  49.0 4.9 collective-permute-done.23
  56.8 5.2 collective-permute-done.16
  62.1 5.1 collective-permute-done.12
  68.2 5.3 collective-permute-done.20
  76.0 16.0 %collective-permute-done.17 = bf16[2,2,1,1,1,32,4096]{6,5,1,0,4,3,2:T(8,128)(2,1)S(1)} collective-permute-done((bf16[2,2,1,1,1,32,4096]{6,5,1,0,4,3,2:T(8,128)(2,1)S(1)}, bf16[2,2,1,1,1,32,4096]{6,5,1,0,4,3,2:T(8,128)(2,1)S(1)}, u32[]{:S(2)}, u32[]{:S(2)}) %collective-permute-start.17) | collective-permute-done | bytes 1048608 | tf_op jit(solution)/shard_map/ppermute | solution.py:493
  95.7 3.1 broadcast_select_fusion.4
  99.2 6.1 %fusion.6.q_ref.k_ref.v_ref = bf16[1056,1536]{1,0:T(8,128)(2,1)S(1)} fusion(bf16[1024,1536]{1,0:T(8,128)(2,1)} %bitcast.213, f32[1536]{0:T(1024)S(1)} %get-tuple-element.208, bf16[32,1024]{1,0:T(8,128)(2,1)S(1)} %bitcast.258, bf16[1024,1024]{1,0:T(8,128)(2,1)} %bitcast.220), kind=kOutput, calls=%fused_computation.19 | convolution fusion | flops 3329458176 | bytes 8558592 | tf_op jit(solution)/shard_map/dot_general | solution.py:27
  105.2 21.8 %shard_map.237 = (bf16[1056,512]{1,0:T(8,128)(2,1)S(1)}, f32[4,4,512]{2,1,0:T(4,128)S(1)}, f32[4,1,64]{2,1,0:T(1,128)S(1)}) custom-call(s32[2,4]{1,0:T(2,128)S(1)} %pad_add_fusion.bounds, s32[4,512]{1,0:T(4,128)S(1)} %constant_dynamic-update-slice_fusion.segrow, s32[1024,1]{1,0:T(8,128)S(1)} %copy.41.segcol, bf16[1056,1536]{1,0:T(8,128)(2,1)S(1)} %fusion.6.q_ref.k_ref.v_ref, ...), custom_call_target="tpu_custom_call" | custom-call | tf_op jit(solution)/shard_map/pallas_call | solution.py:124
  127.1 3.3 broadcast_select_fusion.7
  131.1 4.0 fusion.7.q_ref.k_ref.v_ref
  135.3 21.8 %shard_map.238 = (bf16[1056,512]{1,0:T(8,128)(2,1)S(1)}, f32[4,4,512]{2,1,0:T(4,128)S(1)}, f32[4,1,64]{2,1,0:T(1,128)S(1)}) custom-call(s32[2,4]{1,0:T(2,128)S(1)} %pad_add_fusion.bounds, s32[4,512]{1,0:T(4,128)S(1)} %constant_dynamic-update-slice_fusion.segrow, s32[1024,1]{1,0:T(8,128)S(1)} %copy.41.segcol, bf16[1056,1536]{1,0:T(8,128)(2,1)S(1)} %fusion.7.q_ref.k_ref.v_ref, ...), custom_call_target="tpu_custom_call" | custom-call | tf_op jit(solution)/shard_map/pallas_call | solution.py:124
  158.4 4.7 broadcast_select_fusion.3
  167.0 5.2 collective-permute-done.22
  181.4 5.2 broadcast_select_fusion.1
  186.7 19.8 %fusion.4 = (bf16[1056,4096]{1,0:T(8,128)(2,1)}, bf16[1056,4096]{1,0:T(8,128)(2,1)}) fusion(f32[4096]{0:T(1024)S(1)} %fusion.28, bf16[1024,4096]{1,0:T(8,128)(2,1)S(1)} %bitcast.184, f32[1056,1024]{1,0:T(8,128)S(1)} %get-tuple-element.216, f32[1024]{0:T(1024)S(1)} %add.206, f32[1024]{0:T(1024)S(1)} %mul.85, f32[1056]{0:T(1024)S(1)} %add_rsqrt_fusion.1, ...), kind=kOutput, calls=%fused_computation.7 | convolution fusion | flops 8915681280 | bytes 30048512 | tf_op jit(solution)/shard_map/dot_general | solution.py:27
  207.5 16.1 %fusion.47 = (f32[1056]{0:T(1024)S(1)}, f32[1056,1024]{1,0:T(8,128)S(1)}) fusion(f32[1024]{0:T(1024)S(1)} %add.214, bf16[1056,4096]{1,0:T(8,128)(2,1)} %get-tuple-element.114, bf16[4096,1024]{1,0:T(8,128)(2,1)S(1)} %bitcast.188, f32[1024]{0:T(1024)S(1)} %add.206, f32[1024]{0:T(1024)S(1)} %mul.85, f32[1056]{0:T(1024)S(1)} %add_rsqrt_fusion.1, ...), kind=kOutput, calls=%fused_computation.267 | convolution fusion | flops 8865938432 | bytes 25715072 | tf_op jit(solution)/shard_map/dot_general | solution.py:27
  227.6 12.9 %shard_map.239 = bf16[32,32,128]{2,1,0:T(8,128)(2,1)} custom-call(bf16[32,128]{1,0:T(8,128)(2,1)} %slice.232.mine_ref), custom_call_target="tpu_custom_call" | custom-call | tf_op jit(solution)/shard_map/pallas_call | solution.py:400
  241.5 9.6 %shard_map.240 = (f32[3,32,8]{2,1,0:T(8,128)S(1)}, f32[3,1024,8]{2,1,0:T(8,128)S(1)}) custom-call(bf16[1024,128]{1,0:T(8,128)(2,1)S(1)} %slice.231.doc_ref, bf16[1024,8]{1,0:T(8,128)(2,1)S(1)} %convert_convert_fusion.member_ref, bf16[1024,128]{1,0:T(8,128)(2,1)S(1)} %bitcast.173), custom_call_target="tpu_custom_call" | custom-call | tf_op jit(solution)/shard_map/pallas_call | solution.py:296
  251.8 11.3 %shard_map.241 = f32[8,128]{1,0:T(8,128)} custom-call(f32[8,128]{1,0:T(8,128)} %pad.4.mine_ref), custom_call_target="tpu_custom_call" | custom-call | tf_op jit(solution)/shard_map/pallas_call | solution.py:400
  265.5 13.8 %shard_map.242 = (f32[1024,128]{1,0:T(8,128)S(1)}, f32[1024,128]{1,0:T(8,128)S(1)}) custom-call(bf16[1024,128]{1,0:T(8,128)(2,1)S(1)} %slice.231.doc_ref, bf16[8,1024]{1,0:T(8,128)(2,1)S(1)} %convert_convert_fusion.1.member_t_ref, bf16[1024,128]{1,0:T(8,128)(2,1)S(1)} %bitcast.174, f32[3,1024,8]{2,1,0:T(8,128)S(1)} %get-tuple-element.116.sums_ref, ...), custom_call_target="tpu_custom_call" | custom-call | tf_op jit(solution)/shard_map/pallas_call | solution.py:321
  280.0 12.6 %shard_map.243 = f32[32,128]{1,0:T(8,128)} custom-call(bf16[32,32,128]{2,1,0:T(8,128)(2,1)} %bitcast.231), custom_call_target="tpu_custom_call" | custom-call | tf_op jit(solution)/shard_map/pallas_call | solution.py:400
  293.3 4.1 multiply_reduce_fusion
  297.5 2.8 convert_reduce_fusion.1
  300.4 11.8 %convolution_convert_fusion = bf16[4096,1024]{1,0:T(8,128)(2,1)S(1)} fusion(bf16[1056,4096]{1,0:T(8,128)(2,1)S(1)} %bitcast.283, bf16[1056,1024]{1,0:T(8,128)(2,1)S(1)} %get-tuple-element.119), kind=kOutput, calls=%fused_computation.18 | convolution fusion | flops 8862564352 | bytes 19202048 | tf_op jit(solution)/shard_map/dot_general | solution.py:37
  312.2 3.0 constant_dynamic-slice_fusion.37
  317.3 15.8 %convert_reduce_fusion = (f32[4096]{0:T(1024)S(1)}, bf16[1056,4096]{1,0:T(8,128)(2,1)}) fusion(bf16[1056,4096]{1,0:T(8,128)(2,1)} %get-tuple-element.120, bf16[1056,1024]{1,0:T(8,128)(2,1)S(1)} %get-tuple-element.119, bf16[4096,1024]{1,0:T(8,128)(2,1)} %bitcast.189), kind=kOutput, calls=%fused_computation.8 | convolution fusion | flops 8879992832 | bytes 27869184 | tf_op jit(solution)/shard_map/dot_general | solution.py:31
  333.1 14.7 %convolution_convert_fusion.1 = bf16[1024,4096]{1,0:T(8,128)(2,1)S(1)} fusion(bf16[1056,4096]{1,0:T(8,128)(2,1)} %get-tuple-element.122, f32[1056,1024]{1,0:T(8,128)S(1)} %bitcast.178, f32[1024]{0:T(1024)S(1)} %add.206, f32[1024]{0:T(1024)S(1)} %mul.85, f32[1056]{0:T(1024)S(1)} %add_rsqrt_fusion.1, f32[1056]{0:T(1024)S(1)} %broadcast_multiply_fusion.5), kind=kOutput, calls=%fused_computation.21 | convolution fusion | flops 8867971072 | bytes 21381376 | tf_op jit(solution)/shard_map/dot_general | solution.py:37
  354.5 6.1 %add_convert_fusion.1 = bf16[2,2,2,2,1,128,1024]{6,5,4,3,2,1,0:T(8,128)(2,1)S(1)} fusion(bf16[2,2,2,2,1,128,1024]{6,5,4,3,2,1,0:T(8,128)(2,1)} %collective-permute-done.30, bf16[2,2,2,2,2,128,1024]{6,5,4,3,2,1,0:T(8,128)(2,1)} %bitcast.193, s32[]{:T(128)S(6)} %select_n.471), kind=kLoop, calls=%fused_computation.15 | loop fusion | flops 8388608 | bytes 12582916 | tf_op jit(solution)/shard_map/convert_element_type | solution.py:469
  366.1 16.2 %multiply_reduce_fusion.1 = (f32[1024]{0:T(1024)S(1)}, f32[1056]{0:T(1024)S(1)}, f32[1056]{0:T(1024)S(1)}, f32[1024]{0:T(1024)S(1)}, f32[1056,1024]{1,0:T(8,128)}) fusion(f32[1056,1024]{1,0:T(8,128)S(1)} %bitcast.180, f32[1056]{0:T(1024)S(1)} %add_rsqrt_fusion.1, f32[1056]{0:T(1024)S(1)} %broadcast_multiply_fusion.5, f32[1024]{0:T(1024)S(1)} %mul.85, ...), kind=kOutput, calls=%fused_computation.31 | convolution fusion | flops 8869179392 | bytes 30044672 | tf_op jit(solution)/shard_map/dot_general | solution.py:31
  382.5 5.8 fusion.39
  388.3 5.8 add_convert_fusion
  400.0 3.3 convolution_convert_fusion.7
  418.2 27.5 %shard_map.244 = bf16[1056,1536]{1,0:T(8,128)(2,1)} custom-call(s32[2,4]{1,0:T(2,128)} %copy-done.12, s32[4,512]{1,0:T(4,128)} %copy-done.9, s32[1024,1]{1,0:T(8,128)} %copy-done.2, bf16[1056,1536]{1,0:T(8,128)(2,1)} %copy-done.1, bf16[1056,1536]{1,0:T(8,128)(2,1)} %copy-done.1, bf16[1056,1536]{1,0:T(8,128)(2,1)} %copy-done.1, ...), custom_call_target="tpu_custom_call" | custom-call | tf_op jit(solution)/shard_map/pallas_call | solution.py:201
  445.7 7.0 %convolution_convert_fusion.3 = bf16[1024,1536]{1,0:T(8,128)(2,1)S(1)} fusion(bf16[1056,1536]{1,0:T(8,128)(2,1)} %shard_map.244, bf16[32,1024]{1,0:T(8,128)(2,1)S(1)} %bitcast.261, bf16[1024,1024]{1,0:T(8,128)(2,1)} %bitcast.221), kind=kOutput, calls=%fused_computation.53 | convolution fusion | flops 3327787008 | bytes 8552448 | tf_op jit(solution)/shard_map/dot_general | solution.py:37
  463.8 27.2 %shard_map.245 = bf16[1056,1536]{1,0:T(8,128)(2,1)} custom-call(s32[2,4]{1,0:T(2,128)} %copy-done.12, s32[4,512]{1,0:T(4,128)} %copy-done.9, s32[1024,1]{1,0:T(8,128)} %copy-done.2, bf16[1056,1536]{1,0:T(8,128)(2,1)} %copy-done, bf16[1056,1536]{1,0:T(8,128)(2,1)} %copy-done, bf16[1056,1536]{1,0:T(8,128)(2,1)} %copy-done, ...), custom_call_target="tpu_custom_call" | custom-call | tf_op jit(solution)/shard_map/pallas_call | solution.py:201
  491.0 7.9 %convolution_add_fusion.7 = f32[1056,1024]{1,0:T(8,128)} fusion(f32[1056,1024]{1,0:T(8,128)} %get-tuple-element.183, bf16[1056,1536]{1,0:T(8,128)(2,1)S(1)} %copy-done.22, bf16[1024,1536]{1,0:T(8,128)(2,1)} %bitcast.214), kind=kOutput, calls=%fused_computation.28 | convolution fusion | flops 3322970112 | bytes 15040512 | tf_op jit(solution)/shard_map/dot_general | solution.py:31
  510.0 2.8 collective-permute-start.38
  513.2 5.7 convolution_convert_fusion.2
  523.8 5.7 convolution_add_fusion.6
  545.0 6.2 %collective-permute-done.39 = bf16[2,2,1,1,1,32,1536]{6,5,4,3,2,1,0:T(8,128)(2,1)S(1)} collective-permute-done((bf16[2,2,1,1,1,32,1536]{6,5,4,3,2,1,0:T(8,128)(2,1)S(1)}, bf16[2,2,1,1,1,32,1536]{6,5,4,3,2,1,0:T(8,128)(2,1)S(1)}, u32[]{:S(2)}, u32[]{:S(2)}) %collective-permute-start.39) | collective-permute-done | bytes 393248 | tf_op jit(solution)/shard_map/ppermute | solution.py:493
  551.4 7.8 %collective-permute-done.44 = bf16[2,2,2,1,1,32,768]{6,5,4,3,2,1,0:T(8,128)(2,1)S(1)} collective-permute-done((bf16[2,2,2,1,1,32,768]{6,5,4,3,2,1,0:T(8,128)(2,1)S(1)}, bf16[2,2,2,1,1,32,768]{6,5,4,3,2,1,0:T(8,128)(2,1)S(1)}, u32[]{:S(2)}, u32[]{:S(2)}) %collective-permute-start.44) | collective-permute-done | bytes 393248 | tf_op jit(solution)/shard_map/ppermute | solution.py:493
  561.5 7.3 %collective-permute-done.54 = bf16[2,1,1,1,1,32,1152]{6,5,4,3,2,1,0:T(8,128)(2,1)S(1)} collective-permute-done((bf16[2,1,1,1,1,32,1152]{6,5,4,3,2,1,0:T(8,128)(2,1)S(1)}, bf16[2,1,1,1,1,32,1152]{6,5,4,3,2,1,0:T(8,128)(2,1)S(1)}, u32[]{:S(2)}, u32[]{:S(2)}) %collective-permute-start.54) | collective-permute-done | bytes 147488 | tf_op jit(solution)/shard_map/ppermute | solution.py:493
  572.5 4.3 collective-permute-done.55
  593.0 2.9 collective-permute-done.49
  (446 shorter events, 167.3 us)
Async XLA Ops:
  3.0 20.2 %collective-permute-start.5 = (bf16[1,1,1,1,1,1,384]{6,5,4,3,2,1,0:T(2,128)(2,1)S(1)}, bf16[1,1,1,1,1,1,384]{6,5,4,3,2,1,0:T(2,128)(2,1)S(1)}, u32[]{:S(2)}, u32[]{:S(2)}) collective-permute-start(bf16[1,1,1,1,1,1,384]{6,5,4,3,2,1,0:T(2,128)(2,1)S(1)} %reshape_broadcast_in_dim.4), channel_id=1, source_target_pairs={{0,16},{1,17},{2,18},{3,19},{4,20},{5,21},{6,22},{7,23},{8,24},{9,... | collective-permute-start | bytes 2312 | tf_op jit(solution)/shard_map/ppermute | solution.py:493
  9.5 11.4 %collective-permute-start = (bf16[1,1,1,1,1,32,1536]{6,5,4,3,2,1,0:T(8,128)(2,1)S(1)}, bf16[1,1,1,1,1,32,1536]{6,5,4,3,2,1,0:T(8,128)(2,1)S(1)}, u32[]{:S(2)}, u32[]{:S(2)}) collective-permute-start(bf16[1,1,1,1,1,32,1536]{6,5,4,3,2,1,0:T(8,128)(2,1)S(1)} %get-tuple-element.194), channel_id=1, source_target_pairs={{0,16},{1,17},{2,18},{3,19},{4,20},{5,21},{6,22},{7,23},{8,24},{9,... | collective-permute-start | bytes 294920 | tf_op jit(solution)/shard_map/ppermute | solution.py:493
  21.0 12.7 %collective-permute-start.1 = (bf16[2,1,1,1,1,32,1536]{6,5,0,4,3,2,1:T(8,128)(2,1)S(1)}, bf16[2,1,1,1,1,32,1536]{6,5,0,4,3,2,1:T(8,128)(2,1)S(1)}, u32[]{:S(2)}, u32[]{:S(2)}) collective-permute-start(bf16[2,1,1,1,1,32,1536]{6,5,0,4,3,2,1:T(8,128)(2,1)S(1)} %get-tuple-element.214), channel_id=1, source_target_pairs={{0,8},{1,9},{2,10},{3,11},{4,12},{5,13},{6,14},{7,15},{8,0},{9,1},... | collective-permute-start | bytes 589832 | tf_op jit(solution)/shard_map/ppermute | solution.py:493
  21.1 14.9 %collective-permute-start.8 = (bf16[2,1,1,1,1,32,1536]{6,5,0,4,3,2,1:T(8,128)(2,1)S(1)}, bf16[2,1,1,1,1,32,1536]{6,5,0,4,3,2,1:T(8,128)(2,1)S(1)}, u32[]{:S(2)}, u32[]{:S(2)}) collective-permute-start(bf16[2,1,1,1,1,32,1536]{6,5,0,4,3,2,1:T(8,128)(2,1)S(1)} %get-tuple-element.213), channel_id=1, source_target_pairs={{0,8},{1,9},{2,10},{3,11},{4,12},{5,13},{6,14},{7,15},{8,0},{9,1},... | collective-permute-start | bytes 589832 | tf_op jit(solution)/shard_map/ppermute | solution.py:493
  23.2 16.1 %collective-permute-start.7 = (bf16[2,1,1,1,1,1,384]{6,0,5,4,3,2,1:T(2,128)(2,1)S(1)}, bf16[2,1,1,1,1,1,384]{6,0,5,4,3,2,1:T(2,128)(2,1)S(1)}, u32[]{:S(2)}, u32[]{:S(2)}) collective-permute-start(bf16[2,1,1,1,1,1,384]{6,0,5,4,3,2,1:T(2,128)(2,1)S(1)} %broadcast_select_fusion.29), channel_id=1, source_target_pairs={{0,8},{1,9},{2,10},{3,11},{4,12},{5,13},{6,14},{7,15},{8,0},{9,1},... | collective-permute-start | bytes 4616 | tf_op jit(solution)/shard_map/ppermute | solution.py:493
  23.3 15.9 %collective-permute-start.18 = (bf16[1,1,1,1,1,32,1152]{6,5,4,3,2,1,0:T(8,128)(2,1)S(1)}, bf16[1,1,1,1,1,32,1152]{6,5,4,3,2,1,0:T(8,128)(2,1)S(1)}, u32[]{:S(2)}, u32[]{:S(2)}) collective-permute-start(bf16[1,1,1,1,1,32,1152]{6,5,4,3,2,1,0:T(8,128)(2,1)S(1)} %maximum_bitcast_fusion), channel_id=1, source_target_pairs={{0,16},{1,17},{2,18},{3,19},{4,20},{5,21},{6,22},{7,23},{8,24},{9,... | collective-permute-start | bytes 221192 | tf_op jit(solution)/shard_map/ppermute | solution.py:493
  25.0 16.3 %collective-permute-start.15 = (bf16[1,1,1,1,1,32,4096]{6,5,4,3,2,1,0:T(8,128)(2,1)}, bf16[1,1,1,1,1,32,4096]{6,5,4,3,2,1,0:T(8,128)(2,1)S(1)}, u32[]{:S(2)}, u32[]{:S(2)}) collective-permute-start(bf16[1,1,1,1,1,32,4096]{6,5,4,3,2,1,0:T(8,128)(2,1)} %bitcast.246), channel_id=1, source_target_pairs={{0,16},{1,17},{2,18},{3,19},{4,20},{5,21},{6,22},{7,23},{8,24},{9,... | collective-permute-start | bytes 786440 | tf_op jit(solution)/shard_map/ppermute | solution.py:493
  39.4 14.4 %collective-permute-start.9 = (bf16[2,2,1,1,1,1,384]{6,1,0,5,4,3,2:T(2,128)(2,1)S(1)}, bf16[2,2,1,1,1,1,384]{6,1,0,5,4,3,2:T(2,128)(2,1)S(1)}, u32[]{:S(2)}, u32[]{:S(2)}) collective-permute-start(bf16[2,2,1,1,1,1,384]{6,1,0,5,4,3,2:T(2,128)(2,1)S(1)} %broadcast_select_fusion.28), channel_id=1, source_target_pairs={{0,2},{1,3},{2,0},{3,1},{4,6},{5,7},{6,4},{7,5},{8,10},{9,11},{10,... | collective-permute-start | bytes 9224 | tf_op jit(solution)/shard_map/ppermute | solution.py:493
  41.3 12.5 %collective-permute-start.23 = (bf16[1,1,1,1,1,128,1024]{6,5,4,3,2,1,0:T(8,128)(2,1)S(1)}, bf16[1,1,1,1,1,128,1024]{6,5,4,3,2,1,0:T(8,128)(2,1)S(1)}, u32[]{:S(2)}, u32[]{:S(2)}) collective-permute-start(bf16[1,1,1,1,1,128,1024]{6,5,4,3,2,1,0:T(8,128)(2,1)S(1)} %bitcast.247), channel_id=1, source_target_pairs={{0,16},{1,17},{2,18},{3,19},{4,20},{5,21},{6,22},{7,23},{8,24},{9,... | collective-permute-start | bytes 786440 | tf_op jit(solution)/shard_map/ppermute | solution.py:493
  45.4 16.6 %collective-permute-start.16 = (bf16[2,1,1,1,1,32,4096]{6,5,0,4,3,2,1:T(8,128)(2,1)S(1)}, bf16[2,1,1,1,1,32,4096]{6,5,0,4,3,2,1:T(8,128)(2,1)S(1)}, u32[]{:S(2)}, u32[]{:S(2)}) collective-permute-start(bf16[2,1,1,1,1,32,4096]{6,5,0,4,3,2,1:T(8,128)(2,1)S(1)} %broadcast_select_fusion.18), channel_id=1, source_target_pairs={{0,8},{1,9},{2,10},{3,11},{4,12},{5,13},{6,14},{7,15},{8,0},{9,1},... | collective-permute-start | bytes 1572872 | tf_op jit(solution)/shard_map/ppermute | solution.py:493
  46.7 20.5 %collective-permute-start.12 = (bf16[2,2,2,1,1,32,1536]{6,5,2,1,0,4,3:T(8,128)(2,1)S(1)}, bf16[2,2,2,1,1,32,1536]{6,5,2,1,0,4,3:T(8,128)(2,1)S(1)}, u32[]{:S(2)}, u32[]{:S(2)}) collective-permute-start(bf16[2,2,2,1,1,32,1536]{6,5,2,1,0,4,3:T(8,128)(2,1)S(1)} %broadcast_select_fusion.14), channel_id=1, source_target_pairs={{0,2},{1,3},{2,0},{3,1},{4,6},{5,7},{6,4},{7,5},{8,10},{9,11},{10,... | collective-permute-start | bytes 2359304 | tf_op jit(solution)/shard_map/ppermute | solution.py:493
  47.4 20.5 %collective-permute-start.3 = (bf16[2,2,1,2,1,32,1536]{6,5,3,1,0,4,2:T(8,128)(2,1)S(1)}, bf16[2,2,1,2,1,32,1536]{6,5,3,1,0,4,2:T(8,128)(2,1)S(1)}, u32[]{:S(2)}, u32[]{:S(2)}) collective-permute-start(bf16[2,2,1,2,1,32,1536]{6,5,3,1,0,4,2:T(8,128)(2,1)S(1)} %broadcast_select_fusion.15), channel_id=1, source_target_pairs={{0,4},{1,5},{2,6},{3,7},{4,0},{5,1},{6,2},{7,3},{8,12},{9,13},{10,... | collective-permute-start | bytes 2359304 | tf_op jit(solution)/shard_map/ppermute | solution.py:493
  53.9 20.5 %collective-permute-start.11 = (bf16[2,2,1,2,1,1,384]{6,3,1,0,5,4,2:T(2,128)(2,1)S(1)}, bf16[2,2,1,2,1,1,384]{6,3,1,0,5,4,2:T(2,128)(2,1)S(1)}, u32[]{:S(2)}, u32[]{:S(2)}) collective-permute-start(bf16[2,2,1,2,1,1,384]{6,3,1,0,5,4,2:T(2,128)(2,1)S(1)} %broadcast_select_fusion.27), channel_id=1, source_target_pairs={{0,4},{1,5},{2,6},{3,7},{4,0},{5,1},{6,2},{7,3},{8,12},{9,13},{10,... | collective-permute-start | bytes 18440 | tf_op jit(solution)/shard_map/ppermute | solution.py:493
  55.2 18.3 %collective-permute-start.20 = (bf16[2,2,1,1,1,32,1152]{6,5,1,0,4,3,2:T(8,128)(2,1)S(1)}, bf16[2,2,1,1,1,32,1152]{6,5,1,0,4,3,2:T(8,128)(2,1)S(1)}, u32[]{:S(2)}, u32[]{:S(2)}) collective-permute-start(bf16[2,2,1,1,1,32,1152]{6,5,1,0,4,3,2:T(8,128)(2,1)S(1)} %broadcast_select_fusion.21), channel_id=1, source_target_pairs={{0,2},{1,3},{2,0},{3,1},{4,6},{5,7},{6,4},{7,5},{8,10},{9,11},{10,... | collective-permute-start | bytes 884744 | tf_op jit(solution)/shard_map/ppermute | solution.py:493
  62.0 12.3 %collective-permute-start.24 = (bf16[2,1,1,1,1,128,1024]{6,5,0,4,3,2,1:T(8,128)(2,1)S(1)}, bf16[2,1,1,1,1,128,1024]{6,5,0,4,3,2,1:T(8,128)(2,1)S(1)}, u32[]{:S(2)}, u32[]{:S(2)}) collective-permute-start(bf16[2,1,1,1,1,128,1024]{6,5,0,4,3,2,1:T(8,128)(2,1)S(1)} %broadcast_select_fusion.17), channel_id=1, source_target_pairs={{0,8},{1,9},{2,10},{3,11},{4,12},{5,13},{6,14},{7,15},{8,0},{9,1},... | collective-permute-start | bytes 1572872 | tf_op jit(solution)/shard_map/ppermute | solution.py:493
  67.2 24.8 %collective-permute-start.17 = (bf16[2,2,1,1,1,32,4096]{6,5,1,0,4,3,2:T(8,128)(2,1)S(1)}, bf16[2,2,1,1,1,32,4096]{6,5,1,0,4,3,2:T(8,128)(2,1)S(1)}, u32[]{:S(2)}, u32[]{:S(2)}) collective-permute-start(bf16[2,2,1,1,1,32,4096]{6,5,1,0,4,3,2:T(8,128)(2,1)S(1)} %broadcast_select_fusion.13), channel_id=1, source_target_pairs={{0,2},{1,3},{2,0},{3,1},{4,6},{5,7},{6,4},{7,5},{8,10},{9,11},{10,... | collective-permute-start | bytes 3145736 | tf_op jit(solution)/shard_map/ppermute | solution.py:493
  68.1 27.0 %collective-permute-start.4 = (bf16[2,2,2,2,1,32,1536]{6,5,3,2,1,0,4:T(8,128)(2,1)S(1)}, bf16[2,2,2,2,1,32,1536]{6,5,3,2,1,0,4:T(8,128)(2,1)S(1)}, u32[]{:S(2)}, u32[]{:S(2)}) collective-permute-start(bf16[2,2,2,2,1,32,1536]{6,5,3,2,1,0,4:T(8,128)(2,1)S(1)} %broadcast_select_fusion.10), channel_id=1, source_target_pairs={{0,1},{1,0},{2,3},{3,2},{4,5},{5,4},{6,7},{7,6},{8,9},{9,8},{10,11... | collective-permute-start | bytes 4718600 | tf_op jit(solution)/shard_map/ppermute | solution.py:493
  73.5 22.1 %collective-permute-start.14 = (bf16[2,2,2,2,1,32,1536]{6,5,3,2,1,0,4:T(8,128)(2,1)S(1)}, bf16[2,2,2,2,1,32,1536]{6,5,3,2,1,0,4:T(8,128)(2,1)S(1)}, u32[]{:S(2)}, u32[]{:S(2)}) collective-permute-start(bf16[2,2,2,2,1,32,1536]{6,5,3,2,1,0,4:T(8,128)(2,1)S(1)} %broadcast_select_fusion.9), channel_id=1, source_target_pairs={{0,1},{1,0},{2,3},{3,2},{4,5},{5,4},{6,7},{7,6},{8,9},{9,8},{10,11... | collective-permute-start | bytes 4718600 | tf_op jit(solution)/shard_map/ppermute | solution.py:493
  74.5 24.3 %collective-permute-start.13 = (bf16[2,2,2,2,1,1,384]{6,3,2,1,0,5,4:T(2,128)(2,1)S(1)}, bf16[2,2,2,2,1,1,384]{6,3,2,1,0,5,4:T(2,128)(2,1)S(1)}, u32[]{:S(2)}, u32[]{:S(2)}) collective-permute-start(bf16[2,2,2,2,1,1,384]{6,3,2,1,0,5,4:T(2,128)(2,1)S(1)} %broadcast_select_fusion.26), channel_id=1, source_target_pairs={{0,1},{1,0},{2,3},{3,2},{4,5},{5,4},{6,7},{7,6},{8,9},{9,8},{10,11... | collective-permute-start | bytes 36872 | tf_op jit(solution)/shard_map/ppermute | solution.py:493
  74.6 60.7 %collective-permute-start.21 = (bf16[2,2,1,2,1,32,1152]{6,5,3,1,0,4,2:T(8,128)(2,1)S(1)}, bf16[2,2,1,2,1,32,1152]{6,5,3,1,0,4,2:T(8,128)(2,1)}, u32[]{:S(2)}, u32[]{:S(2)}) collective-permute-start(bf16[2,2,1,2,1,32,1152]{6,5,3,1,0,4,2:T(8,128)(2,1)S(1)} %broadcast_select_fusion.16), channel_id=1, source_target_pairs={{0,4},{1,5},{2,6},{3,7},{4,0},{5,1},{6,2},{7,3},{8,12},{9,13},{10,... | collective-permute-start | bytes 1769480 | tf_op jit(solution)/shard_map/ppermute | solution.py:493
  92.0 35.1 %collective-permute-start.25 = (bf16[2,2,1,1,1,128,1024]{6,5,1,0,4,3,2:T(8,128)(2,1)S(1)}, bf16[2,2,1,1,1,128,1024]{6,5,1,0,4,3,2:T(8,128)(2,1)}, u32[]{:S(2)}, u32[]{:S(2)}) collective-permute-start(bf16[2,2,1,1,1,128,1024]{6,5,1,0,4,3,2:T(8,128)(2,1)S(1)} %broadcast_select_fusion.12), channel_id=1, source_target_pairs={{0,4},{1,5},{2,6},{3,7},{4,0},{5,1},{6,2},{7,3},{8,12},{9,13},{10,... | collective-permute-start | bytes 3145736 | tf_op jit(solution)/shard_map/ppermute | solution.py:493
  95.1 63.2 %collective-permute-start.26 = (bf16[2,2,1,2,1,32,4096]{6,5,4,3,2,1,0:T(8,128)(2,1)}, bf16[2,2,1,2,1,32,4096]{6,5,4,3,2,1,0:T(8,128)(2,1)}, u32[]{:S(2)}, u32[]{:S(2)}) collective-permute-start(bf16[2,2,1,2,1,32,4096]{6,5,4,3,2,1,0:T(8,128)(2,1)} %broadcast_select_fusion.8), channel_id=1, source_target_pairs={{0,4},{1,5},{2,6},{3,7},{4,0},{5,1},{6,2},{7,3},{8,12},{9,13},{10,... | collective-permute-start | bytes 6291464 | tf_op jit(solution)/shard_map/ppermute | solution.py:493
  130.4 45.0 %collective-permute-start.27 = (bf16[2,2,2,1,1,128,1024]{6,5,4,3,2,1,0:T(8,128)(2,1)}, bf16[2,2,2,1,1,128,1024]{6,5,4,3,2,1,0:T(8,128)(2,1)}, u32[]{:S(2)}, u32[]{:S(2)}) collective-permute-start(bf16[2,2,2,1,1,128,1024]{6,5,4,3,2,1,0:T(8,128)(2,1)} %broadcast_select_fusion.7), channel_id=1, source_target_pairs={{0,2},{1,3},{2,0},{3,1},{4,6},{5,7},{6,4},{7,5},{8,10},{9,11},{10,... | collective-permute-start | bytes 6291464 | tf_op jit(solution)/shard_map/ppermute | solution.py:493
  163.1 18.4 %collective-permute-start.28 = (bf16[2,2,2,2,1,32,4096]{6,5,4,3,2,1,0:T(8,128)(2,1)}, bf16[2,2,2,2,1,32,4096]{6,5,4,3,2,1,0:T(8,128)(2,1)}, u32[]{:S(2)}, u32[]{:S(2)}) collective-permute-start(bf16[2,2,2,2,1,32,4096]{6,5,4,3,2,1,0:T(8,128)(2,1)} %broadcast_select_fusion.3), channel_id=1, source_target_pairs={{0,1},{1,0},{2,3},{3,2},{4,5},{5,4},{6,7},{7,6},{8,9},{9,8},{10,11... | collective-permute-start | bytes 12582920 | tf_op jit(solution)/shard_map/ppermute | solution.py:493
  178.2 28.2 %collective-permute-start.29 = (bf16[2,2,2,2,1,128,1024]{6,5,4,3,2,1,0:T(8,128)(2,1)S(1)}, bf16[2,2,2,2,1,128,1024]{6,5,4,3,2,1,0:T(8,128)(2,1)S(1)}, u32[]{:S(2)}, u32[]{:S(2)}) collective-permute-start(bf16[2,2,2,2,1,128,1024]{6,5,4,3,2,1,0:T(8,128)(2,1)S(1)} %broadcast_select_fusion.2), channel_id=1, source_target_pairs={{0,1},{1,0},{2,3},{3,2},{4,5},{5,4},{6,7},{7,6},{8,9},{9,8},{10,11... | collective-permute-start | bytes 12582920 | tf_op jit(solution)/shard_map/ppermute | solution.py:493
  316.9 37.6 %collective-permute-start.30 = (bf16[2,2,2,2,1,128,1024]{6,5,4,3,2,1,0:T(8,128)(2,1)}, bf16[2,2,2,2,1,128,1024]{6,5,4,3,2,1,0:T(8,128)(2,1)}, u32[]{:S(2)}, u32[]{:S(2)}) collective-permute-start(bf16[2,2,2,2,1,128,1024]{6,5,4,3,2,1,0:T(8,128)(2,1)} %constant_dynamic-slice_fusion.37), channel_id=1, source_target_pairs={{0,1},{1,0},{2,3},{3,2},{4,5},{5,4},{6,7},{7,6},{8,9},{9,8},{10,11... | collective-permute-start | bytes 12582920 | tf_op jit(solution)/shard_map/ppermute | solution.py:493
  352.6 35.7 %collective-permute-start.31 = (bf16[2,2,2,2,1,32,4096]{6,5,4,3,2,1,0:T(8,128)(2,1)}, bf16[2,2,2,2,1,32,4096]{6,5,4,3,2,1,0:T(8,128)(2,1)}, u32[]{:S(2)}, u32[]{:S(2)}) collective-permute-start(bf16[2,2,2,2,1,32,4096]{6,5,4,3,2,1,0:T(8,128)(2,1)} %constant_dynamic-slice_fusion.36), channel_id=1, source_target_pairs={{0,1},{1,0},{2,3},{3,2},{4,5},{5,4},{6,7},{7,6},{8,9},{9,8},{10,11... | collective-permute-start | bytes 12582920 | tf_op jit(solution)/shard_map/ppermute | solution.py:493
  364.3 48.0 %collective-permute-start.32 = (bf16[2,2,2,1,1,128,1024]{6,5,4,3,2,1,0:T(8,128)(2,1)}, bf16[2,2,2,1,1,128,1024]{6,5,4,3,2,1,0:T(8,128)(2,1)}, u32[]{:S(2)}, u32[]{:S(2)}) collective-permute-start(bf16[2,2,2,1,1,128,1024]{6,5,4,3,2,1,0:T(8,128)(2,1)} %constant_dynamic-slice_fusion.35), channel_id=1, source_target_pairs={{0,2},{1,3},{2,0},{3,1},{4,6},{5,7},{6,4},{7,5},{8,10},{9,11},{10,... | collective-permute-start | bytes 6291464 | tf_op jit(solution)/shard_map/ppermute | solution.py:493
  397.6 58.0 %collective-permute-start.34 = (bf16[2,2,1,2,1,32,4096]{6,5,4,3,2,1,0:T(8,128)(2,1)}, bf16[2,2,1,2,1,32,4096]{6,5,4,3,2,1,0:T(8,128)(2,1)}, u32[]{:S(2)}, u32[]{:S(2)}) collective-permute-start(bf16[2,2,1,2,1,32,4096]{6,5,4,3,2,1,0:T(8,128)(2,1)} %constant_dynamic-slice_fusion.34), channel_id=1, source_target_pairs={{0,4},{1,5},{2,6},{3,7},{4,0},{5,1},{6,2},{7,3},{8,12},{9,13},{10,... | collective-permute-start | bytes 6291464 | tf_op jit(solution)/shard_map/ppermute | solution.py:493
  408.6 47.4 %collective-permute-start.33 = (bf16[2,2,2,2,1,32,1152]{6,5,4,3,2,1,0:T(8,128)(2,1)}, bf16[2,2,2,2,1,32,1152]{6,5,4,3,2,1,0:T(8,128)(2,1)}, u32[]{:S(2)}, u32[]{:S(2)}) collective-permute-start(bf16[2,2,2,2,1,32,1152]{6,5,4,3,2,1,0:T(8,128)(2,1)} %constant_dynamic-slice_fusion.33), channel_id=1, source_target_pairs={{0,1},{1,0},{2,3},{3,2},{4,5},{5,4},{6,7},{7,6},{8,9},{9,8},{10,11... | collective-permute-start | bytes 3538952 | tf_op jit(solution)/shard_map/ppermute | solution.py:493
  415.9 83.0 %collective-permute-start.36 = (bf16[2,2,1,1,1,128,1024]{6,5,4,3,2,1,0:T(8,128)(2,1)}, bf16[2,2,1,1,1,128,1024]{6,5,4,3,2,1,0:T(8,128)(2,1)}, u32[]{:S(2)}, u32[]{:S(2)}) collective-permute-start(bf16[2,2,1,1,1,128,1024]{6,5,4,3,2,1,0:T(8,128)(2,1)} %constant_dynamic-slice_fusion.32), channel_id=1, source_target_pairs={{0,4},{1,5},{2,6},{3,7},{4,0},{5,1},{6,2},{7,3},{8,12},{9,13},{10,... | collective-permute-start | bytes 3145736 | tf_op jit(solution)/shard_map/ppermute | solution.py:493
  458.9 63.0 %collective-permute-start.52 = (bf16[2,2,1,2,1,32,1152]{6,5,4,3,2,1,0:T(8,128)(2,1)}, bf16[2,2,1,2,1,32,1152]{6,5,4,3,2,1,0:T(8,128)(2,1)}, u32[]{:S(2)}, u32[]{:S(2)}) collective-permute-start(bf16[2,2,1,2,1,32,1152]{6,5,4,3,2,1,0:T(8,128)(2,1)} %constant_dynamic-slice_fusion.30), channel_id=1, source_target_pairs={{0,4},{1,5},{2,6},{3,7},{4,0},{5,1},{6,2},{7,3},{8,12},{9,13},{10,... | collective-permute-start | bytes 1769480 | tf_op jit(solution)/shard_map/ppermute | solution.py:493
  462.4 39.3 %collective-permute-start.35 = (bf16[2,2,1,1,1,32,4096]{6,5,4,3,2,1,0:T(8,128)(2,1)}, bf16[2,2,1,1,1,32,4096]{6,5,4,3,2,1,0:T(8,128)(2,1)}, u32[]{:S(2)}, u32[]{:S(2)}) collective-permute-start(bf16[2,2,1,1,1,32,4096]{6,5,4,3,2,1,0:T(8,128)(2,1)} %constant_dynamic-slice_fusion.29), channel_id=1, source_target_pairs={{0,2},{1,3},{2,0},{3,1},{4,6},{5,7},{6,4},{7,5},{8,10},{9,11},{10,... | collective-permute-start | bytes 3145736 | tf_op jit(solution)/shard_map/ppermute | solution.py:493
  463.8 42.2 %collective-permute-start.37 = (bf16[2,2,2,2,1,32,1536]{6,5,4,3,2,1,0:T(8,128)(2,1)}, bf16[2,2,2,2,1,32,1536]{6,5,4,3,2,1,0:T(8,128)(2,1)}, u32[]{:S(2)}, u32[]{:S(2)}) collective-permute-start(bf16[2,2,2,2,1,32,1536]{6,5,4,3,2,1,0:T(8,128)(2,1)} %constant_dynamic-slice_fusion.31), channel_id=1, source_target_pairs={{0,1},{1,0},{2,3},{3,2},{4,5},{5,4},{6,7},{7,6},{8,9},{9,8},{10,11... | collective-permute-start | bytes 4718600 | tf_op jit(solution)/shard_map/ppermute | solution.py:493
  501.6 35.3 %collective-permute-start.58 = (bf16[2,1,1,1,1,128,1024]{6,5,4,3,2,1,0:T(8,128)(2,1)}, bf16[2,1,1,1,1,128,1024]{6,5,4,3,2,1,0:T(8,128)(2,1)}, u32[]{:S(2)}, u32[]{:S(2)}) collective-permute-start(bf16[2,1,1,1,1,128,1024]{6,5,4,3,2,1,0:T(8,128)(2,1)} %constant_dynamic-slice_fusion.27), channel_id=1, source_target_pairs={{0,8},{1,9},{2,10},{3,11},{4,12},{5,13},{6,14},{7,15},{8,0},{9,1},... | collective-permute-start | bytes 1572872 | tf_op jit(solution)/shard_map/ppermute | solution.py:493
  504.0 33.7 %collective-permute-start.56 = (bf16[2,1,1,1,1,32,4096]{6,5,4,3,2,1,0:T(8,128)(2,1)}, bf16[2,1,1,1,1,32,4096]{6,5,4,3,2,1,0:T(8,128)(2,1)}, u32[]{:S(2)}, u32[]{:S(2)}) collective-permute-start(bf16[2,1,1,1,1,32,4096]{6,5,4,3,2,1,0:T(8,128)(2,1)} %constant_dynamic-slice_fusion.28), channel_id=1, source_target_pairs={{0,8},{1,9},{2,10},{3,11},{4,12},{5,13},{6,14},{7,15},{8,0},{9,1},... | collective-permute-start | bytes 1572872 | tf_op jit(solution)/shard_map/ppermute | solution.py:493
  510.0 22.8 %collective-permute-start.38 = (bf16[2,2,1,2,1,32,1536]{6,5,4,3,2,1,0:T(8,128)(2,1)}, bf16[2,2,1,2,1,32,1536]{6,5,4,3,2,1,0:T(8,128)(2,1)}, u32[]{:S(2)}, u32[]{:S(2)}) collective-permute-start(bf16[2,2,1,2,1,32,1536]{6,5,4,3,2,1,0:T(8,128)(2,1)} %constant_dynamic-slice_fusion.26), channel_id=1, source_target_pairs={{0,4},{1,5},{2,6},{3,7},{4,0},{5,1},{6,2},{7,3},{8,12},{9,13},{10,... | collective-permute-start | bytes 2359304 | tf_op jit(solution)/shard_map/ppermute | solution.py:493
  521.8 11.3 %collective-permute-start.41 = (bf16[2,2,2,2,1,32,768]{6,5,4,3,2,1,0:T(8,128)(2,1)S(1)}, bf16[2,2,2,2,1,32,768]{6,5,4,3,2,1,0:T(8,128)(2,1)S(1)}, u32[]{:S(2)}, u32[]{:S(2)}) collective-permute-start(bf16[2,2,2,2,1,32,768]{6,5,4,3,2,1,0:T(8,128)(2,1)S(1)} %constant_dynamic-slice_fusion.24), channel_id=1, source_target_pairs={{0,1},{1,0},{2,3},{3,2},{4,5},{5,4},{6,7},{7,6},{8,9},{9,8},{10,11... | collective-permute-start | bytes 2359304 | tf_op jit(solution)/shard_map/ppermute | solution.py:493
  522.0 10.7 %collective-permute-start.60 = (f32[2,2,2,2,1,1,384]{6,5,4,3,2,1,0:T(1,128)S(1)}, f32[2,2,2,2,1,1,384]{6,5,4,3,2,1,0:T(1,128)S(1)}, u32[]{:S(2)}, u32[]{:S(2)}) collective-permute-start(f32[2,2,2,2,1,1,384]{6,5,4,3,2,1,0:T(1,128)S(1)} %fusion.21), channel_id=1, source_target_pairs={{0,1},{1,0},{2,3},{3,2},{4,5},{5,4},{6,7},{7,6},{8,9},{9,8},{10,11... | collective-permute-start | bytes 73736 | tf_op jit(solution)/shard_map/ppermute | solution.py:493
  532.8 11.4 %collective-permute-start.53 = (bf16[2,2,1,1,1,32,1152]{6,5,4,3,2,1,0:T(8,128)(2,1)S(1)}, bf16[2,2,1,1,1,32,1152]{6,5,4,3,2,1,0:T(8,128)(2,1)S(1)}, u32[]{:S(2)}, u32[]{:S(2)}) collective-permute-start(bf16[2,2,1,1,1,32,1152]{6,5,4,3,2,1,0:T(8,128)(2,1)S(1)} %constant_dynamic-slice_fusion.12), channel_id=1, source_target_pairs={{0,2},{1,3},{2,0},{3,1},{4,6},{5,7},{6,4},{7,5},{8,10},{9,11},{10,... | collective-permute-start | bytes 884744 | tf_op jit(solution)/shard_map/ppermute | solution.py:493
  535.3 15.9 %collective-permute-start.39 = (bf16[2,2,1,1,1,32,1536]{6,5,4,3,2,1,0:T(8,128)(2,1)S(1)}, bf16[2,2,1,1,1,32,1536]{6,5,4,3,2,1,0:T(8,128)(2,1)S(1)}, u32[]{:S(2)}, u32[]{:S(2)}) collective-permute-start(bf16[2,2,1,1,1,32,1536]{6,5,4,3,2,1,0:T(8,128)(2,1)S(1)} %constant_dynamic-slice_fusion.23), channel_id=1, source_target_pairs={{0,2},{1,3},{2,0},{3,1},{4,6},{5,7},{6,4},{7,5},{8,10},{9,11},{10,... | collective-permute-start | bytes 1179656 | tf_op jit(solution)/shard_map/ppermute | solution.py:493
  537.0 22.2 %collective-permute-start.44 = (bf16[2,2,2,1,1,32,768]{6,5,4,3,2,1,0:T(8,128)(2,1)S(1)}, bf16[2,2,2,1,1,32,768]{6,5,4,3,2,1,0:T(8,128)(2,1)S(1)}, u32[]{:S(2)}, u32[]{:S(2)}) collective-permute-start(bf16[2,2,2,1,1,32,768]{6,5,4,3,2,1,0:T(8,128)(2,1)S(1)} %constant_dynamic-slice_fusion.21), channel_id=1, source_target_pairs={{0,2},{1,3},{2,0},{3,1},{4,6},{5,7},{6,4},{7,5},{8,10},{9,11},{10,... | collective-permute-start | bytes 1179656 | tf_op jit(solution)/shard_map/ppermute | solution.py:493
  540.2 48.9 %collective-permute-start.59 = (bf16[1,1,1,1,1,128,1024]{6,5,4,3,2,1,0:T(8,128)(2,1)S(1)}, bf16[1,1,1,1,1,128,1024]{6,5,4,3,2,1,0:T(8,128)(2,1)S(1)}, u32[]{:S(2)}, u32[]{:S(2)}) collective-permute-start(bf16[1,1,1,1,1,128,1024]{6,5,4,3,2,1,0:T(8,128)(2,1)S(1)} %constant_dynamic-slice_fusion.8), channel_id=1, source_target_pairs={{0,16},{1,17},{2,18},{3,19},{4,20},{5,21},{6,22},{7,23},{8,24},{9,... | collective-permute-start | bytes 786440 | tf_op jit(solution)/shard_map/ppermute | solution.py:493
  542.5 17.8 %collective-permute-start.43 = (bf16[2,2,1,2,1,32,768]{6,5,4,3,2,1,0:T(8,128)(2,1)S(1)}, bf16[2,2,1,2,1,32,768]{6,5,4,3,2,1,0:T(8,128)(2,1)S(1)}, u32[]{:S(2)}, u32[]{:S(2)}) collective-permute-start(bf16[2,2,1,2,1,32,768]{6,5,4,3,2,1,0:T(8,128)(2,1)S(1)} %constant_dynamic-slice_fusion.22), channel_id=1, source_target_pairs={{0,4},{1,5},{2,6},{3,7},{4,0},{5,1},{6,2},{7,3},{8,12},{9,13},{10,... | collective-permute-start | bytes 1179656 | tf_op jit(solution)/shard_map/ppermute | solution.py:493
  544.2 45.7 %collective-permute-start.57 = (bf16[1,1,1,1,1,32,4096]{6,5,4,3,2,1,0:T(8,128)(2,1)S(1)}, bf16[1,1,1,1,1,32,4096]{6,5,4,3,2,1,0:T(8,128)(2,1)S(1)}, u32[]{:S(2)}, u32[]{:S(2)}) collective-permute-start(bf16[1,1,1,1,1,32,4096]{6,5,4,3,2,1,0:T(8,128)(2,1)S(1)} %constant_dynamic-slice_fusion.9), channel_id=1, source_target_pairs={{0,16},{1,17},{2,18},{3,19},{4,20},{5,21},{6,22},{7,23},{8,24},{9,... | collective-permute-start | bytes 786440 | tf_op jit(solution)/shard_map/ppermute | solution.py:493
  560.5 10.6 %collective-permute-start.46 = (bf16[2,2,1,1,1,32,768]{6,5,4,3,2,1,0:T(8,128)(2,1)S(1)}, bf16[2,2,1,1,1,32,768]{6,5,4,3,2,1,0:T(8,128)(2,1)S(1)}, u32[]{:S(2)}, u32[]{:S(2)}) collective-permute-start(bf16[2,2,1,1,1,32,768]{6,5,4,3,2,1,0:T(8,128)(2,1)S(1)} %constant_dynamic-slice_fusion.19), channel_id=1, source_target_pairs={{0,2},{1,3},{2,0},{3,1},{4,6},{5,7},{6,4},{7,5},{8,10},{9,11},{10,... | collective-permute-start | bytes 589832 | tf_op jit(solution)/shard_map/ppermute | solution.py:493
  568.8 11.3 %collective-permute-start.42 = (bf16[2,1,1,1,1,32,1536]{6,5,4,3,2,1,0:T(8,128)(2,1)S(1)}, bf16[2,1,1,1,1,32,1536]{6,5,4,3,2,1,0:T(8,128)(2,1)S(1)}, u32[]{:S(2)}, u32[]{:S(2)}) collective-permute-start(bf16[2,1,1,1,1,32,1536]{6,5,4,3,2,1,0:T(8,128)(2,1)S(1)} %constant_dynamic-slice_fusion.20), channel_id=1, source_target_pairs={{0,8},{1,9},{2,10},{3,11},{4,12},{5,13},{6,14},{7,15},{8,0},{9,1},... | collective-permute-start | bytes 589832 | tf_op jit(solution)/shard_map/ppermute | solution.py:493
  568.9 11.3 %collective-permute-start.63 = (f32[2,1,1,1,1,1,384]{6,5,4,3,2,1,0:T(1,128)S(1)}, f32[2,1,1,1,1,1,384]{6,5,4,3,2,1,0:T(1,128)S(1)}, u32[]{:S(2)}, u32[]{:S(2)}) collective-permute-start(f32[2,1,1,1,1,1,384]{6,5,4,3,2,1,0:T(1,128)S(1)} %constant_dynamic-slice_fusion.2), channel_id=1, source_target_pairs={{0,8},{1,9},{2,10},{3,11},{4,12},{5,13},{6,14},{7,15},{8,0},{9,1},... | collective-permute-start | bytes 9224 | tf_op jit(solution)/shard_map/ppermute | solution.py:493
  (80 other events, 1147.2 us)
